TPU v7x, 32 devices: a whole 2x2x4 slice. The times are simulated.
32 devices in a mesh: dp: 16 (over z, y, x), rep: 2 (over core).
Axes of the slice: x: 2, y: 2, z: 4, core: 2. Of those that a mesh axis runs over, the one named last changes fastest.
Arguments:
- tokens: bfloat16 [2, 16384, 768], P(None, ('dp', 'rep')), may hold values from -6 to 6
- doc_lengths: int32 [2, 32, 6], P(None, ('dp', 'rep')), may hold values from 1 to 256, 512 in all within a row
- cotangent: bfloat16 [2, 16384, 768], P(None, ('dp', 'rep')), may hold values from -6 to 6
- attn_gain: bfloat16 [768], P('dp'), may hold values from 0.5 to 1.5
- attn_shift: bfloat16 [768], P('dp'), may hold values from -1 to 1
- qkv_weight: bfloat16 [768, 2304], P('dp'), may hold values from -0.21875 to 0.21875
- qkv_bias: bfloat16 [2304], P('dp'), may hold values from -1 to 1
- out_weight: bfloat16 [768, 768], P('dp'), may hold values from -0.625 to 0.625
- out_bias: bfloat16 [768], P('dp'), may hold values from -1 to 1
- mlp_gain: bfloat16 [768], P('dp'), may hold values from 0.5 to 1.5
- mlp_shift: bfloat16 [768], P('dp'), may hold values from -1 to 1
- fc_weight: bfloat16 [768, 3072], P('dp'), may hold values from -0.21875 to 0.21875
- fc_bias: bfloat16 [3072], P('dp'), may hold values from -1 to 1
- proj_weight: bfloat16 [3072, 768], P('dp'), may hold values from -0.15625 to 0.15625
- proj_bias: bfloat16 [768], P('dp'), may hold values from -1 to 1
Outputs:
- activations: bfloat16 [2, 16384, 768], P(None, ('dp', 'rep'))
- input_grad: bfloat16 [2, 16384, 768], P(None, ('dp', 'rep'))
- grad_attn_gain: float32 [768], P('dp')
- grad_attn_shift: float32 [768], P('dp')
- grad_qkv_weight: float32 [768, 2304], P('dp')
- grad_qkv_bias: float32 [2304], P('dp')
- grad_out_weight: float32 [768, 768], P('dp')
- grad_out_bias: float32 [768], P('dp')
- grad_mlp_gain: float32 [768], P('dp')
- grad_mlp_shift: float32 [768], P('dp')
- grad_fc_weight: float32 [768, 3072], P('dp')
- grad_fc_bias: float32 [3072], P('dp')
- grad_proj_weight: float32 [3072, 768], P('dp')
- grad_proj_bias: float32 [768], P('dp')
Inputs may be any that keep to these rules, and one draw needn't show every extreme that they name: `doc_lengths`: each row of 6 lengths sums to 512, and its largest is 256.
All inputs are finite; a program needn't handle non-finite values.
Results may differ from a plain program's by a relative error of at most 0.015.
Values may be sent and summed in bfloat16 or wider, within the bound.
No kernel may reach another device: no remote copies, remote signals or barrier semaphores. Data moves between devices by JAX's collectives and lax.ppermute only.
A program may use at most 320 MiB of HBM per device.

v0:
```python
import functools

import jax
import jax.numpy as jnp
from jax import lax
from jax.experimental import pallas as pl
from jax.experimental.pallas import tpu as pltpu
from jax.sharding import PartitionSpec as P

H = 12
HD = 64
USES = 2
BOTH = ("dp", "rep")


eps_norm = 1e-05


def layer_norm(values, gain, shift):
    center = values - jnp.mean(values, axis=-1, keepdims=True)
    spread = jnp.mean(center * center, axis=-1, keepdims=True)
    return center * lax.rsqrt(spread + eps_norm) * gain + shift


def segment_ids(lengths_row, count):
    ends = jnp.cumsum(lengths_row)
    places = jnp.arange(count, dtype=jnp.int32)
    return jnp.sum((places[:, None] >= ends[None, :]).astype(jnp.int32), axis=1)


def outer_sum(left, right):
    return lax.dot_general(
        left, right, (((0,), (0,)), ((), ())), preferred_element_type=jnp.float32
    )


def times_transpose(left, right):
    return lax.dot_general(
        left, right, (((1,), (1,)), ((), ())), preferred_element_type=jnp.float32
    )


def swap(value, bits):
    return lax.ppermute(value, BOTH, [(i, i ^ bits) for i in range(32)])


CORE, X, Y, Z1, Z2, Z3 = (1, 2, 4, 8, 16, 24)


def place_kernel(me_ref, *refs):
    sources, (target, sems) = (refs[:16], refs[16:])
    me = me_ref[0]
    copies = []
    for slot, source in enumerate(sources):
        core, rest = (slot // 8, slot % 8)
        for inner in range(2):
            z_rel = (rest // 4) * 2 + inner
            rel = z_rel * 8 + (rest % 4) * 2 + core
            copies.append(
                pltpu.make_async_copy(
                    source.at[inner], target.at[rel ^ me], sems.at[2 * slot + inner]
                )
            )
    for copy in copies:
        copy.start()
    for copy in copies:
        copy.wait()


def place(me, sources, rows, width):
    placed = pl.pallas_call(
        place_kernel,
        out_shape=jax.ShapeDtypeStruct((32, rows, width), jnp.bfloat16),
        in_specs=[pl.BlockSpec(memory_space=pltpu.SMEM)]
        + [pl.BlockSpec(memory_space=pl.ANY)] * 16,
        out_specs=pl.BlockSpec(memory_space=pltpu.VMEM),
        scratch_shapes=[pltpu.SemaphoreType.DMA((32,))],
    )(me, *sources)
    return placed.reshape(32 * rows, width)


def gather_rows(piece, me):
    rows, width = piece.shape
    piece = piece[None]
    first, second, third = (swap(piece, Z1), swap(piece, Z2), swap(piece, Z3))
    near = jnp.concatenate([piece, first])
    far = jnp.concatenate([second, third])
    near_y, near_x = (swap(near, Y), swap(near, X))
    far_x, far_y = (swap(far, X), swap(far, Y))
    near_xy = swap(near_y, X)
    far_xy = swap(far_x, Y)
    mine = [near, near_x, near_y, near_xy, far, far_x, far_y, far_xy]
    theirs = [swap(part, CORE) for part in mine]
    return place(me, mine + theirs, rows, width)


def pick(array, axis, index):
    return lax.dynamic_index_in_dim(array, index, axis, keepdims=False)


def low(value):
    return value.astype(jnp.bfloat16)


def wide(value):
    return value.astype(jnp.float32)


def reduce_rows(grad, spot):
    z_pair, z_low, y, x, core = spot
    rows, width = (grad.shape[0] // 32, grad.shape[1])
    parts = grad.reshape(2, 2, 2, 2, 2, rows, width)
    got = swap(pick(parts, 4, 1 - core), CORE)
    mine = pick(parts, 4, core)
    near, near_got = (pick(mine, 0, z_pair), pick(got, 0, z_pair))
    far, far_got = (pick(mine, 0, 1 - z_pair), pick(got, 0, 1 - z_pair))

    def add(left, right):
        return low(wide(left) + wide(right))

    near_sent = swap(add(pick(near, 2, 1 - x), pick(near_got, 2, 1 - x)), X)
    far_sent = swap(add(pick(far, 1, 1 - y), pick(far_got, 1, 1 - y)), Y)

    def add3(left, middle, right):
        return low(wide(left) + wide(middle) + wide(right))

    near_x, near_x_got = (pick(near, 2, x), pick(near_got, 2, x))
    far_y, far_y_got = (pick(far, 1, y), pick(far_got, 1, y))
    near_next = swap(
        add3(pick(near_x, 1, 1 - y), pick(near_x_got, 1, 1 - y), pick(near_sent, 1, 1 - y)), Y
    )
    far_next = swap(
        add3(pick(far_y, 1, 1 - x), pick(far_y_got, 1, 1 - x), pick(far_sent, 1, 1 - x)), X
    )

    def add4(a, b, c, d):
        return wide(a) + wide(b) + wide(c) + wide(d)

    near_last = (pick(near_x, 1, y), pick(near_x_got, 1, y), pick(near_sent, 1, y), near_next)
    far_last = (pick(far_y, 1, x), pick(far_y_got, 1, x), pick(far_sent, 1, x), far_next)

    def row(parts4, index):
        return add4(*[pick(part, 0, index) for part in parts4])

    one = swap(low(row(near_last, 1 - z_low)), Z1)
    two = swap(low(row(far_last, z_low)), Z2)
    three = swap(low(row(far_last, 1 - z_low)), Z3)
    return row(near_last, z_low) + wide(one) + wide(two) + wide(three)


def both_halves(half, core):
    other = swap(half, CORE)
    return jnp.where(
        core == 0, jnp.concatenate([half, other]), jnp.concatenate([other, half])
    )


def gather_small(pieces, spot):
    z_pair, z_low, y, x, core = spot
    sizes = [piece.shape[0] for piece in pieces]
    packed = jnp.concatenate(pieces)
    packed = jnp.pad(packed, (0, 1024 - packed.shape[0])).reshape(8, 128)
    group = jnp.stack([packed, swap(packed, Z1), swap(packed, Z2), swap(packed, Z3)])
    group = jnp.stack([group, swap(group, X)])
    group = jnp.stack([group, swap(group, Y)])
    group = group.reshape(2, 2, 2, 2, 1024)
    for axis, bit in enumerate((y, x, z_pair, z_low)):
        group = jnp.where(bit == 1, jnp.flip(group, axis), group)
    group = jnp.transpose(group, (2, 3, 0, 1, 4)).reshape(16, 1024)
    vectors, start = ([], 0)
    for size in sizes:
        vectors.append(group[:, start : start + size].reshape(-1))
        start += size
    return vectors


def reduce_small(vectors, dp):
    sizes = [vector.shape[0] // 16 for vector in vectors]
    packed = jnp.concatenate([vector.reshape(16, -1) for vector in vectors], axis=1)
    packed = jnp.pad(packed, ((0, 0), (0, 640 - packed.shape[1])))
    for bits in (CORE, X, Y, Z1, Z2):
        packed = packed + swap(packed, bits)
    own = pick(packed, 0, dp)
    parts, start = ([], 0)
    for size in sizes:
        parts.append(own[start : start + size])
        start += size
    return parts


def gather_all(weights, spot, me):
    gain_a, shift_a, qkv, qbias, out, obias, gain_m, shift_m, fc, fbias, proj, pbias = weights
    core = spot[4]

    def half(weight):
        rows = weight.shape[0] // 2
        return lax.dynamic_slice_in_dim(weight, core * rows, rows, 0)

    small = gather_small([gain_a, shift_a, qbias, obias, gain_m, shift_m, fbias, pbias], spot)
    first = gather_rows(jnp.concatenate([half(qkv), half(out)], axis=1), me)
    whole_fc = gather_rows(half(fc), me)
    whole_proj = gather_rows(half(proj), me)
    width = qkv.shape[1]
    gain_a, shift_a, qbias, obias, gain_m, shift_m, fbias, pbias = small
    return (
        gain_a,
        shift_a,
        first[:, :width],
        qbias,
        first[:, width:],
        obias,
        gain_m,
        shift_m,
        whole_fc,
        fbias,
        whole_proj,
        pbias,
    )


def reduce_all(grads, spot, dp):
    core = spot[4]
    matrices = {}
    for index in (10, 8, 4, 2):
        matrices[index] = both_halves(reduce_rows(low(grads[index]), spot), core)
    order = (0, 1, 3, 5, 6, 7, 9, 11)
    small = reduce_small([grads[index] for index in order], dp)
    result = list(grads)
    for index, part in zip(order, small):
        result[index] = part
    for index, part in matrices.items():
        result[index] = part
    return tuple(result)


def block_scores(query, keys, segs, start, length):
    count = keys.shape[0]
    query_pos = start + jnp.arange(length, dtype=jnp.int32)
    key_pos = jnp.arange(count, dtype=jnp.int32)
    allowed = (segs[:, None] == segs[None, :]) & (key_pos[None, :] <= query_pos[:, None])
    scores = jnp.einsum("qhd,khd->hqk", query, keys, preferred_element_type=jnp.float32) * 0.125
    return jnp.where(allowed[None], scores, -1e30)


def attend_forward(query, keys, values, segs):
    count = query.shape[0]
    scores = block_scores(query, keys, segs, 0, count)
    top = jnp.max(scores, axis=-1, keepdims=True)
    expo = jnp.exp(scores - top)
    total = jnp.sum(expo, axis=-1, keepdims=True)
    probs = (expo / total).astype(jnp.bfloat16)
    result = jnp.einsum("hqk,khd->qhd", probs, values, preferred_element_type=jnp.float32)
    return (result.astype(jnp.bfloat16).reshape(count, H * HD), (top + jnp.log(total))[..., 0])


def attend_backward(query, keys, values, segs, logsum, grad_att):
    count = query.shape[0]
    scores = block_scores(query, keys, segs, 0, count)
    probs = jnp.exp(scores - logsum[..., None])
    grad_values = jnp.einsum(
        "hqk,qhd->khd", probs.astype(jnp.bfloat16), grad_att, preferred_element_type=jnp.float32
    )
    grad_probs = jnp.einsum("qhd,khd->hqk", grad_att, values, preferred_element_type=jnp.float32)
    grad_scores = probs * (grad_probs - jnp.sum(probs * grad_probs, axis=-1, keepdims=True))
    score_low = grad_scores.astype(jnp.bfloat16)
    grad_query = (
        jnp.einsum("hqk,khd->qhd", score_low, keys, preferred_element_type=jnp.float32) * 0.125
    )
    grad_keys = (
        jnp.einsum("hqk,qhd->khd", score_low, query, preferred_element_type=jnp.float32) * 0.125
    )
    return jnp.stack([grad_query, grad_keys, grad_values], axis=1).reshape(count, 3 * H * HD)


def layer_forward(inputs, weights, segs):
    tokens = segs[0].shape[0]
    normed_a = low(layer_norm(inputs, wide(weights[0]), wide(weights[1])))
    mixed = low(
        jnp.dot(normed_a, weights[2], preferred_element_type=jnp.float32) + wide(weights[3])
    )
    attended, logsum = ([], [])
    for index, seg in enumerate(segs):
        heads = mixed[index * tokens : (index + 1) * tokens].reshape(tokens, 3, H, HD)
        one, log_one = attend_forward(heads[:, 0], heads[:, 1], heads[:, 2], seg)
        attended.append(one)
        logsum.append(log_one)
    attended = jnp.concatenate(attended)
    hidden = inputs + (
        jnp.dot(attended, weights[4], preferred_element_type=jnp.float32) + wide(weights[5])
    )
    normed_m = low(layer_norm(hidden, wide(weights[6]), wide(weights[7])))
    expanded = jnp.dot(normed_m, weights[8], preferred_element_type=jnp.float32) + wide(weights[9])
    activated = low(jax.nn.gelu(expanded, approximate=True))
    result = hidden + (
        jnp.dot(activated, weights[10], preferred_element_type=jnp.float32) + wide(weights[11])
    )
    return (
        result,
        (inputs, normed_a, mixed, logsum, attended, hidden, normed_m, expanded, activated),
    )


def layer_backward(grad, weights, saved, segs):
    inputs, normed_a, mixed, logsum, attended, hidden, normed_m, expanded, activated = saved
    tokens = segs[0].shape[0]
    grad_low = low(grad)
    grad_proj = outer_sum(activated, grad_low)
    grad_pbias = jnp.sum(wide(grad_low), axis=0)
    grad_act = times_transpose(grad_low, weights[10])
    unused, gelu_back = jax.vjp(lambda point: jax.nn.gelu(point, approximate=True), expanded)
    grad_exp = low(gelu_back(grad_act)[0])
    grad_fc = outer_sum(normed_m, grad_exp)
    grad_fbias = jnp.sum(wide(grad_exp), axis=0)
    grad_normm = times_transpose(grad_exp, weights[8])
    unused, norm_back = jax.vjp(layer_norm, hidden, wide(weights[6]), wide(weights[7]))
    grad_norm, grad_mgain, grad_mshift = norm_back(grad_normm)
    grad_hidden = grad + grad_norm
    hidden_low = low(grad_hidden)
    grad_out = outer_sum(attended, hidden_low)
    grad_obias = jnp.sum(wide(hidden_low), axis=0)
    grad_att = low(times_transpose(hidden_low, weights[4]))
    grad_mixed = []
    for index, seg in enumerate(segs):
        rows = slice(index * tokens, (index + 1) * tokens)
        heads = mixed[rows].reshape(tokens, 3, H, HD)
        grad_mixed.append(
            attend_backward(
                heads[:, 0],
                heads[:, 1],
                heads[:, 2],
                seg,
                logsum[index],
                grad_att[rows].reshape(tokens, H, HD),
            )
        )
    grad_mixed = low(jnp.concatenate(grad_mixed))
    grad_qkv = outer_sum(normed_a, grad_mixed)
    grad_qbias = jnp.sum(wide(grad_mixed), axis=0)
    grad_norma = times_transpose(grad_mixed, weights[2])
    unused, first_back = jax.vjp(layer_norm, inputs, wide(weights[0]), wide(weights[1]))
    grad_inputs, grad_again, grad_ashift = first_back(grad_norma)
    grads = (
        grad_again,
        grad_ashift,
        grad_qkv,
        grad_qbias,
        grad_out,
        grad_obias,
        grad_mgain,
        grad_mshift,
        grad_fc,
        grad_fbias,
        grad_proj,
        grad_pbias,
    )
    return (grad_hidden + grad_inputs, grads)


def shards(custom, tokens, doc_lengths, cotangent, *weights):
    micro, count, width = tokens.shape
    dp, core = (lax.axis_index("dp"), lax.axis_index("rep"))
    spot = (dp // 8, dp // 4 % 2, dp // 2 % 2, dp % 2, core)
    me = (dp * 2 + core).astype(jnp.int32).reshape(1)
    if custom:
        whole = gather_all(weights, spot, me)
    else:
        whole = tuple(lax.all_gather(weight, "dp", axis=0, tiled=True) for weight in weights)
    segs = [segment_ids(doc_lengths[index, 0], count) for index in range(micro)]
    current = wide(tokens.reshape(micro * count, width))
    kept = []
    for use in range(USES):
        current, saved = layer_forward(current, whole, segs)
        kept.append(saved)
    grad = wide(cotangent.reshape(micro * count, width))
    summed = None
    for use in range(USES - 1, -1, -1):
        grad, grads = layer_backward(grad, whole, kept[use], segs)
        summed = grads if summed is None else jax.tree.map(jnp.add, summed, grads)
    if custom:
        final = reduce_all(summed, spot, dp)
    else:
        final = tuple(
            wide(
                lax.psum(
                    low(lax.psum_scatter(value, "dp", scatter_dimension=0, tiled=True)), "rep"
                )
            )
            for value in summed
        )
    return (low(current).reshape(tokens.shape), low(grad).reshape(tokens.shape), *final)


def solution(mesh):
    custom = mesh.shape["dp"] == 16 and mesh.shape["rep"] == 2
    placed = tuple(
        P("dp", None) if index in (2, 4, 8, 10) else P("dp") for index in range(12)
    )
    rows = P(None, BOTH, None)
    return jax.shard_map(
        functools.partial(shards, custom),
        mesh=mesh,
        in_specs=(rows, rows, rows, *placed),
        out_specs=(rows, rows, *placed),
        check_vma=False,
    )
```

profile of v0, /device:TPU:1, one launch (start us, length us, event | category | flops | bytes accessed | tf_op | source)
XLA Modules:
  0.0 664.1 jit_solution(1409686256324416297)
XLA Ops:
  0.7 5.6 concatenate.67
  6.2 4.2 collective-permute-start.2
  10.8 3.2 collective-permute-start.44
  37.5 3.6 collective-permute-done.5
  42.2 5.7 collective-permute-done.9
  48.2 6.6 collective-permute-done.10
  54.8 8.8 %collective-permute-start.14 = (bf16[2,24,3072]{2,1,0:T(8,128)(2,1)S(1)}, bf16[2,24,3072]{2,1,0:T(8,128)(2,1)S(1)}, u32[]{:S(2)}, u32[]{:S(2)}) collective-permute-start(bf16[2,24,3072]{2,1,0:T(8,128)(2,1)S(1)} %pad_maximum_fusion.16.refs_0_), channel_id=1, source_target_pairs={{0,1},{1,0},{2,3},{3,2},{4,5},{5,4},{6,7},{7,6},{8,9},{9,8},{10,11... | collective-permute-start | bytes 884744 | tf_op jit(solution)/shard_map/ppermute | solution.py:44
  71.2 5.9 collective-permute-done.26
  81.5 4.7 collective-permute-done.12.refs_6_
  88.0 4.5 collective-permute-done.13.refs_7_
  98.4 4.8 shard_map.254
  103.2 6.3 add_convert_fusion.3
  112.1 4.3 copy.172
  116.4 4.3 copy.174
  120.7 3.4 fusion.42
  128.7 5.8 fusion.77
  141.3 4.7 fusion.78
  150.2 3.7 collective-permute-done.25.refs_3_
  163.9 4.8 shard_map.255
  175.0 10.7 %fusion.190 = f32[1024,3072]{1,0:T(8,128)} fusion(bf16[768,3072]{1,0:T(8,128)(2,1)} %bitcast.717, f32[1024,768]{1,0:T(8,128)S(1)} %copy-done.13, f32[768]{0:T(1024)S(1)} %reshape.1036, f32[768]{0:T(1024)S(1)} %reshape.1035, f32[1024]{0:T(1024)S(1)} %fusion.157, f32[1024]{0:T(1024)S(1)} %broadcast_multiply_fusion.2), kind=kOutput, calls=%fused_computation.420 | convolution fusion | flops 4835770368 | bytes 20461568 | tf_op jit(solution)/shard_map/dot_general | solution.py:292
  192.6 4.8 shard_map.256
  197.5 12.2 %fusion.205 = (f32[1024]{0:T(1024)S(1)}, f32[1024,768]{1,0:T(8,128)S(1)}) fusion(f32[1024,768]{1,0:T(8,128)S(1)} %copy-done.13, f32[768]{0:T(1024)S(1)} %copy-done.123, bf16[3072,768]{1,0:T(8,128)(2,1)} %bitcast.723, f32[1024,3072]{1,0:T(8,128)} %fusion.190, f32[3072]{0:T(1024)S(1)} %copy-done.118), kind=kOutput, calls=%fused_computation.433 | convolution fusion | flops 4865653760 | bytes 23612416 | tf_op jit(solution)/shard_map/dot_general | solution.py:295
  210.3 6.9 %add_convert_fusion.2 = bf16[1024,2304]{1,0:T(8,128)(2,1)S(1)} fusion(f32[2304]{0:T(1024)S(1)} %copy-done.121, bf16[768,3072]{1,0:T(8,128)(2,1)} %bitcast.707, f32[1024,768]{1,0:T(8,128)S(1)} %get-tuple-element.102, f32[1024]{0:T(1024)S(1)} %fusion.158, f32[1024]{0:T(1024)S(1)} %broadcast_multiply_fusion.1, f32[768]{0:T(1024)S(1)} %copy-done.113, ...), kind=kOutput, calls=%fused_computation.63 | convolution fusion | flops 3632529408 | bytes 11426816 | tf_op jit(solution)/shard_map/dot_general | solution.py:279
  219.8 3.2 copy.178
  229.7 4.4 fusion.75
  241.7 3.8 fusion.76
  249.3 10.7 %fusion.192 = f32[1024,3072]{1,0:T(8,128)} fusion(bf16[768,3072]{1,0:T(8,128)(2,1)} %bitcast.718, f32[1024,768]{1,0:T(8,128)S(1)} %get-tuple-element.108, f32[1024]{0:T(1024)S(1)} %fusion.159, f32[1024]{0:T(1024)S(1)} %broadcast_multiply_fusion, f32[768]{0:T(1024)S(1)} %reshape.1036, f32[768]{0:T(1024)S(1)} %reshape.1035), kind=kOutput, calls=%fused_computation.422 | convolution fusion | flops 4835770368 | bytes 20461568 | tf_op jit(solution)/shard_map/dot_general | solution.py:292
  260.0 11.8 %add_convert_fusion.6 = bf16[1024,768]{1,0:T(8,128)(2,1)} fusion(f32[1024,768]{1,0:T(8,128)S(1)} %get-tuple-element.108, bf16[3072,768]{1,0:T(8,128)(2,1)S(1)} %bitcast.728, f32[768]{0:T(1024)S(1)} %copy-done.123, f32[1024,3072]{1,0:T(8,128)} %fusion.192, f32[3072]{0:T(1024)S(1)} %copy-done.118), kind=kOutput, calls=%fused_computation.117 | convolution fusion | flops 4865654784 | bytes 22035456 | tf_op jit(solution)/shard_map/dot_general | solution.py:295
  271.8 16.8 %convert_reduce_fusion.1 = (f32[3072]{0:T(1024)}, bf16[1024,3072]{1,0:T(8,128)(2,1)}) fusion(f32[1024,3072]{1,0:T(8,128)} %fusion.192, f32[3072]{0:T(1024)S(1)} %copy-done.118, bf16[3072,768]{1,0:T(8,128)(2,1)} %bitcast.724, bf16[1024,768]{1,0:T(8,128)(2,1)S(1)} %bitcast.684), kind=kOutput, calls=%fused_computation.24 | convolution fusion | flops 4904186880 | bytes 25190400 | tf_op jit(solution)/shard_map/dot_general | solution.py:38
  288.7 12.9 %fusion.193 = f32[3072,768]{1,0:T(8,128)} fusion(bf16[1024,768]{1,0:T(8,128)(2,1)S(1)} %bitcast.685, f32[1024,3072]{1,0:T(8,128)} %fusion.192, f32[3072]{0:T(1024)S(1)} %copy-done.118), kind=kOutput, calls=%fused_computation.423 | convolution fusion | flops 4863295488 | bytes 23605248 | tf_op jit(solution)/shard_map/dot_general | solution.py:32
  301.5 9.8 %multiply_reduce_fusion.5 = (f32[768]{0:T(1024)}, f32[1024]{0:T(1024)S(1)}, f32[768]{0:T(1024)}, f32[1024,768]{1,0:T(8,128)S(1)}) fusion(f32[1024,768]{1,0:T(8,128)S(1)} %get-tuple-element.108, f32[1024]{0:T(1024)S(1)} %fusion.159, f32[1024]{0:T(1024)S(1)} %broadcast_multiply_fusion, f32[768]{0:T(1024)S(1)} %reshape.1035, ...), kind=kOutput, calls=%fused_computation.106 | convolution fusion | flops 4838126592 | bytes 17323008 | tf_op jit(solution)/shard_map/dot_general | solution.py:38
  311.3 10.7 %fusion.191 = f32[768,3072]{1,0:T(8,128)} fusion(bf16[1024,3072]{1,0:T(8,128)(2,1)} %get-tuple-element.122, f32[1024,768]{1,0:T(8,128)S(1)} %get-tuple-element.108, f32[1024]{0:T(1024)S(1)} %fusion.159, f32[1024]{0:T(1024)S(1)} %broadcast_multiply_fusion, f32[768]{0:T(1024)S(1)} %reshape.1036, f32[768]{0:T(1024)S(1)} %reshape.1035), kind=kOutput, calls=%fused_computation.421 | convolution fusion | flops 4835770368 | bytes 18888704 | tf_op jit(solution)/shard_map/dot_general | solution.py:32
  331.9 3.9 fusion.89
  335.8 7.8 %multiply_reduce_fusion.3 = (f32[12,512]{1,0:T(8,128)S(1)}, f32[12,512,512]{1,2,0:T(8,128)}) fusion(f32[12,512]{1,0:T(8,128)S(1)} %log_add_fusion.3, f32[12,512,512]{1,2,0:T(8,128)S(1)} %get-tuple-element.106, pred[512,512]{0,1:T(8,128)(4,1)S(1)} %copy-done.20, bf16[512,12,64]{0,2,1:T(8,128)(2,1)S(1)} %bitcast.739, bf16[512,3,12,64]{0,3,2,1:T(8,128)(2,1)} %bitcast.674), kind=kOutput, calls=%fused_computation.35 | convolution fusion | flops 418375680 | bytes 27049984 | tf_op jit(solution)/shard_map/qhd,khd->hqk/dot_general | solution.py:263
  343.6 10.8 %multiply_convert_fusion.3 = bf16[12,512,512]{1,2,0:T(8,128)(2,1)} fusion(f32[12,512,512]{1,2,0:T(8,128)} %get-tuple-element.113, f32[12,512]{1,0:T(8,128)S(1)} %get-tuple-element.112, f32[12,512]{1,0:T(8,128)S(1)} %log_add_fusion.3, f32[12,512,512]{1,2,0:T(8,128)S(1)} %get-tuple-element.106, pred[512,512]{0,1:T(8,128)(4,1)} %copy-done.18), kind=kLoop, calls=%fused_computation.34 | loop fusion | flops 18874368 | bytes 31768576 | tf_op jit(solution)/shard_map/convert_element_type | solution.py:265
  354.4 4.9 fusion.93
  359.4 4.9 fusion.92
  364.3 3.9 fusion.86
  368.3 7.8 %multiply_reduce_fusion.2 = (f32[12,512]{1,0:T(8,128)S(1)}, f32[12,512,512]{1,2,0:T(8,128)}) fusion(f32[12,512]{1,0:T(8,128)S(1)} %copy-done.91, f32[12,512,512]{1,2,0:T(8,128)S(1)} %bitcast.654, pred[512,512]{0,1:T(8,128)(4,1)S(1)} %copy-done.16, bf16[512,12,64]{0,2,1:T(8,128)(2,1)S(1)} %bitcast.737, bf16[512,3,12,64]{0,3,2,1:T(8,128)(2,1)} %bitcast.669), kind=kOutput, calls=%fused_computation.32 | convolution fusion | flops 418375680 | bytes 27049984 | tf_op jit(solution)/shard_map/qhd,khd->hqk/dot_general | solution.py:263
  376.1 7.3 %multiply_convert_fusion.2 = bf16[12,512,512]{1,2,0:T(8,128)(2,1)S(1)} fusion(f32[12,512,512]{1,2,0:T(8,128)} %get-tuple-element.111, f32[12,512]{1,0:T(8,128)S(1)} %get-tuple-element.110, f32[12,512]{1,0:T(8,128)S(1)} %copy-done.91, f32[12,512,512]{1,2,0:T(8,128)S(1)} %bitcast.654, pred[512,512]{0,1:T(8,128)(4,1)S(1)} %copy-done.16), kind=kLoop, calls=%fused_computation.31 | loop fusion | flops 18874368 | bytes 31768576 | tf_op jit(solution)/shard_map/convert_element_type | solution.py:265
  390.5 5.2 multiply_reduce_fusion.6
  395.7 7.2 %fusion.79 = f32[768,2304]{1,0:T(8,128)} fusion(bf16[512,2304]{0,1:T(8,128)(2,1)S(1)} %bitcast.697, bf16[512,2304]{0,1:T(8,128)(2,1)S(1)} %bitcast.694, f32[1024,768]{1,0:T(8,128)S(1)} %copy-done.35, f32[1024]{0:T(1024)S(1)} %copy-done.117, f32[1024]{0:T(1024)S(1)} %copy-done.103, f32[768]{0:T(1024)S(1)} %copy-done.114, f32[768]{0:T(1024)S(1)} %copy-done.96), kind=kOutput, calls=%fused_computation.161 | convolution fusion | flops 3637248000 | bytes 14956544 | tf_op jit(solution)/shard_map/dot_general | solution.py:32
  405.5 17.5 %convert_reduce_fusion = (f32[3072]{0:T(1024)S(1)}, bf16[1024,3072]{1,0:T(8,128)(2,1)}) fusion(f32[1024,3072]{1,0:T(8,128)} %fusion.190, f32[3072]{0:T(1024)S(1)} %copy-done.119, bf16[3072,768]{1,0:T(8,128)(2,1)} %bitcast.725, f32[1024,768]{1,0:T(8,128)S(1)} %get-tuple-element.28), kind=kOutput, calls=%fused_computation.23 | convolution fusion | flops 4904973312 | bytes 26763264 | tf_op jit(solution)/shard_map/dot_general | solution.py:38
  423.0 7.9 %multiply_reduce_fusion.4 = (f32[768]{0:T(1024)S(1)}, f32[1024]{0:T(1024)S(1)}, f32[768]{0:T(1024)S(1)}, f32[1024,768]{1,0:T(8,128)S(1)}) fusion(f32[1024,768]{1,0:T(8,128)S(1)} %copy-done.14, f32[1024]{0:T(1024)S(1)} %copy-done.93, f32[1024]{0:T(1024)S(1)} %copy-done.57, f32[768]{0:T(1024)S(1)} %reshape.1035, bf16[1024,3072]{1,0:T(8,128)(2,1)} %get-tuple-element.124, ...), kind=kOutput, calls=%fused_computation.105 | convolution fusion | flops 4838126592 | bytes 17323008 | tf_op jit(solution)/shard_map/dot_general | solution.py:38
  434.0 4.0 convolution_convert_fusion
  439.1 3.9 fusion.83
  443.0 7.5 %multiply_reduce_fusion.1 = (f32[12,512]{1,0:T(8,128)S(1)}, f32[12,512,512]{1,2,0:T(8,128)}) fusion(f32[12,512]{1,0:T(8,128)S(1)} %copy-done.90, f32[12,512,512]{1,2,0:T(8,128)S(1)} %bitcast.652, pred[512,512]{0,1:T(8,128)(4,1)S(1)} %copy-done.21, bf16[512,12,64]{0,2,1:T(8,128)(2,1)S(1)} %bitcast.741, bf16[512,3,12,64]{0,3,2,1:T(8,128)(2,1)S(1)} %bitcast.664), kind=kOutput, calls=%fused_computation.29 | convolution fusion | flops 418375680 | bytes 27058176 | tf_op jit(solution)/shard_map/qhd,khd->hqk/dot_general | solution.py:263
  450.5 10.8 %multiply_convert_fusion.1 = bf16[12,512,512]{1,2,0:T(8,128)(2,1)} fusion(f32[12,512,512]{1,2,0:T(8,128)} %get-tuple-element.119, f32[12,512]{1,0:T(8,128)S(1)} %get-tuple-element.118, f32[12,512]{1,0:T(8,128)S(1)} %copy-done.90, f32[12,512,512]{1,2,0:T(8,128)S(1)} %bitcast.652, pred[512,512]{0,1:T(8,128)(4,1)S(1)} %copy-done.21), kind=kLoop, calls=%fused_computation.28 | loop fusion | flops 18874368 | bytes 31768576 | tf_op jit(solution)/shard_map/convert_element_type | solution.py:265
  461.3 5.8 fusion.97
  467.1 4.9 fusion.96
  475.2 7.0 %multiply_reduce_fusion = (f32[12,512]{1,0:T(8,128)S(1)}, f32[12,512,512]{1,2,0:T(8,128)}) fusion(f32[12,512]{1,0:T(8,128)S(1)} %copy-done.89, f32[12,512,512]{1,2,0:T(8,128)S(1)} %bitcast.650, pred[512,512]{0,1:T(8,128)(4,1)S(1)} %copy-done.17, bf16[512,12,64]{0,2,1:T(8,128)(2,1)S(1)} %bitcast.735, bf16[512,3,12,64]{0,3,2,1:T(8,128)(2,1)S(1)} %bitcast.659), kind=kOutput, calls=%fused_computation.26 | convolution fusion | flops 418375680 | bytes 27058176 | tf_op jit(solution)/shard_map/qhd,khd->hqk/dot_general | solution.py:263
  482.3 7.1 %multiply_convert_fusion = bf16[12,512,512]{1,2,0:T(8,128)(2,1)S(1)} fusion(f32[12,512,512]{1,2,0:T(8,128)} %get-tuple-element.117, f32[12,512]{1,0:T(8,128)S(1)} %get-tuple-element.116, f32[12,512]{1,0:T(8,128)S(1)} %copy-done.89, f32[12,512,512]{1,2,0:T(8,128)S(1)} %bitcast.650, pred[512,512]{0,1:T(8,128)(4,1)S(1)} %copy-done.17), kind=kLoop, calls=%fused_computation.25 | loop fusion | flops 18874368 | bytes 31768576 | tf_op jit(solution)/shard_map/convert_element_type | solution.py:265
  495.9 6.2 fusion.194
  504.0 13.8 %add_convert_fusion = bf16[3072,768]{1,0:T(8,128)(2,1)} fusion(f32[3072,768]{1,0:T(8,128)} %fusion.193, f32[1024,768]{1,0:T(8,128)S(1)} %copy-done.8, f32[1024,3072]{1,0:T(8,128)} %fusion.190, f32[3072]{0:T(1024)S(1)} %copy-done.119), kind=kOutput, calls=%fused_computation.59 | convolution fusion | flops 4868800512 | bytes 29896704 | tf_op jit(solution)/shard_map/dot_general | solution.py:32
  517.9 11.0 %add_convert_fusion.1 = bf16[768,3072]{1,0:T(8,128)(2,1)} fusion(f32[768,3072]{1,0:T(8,128)S(1)} %bitcast.656, bf16[1024,3072]{1,0:T(8,128)(2,1)} %get-tuple-element.124, f32[1024,768]{1,0:T(8,128)} %copy-done.12, f32[768]{0:T(1024)S(1)} %copy-done.55, f32[768]{0:T(1024)S(1)} %reshape.1035, f32[1024]{0:T(1024)S(1)} %copy-done.93, f32[1024]{0:T(1024)S(1)} %copy-done.57), kind=kOutput, calls=%fused_computation.60 | convolution fusion | flops 4840488960 | bytes 23607296 | tf_op jit(solution)/shard_map/dot_general | solution.py:32
  529.3 5.1 add_convert_fusion.10
  536.6 8.9 %add_convert_fusion.4 = bf16[768,2304]{1,0:T(8,128)(2,1)} fusion(f32[768,2304]{1,0:T(8,128)} %fusion.79, bf16[1024,768]{1,0:T(8,128)(2,1)S(1)} %copy-done.44, bf16[512,2304]{0,1:T(8,128)(2,1)} %bitcast.691, bf16[512,2304]{0,1:T(8,128)(2,1)} %bitcast.688), kind=kOutput, calls=%fused_computation.65 | convolution fusion | flops 3636854784 | bytes 16908288 | tf_op jit(solution)/shard_map/dot_general | solution.py:32
  583.4 6.3 collective-permute-start.78
  597.9 7.2 %collective-permute-done.89 = bf16[2,2,96,768]{3,2,1,0:T(8,128)(2,1)S(1)} collective-permute-done((bf16[2,2,96,768]{3,2,1,0:T(8,128)(2,1)S(1)}, bf16[2,2,96,768]{3,2,1,0:T(8,128)(2,1)S(1)}, u32[]{:S(2)}, u32[]{:S(2)}) %collective-permute-start.89) | collective-permute-done | bytes 589856 | tf_op jit(solution)/shard_map/ppermute | solution.py:44
  607.0 10.7 %collective-permute-done.80 = bf16[2,2,24,3072]{3,2,1,0:T(8,128)(2,1)S(1)} collective-permute-done((bf16[2,2,24,3072]{3,2,1,0:T(8,128)(2,1)S(1)}, bf16[2,2,24,3072]{3,2,1,0:T(8,128)(2,1)S(1)}, u32[]{:S(2)}, u32[]{:S(2)}) %collective-permute-start.80) | collective-permute-done | bytes 589856 | tf_op jit(solution)/shard_map/ppermute | solution.py:44
  621.3 10.7 %collective-permute-start.69 = (f32[24,2304]{1,0:T(8,128)S(1)}, f32[24,2304]{1,0:T(8,128)S(1)}, u32[]{:S(2)}, u32[]{:S(2)}) collective-permute-start(f32[24,2304]{1,0:T(8,128)S(1)} %fusion.147), channel_id=1, source_target_pairs={{0,1},{1,0},{2,3},{3,2},{4,5},{5,4},{6,7},{7,6},{8,9},{9,8},{10,11... | collective-permute-start | bytes 663560 | tf_op jit(solution)/shard_map/ppermute | solution.py:44
  636.5 9.2 %collective-permute-done.94 = bf16[96,768]{1,0:T(8,128)(2,1)S(1)} collective-permute-done((bf16[96,768]{1,0:T(8,128)(2,1)S(1)}, bf16[96,768]{1,0:T(8,128)(2,1)S(1)}, u32[]{:S(2)}, u32[]{:S(2)}) %collective-permute-start.94) | collective-permute-done | bytes 147488 | tf_op jit(solution)/shard_map/ppermute | solution.py:44
  647.2 5.1 collective-permute-start.82
  656.2 4.1 collective-permute-done.82
  (667 shorter events, 208.6 us)
Async XLA Ops:
  6.2 15.2 %collective-permute-start.2 = (bf16[8,128]{1,0:T(8,128)(2,1)S(1)}, bf16[8,128]{1,0:T(8,128)(2,1)S(1)}, u32[]{:S(2)}, u32[]{:S(2)}) collective-permute-start(bf16[8,128]{1,0:T(8,128)(2,1)S(1)} %get-tuple-element.92), channel_id=1, source_target_pairs={{0,24},{1,25},{2,26},{3,27},{4,28},{5,29},{6,30},{7,31},{8,16},{9,... | collective-permute-start | bytes 6152 | tf_op jit(solution)/shard_map/ppermute | solution.py:44
  10.4 11.4 %collective-permute-start.1 = (bf16[8,128]{1,0:T(8,128)(2,1)S(1)}, bf16[8,128]{1,0:T(8,128)(2,1)S(1)}, u32[]{:S(2)}, u32[]{:S(2)}) collective-permute-start(bf16[8,128]{1,0:T(8,128)(2,1)S(1)} %get-tuple-element.92), channel_id=1, source_target_pairs={{0,16},{1,17},{2,18},{3,19},{4,20},{5,21},{6,22},{7,23},{8,24},{9,... | collective-permute-start | bytes 6152 | tf_op jit(solution)/shard_map/ppermute | solution.py:44
  10.5 14.6 %collective-permute-start = (bf16[8,128]{1,0:T(8,128)(2,1)S(1)}, bf16[8,128]{1,0:T(8,128)(2,1)S(1)}, u32[]{:S(2)}, u32[]{:S(2)}) collective-permute-start(bf16[8,128]{1,0:T(8,128)(2,1)S(1)} %get-tuple-element.92), channel_id=1, source_target_pairs={{0,8},{1,9},{2,10},{3,11},{4,12},{5,13},{6,14},{7,15},{8,0},{9,1},... | collective-permute-start | bytes 6152 | tf_op jit(solution)/shard_map/ppermute | solution.py:44
  10.8 52.8 %collective-permute-start.44 = (bf16[1,96,768]{2,1,0:T(8,128)(2,1)S(1)}, bf16[1,96,768]{2,1,0:T(8,128)(2,1)}, u32[]{:S(2)}, u32[]{:S(2)}) collective-permute-start(bf16[1,96,768]{2,1,0:T(8,128)(2,1)S(1)} %dynamic-slice_bitcast_fusion.4), channel_id=1, source_target_pairs={{0,24},{1,25},{2,26},{3,27},{4,28},{5,29},{6,30},{7,31},{8,16},{9,... | collective-permute-start | bytes 442376 | tf_op jit(solution)/shard_map/ppermute | solution.py:44
  14.1 50.9 %collective-permute-start.43 = (bf16[1,96,768]{2,1,0:T(8,128)(2,1)S(1)}, bf16[1,96,768]{2,1,0:T(8,128)(2,1)}, u32[]{:S(2)}, u32[]{:S(2)}) collective-permute-start(bf16[1,96,768]{2,1,0:T(8,128)(2,1)S(1)} %dynamic-slice_bitcast_fusion.4), channel_id=1, source_target_pairs={{0,16},{1,17},{2,18},{3,19},{4,20},{5,21},{6,22},{7,23},{8,24},{9,... | collective-permute-start | bytes 442376 | tf_op jit(solution)/shard_map/ppermute | solution.py:44
  21.4 44.8 %collective-permute-start.39 = (bf16[1,96,768]{2,1,0:T(8,128)(2,1)S(1)}, bf16[1,96,768]{2,1,0:T(8,128)(2,1)}, u32[]{:S(2)}, u32[]{:S(2)}) collective-permute-start(bf16[1,96,768]{2,1,0:T(8,128)(2,1)S(1)} %dynamic-slice_bitcast_fusion.4), channel_id=1, source_target_pairs={{0,8},{1,9},{2,10},{3,11},{4,12},{5,13},{6,14},{7,15},{8,0},{9,1},... | collective-permute-start | bytes 442376 | tf_op jit(solution)/shard_map/ppermute | solution.py:44
  21.8 46.2 %collective-permute-start.27 = (bf16[1,24,3072]{2,1,0:T(8,128)(2,1)S(1)}, bf16[1,24,3072]{2,1,0:T(8,128)(2,1)}, u32[]{:S(2)}, u32[]{:S(2)}) collective-permute-start(bf16[1,24,3072]{2,1,0:T(8,128)(2,1)S(1)} %dynamic-slice_bitcast_fusion.5), channel_id=1, source_target_pairs={{0,24},{1,25},{2,26},{3,27},{4,28},{5,29},{6,30},{7,31},{8,16},{9,... | collective-permute-start | bytes 442376 | tf_op jit(solution)/shard_map/ppermute | solution.py:44
  54.8 22.8 %collective-permute-start.14 = (bf16[2,24,3072]{2,1,0:T(8,128)(2,1)S(1)}, bf16[2,24,3072]{2,1,0:T(8,128)(2,1)S(1)}, u32[]{:S(2)}, u32[]{:S(2)}) collective-permute-start(bf16[2,24,3072]{2,1,0:T(8,128)(2,1)S(1)} %pad_maximum_fusion.16.refs_0_), channel_id=1, source_target_pairs={{0,1},{1,0},{2,3},{3,2},{4,5},{5,4},{6,7},{7,6},{8,9},{9,8},{10,11... | collective-permute-start | bytes 884744 | tf_op jit(solution)/shard_map/ppermute | solution.py:44
  63.6 14.2 %collective-permute-start.7 = (bf16[2,24,3072]{2,1,0:T(8,128)(2,1)S(1)}, bf16[2,24,3072]{2,1,0:T(8,128)(2,1)S(1)}, u32[]{:S(2)}, u32[]{:S(2)}) collective-permute-start(bf16[2,24,3072]{2,1,0:T(8,128)(2,1)S(1)} %pad_maximum_fusion.16.refs_0_), channel_id=1, source_target_pairs={{0,4},{1,5},{2,6},{3,7},{4,0},{5,1},{6,2},{7,3},{8,12},{9,13},{10,... | collective-permute-start | bytes 884744 | tf_op jit(solution)/shard_map/ppermute | solution.py:44
  65.0 13.2 %collective-permute-start.6 = (bf16[2,24,3072]{2,1,0:T(8,128)(2,1)S(1)}, bf16[2,24,3072]{2,1,0:T(8,128)(2,1)S(1)}, u32[]{:S(2)}, u32[]{:S(2)}) collective-permute-start(bf16[2,24,3072]{2,1,0:T(8,128)(2,1)S(1)} %pad_maximum_fusion.16.refs_0_), channel_id=1, source_target_pairs={{0,2},{1,3},{2,0},{3,1},{4,6},{5,7},{6,4},{7,5},{8,10},{9,11},{10,... | collective-permute-start | bytes 884744 | tf_op jit(solution)/shard_map/ppermute | solution.py:44
  66.2 13.4 %collective-permute-start.11 = (bf16[2,24,3072]{2,1,0:T(8,128)(2,1)S(1)}, bf16[2,24,3072]{2,1,0:T(8,128)(2,1)S(1)}, u32[]{:S(2)}, u32[]{:S(2)}) collective-permute-start(bf16[2,24,3072]{2,1,0:T(8,128)(2,1)S(1)} %constant_dynamic-update-slice_fusion.refs_4_), channel_id=1, source_target_pairs={{0,2},{1,3},{2,0},{3,1},{4,6},{5,7},{6,4},{7,5},{8,10},{9,11},{10,... | collective-permute-start | bytes 884744 | tf_op jit(solution)/shard_map/ppermute | solution.py:44
  68.0 9.1 %collective-permute-start.26 = (bf16[1,24,3072]{2,1,0:T(8,128)(2,1)S(1)}, bf16[1,24,3072]{2,1,0:T(8,128)(2,1)S(1)}, u32[]{:S(2)}, u32[]{:S(2)}) collective-permute-start(bf16[1,24,3072]{2,1,0:T(8,128)(2,1)S(1)} %dynamic-slice_bitcast_fusion.5), channel_id=1, source_target_pairs={{0,16},{1,17},{2,18},{3,19},{4,20},{5,21},{6,22},{7,23},{8,24},{9,... | collective-permute-start | bytes 442376 | tf_op jit(solution)/shard_map/ppermute | solution.py:44
  77.6 8.6 %collective-permute-start.12 = (bf16[2,24,3072]{2,1,0:T(8,128)(2,1)S(1)}, bf16[2,24,3072]{2,1,0:T(8,128)(2,1)S(1)}, u32[]{:S(2)}, u32[]{:S(2)}) collective-permute-start(bf16[2,24,3072]{2,1,0:T(8,128)(2,1)S(1)} %constant_dynamic-update-slice_fusion.refs_4_), channel_id=1, source_target_pairs={{0,4},{1,5},{2,6},{3,7},{4,0},{5,1},{6,2},{7,3},{8,12},{9,13},{10,... | collective-permute-start | bytes 884744 | tf_op jit(solution)/shard_map/ppermute | solution.py:44
  77.9 9.7 %collective-permute-start.16 = (bf16[2,24,3072]{2,1,0:T(8,128)(2,1)S(1)}, bf16[2,24,3072]{2,1,0:T(8,128)(2,1)S(1)}, u32[]{:S(2)}, u32[]{:S(2)}) collective-permute-start(bf16[2,24,3072]{2,1,0:T(8,128)(2,1)S(1)} %collective-permute-done.7.refs_2_), channel_id=1, source_target_pairs={{0,1},{1,0},{2,3},{3,2},{4,5},{5,4},{6,7},{7,6},{8,9},{9,8},{10,11... | collective-permute-start | bytes 884744 | tf_op jit(solution)/shard_map/ppermute | solution.py:44
  78.2 9.4 %collective-permute-start.8 = (bf16[2,24,3072]{2,1,0:T(8,128)(2,1)S(1)}, bf16[2,24,3072]{2,1,0:T(8,128)(2,1)S(1)}, u32[]{:S(2)}, u32[]{:S(2)}) collective-permute-start(bf16[2,24,3072]{2,1,0:T(8,128)(2,1)S(1)} %collective-permute-done.7.refs_2_), channel_id=1, source_target_pairs={{0,2},{1,3},{2,0},{3,1},{4,6},{5,7},{6,4},{7,5},{8,10},{9,11},{10,... | collective-permute-start | bytes 884744 | tf_op jit(solution)/shard_map/ppermute | solution.py:44
  79.6 12.9 %collective-permute-start.13 = (bf16[2,24,3072]{2,1,0:T(8,128)(2,1)S(1)}, bf16[2,24,3072]{2,1,0:T(8,128)(2,1)S(1)}, u32[]{:S(2)}, u32[]{:S(2)}) collective-permute-start(bf16[2,24,3072]{2,1,0:T(8,128)(2,1)S(1)} %collective-permute-done.11.refs_5_), channel_id=1, source_target_pairs={{0,4},{1,5},{2,6},{3,7},{4,0},{5,1},{6,2},{7,3},{8,12},{9,13},{10,... | collective-permute-start | bytes 884744 | tf_op jit(solution)/shard_map/ppermute | solution.py:44
  80.7 14.0 %collective-permute-start.19 = (bf16[2,24,3072]{2,1,0:T(8,128)(2,1)S(1)}, bf16[2,24,3072]{2,1,0:T(8,128)(2,1)S(1)}, u32[]{:S(2)}, u32[]{:S(2)}) collective-permute-start(bf16[2,24,3072]{2,1,0:T(8,128)(2,1)S(1)} %collective-permute-done.11.refs_5_), channel_id=1, source_target_pairs={{0,1},{1,0},{2,3},{3,2},{4,5},{5,4},{6,7},{7,6},{8,9},{9,8},{10,11... | collective-permute-start | bytes 884744 | tf_op jit(solution)/shard_map/ppermute | solution.py:44
  94.3 44.8 %collective-permute-start.31 = (bf16[2,24,3072]{2,1,0:T(8,128)(2,1)S(1)}, bf16[2,24,3072]{2,1,0:T(8,128)(2,1)}, u32[]{:S(2)}, u32[]{:S(2)}) collective-permute-start(bf16[2,24,3072]{2,1,0:T(8,128)(2,1)S(1)} %pad_maximum_fusion.17.refs_0_), channel_id=1, source_target_pairs={{0,1},{1,0},{2,3},{3,2},{4,5},{5,4},{6,7},{7,6},{8,9},{9,8},{10,11... | collective-permute-start | bytes 884744 | tf_op jit(solution)/shard_map/ppermute | solution.py:44
  94.5 45.0 %collective-permute-start.24 = (bf16[2,24,3072]{2,1,0:T(8,128)(2,1)S(1)}, bf16[2,24,3072]{2,1,0:T(8,128)(2,1)}, u32[]{:S(2)}, u32[]{:S(2)}) collective-permute-start(bf16[2,24,3072]{2,1,0:T(8,128)(2,1)S(1)} %pad_maximum_fusion.17.refs_0_), channel_id=1, source_target_pairs={{0,4},{1,5},{2,6},{3,7},{4,0},{5,1},{6,2},{7,3},{8,12},{9,13},{10,... | collective-permute-start | bytes 884744 | tf_op jit(solution)/shard_map/ppermute | solution.py:44
  94.7 45.3 %collective-permute-start.23 = (bf16[2,24,3072]{2,1,0:T(8,128)(2,1)S(1)}, bf16[2,24,3072]{2,1,0:T(8,128)(2,1)}, u32[]{:S(2)}, u32[]{:S(2)}) collective-permute-start(bf16[2,24,3072]{2,1,0:T(8,128)(2,1)S(1)} %pad_maximum_fusion.17.refs_0_), channel_id=1, source_target_pairs={{0,2},{1,3},{2,0},{3,1},{4,6},{5,7},{6,4},{7,5},{8,10},{9,11},{10,... | collective-permute-start | bytes 884744 | tf_op jit(solution)/shard_map/ppermute | solution.py:44
  96.0 53.4 %collective-permute-start.35 = (bf16[2,24,3072]{2,1,0:T(8,128)(2,1)S(1)}, bf16[2,24,3072]{2,1,0:T(8,128)(2,1)}, u32[]{:S(2)}, u32[]{:S(2)}) collective-permute-start(bf16[2,24,3072]{2,1,0:T(8,128)(2,1)S(1)} %constant_dynamic-update-slice_fusion.2.refs_4_), channel_id=1, source_target_pairs={{0,1},{1,0},{2,3},{3,2},{4,5},{5,4},{6,7},{7,6},{8,9},{9,8},{10,11... | collective-permute-start | bytes 884744 | tf_op jit(solution)/shard_map/ppermute | solution.py:44
  96.9 52.7 %collective-permute-start.29 = (bf16[2,24,3072]{2,1,0:T(8,128)(2,1)S(1)}, bf16[2,24,3072]{2,1,0:T(8,128)(2,1)}, u32[]{:S(2)}, u32[]{:S(2)}) collective-permute-start(bf16[2,24,3072]{2,1,0:T(8,128)(2,1)S(1)} %constant_dynamic-update-slice_fusion.2.refs_4_), channel_id=1, source_target_pairs={{0,4},{1,5},{2,6},{3,7},{4,0},{5,1},{6,2},{7,3},{8,12},{9,13},{10,... | collective-permute-start | bytes 884744 | tf_op jit(solution)/shard_map/ppermute | solution.py:44
  139.2 8.4 %collective-permute-start.28 = (bf16[2,24,3072]{2,1,0:T(8,128)(2,1)S(1)}, bf16[2,24,3072]{2,1,0:T(8,128)(2,1)S(1)}, u32[]{:S(2)}, u32[]{:S(2)}) collective-permute-start(bf16[2,24,3072]{2,1,0:T(8,128)(2,1)S(1)} %constant_dynamic-update-slice_fusion.2.refs_4_), channel_id=1, source_target_pairs={{0,2},{1,3},{2,0},{3,1},{4,6},{5,7},{6,4},{7,5},{8,10},{9,11},{10,... | collective-permute-start | bytes 884744 | tf_op jit(solution)/shard_map/ppermute | solution.py:44
  139.5 10.5 %collective-permute-start.33 = (bf16[2,24,3072]{2,1,0:T(8,128)(2,1)}, bf16[2,24,3072]{2,1,0:T(8,128)(2,1)S(1)}, u32[]{:S(2)}, u32[]{:S(2)}) collective-permute-start(bf16[2,24,3072]{2,1,0:T(8,128)(2,1)} %collective-permute-done.24.refs_2_), channel_id=1, source_target_pairs={{0,1},{1,0},{2,3},{3,2},{4,5},{5,4},{6,7},{7,6},{8,9},{9,8},{10,11... | collective-permute-start | bytes 884744 | tf_op jit(solution)/shard_map/ppermute | solution.py:44
  140.1 13.8 %collective-permute-start.25 = (bf16[2,24,3072]{2,1,0:T(8,128)(2,1)}, bf16[2,24,3072]{2,1,0:T(8,128)(2,1)S(1)}, u32[]{:S(2)}, u32[]{:S(2)}) collective-permute-start(bf16[2,24,3072]{2,1,0:T(8,128)(2,1)} %collective-permute-done.24.refs_2_), channel_id=1, source_target_pairs={{0,2},{1,3},{2,0},{3,1},{4,6},{5,7},{6,4},{7,5},{8,10},{9,11},{10,... | collective-permute-start | bytes 884744 | tf_op jit(solution)/shard_map/ppermute | solution.py:44
  147.5 11.7 %collective-permute-start.36 = (bf16[2,24,3072]{2,1,0:T(8,128)(2,1)S(1)}, bf16[2,24,3072]{2,1,0:T(8,128)(2,1)S(1)}, u32[]{:S(2)}, u32[]{:S(2)}) collective-permute-start(bf16[2,24,3072]{2,1,0:T(8,128)(2,1)S(1)} %collective-permute-done.28.refs_5_), channel_id=1, source_target_pairs={{0,1},{1,0},{2,3},{3,2},{4,5},{5,4},{6,7},{7,6},{8,9},{9,8},{10,11... | collective-permute-start | bytes 884744 | tf_op jit(solution)/shard_map/ppermute | solution.py:44
  149.4 8.6 %collective-permute-start.30 = (bf16[2,24,3072]{2,1,0:T(8,128)(2,1)S(1)}, bf16[2,24,3072]{2,1,0:T(8,128)(2,1)S(1)}, u32[]{:S(2)}, u32[]{:S(2)}) collective-permute-start(bf16[2,24,3072]{2,1,0:T(8,128)(2,1)S(1)} %collective-permute-done.28.refs_5_), channel_id=1, source_target_pairs={{0,4},{1,5},{2,6},{3,7},{4,0},{5,1},{6,2},{7,3},{8,12},{9,13},{10,... | collective-permute-start | bytes 884744 | tf_op jit(solution)/shard_map/ppermute | solution.py:44
  149.7 9.2 %collective-permute-start.32 = (bf16[2,24,3072]{2,1,0:T(8,128)(2,1)}, bf16[2,24,3072]{2,1,0:T(8,128)(2,1)S(1)}, u32[]{:S(2)}, u32[]{:S(2)}) collective-permute-start(bf16[2,24,3072]{2,1,0:T(8,128)(2,1)} %collective-permute-done.23.refs_1_), channel_id=1, source_target_pairs={{0,1},{1,0},{2,3},{3,2},{4,5},{5,4},{6,7},{7,6},{8,9},{9,8},{10,11... | collective-permute-start | bytes 884744 | tf_op jit(solution)/shard_map/ppermute | solution.py:44
  150.0 8.9 %collective-permute-start.37 = (bf16[2,24,3072]{2,1,0:T(8,128)(2,1)}, bf16[2,24,3072]{2,1,0:T(8,128)(2,1)S(1)}, u32[]{:S(2)}, u32[]{:S(2)}) collective-permute-start(bf16[2,24,3072]{2,1,0:T(8,128)(2,1)} %collective-permute-done.29.refs_6_), channel_id=1, source_target_pairs={{0,1},{1,0},{2,3},{3,2},{4,5},{5,4},{6,7},{7,6},{8,9},{9,8},{10,11... | collective-permute-start | bytes 884744 | tf_op jit(solution)/shard_map/ppermute | solution.py:44
  158.8 10.6 %collective-permute-start.48 = (bf16[2,96,768]{2,1,0:T(8,128)(2,1)}, bf16[2,96,768]{2,1,0:T(8,128)(2,1)}, u32[]{:S(2)}, u32[]{:S(2)}) collective-permute-start(bf16[2,96,768]{2,1,0:T(8,128)(2,1)} %pad_maximum_fusion.18.refs_0_), channel_id=1, source_target_pairs={{0,1},{1,0},{2,3},{3,2},{4,5},{5,4},{6,7},{7,6},{8,9},{9,8},{10,11... | collective-permute-start | bytes 884744 | tf_op jit(solution)/shard_map/ppermute | solution.py:44
  158.9 11.7 %collective-permute-start.41 = (bf16[2,96,768]{2,1,0:T(8,128)(2,1)}, bf16[2,96,768]{2,1,0:T(8,128)(2,1)}, u32[]{:S(2)}, u32[]{:S(2)}) collective-permute-start(bf16[2,96,768]{2,1,0:T(8,128)(2,1)} %pad_maximum_fusion.18.refs_0_), channel_id=1, source_target_pairs={{0,4},{1,5},{2,6},{3,7},{4,0},{5,1},{6,2},{7,3},{8,12},{9,13},{10,... | collective-permute-start | bytes 884744 | tf_op jit(solution)/shard_map/ppermute | solution.py:44
  159.3 12.0 %collective-permute-start.40 = (bf16[2,96,768]{2,1,0:T(8,128)(2,1)}, bf16[2,96,768]{2,1,0:T(8,128)(2,1)}, u32[]{:S(2)}, u32[]{:S(2)}) collective-permute-start(bf16[2,96,768]{2,1,0:T(8,128)(2,1)} %pad_maximum_fusion.18.refs_0_), channel_id=1, source_target_pairs={{0,2},{1,3},{2,0},{3,1},{4,6},{5,7},{6,4},{7,5},{8,10},{9,11},{10,... | collective-permute-start | bytes 884744 | tf_op jit(solution)/shard_map/ppermute | solution.py:44
  159.5 14.2 %collective-permute-start.45 = (bf16[2,96,768]{2,1,0:T(8,128)(2,1)}, bf16[2,96,768]{2,1,0:T(8,128)(2,1)}, u32[]{:S(2)}, u32[]{:S(2)}) collective-permute-start(bf16[2,96,768]{2,1,0:T(8,128)(2,1)} %constant_dynamic-update-slice_fusion.4.refs_4_), channel_id=1, source_target_pairs={{0,2},{1,3},{2,0},{3,1},{4,6},{5,7},{6,4},{7,5},{8,10},{9,11},{10,... | collective-permute-start | bytes 884744 | tf_op jit(solution)/shard_map/ppermute | solution.py:44
  162.6 23.1 %collective-permute-start.52 = (bf16[2,96,768]{2,1,0:T(8,128)(2,1)}, bf16[2,96,768]{2,1,0:T(8,128)(2,1)}, u32[]{:S(2)}, u32[]{:S(2)}) collective-permute-start(bf16[2,96,768]{2,1,0:T(8,128)(2,1)} %constant_dynamic-update-slice_fusion.4.refs_4_), channel_id=1, source_target_pairs={{0,1},{1,0},{2,3},{3,2},{4,5},{5,4},{6,7},{7,6},{8,9},{9,8},{10,11... | collective-permute-start | bytes 884744 | tf_op jit(solution)/shard_map/ppermute | solution.py:44
  169.4 19.3 %collective-permute-start.46 = (bf16[2,96,768]{2,1,0:T(8,128)(2,1)}, bf16[2,96,768]{2,1,0:T(8,128)(2,1)S(1)}, u32[]{:S(2)}, u32[]{:S(2)}) collective-permute-start(bf16[2,96,768]{2,1,0:T(8,128)(2,1)} %constant_dynamic-update-slice_fusion.4.refs_4_), channel_id=1, source_target_pairs={{0,4},{1,5},{2,6},{3,7},{4,0},{5,1},{6,2},{7,3},{8,12},{9,13},{10,... | collective-permute-start | bytes 884744 | tf_op jit(solution)/shard_map/ppermute | solution.py:44
  170.7 18.1 %collective-permute-start.50 = (bf16[2,96,768]{2,1,0:T(8,128)(2,1)}, bf16[2,96,768]{2,1,0:T(8,128)(2,1)S(1)}, u32[]{:S(2)}, u32[]{:S(2)}) collective-permute-start(bf16[2,96,768]{2,1,0:T(8,128)(2,1)} %collective-permute-done.41.refs_2_), channel_id=1, source_target_pairs={{0,1},{1,0},{2,3},{3,2},{4,5},{5,4},{6,7},{7,6},{8,9},{9,8},{10,11... | collective-permute-start | bytes 884744 | tf_op jit(solution)/shard_map/ppermute | solution.py:44
  171.2 18.0 %collective-permute-start.42 = (bf16[2,96,768]{2,1,0:T(8,128)(2,1)}, bf16[2,96,768]{2,1,0:T(8,128)(2,1)S(1)}, u32[]{:S(2)}, u32[]{:S(2)}) collective-permute-start(bf16[2,96,768]{2,1,0:T(8,128)(2,1)} %collective-permute-done.41.refs_2_), channel_id=1, source_target_pairs={{0,2},{1,3},{2,0},{3,1},{4,6},{5,7},{6,4},{7,5},{8,10},{9,11},{10,... | collective-permute-start | bytes 884744 | tf_op jit(solution)/shard_map/ppermute | solution.py:44
  173.8 15.6 %collective-permute-start.47 = (bf16[2,96,768]{2,1,0:T(8,128)(2,1)}, bf16[2,96,768]{2,1,0:T(8,128)(2,1)S(1)}, u32[]{:S(2)}, u32[]{:S(2)}) collective-permute-start(bf16[2,96,768]{2,1,0:T(8,128)(2,1)} %collective-permute-done.45.refs_5_), channel_id=1, source_target_pairs={{0,4},{1,5},{2,6},{3,7},{4,0},{5,1},{6,2},{7,3},{8,12},{9,13},{10,... | collective-permute-start | bytes 884744 | tf_op jit(solution)/shard_map/ppermute | solution.py:44
  536.4 23.5 %collective-permute-start.70 = (bf16[2,2,2,2,24,768]{5,4,3,2,1,0:T(8,128)(2,1)}, bf16[2,2,2,2,24,768]{5,4,3,2,1,0:T(8,128)(2,1)}, u32[]{:S(2)}, u32[]{:S(2)}) collective-permute-start(bf16[2,2,2,2,24,768]{5,4,3,2,1,0:T(8,128)(2,1)} %dynamic-slice_bitcast_fusion.3), channel_id=1, source_target_pairs={{0,1},{1,0},{2,3},{3,2},{4,5},{5,4},{6,7},{7,6},{8,9},{9,8},{10,11... | collective-permute-start | bytes 1769480 | tf_op jit(solution)/shard_map/ppermute | solution.py:44
  551.0 26.0 %collective-permute-start.61 = (bf16[2,2,2,2,24,2304]{5,4,3,2,1,0:T(8,128)(2,1)S(1)}, bf16[2,2,2,2,24,2304]{5,4,3,2,1,0:T(8,128)(2,1)S(1)}, u32[]{:S(2)}, u32[]{:S(2)}) collective-permute-start(bf16[2,2,2,2,24,2304]{5,4,3,2,1,0:T(8,128)(2,1)S(1)} %dynamic-slice_bitcast_fusion.2), channel_id=1, source_target_pairs={{0,1},{1,0},{2,3},{3,2},{4,5},{5,4},{6,7},{7,6},{8,9},{9,8},{10,11... | collective-permute-start | bytes 5308424 | tf_op jit(solution)/shard_map/ppermute | solution.py:44
  556.2 35.5 %collective-permute-start.88 = (bf16[2,2,2,2,96,768]{5,4,3,2,1,0:T(8,128)(2,1)S(1)}, bf16[2,2,2,2,96,768]{5,4,3,2,1,0:T(8,128)(2,1)S(1)}, u32[]{:S(2)}, u32[]{:S(2)}) collective-permute-start(bf16[2,2,2,2,96,768]{5,4,3,2,1,0:T(8,128)(2,1)S(1)} %dynamic-slice_bitcast_fusion), channel_id=1, source_target_pairs={{0,1},{1,0},{2,3},{3,2},{4,5},{5,4},{6,7},{7,6},{8,9},{9,8},{10,11... | collective-permute-start | bytes 7077896 | tf_op jit(solution)/shard_map/ppermute | solution.py:44
  556.9 36.2 %collective-permute-start.79 = (bf16[2,2,2,2,24,3072]{5,4,3,2,1,0:T(8,128)(2,1)S(1)}, bf16[2,2,2,2,24,3072]{5,4,3,2,1,0:T(8,128)(2,1)S(1)}, u32[]{:S(2)}, u32[]{:S(2)}) collective-permute-start(bf16[2,2,2,2,24,3072]{5,4,3,2,1,0:T(8,128)(2,1)S(1)} %dynamic-slice_bitcast_fusion.1), channel_id=1, source_target_pairs={{0,1},{1,0},{2,3},{3,2},{4,5},{5,4},{6,7},{7,6},{8,9},{9,8},{10,11... | collective-permute-start | bytes 7077896 | tf_op jit(solution)/shard_map/ppermute | solution.py:44
  577.5 12.1 %collective-permute-start.62 = (bf16[2,2,24,2304]{3,2,1,0:T(8,128)(2,1)S(1)}, bf16[2,2,24,2304]{3,2,1,0:T(8,128)(2,1)S(1)}, u32[]{:S(2)}, u32[]{:S(2)}) collective-permute-start(bf16[2,2,24,2304]{3,2,1,0:T(8,128)(2,1)S(1)} %get-tuple-element.58), channel_id=1, source_target_pairs={{0,2},{1,3},{2,0},{3,1},{4,6},{5,7},{6,4},{7,5},{8,10},{9,11},{10,... | collective-permute-start | bytes 1327112 | tf_op jit(solution)/shard_map/ppermute | solution.py:44
  580.0 9.6 %collective-permute-start.65 = (bf16[2,2,24,2304]{3,2,1,0:T(8,128)(2,1)S(1)}, bf16[2,2,24,2304]{3,2,1,0:T(8,128)(2,1)S(1)}, u32[]{:S(2)}, u32[]{:S(2)}) collective-permute-start(bf16[2,2,24,2304]{3,2,1,0:T(8,128)(2,1)S(1)} %get-tuple-element.59), channel_id=1, source_target_pairs={{0,4},{1,5},{2,6},{3,7},{4,0},{5,1},{6,2},{7,3},{8,12},{9,13},{10,... | collective-permute-start | bytes 1327112 | tf_op jit(solution)/shard_map/ppermute | solution.py:44
  583.4 10.3 %collective-permute-start.78 = (f32[24,768]{1,0:T(8,128)S(1)}, f32[24,768]{1,0:T(8,128)S(1)}, u32[]{:S(2)}, u32[]{:S(2)}) collective-permute-start(f32[24,768]{1,0:T(8,128)S(1)} %fusion.155), channel_id=1, source_target_pairs={{0,1},{1,0},{2,3},{3,2},{4,5},{5,4},{6,7},{7,6},{8,9},{9,8},{10,11... | collective-permute-start | bytes 221192 | tf_op jit(solution)/shard_map/ppermute | solution.py:44
  592.0 13.1 %collective-permute-start.89 = (bf16[2,2,96,768]{3,2,1,0:T(8,128)(2,1)S(1)}, bf16[2,2,96,768]{3,2,1,0:T(8,128)(2,1)S(1)}, u32[]{:S(2)}, u32[]{:S(2)}) collective-permute-start(bf16[2,2,96,768]{3,2,1,0:T(8,128)(2,1)S(1)} %get-tuple-element.46), channel_id=1, source_target_pairs={{0,2},{1,3},{2,0},{3,1},{4,6},{5,7},{6,4},{7,5},{8,10},{9,11},{10,... | collective-permute-start | bytes 1769480 | tf_op jit(solution)/shard_map/ppermute | solution.py:44
  593.1 13.6 %collective-permute-start.92 = (bf16[2,2,96,768]{3,2,1,0:T(8,128)(2,1)S(1)}, bf16[2,2,96,768]{3,2,1,0:T(8,128)(2,1)S(1)}, u32[]{:S(2)}, u32[]{:S(2)}) collective-permute-start(bf16[2,2,96,768]{3,2,1,0:T(8,128)(2,1)S(1)} %get-tuple-element.47), channel_id=1, source_target_pairs={{0,4},{1,5},{2,6},{3,7},{4,0},{5,1},{6,2},{7,3},{8,12},{9,13},{10,... | collective-permute-start | bytes 1769480 | tf_op jit(solution)/shard_map/ppermute | solution.py:44
  593.7 24.0 %collective-permute-start.80 = (bf16[2,2,24,3072]{3,2,1,0:T(8,128)(2,1)S(1)}, bf16[2,2,24,3072]{3,2,1,0:T(8,128)(2,1)S(1)}, u32[]{:S(2)}, u32[]{:S(2)}) collective-permute-start(bf16[2,2,24,3072]{3,2,1,0:T(8,128)(2,1)S(1)} %get-tuple-element.51), channel_id=1, source_target_pairs={{0,2},{1,3},{2,0},{3,1},{4,6},{5,7},{6,4},{7,5},{8,10},{9,11},{10,... | collective-permute-start | bytes 1769480 | tf_op jit(solution)/shard_map/ppermute | solution.py:44
  596.6 22.3 %collective-permute-start.83 = (bf16[2,2,24,3072]{3,2,1,0:T(8,128)(2,1)S(1)}, bf16[2,2,24,3072]{3,2,1,0:T(8,128)(2,1)S(1)}, u32[]{:S(2)}, u32[]{:S(2)}) collective-permute-start(bf16[2,2,24,3072]{3,2,1,0:T(8,128)(2,1)S(1)} %get-tuple-element.52), channel_id=1, source_target_pairs={{0,4},{1,5},{2,6},{3,7},{4,0},{5,1},{6,2},{7,3},{8,12},{9,13},{10,... | collective-permute-start | bytes 1769480 | tf_op jit(solution)/shard_map/ppermute | solution.py:44
  597.6 22.6 %collective-permute-start.67 = (bf16[24,2304]{1,0:T(8,128)(2,1)S(1)}, bf16[24,2304]{1,0:T(8,128)(2,1)S(1)}, u32[]{:S(2)}, u32[]{:S(2)}) collective-permute-start(bf16[24,2304]{1,0:T(8,128)(2,1)S(1)} %get-tuple-element.53), channel_id=1, source_target_pairs={{0,16},{1,17},{2,18},{3,19},{4,20},{5,21},{6,22},{7,23},{8,24},{9,... | collective-permute-start | bytes 331784 | tf_op jit(solution)/shard_map/ppermute | solution.py:44
  605.1 15.8 %collective-permute-start.68 = (bf16[24,2304]{1,0:T(8,128)(2,1)S(1)}, bf16[24,2304]{1,0:T(8,128)(2,1)S(1)}, u32[]{:S(2)}, u32[]{:S(2)}) collective-permute-start(bf16[24,2304]{1,0:T(8,128)(2,1)S(1)} %get-tuple-element.54), channel_id=1, source_target_pairs={{0,24},{1,25},{2,26},{3,27},{4,28},{5,29},{6,30},{7,31},{8,16},{9,... | collective-permute-start | bytes 331784 | tf_op jit(solution)/shard_map/ppermute | solution.py:44
  606.8 14.4 %collective-permute-start.64 = (bf16[24,2304]{1,0:T(8,128)(2,1)S(1)}, bf16[24,2304]{1,0:T(8,128)(2,1)S(1)}, u32[]{:S(2)}, u32[]{:S(2)}) collective-permute-start(bf16[24,2304]{1,0:T(8,128)(2,1)S(1)} %get-tuple-element.55), channel_id=1, source_target_pairs={{0,8},{1,9},{2,10},{3,11},{4,12},{5,13},{6,14},{7,15},{8,0},{9,1},... | collective-permute-start | bytes 331784 | tf_op jit(solution)/shard_map/ppermute | solution.py:44
  617.7 14.2 %collective-permute-start.90 = (bf16[2,96,768]{2,1,0:T(8,128)(2,1)S(1)}, bf16[2,96,768]{2,1,0:T(8,128)(2,1)S(1)}, u32[]{:S(2)}, u32[]{:S(2)}) collective-permute-start(bf16[2,96,768]{2,1,0:T(8,128)(2,1)S(1)} %get-tuple-element.44), channel_id=1, source_target_pairs={{0,4},{1,5},{2,6},{3,7},{4,0},{5,1},{6,2},{7,3},{8,12},{9,13},{10,... | collective-permute-start | bytes 884744 | tf_op jit(solution)/shard_map/ppermute | solution.py:44
  618.8 13.1 %collective-permute-start.93 = (bf16[2,96,768]{2,1,0:T(8,128)(2,1)S(1)}, bf16[2,96,768]{2,1,0:T(8,128)(2,1)S(1)}, u32[]{:S(2)}, u32[]{:S(2)}) collective-permute-start(bf16[2,96,768]{2,1,0:T(8,128)(2,1)S(1)} %get-tuple-element.45), channel_id=1, source_target_pairs={{0,2},{1,3},{2,0},{3,1},{4,6},{5,7},{6,4},{7,5},{8,10},{9,11},{10,... | collective-permute-start | bytes 884744 | tf_op jit(solution)/shard_map/ppermute | solution.py:44
  620.2 14.1 %collective-permute-start.81 = (bf16[2,24,3072]{2,1,0:T(8,128)(2,1)S(1)}, bf16[2,24,3072]{2,1,0:T(8,128)(2,1)S(1)}, u32[]{:S(2)}, u32[]{:S(2)}) collective-permute-start(bf16[2,24,3072]{2,1,0:T(8,128)(2,1)S(1)} %get-tuple-element.49), channel_id=1, source_target_pairs={{0,4},{1,5},{2,6},{3,7},{4,0},{5,1},{6,2},{7,3},{8,12},{9,13},{10,... | collective-permute-start | bytes 884744 | tf_op jit(solution)/shard_map/ppermute | solution.py:44
  620.9 14.0 %collective-permute-start.84 = (bf16[2,24,3072]{2,1,0:T(8,128)(2,1)S(1)}, bf16[2,24,3072]{2,1,0:T(8,128)(2,1)S(1)}, u32[]{:S(2)}, u32[]{:S(2)}) collective-permute-start(bf16[2,24,3072]{2,1,0:T(8,128)(2,1)S(1)} %get-tuple-element.50), channel_id=1, source_target_pairs={{0,2},{1,3},{2,0},{3,1},{4,6},{5,7},{6,4},{7,5},{8,10},{9,11},{10,... | collective-permute-start | bytes 884744 | tf_op jit(solution)/shard_map/ppermute | solution.py:44
  621.3 40.0 %collective-permute-start.69 = (f32[24,2304]{1,0:T(8,128)S(1)}, f32[24,2304]{1,0:T(8,128)S(1)}, u32[]{:S(2)}, u32[]{:S(2)}) collective-permute-start(f32[24,2304]{1,0:T(8,128)S(1)} %fusion.147), channel_id=1, source_target_pairs={{0,1},{1,0},{2,3},{3,2},{4,5},{5,4},{6,7},{7,6},{8,9},{9,8},{10,11... | collective-permute-start | bytes 663560 | tf_op jit(solution)/shard_map/ppermute | solution.py:44
  632.2 13.5 %collective-permute-start.94 = (bf16[96,768]{1,0:T(8,128)(2,1)S(1)}, bf16[96,768]{1,0:T(8,128)(2,1)S(1)}, u32[]{:S(2)}, u32[]{:S(2)}) collective-permute-start(bf16[96,768]{1,0:T(8,128)(2,1)S(1)} %get-tuple-element.39), channel_id=1, source_target_pairs={{0,16},{1,17},{2,18},{3,19},{4,20},{5,21},{6,22},{7,23},{8,24},{9,... | collective-permute-start | bytes 442376 | tf_op jit(solution)/shard_map/ppermute | solution.py:44
  632.6 14.5 %collective-permute-start.95 = (bf16[96,768]{1,0:T(8,128)(2,1)S(1)}, bf16[96,768]{1,0:T(8,128)(2,1)S(1)}, u32[]{:S(2)}, u32[]{:S(2)}) collective-permute-start(bf16[96,768]{1,0:T(8,128)(2,1)S(1)} %get-tuple-element.40), channel_id=1, source_target_pairs={{0,24},{1,25},{2,26},{3,27},{4,28},{5,29},{6,30},{7,31},{8,16},{9,... | collective-permute-start | bytes 442376 | tf_op jit(solution)/shard_map/ppermute | solution.py:44
  634.3 18.0 %collective-permute-start.91 = (bf16[96,768]{1,0:T(8,128)(2,1)S(1)}, bf16[96,768]{1,0:T(8,128)(2,1)S(1)}, u32[]{:S(2)}, u32[]{:S(2)}) collective-permute-start(bf16[96,768]{1,0:T(8,128)(2,1)S(1)} %get-tuple-element.43), channel_id=1, source_target_pairs={{0,8},{1,9},{2,10},{3,11},{4,12},{5,13},{6,14},{7,15},{8,0},{9,1},... | collective-permute-start | bytes 442376 | tf_op jit(solution)/shard_map/ppermute | solution.py:44
  635.2 21.1 %collective-permute-start.85 = (bf16[24,3072]{1,0:T(8,128)(2,1)S(1)}, bf16[24,3072]{1,0:T(8,128)(2,1)S(1)}, u32[]{:S(2)}, u32[]{:S(2)}) collective-permute-start(bf16[24,3072]{1,0:T(8,128)(2,1)S(1)} %get-tuple-element.41), channel_id=1, source_target_pairs={{0,16},{1,17},{2,18},{3,19},{4,20},{5,21},{6,22},{7,23},{8,24},{9,... | collective-permute-start | bytes 442376 | tf_op jit(solution)/shard_map/ppermute | solution.py:44
  645.7 10.5 %collective-permute-start.86 = (bf16[24,3072]{1,0:T(8,128)(2,1)S(1)}, bf16[24,3072]{1,0:T(8,128)(2,1)S(1)}, u32[]{:S(2)}, u32[]{:S(2)}) collective-permute-start(bf16[24,3072]{1,0:T(8,128)(2,1)S(1)} %get-tuple-element.42), channel_id=1, source_target_pairs={{0,24},{1,25},{2,26},{3,27},{4,28},{5,29},{6,30},{7,31},{8,16},{9,... | collective-permute-start | bytes 442376 | tf_op jit(solution)/shard_map/ppermute | solution.py:44
  647.2 13.2 %collective-permute-start.82 = (bf16[24,3072]{1,0:T(8,128)(2,1)S(1)}, bf16[24,3072]{1,0:T(8,128)(2,1)S(1)}, u32[]{:S(2)}, u32[]{:S(2)}) collective-permute-start(bf16[24,3072]{1,0:T(8,128)(2,1)S(1)} %get-tuple-element.48), channel_id=1, source_target_pairs={{0,8},{1,9},{2,10},{3,11},{4,12},{5,13},{6,14},{7,15},{8,0},{9,1},... | collective-permute-start | bytes 442376 | tf_op jit(solution)/shard_map/ppermute | solution.py:44
  652.5 9.6 %collective-permute-start.96 = (f32[96,768]{1,0:T(8,128)S(1)}, f32[96,768]{1,0:T(8,128)S(1)}, u32[]{:S(2)}, u32[]{:S(2)}) collective-permute-start(f32[96,768]{1,0:T(8,128)S(1)} %fusion.133), channel_id=1, source_target_pairs={{0,1},{1,0},{2,3},{3,2},{4,5},{5,4},{6,7},{7,6},{8,9},{9,8},{10,11... | collective-permute-start | bytes 884744 | tf_op jit(solution)/shard_map/ppermute | solution.py:44
  (193 other events, 2435.5 us)
where the time goes:
time: 668 us; the launch traced here: 664 us
  matrix products  308 us (46%)
  starting transfers between devices  105 us (16%)
  other arithmetic  87 us (13%)
  waiting for transfers between devices  85.9 us (13%)
  local copies, waits for them, and re-layouts  60.6 us (9%)
  Pallas kernels  14.5 us (2%)
    ppermute x97, starting transfers between devices, swap(): return lax.ppermute(value, BOTH, [(i, i ^ bits) for i in range(32)])  105 us
    ppermute x97, waiting for transfers between devices, swap(): return lax.ppermute(value, BOTH, [(i, i ^ bits) for i in range(32)])  85.9 us
    dot_general x8, matrix products, outer_sum(): lax.dot_general(left, right, (((0,), (0,)), ((), ())), preferred_element_...  72.4 us
    dot_general x8, matrix products, times_transpose(): lax.dot_general(left, right, (((1,), (1,)), ((), ())), preferred_element_...  70.1 us
    convert_element_type x4, other arithmetic, attend_backward(): score_low = grad_scores.astype(jnp.bfloat16)  36 us
    dot_general x4, matrix products, attend_backward(): jnp.einsum('qhd,khd->hqk', grad_att, values, preferred_element_type=jnp.f...  30.1 us
    dot_general x2, matrix products, layer_forward(): jnp.dot(activated, weights[10], preferred_element_type=jnp.float32)  24 us
    dot_general x2, matrix products, layer_forward(): jnp.dot(normed_m, weights[8], preferred_element_type=jnp.float32)  21.5 us
  transfers between devices with their start and end apart: 97, of which 27 were waited for; matrix products, arithmetic and copies ran while one was open for 16% of the time, Pallas kernels for 1%

commit v1 on v0

v1 whole, which is shorter than its diff:
```python
import functools
import math

import jax
import jax.numpy as jnp
from jax import lax
from jax.experimental import pallas as pl
from jax.experimental.pallas import tpu as pltpu
from jax.sharding import PartitionSpec as P

H = 12
HD = 64
USES = 2
LONGEST = 256
BOTH = ("dp", "rep")


NORM_EPS = 1e-05
BLOCK = 128
FEATURES = H * HD
VMEM_LIMIT = 60 << 20


def dot(left, right):
    return jnp.dot(left, right, preferred_element_type=jnp.float32)


def norm_parts(values):
    center = values - jnp.mean(values, axis=-1, keepdims=True)
    spread = jnp.mean(center * center, axis=-1, keepdims=True)
    scale = lax.rsqrt(spread + NORM_EPS)
    return (center * scale, scale)


def norm_back(normed, scale, gain, grad):
    inner = grad * gain
    first = jnp.mean(inner, axis=-1, keepdims=True)
    second = jnp.mean(inner * normed, axis=-1, keepdims=True)
    return (inner - first - normed * second) * scale


def segment_of(places, lengths, docs):
    end = jnp.int32(0)
    segment = jnp.zeros(places.shape, jnp.int32)
    for doc in range(docs):
        end = end + lengths[doc]
        segment = segment + (places >= end).astype(jnp.int32)
    return segment


def allowed_bias(count, lengths, docs, query_axis):
    query_shape = (count, 1) if query_axis == 0 else (1, count)
    key_shape = (1, count) if query_axis == 0 else (count, 1)
    query = lax.broadcasted_iota(jnp.int32, query_shape, query_axis)
    key = lax.broadcasted_iota(jnp.int32, key_shape, 1 - query_axis)
    same = segment_of(query, lengths, docs) == segment_of(key, lengths, docs)
    return jnp.where(same & (key <= query), 0.0, -1e30).astype(jnp.float32)


def head_split(pair):
    left = lax.broadcasted_iota(jnp.int32, pair.shape, 1) < HD
    zero = jnp.zeros_like(pair)
    return jnp.concatenate([jnp.where(left, pair, zero), jnp.where(left, zero, pair)], axis=0)


def head_join(stacked):
    count = stacked.shape[0] // 2
    left = lax.broadcasted_iota(jnp.int32, (count, 2 * HD), 1) < HD
    return jnp.where(left, stacked[:count], stacked[count:])


def attention_forward_kernel(
    docs,
    back,
    lengths_ref,
    state_ref,
    gain_ref,
    shift_ref,
    weight_ref,
    qbias_ref,
    obias_ref,
    gain2_ref,
    shift2_ref,
    normed_ref,
    mixed_ref,
    att_ref,
    lse_ref,
    hidden_ref,
    normed2_ref,
    bias_ref,
    lse_cols,
):
    micro = pl.program_id(0)
    state = state_ref[...].astype(jnp.float32)
    count = state.shape[0]
    normed = (norm_parts(state)[0] * gain_ref[...] + shift_ref[...]).astype(jnp.bfloat16)
    normed_ref[...] = normed
    for part in range(3):
        columns = slice(part * FEATURES, (part + 1) * FEATURES)
        mixed_ref[:, columns] = (dot(normed, weight_ref[part]) + qbias_ref[:, columns]).astype(
            jnp.bfloat16
        )
    bias_ref[...] = allowed_bias(count, [lengths_ref[micro, d] for d in range(docs)], docs, 0)
    lse_cols[...] = jnp.zeros_like(lse_cols)

    def one_pair(pair, carry):
        lanes = pl.multiple_of(pair * 2 * HD, 2 * HD)
        for block in range(count // BLOCK):
            rows = slice(block * BLOCK, (block + 1) * BLOCK)
            low_key = max(0, block - back) * BLOCK
            keys = slice(low_key, (block + 1) * BLOCK)
            query = head_split(mixed_ref[rows, pl.ds(lanes, 2 * HD)])
            key = mixed_ref[keys, pl.ds(FEATURES + lanes, 2 * HD)]
            value = mixed_ref[keys, pl.ds(2 * FEATURES + lanes, 2 * HD)]
            scores = lax.dot_general(
                query, key, (((1,), (1,)), ((), ())), preferred_element_type=jnp.float32
            )
            bias = bias_ref[rows, keys]
            scores = scores * 0.125 + jnp.concatenate([bias, bias], axis=0)
            top = jnp.max(scores, axis=-1, keepdims=True)
            expo = jnp.exp(scores - top)
            total = jnp.sum(expo, axis=-1, keepdims=True)
            result = dot(expo.astype(jnp.bfloat16), value) / total
            att_ref[rows, pl.ds(lanes, 2 * HD)] = head_join(result).astype(jnp.bfloat16)
            lse = top + jnp.log(total)
            lane = lax.broadcasted_iota(jnp.int32, (BLOCK, 128), 1)
            lse_cols[rows, :] += jnp.where(lane == 2 * pair, lse[:BLOCK], 0.0) + jnp.where(
                lane == 2 * pair + 1, lse[BLOCK:], 0.0
            )
        return carry

    lax.fori_loop(0, H // 2, one_pair, 0)
    lse = jnp.transpose(lse_cols[...])
    for index in range(H):
        lse_ref[index] = lse[index : index + 1]
    hidden = state + (dot(att_ref[...], weight_ref[3]) + obias_ref[...])
    hidden_ref[...] = hidden
    normed2_ref[...] = (norm_parts(hidden)[0] * gain2_ref[...] + shift2_ref[...]).astype(
        jnp.bfloat16
    )


def whole(array):
    dims = len(array.shape)
    return pl.BlockSpec(array.shape, lambda *unused: (0,) * dims, pipeline_mode=pl.Buffered(1))


SMEM = pl.BlockSpec(memory_space=pltpu.SMEM)


def rows_of(count, width):
    return pl.BlockSpec((count, width), lambda i: (i, 0))


def params():
    return pltpu.CompilerParams(vmem_limit_bytes=VMEM_LIMIT)


def cost(flops, transcendentals, *arrays):
    size = sum(math.prod(a.shape) * a.dtype.itemsize for a in arrays)
    return pl.CostEstimate(
        flops=int(flops), transcendentals=int(transcendentals), bytes_accessed=int(size)
    )


def attention_forward(lengths, state, count, back, gain, shift, weight, qbias, obias, gain2, shift2):
    rows = state.shape[0]
    micro, docs = lengths.shape
    width = FEATURES
    shape = jax.ShapeDtypeStruct
    outs = (
        shape((rows, width), jnp.bfloat16),
        shape((rows, 3 * width), jnp.bfloat16),
        shape((rows, width), jnp.bfloat16),
        shape((micro * H, 1, count), jnp.float32),
        shape((rows, width), jnp.float32),
        shape((rows, width), jnp.bfloat16),
    )
    weights = (gain, shift, weight, qbias, obias, gain2, shift2)
    return pl.pallas_call(
        functools.partial(attention_forward_kernel, docs, back),
        grid=(micro,),
        out_shape=outs,
        in_specs=[SMEM, rows_of(count, width)] + [whole(w) for w in weights],
        out_specs=(
            rows_of(count, width),
            rows_of(count, 3 * width),
            rows_of(count, width),
            pl.BlockSpec((H, 1, count), lambda i: (i, 0, 0)),
            rows_of(count, width),
            rows_of(count, width),
        ),
        scratch_shapes=[
            pltpu.VMEM((count, count), jnp.float32),
            pltpu.VMEM((count, 128), jnp.float32),
        ],
        compiler_params=params(),
        cost_estimate=cost(
            8 * rows * width * width + 4 * rows * count * width, rows * count * H, state, *weights, *outs
        ),
        name="attention_forward",
    )(lengths, state, *weights)


GELU_C = 0.7978845608028654
GELU_K = 0.044715 * GELU_C


def gelu_gate(value):
    square = value * value
    gate = 0.5 * jnp.tanh(value * (GELU_C + GELU_K * square)) + 0.5
    return (gate, square)


def mlp_forward_kernel(
    last, hidden_ref, normed_ref, fc_ref, fbias_ref, proj_ref, pbias_ref, expanded_ref, *rest
):
    final_ref, state_ref = rest if last else (None, rest[0])
    step = pl.program_id(0)
    chunk = 256

    @pl.when(step == 0)
    def _():
        state_ref[...] = hidden_ref[...] + pbias_ref[...]

    for start in range(0, normed_ref.shape[0], chunk):
        rows = slice(start, start + chunk)
        expanded = dot(normed_ref[rows, :], square_of(fc_ref)) + fbias_ref[...]
        expanded_ref[rows, :] = expanded.astype(expanded_ref.dtype)
        gate, unused = gelu_gate(expanded)
        activated = (expanded * gate).astype(jnp.bfloat16)
        state_ref[rows, :] += dot(activated, square_of(proj_ref))

    if last:

        @pl.when(step == pl.num_programs(0) - 1)
        def _():
            final_ref[...] = state_ref[...].astype(jnp.bfloat16)


def square_of(ref):
    return ref[...].reshape(FEATURES, FEATURES)


FC_BLOCK = pl.BlockSpec((16, 1, 1, 48, FEATURES), lambda i: (0, i // 2, i % 2, 0, 0))
PROJ_BLOCK = pl.BlockSpec((4, 2, 2, 48, FEATURES), lambda i: (i, 0, 1, 0, 0))


def mlp_forward(hidden, normed, mlp, fbias, pbias, last):
    rows, width = hidden.shape
    block = width
    hidden_units = 4 * block
    shape = jax.ShapeDtypeStruct
    outs = (
        shape((rows, hidden_units), jnp.bfloat16),
        shape((rows, width), jnp.bfloat16 if last else jnp.float32),
    )
    specs = (
        pl.BlockSpec((rows, block), lambda i: (0, i)),
        pl.BlockSpec((rows, width), lambda i: (0, 0)),
    )
    return pl.pallas_call(
        functools.partial(mlp_forward_kernel, last),
        grid=(hidden_units // block,),
        out_shape=outs,
        in_specs=[
            whole(hidden),
            whole(normed),
            FC_BLOCK,
            pl.BlockSpec((1, block), lambda i: (0, i)),
            PROJ_BLOCK,
            whole(pbias),
        ],
        out_specs=specs,
        scratch_shapes=[pltpu.VMEM((rows, width), jnp.float32)] if last else [],
        compiler_params=params(),
        cost_estimate=cost(
            4 * rows * width * hidden_units, rows * hidden_units, hidden, normed, mlp, *outs
        ),
        name="mlp_forward",
    )(hidden, normed, mlp, fbias, mlp, pbias)


def transposed_dot(left, right):
    return lax.dot_general(
        left, right, (((0,), (0,)), ((), ())), preferred_element_type=jnp.float32
    )


def dot_transposed(left, right):
    return lax.dot_general(
        left, right, (((1,), (1,)), ((), ())), preferred_element_type=jnp.float32
    )


def transposed_dot(left, right):
    return lax.dot_general(
        left, right, (((0,), (0,)), ((), ())), preferred_element_type=jnp.float32
    )


def dot_transposed(left, right):
    return lax.dot_general(
        left, right, (((1,), (1,)), ((), ())), preferred_element_type=jnp.float32
    )


def store_halves(core, value, mine_ref, theirs_ref, earlier):
    half = value.shape[1] // 2
    left, right = (value[:, :half], value[:, half:])
    mine = jnp.where(core == 0, left, right)
    theirs = jnp.where(core == 0, right, left)
    if earlier is not None:
        mine = mine + earlier[0][0].astype(jnp.float32)
        theirs = theirs + earlier[1][0].astype(jnp.float32)
    mine_ref[0] = mine.astype(mine_ref.dtype)
    theirs_ref[0] = theirs.astype(theirs_ref.dtype)


def mlp_backward_kernel(
    more,
    core_ref,
    grad_ref,
    hidden_ref,
    normed_ref,
    expanded_ref,
    fc_ref,
    proj_ref,
    gain_ref,
    *rest,
):
    earlier = rest[:8] if more else (None,) * 8
    if more:
        rest = rest[8:]
    (
        dhid_ref,
        fc_mine,
        fc_theirs,
        proj_mine,
        proj_theirs,
        dfbias_ref,
        dpbias_ref,
        dgain_ref,
        dshift_ref,
        low_ref,
        normed_t,
        acc_ref,
        act_ref,
        ge_ref,
    ) = rest
    step = pl.program_id(0)
    core = core_ref[0]
    rows = grad_ref.shape[0]
    chunk = 256

    @pl.when(step == 0)
    def _():
        low_grad = grad_ref[...].astype(jnp.bfloat16)
        low_ref[...] = low_grad
        dpbias = jnp.sum(low_grad.astype(jnp.float32), axis=0, keepdims=True)
        dpbias_ref[...] = dpbias + earlier[5][...] if more else dpbias
        normed_t[...] = jnp.transpose(normed_ref[...])
        acc_ref[...] = jnp.zeros_like(acc_ref)

    bias_sum = jnp.zeros(dfbias_ref.shape[1:], jnp.float32)
    for start in range(0, rows, chunk):
        part = slice(start, start + chunk)
        grad_act = dot_transposed(low_ref[part, :], square_of(proj_ref))
        value = expanded_ref[part, :].astype(jnp.float32)
        gate, square = gelu_gate(value)
        act = value * gate
        slope = gate + act * (1.0 - gate) * (2 * GELU_C + 6 * GELU_K * square)
        act_ref[part, :] = act.astype(jnp.bfloat16)
        grad_exp = (grad_act * slope).astype(jnp.bfloat16)
        ge_ref[part, :] = grad_exp
        bias_sum = bias_sum + jnp.sum(grad_exp.astype(jnp.float32), axis=0, keepdims=True)
        acc_ref[part, :] += dot_transposed(grad_exp, square_of(fc_ref))
    dfbias_ref[0] = bias_sum + earlier[4][0] if more else bias_sum
    dproj = transposed_dot(act_ref[...], low_ref[...])
    store_halves(core, dproj, proj_mine, proj_theirs, earlier[2:4] if more else None)
    dfc = dot(normed_t[...], ge_ref[...])
    store_halves(core, dfc, fc_mine, fc_theirs, earlier[:2] if more else None)

    @pl.when(step == pl.num_programs(0) - 1)
    def _():
        normed, scale = norm_parts(hidden_ref[...])
        grad_norm = acc_ref[...]
        dgain = jnp.sum(grad_norm * normed, axis=0, keepdims=True)
        dshift = jnp.sum(grad_norm, axis=0, keepdims=True)
        dgain_ref[...] = dgain + earlier[6][...] if more else dgain
        dshift_ref[...] = dshift + earlier[7][...] if more else dshift
        dhid_ref[...] = grad_ref[...].astype(jnp.float32) + norm_back(
            normed, scale, gain_ref[...], grad_norm
        )


def mlp_backward(core, grad, hidden, normed, expanded, mlp, gain, earlier=None):
    rows, width = hidden.shape
    blocks, block = (4, width)
    shape = jax.ShapeDtypeStruct
    half = shape((blocks, width, width // 2), jnp.bfloat16)
    row = shape((1, width), jnp.float32)
    outs = (
        shape((rows, width), jnp.float32),
        half,
        half,
        half,
        half,
        shape((blocks, 1, block), jnp.float32),
        row,
        row,
        row,
    )
    halves = pl.BlockSpec((1, width, width // 2), lambda i: (i, 0, 0))
    bias = pl.BlockSpec((1, 1, block), lambda i: (i, 0, 0))
    vector = pl.BlockSpec((1, width), lambda i: (0, 0))
    inputs = [grad, hidden, normed, expanded, mlp, mlp, gain]
    specs = [
        whole(grad),
        whole(hidden),
        whole(normed),
        pl.BlockSpec((rows, block), lambda i: (0, i)),
        FC_BLOCK,
        PROJ_BLOCK,
        whole(gain),
    ]
    summed = [halves, halves, halves, halves, bias, vector, vector, vector]
    if earlier is not None:
        inputs += list(earlier)
        specs += summed
    return pl.pallas_call(
        functools.partial(mlp_backward_kernel, earlier is not None),
        grid=(blocks,),
        out_shape=outs,
        in_specs=[SMEM] + specs,
        out_specs=[pl.BlockSpec((rows, width), lambda i: (0, 0))] + summed,
        scratch_shapes=[
            pltpu.VMEM((rows, width), jnp.bfloat16),
            pltpu.VMEM((width, rows), jnp.bfloat16),
            pltpu.VMEM((rows, width), jnp.float32),
            pltpu.VMEM((rows, block), jnp.bfloat16),
            pltpu.VMEM((rows, block), jnp.bfloat16),
        ],
        compiler_params=params(),
        cost_estimate=cost(8 * rows * width * blocks * block, rows * blocks * block, *inputs, *outs),
        name="mlp_backward",
    )(core, *inputs)


def attention_backward_kernel(
    docs,
    back,
    micro,
    lengths_ref,
    dhid_ref,
    att_ref,
    mixed_ref,
    lse_ref,
    out_ref,
    gmix_ref,
    datt_ref,
    bias_ref,
    delta_ref,
    dq_ref,
):
    count = dhid_ref.shape[0]
    low_grad = dhid_ref[...].astype(jnp.bfloat16)
    datt = dot_transposed(low_grad, out_ref[0]).astype(jnp.bfloat16)
    datt_ref[...] = datt
    product = datt.astype(jnp.float32) * att_ref[...].astype(jnp.float32)
    high = product.astype(jnp.bfloat16)
    rest_low = (product - high.astype(jnp.float32)).astype(jnp.bfloat16)
    feature = lax.broadcasted_iota(jnp.int32, (16, FEATURES), 1)
    head = lax.broadcasted_iota(jnp.int32, (16, FEATURES), 0)
    chosen = ((feature >= head * HD) & (feature < (head + 1) * HD)).astype(jnp.bfloat16)
    delta = dot_transposed(chosen, high) + dot_transposed(chosen, rest_low)
    for index in range(H):
        delta_ref[index] = delta[index : index + 1]
    bias_ref[...] = allowed_bias(count, [lengths_ref[micro, d] for d in range(docs)], docs, 1)

    def one_pair(pair, carry):
        lanes = pl.multiple_of(pair * 2 * HD, 2 * HD)
        dq_ref[...] = jnp.zeros_like(dq_ref)
        for block in range(count // BLOCK):
            keys = slice(block * BLOCK, (block + 1) * BLOCK)
            rows = slice(block * BLOCK, min(count, (block + 1 + back) * BLOCK))
            key = head_split(mixed_ref[keys, pl.ds(FEATURES + lanes, 2 * HD)])
            value = head_split(mixed_ref[keys, pl.ds(2 * FEATURES + lanes, 2 * HD)])
            query = mixed_ref[rows, pl.ds(lanes, 2 * HD)]
            datt_pair = datt_ref[rows, pl.ds(lanes, 2 * HD)]
            scores = dot_transposed(key, query)
            dprobs = dot_transposed(value, datt_pair)
            bias = bias_ref[keys, rows]
            probs_low, dscores_low = ([], [])
            for half in range(2):
                part = slice(half * BLOCK, (half + 1) * BLOCK)
                lse = lse_ref[2 * pair + half, :, rows]
                delta = delta_ref[2 * pair + half, :, rows]
                probs = jnp.exp((scores[part] * 0.125 + bias) - lse)
                dscores = probs * (dprobs[part] - delta)
                probs_low.append(probs.astype(jnp.bfloat16))
                dscores_low.append(dscores.astype(jnp.bfloat16))
            probs_low = jnp.concatenate(probs_low, axis=0)
            dscores_low = jnp.concatenate(dscores_low, axis=0)
            dvalue = head_join(dot(probs_low, datt_pair))
            dkey = head_join(dot(dscores_low, query)) * 0.125
            dq_ref[rows, :] += transposed_dot(dscores_low, key)
            gmix_ref[keys, pl.ds(FEATURES + lanes, 2 * HD)] = dkey.astype(jnp.bfloat16)
            gmix_ref[keys, pl.ds(2 * FEATURES + lanes, 2 * HD)] = dvalue.astype(jnp.bfloat16)
        gmix_ref[:, pl.ds(lanes, 2 * HD)] = (dq_ref[...] * 0.125).astype(jnp.bfloat16)
        return carry

    lax.fori_loop(0, H // 2, one_pair, 0)


def attention_backward(micro, lengths, dhid, count, back, att, mixed, lse, weight):
    width = dhid.shape[1]
    docs = lengths.shape[1]
    outs = jax.ShapeDtypeStruct((count, 3 * width), jnp.bfloat16)
    inputs = [dhid, att, mixed, lse, weight]
    return pl.pallas_call(
        functools.partial(attention_backward_kernel, docs, back, micro),
        grid=(1,),
        out_shape=outs,
        in_specs=[
            SMEM,
            pl.BlockSpec((count, width), lambda i: (micro, 0)),
            pl.BlockSpec((count, width), lambda i: (micro, 0)),
            pl.BlockSpec((count, 3 * width), lambda i: (micro, 0)),
            pl.BlockSpec((H, 1, count), lambda i: (micro, 0, 0)),
            pl.BlockSpec((1, width, width), lambda i: (3, 0, 0)),
        ],
        out_specs=pl.BlockSpec((count, 3 * width), lambda i: (0, 0)),
        scratch_shapes=[
            pltpu.VMEM((count, width), jnp.bfloat16),
            pltpu.VMEM((count, count), jnp.float32),
            pltpu.VMEM((H, 1, count), jnp.float32),
            pltpu.VMEM((count, 2 * HD), jnp.float32),
        ],
        compiler_params=params(),
        cost_estimate=cost(
            2 * count * width * width + 10 * count * count * width, count * count * H, outs, outs
        ),
        name="attention_backward",
    )(lengths, *inputs)


def attention_terms_kernel(more, micro, core_ref, normed_ref, att_ref, dhid_ref, *rest):
    gmix_refs, rest = (rest[:micro], rest[micro:])
    earlier = rest[:3] if more else (None,) * 3
    if more:
        rest = rest[3:]
    mine_ref, theirs_ref, dbias_ref, left_t, right_ref = rest
    step = pl.program_id(0)
    core = core_ref[0]

    @pl.when(step == 0)
    def _():
        left_t[...] = jnp.transpose(normed_ref[...])

    @pl.when(step < 3)
    def _():
        for index, gmix_ref in enumerate(gmix_refs):
            count = gmix_ref.shape[0]
            right_ref[index * count : (index + 1) * count] = gmix_ref[...]

    @pl.when(step == 3)
    def _():
        left_t[...] = jnp.transpose(att_ref[...])
        right_ref[...] = dhid_ref[...].astype(jnp.bfloat16)

    right = right_ref[...]
    dbias = jnp.sum(right.astype(jnp.float32), axis=0, keepdims=True)
    dbias_ref[0] = dbias + earlier[2][0] if more else dbias
    store_halves(
        core, dot(left_t[...], right), mine_ref, theirs_ref, earlier[:2] if more else None
    )


def attention_terms(core, normed, att, gmix, dhid, earlier=None):
    rows, width = dhid.shape
    shape = jax.ShapeDtypeStruct
    outs = (
        shape((4, width, width // 2), jnp.bfloat16),
        shape((4, width, width // 2), jnp.bfloat16),
        shape((4, 1, width), jnp.float32),
    )
    halves = pl.BlockSpec((1, width, width // 2), lambda i: (i, 0, 0))
    summed = [halves, halves, pl.BlockSpec((1, 1, width), lambda i: (i, 0, 0))]
    inputs = [normed, att, dhid, *gmix]
    specs = [whole(normed), whole(att), whole(dhid)] + [
        pl.BlockSpec((part.shape[0], width), lambda i: (0, jnp.minimum(i, 2))) for part in gmix
    ]
    if earlier is not None:
        inputs += list(earlier)
        specs += summed
    return pl.pallas_call(
        functools.partial(attention_terms_kernel, earlier is not None, len(gmix)),
        grid=(4,),
        out_shape=outs,
        in_specs=[SMEM] + specs,
        out_specs=summed,
        scratch_shapes=[
            pltpu.VMEM((width, rows), jnp.bfloat16),
            pltpu.VMEM((rows, width), jnp.bfloat16),
        ],
        compiler_params=params(),
        cost_estimate=cost(8 * rows * width * width, 0, *inputs, *outs),
        name="attention_terms",
    )(core, *inputs)


def attention_input_kernel(more, micro, dhid_ref, state_ref, weight_ref, gain_ref, *rest):
    gmix_refs, rest = (rest[:micro], rest[micro:])
    earlier = rest[:2] if more else None
    if more:
        rest = rest[2:]
    grad_ref, dgain_ref, dshift_ref, gmix_ref = rest
    step = pl.program_id(0)
    each = pl.num_programs(0) // micro
    for index, part_ref in enumerate(gmix_refs):

        @pl.when(step // each == index)
        def _(part_ref=part_ref):
            gmix_ref[...] = part_ref[...]

    grad_norm = dot_transposed(gmix_ref[:, :FEATURES], weight_ref[0])
    for part in range(1, 3):
        grad_norm = grad_norm + dot_transposed(
            gmix_ref[:, part * FEATURES : (part + 1) * FEATURES], weight_ref[part]
        )
    normed, scale = norm_parts(state_ref[...].astype(jnp.float32))
    dgain = jnp.sum(grad_norm * normed, axis=0, keepdims=True)
    dshift = jnp.sum(grad_norm, axis=0, keepdims=True)

    @pl.when(step == 0)
    def _():
        dgain_ref[...] = dgain + earlier[0][...] if more else dgain
        dshift_ref[...] = dshift + earlier[1][...] if more else dshift

    @pl.when(step > 0)
    def _():
        dgain_ref[...] += dgain
        dshift_ref[...] += dshift

    grad = dhid_ref[...] + norm_back(normed, scale, gain_ref[...], grad_norm)
    grad_ref[...] = grad.astype(grad_ref.dtype)


def attention_input(dhid, state, gmix, weight, gain, kind, earlier=None, chunk=256):
    rows, width = dhid.shape
    shape = jax.ShapeDtypeStruct
    vector = pl.BlockSpec((1, width), lambda i: (0, 0))
    outs = (shape((rows, width), kind), shape((1, width), jnp.float32), shape((1, width), jnp.float32))
    inputs = [dhid, state, weight, gain, *gmix]
    each = rows // chunk // len(gmix)
    specs = [
        rows_of(chunk, width),
        rows_of(chunk, width),
        pl.BlockSpec((3, width, width), lambda i: (0, 0, 0), pipeline_mode=pl.Buffered(1)),
        whole(gain),
    ]
    for index in range(len(gmix)):
        specs.append(
            pl.BlockSpec(
                (chunk, 3 * width),
                lambda i, index=index: (jnp.clip(i - index * each, 0, each - 1), 0),
            )
        )
    if earlier is not None:
        inputs += list(earlier)
        specs += [vector, vector]
    return pl.pallas_call(
        functools.partial(attention_input_kernel, earlier is not None, len(gmix)),
        grid=(rows // chunk,),
        out_shape=outs,
        in_specs=specs,
        out_specs=[rows_of(chunk, width), vector, vector],
        scratch_shapes=[pltpu.VMEM((chunk, 3 * width), jnp.bfloat16)],
        compiler_params=params(),
        cost_estimate=cost(6 * rows * width * width, 0, *inputs, *outs),
        name="attention_input",
    )(*inputs)


def place_small_kernel(sizes, me_ref, small_ref, *outs):
    dp = me_ref[0] // 2
    slot = lax.broadcasted_iota(jnp.int32, (16, 1), 0)
    owner = ((slot % 4) * 4 + (slot // 8) * 2 + slot // 4 % 2) ^ dp
    for index, (size, out_ref) in enumerate(zip(sizes, outs)):
        width = 16 * size
        lane = lax.broadcasted_iota(jnp.int32, (256, width), 0)
        column = lax.broadcasted_iota(jnp.int32, (256, width), 1)
        spread = (column % size == lane).astype(jnp.bfloat16)
        rows = jnp.concatenate([small_ref[d, index : index + 1] for d in range(16)], axis=0)
        spread_rows = dot(rows, spread)
        column = lax.broadcasted_iota(jnp.int32, (1, width), 1)
        out_ref[...] = jnp.sum(
            jnp.where(column // size == owner, spread_rows, 0.0), axis=0, keepdims=True
        )


def place_small(me, small, sizes):
    return pl.pallas_call(
        functools.partial(place_small_kernel, sizes),
        out_shape=[jax.ShapeDtypeStruct((1, 16 * size), jnp.float32) for size in sizes],
        in_specs=[SMEM, pl.BlockSpec(memory_space=pltpu.VMEM)],
        out_specs=[pl.BlockSpec(memory_space=pltpu.VMEM)] * len(sizes),
        name="place_small",
    )(me, small)


def swap(value, bits):
    return lax.ppermute(value, BOTH, [(i, i ^ bits) for i in range(32)])


CORE, X, Y, Z1, Z2, Z3 = (1, 2, 4, 8, 16, 24)


def place_kernel(slots, me_ref, *refs):
    sources, (out, sems) = (refs[: len(slots)], refs[len(slots) :])
    me = me_ref[0]
    copies = []
    for source, rels in zip(sources, slots):
        for inner, rel in enumerate(rels):
            copies.append(
                pltpu.make_async_copy(
                    source.at[inner], out.at[:, rel ^ me], sems.at[len(copies)]
                )
            )
    for copy in copies:
        copy.start()
    for copy in copies:
        copy.wait()


def place(me, sources, slots):
    placed = pl.pallas_call(
        functools.partial(place_kernel, slots),
        out_shape=jax.ShapeDtypeStruct((4, 32, 24, FEATURES), jnp.bfloat16),
        in_specs=[SMEM] + [pl.BlockSpec(memory_space=pl.ANY)] * len(sources),
        out_specs=pl.BlockSpec(memory_space=pltpu.VMEM),
        scratch_shapes=[pltpu.SemaphoreType.DMA((32,))],
        name="place",
    )(me, *sources)
    return placed.reshape(4, FEATURES, FEATURES)


def after(values, *others):
    return lax.optimization_barrier((values, others))[0]


def gather_first(piece, me):
    base = (0, Z1, Z2, Z3)
    pieces = lax.optimization_barrier(
        (piece, swap(piece, Z1), swap(piece, Z2), swap(piece, Z3))
    )
    four = jnp.concatenate(pieces)
    four_x, four_y = (swap(four, X), swap(four, Y))
    four_core = swap(four, CORE)
    four_x, four_y, four_core = lax.optimization_barrier((four_x, four_y, four_core))
    near_xy, far_xy = (swap(four_y[:2], X), swap(four_x[2:], Y))
    x_core, y_core = (swap(four_x, CORE), swap(four_y, CORE))
    near_xy, far_xy, x_core, y_core = lax.optimization_barrier((near_xy, far_xy, x_core, y_core))
    parts = [four, four_x, four_y, near_xy, far_xy]
    parts += [four_core, x_core, y_core, swap(near_xy, CORE), swap(far_xy, CORE)]
    slots = [base] + [tuple(rel ^ bits for rel in base) for bits in (X, Y)]
    slots += [(X ^ Y, X ^ Y ^ Z1), (X ^ Y ^ Z2, X ^ Y ^ Z3)]
    slots += [tuple(rel ^ CORE for rel in rels) for rels in slots]
    return (place(me, parts, slots), pieces[1], four_x)


def pick(array, axis, index):
    return lax.dynamic_index_in_dim(array, index, axis, keepdims=False)


def low(value):
    return value.astype(jnp.bfloat16)


def wide(value):
    return value.astype(jnp.float32)


def add(*terms):
    total = wide(terms[0])
    for term in terms[1:]:
        total = total + wide(term)
    return total


class Reduction:
    def __init__(self, spot, views, theirs):
        self.z_pair, self.z_low, self.y, self.x, self.core = spot
        self.views = [[self.by_device(view)] for view in views]
        for terms, part in zip(self.views, theirs):
            terms.append(self.by_device(swap(part[0], CORE), part[1]))

    @staticmethod
    def by_device(view, change=None):
        view = view if change is None else change(view)
        return view.reshape(2, 2, 2, 2, *view.shape[1:])

    def sums(self, pieces, extra=None):
        total = jnp.concatenate([add(*terms) for terms in pieces], axis=-2)
        return total if extra is None else total + wide(extra)

    def chosen(self, pieces, axis, index):
        return [[pick(term, axis, index) for term in terms] for terms in pieces]

    def first(self):
        near = self.chosen(self.views, 0, self.z_pair)
        far = self.chosen(self.views, 0, 1 - self.z_pair)
        near_sent = low(self.sums(self.chosen(near, 2, 1 - self.x)))
        far_sent = low(self.sums(self.chosen(far, 1, 1 - self.y)))
        self.near = self.chosen(near, 2, self.x)
        self.far = self.chosen(far, 1, self.y)
        self.near_in, self.far_in = (swap(near_sent, X), swap(far_sent, Y))
        return (near_sent, far_sent)

    def second(self):
        near, far = (self.near, self.far)
        near_sent = low(
            self.sums(self.chosen(near, 1, 1 - self.y), pick(self.near_in, 1, 1 - self.y))
        )
        far_sent = low(
            self.sums(self.chosen(far, 1, 1 - self.x), pick(self.far_in, 1, 1 - self.x))
        )
        near = self.sums(self.chosen(near, 1, self.y), pick(self.near_in, 1, self.y))
        far = self.sums(self.chosen(far, 1, self.x), pick(self.far_in, 1, self.x))
        self.near, self.far = (low(near), low(far))
        self.near_in, self.far_in = (swap(near_sent, Y), swap(far_sent, X))
        return (near_sent, far_sent)

    def third(self):
        near, far = ((self.near, self.near_in), (self.far, self.far_in))

        def summed(pair, index):
            return add(*[pick(term, 0, index) for term in pair])

        sent = low(jnp.stack([summed(near, 1 - self.z_low), summed(far, 1 - self.z_low)]))
        self.kept = (summed(near, self.z_low), summed(far, self.z_low))
        self.back = swap(sent, Z1)
        return sent

    def last(self):
        far = low(self.kept[1] + wide(self.back[1]))
        half = self.kept[0] + wide(self.back[0]) + wide(swap(far, Z2))
        other = swap(half, CORE)
        core = self.core
        return jnp.where(core == 0, jnp.stack([half, other], -2), jnp.stack([other, half], -2))


def blocks_first(array):
    view = array.reshape(4, 16, 48, array.shape[2])
    return jnp.transpose(view, (1, 0, 2, 3)).reshape(16, 192, array.shape[2])


def rows_first(array):
    return array.reshape(16, 192, array.shape[2])


def reduce_small(small, dp):
    small = jnp.concatenate([part.reshape(-1, FEATURES) for part in small])
    for bits in (CORE, X, Y, Z1, Z2):
        small = small + swap(small, bits)

    def own(start, rows):
        vector = small[start : start + rows].reshape(-1)
        size = vector.shape[0] // 16
        return lax.dynamic_slice_in_dim(vector, dp * size, size)

    return [own(0, 1), own(1, 1), own(2, 3), own(5, 1), own(6, 1), own(7, 1), own(8, 4), own(12, 1)]


def gather_small(pieces, me):
    sizes = tuple(piece.shape[0] for piece in pieces)
    small = jnp.stack([jnp.pad(piece, (0, 256 - piece.shape[0])) for piece in pieces])[None]
    for bits in (Z1, Z2, X, Y):
        small = jnp.concatenate([small, swap(small, bits)])
    return place_small(me, small, sizes)


def gather_all(weights, spot, me):
    gain_a, shift_a, qkv, qbias, out, obias, gain_m, shift_m, fc, fbias, proj, pbias = weights
    core = spot[4]

    def half(weight):
        part = lax.dynamic_slice_in_dim(weight, core * 24, 24, 0)
        return jnp.transpose(part.reshape(24, -1, FEATURES), (1, 0, 2))

    columns = lax.dynamic_slice_in_dim(fc, core * 2 * FEATURES, 2 * FEATURES, 1)
    columns = jnp.transpose(columns.reshape(48, 2, FEATURES), (1, 0, 2))
    across = lax.dynamic_slice_in_dim(proj, core * 96, 96, 0).reshape(2, 48, FEATURES)
    mlp = lax.all_gather(jnp.concatenate([columns, across]), BOTH)
    mlp = mlp.reshape(16, 2, 4, 48, FEATURES)
    first, early, later = gather_first(jnp.concatenate([half(qkv), half(out)])[None], me)
    vectors = [gain_a, shift_a, qbias, obias, gain_m, shift_m, fbias, pbias]
    return (first, mlp, *gather_small(after(vectors, early), me))


def gather_plain(weights):
    whole_ones = [lax.all_gather(weight, "dp", axis=0, tiled=True) for weight in weights]
    gain_a, shift_a, qkv, qbias, out, obias, gain_m, shift_m, fc, fbias, proj, pbias = whole_ones

    def blocks(weight):
        return jnp.transpose(weight.reshape(FEATURES, -1, FEATURES), (1, 0, 2))

    rows = [
        wide(v).reshape(1, -1)
        for v in (gain_a, shift_a, qbias, obias, gain_m, shift_m, fbias, pbias)
    ]
    first = jnp.concatenate([blocks(qkv), blocks(out)])
    fc = blocks(fc).reshape(2, 2, 16, 48, FEATURES)
    fc = jnp.transpose(fc, (2, 0, 1, 3, 4))
    mlp = jnp.concatenate([fc, proj.reshape(16, 2, 2, 48, FEATURES)], axis=2)
    return (first, mlp, *rows)


def reduce_plain(terms):
    matrices, small = terms

    def joined(pair):
        return wide(jnp.concatenate(pair, axis=2))

    def sides(blocks):
        return jnp.transpose(blocks, (1, 0, 2)).reshape(FEATURES, -1)

    first, fc, proj = [joined(pair) for pair in matrices]
    gain_a, shift_a, bias_a, gain_m, shift_m, fbias, pbias = small
    values = (
        gain_a.reshape(-1), shift_a.reshape(-1), sides(first[:3]), bias_a[:3].reshape(-1), first[3],
        bias_a[3].reshape(-1), gain_m.reshape(-1), shift_m.reshape(-1), sides(fc), fbias.reshape(-1),
        proj.reshape(-1, FEATURES), pbias.reshape(-1),
    )
    return tuple(
        wide(lax.psum(low(lax.psum_scatter(v, "dp", scatter_dimension=0, tiled=True)), "rep"))
        for v in values
    )


def forward(tokens, lengths, count, back, weights):
    weight, mlp, gain_a, shift_a, qbias, obias, gain_m, shift_m, fbias, pbias = weights
    state, kept = (tokens, [])
    for use in range(USES):
        normed_a, mixed, att, lse, hidden, normed_m = attention_forward(
            lengths, state, count, back, gain_a, shift_a, weight, qbias, obias, gain_m, shift_m
        )
        expanded, after_mlp = mlp_forward(hidden, normed_m, mlp, fbias, pbias, use == USES - 1)
        kept.append((state, normed_a, mixed, att, lse, hidden, normed_m, expanded))
        state = after_mlp
    return (state, kept)


def shards(custom, tokens, doc_lengths, cotangent, *weights):
    micro, count, width = tokens.shape
    dp, core = (lax.axis_index("dp"), lax.axis_index("rep"))
    spot = (dp // 8, dp // 4 % 2, dp // 2 % 2, dp % 2, core)
    me = (dp * 2 + core).astype(jnp.int32).reshape(1)
    side = core.astype(jnp.int32).reshape(1) if custom else jnp.zeros((1,), jnp.int32)
    back = -(-(LONGEST - 1) // BLOCK)
    lengths = doc_lengths.reshape(micro, doc_lengths.shape[-1])
    whole_ones = gather_all(weights, spot, me) if custom else gather_plain(weights)
    state, kept = forward(
        tokens.reshape(micro * count, width), lengths, count, back, whole_ones
    )
    weight, mlp, gain_a, gain_m = (whole_ones[0], whole_ones[1], whole_ones[2], whole_ones[6])
    grad, mlp_terms, terms, norm = (cotangent.reshape(micro * count, width), None, None, None)
    for use in range(USES - 1, -1, -1):
        before, normed_a, mixed, att, lse, hidden, normed_m, expanded = kept[use]
        dhid, *mlp_terms = mlp_backward(
            side, grad, hidden, normed_m, expanded, mlp, gain_m, mlp_terms
        )
        sending = custom and use == 0
        if sending:
            fc_mine, fc_theirs, proj_mine, proj_theirs = mlp_terms[:4]
            sums = Reduction(
                spot,
                (blocks_first(fc_mine), rows_first(proj_mine)),
                ((fc_theirs, blocks_first), (proj_theirs, rows_first)),
            )
        gmix = []
        for index in range(micro):
            if sending and index == micro - 1:
                dhid, *unused = after((dhid, gmix), sums.first())
                gmix = list(unused[0])
            gmix.append(
                attention_backward(index, lengths, dhid, count, back, att, mixed, lse, weight)
            )
        terms = attention_terms(side, normed_a, att, gmix, dhid, terms)
        if sending:
            gmix, terms, unused = lax.optimization_barrier((gmix, terms, sums.second()))
            attention_sums = Reduction(
                spot, (blocks_first(terms[0]),), ((terms[1], blocks_first),)
            )
        kind = jnp.float32 if use else jnp.bfloat16
        grad, *norm = attention_input(dhid, before, gmix, weight, gain_a, kind, norm)
    small = (norm[0], norm[1], terms[2], mlp_terms[6], mlp_terms[7], mlp_terms[4], mlp_terms[5])
    if custom:
        sums.third()
        attention_sums.first()
        attention_sums.second()
        attention_sums.third()
        fc, proj = jnp.split(sums.last(), 2)
        first = attention_sums.last()

        def columns(array):
            return jnp.transpose(array.reshape(4, 48, width), (1, 0, 2)).reshape(48, 4 * width)

        first = columns(first)
        gain_a, shift_a, qbias, obias, gain_m, shift_m, fbias, pbias = reduce_small(small, dp)
        final = (
            gain_a, shift_a, first[:, : 3 * width], qbias, first[:, 3 * width :], obias,
            gain_m, shift_m, columns(fc), fbias, proj.reshape(192, width), pbias,
        )
    else:
        matrices = (terms[:2], mlp_terms[:2], mlp_terms[2:4])
        final = reduce_plain((matrices, small))
    return (state.reshape(tokens.shape), grad.reshape(tokens.shape), *final)


def solution(mesh):
    custom = mesh.shape["dp"] == 16 and mesh.shape["rep"] == 2
    placed = tuple(
        P("dp", None) if index in (2, 4, 8, 10) else P("dp") for index in range(12)
    )
    rows = P(None, BOTH, None)
    return jax.shard_map(
        functools.partial(shards, custom),
        mesh=mesh,
        in_specs=(rows, rows, rows, *placed),
        out_specs=(rows, rows, *placed),
        check_vma=False,
    )
```

time: 668 us -> 457 us (0.68)
  matrix products: 308 us -> 0 us
  Pallas kernels: 14.5 us -> 268 us
  starting transfers between devices: 105 us -> 40.3 us
  other arithmetic: 87 us -> 23.9 us
  local copies, waits for them, and re-layouts: 60.6 us -> 26.8 us
  between operations: 3.21 us -> 15.2 us
  waiting for transfers between devices: 85.9 us -> 78.8 us
    dot_general x48 -> x0, matrix products: 308 us -> none  [the longest x8 72.4 us: outer_sum(): lax.dot_general(left, right, (((0,), (0,)), ((), ())), preferred_element_...]
    pallas_call x3 -> x16, Pallas kernels: 14.5 us -> 268 us  [the longest x2 68.4 us: mlp_backward(): pl.pallas_call(functools.partial(mlp_backward_kernel, earlier is not None...]
    ppermute x97 -> x38, starting transfers between devices: 105 us -> 40.2 us  [swap(): return lax.ppermute(value, BOTH, [(i, i ^ bits) for i in range(32)])]
    convert_element_type x7 -> x0, other arithmetic: 36.2 us -> none  [the longest x4 36 us: attend_backward(): score_low = grad_scores.astype(jnp.bfloat16)]
    reduce_sum x20 -> x0, other arithmetic: 28 us -> none  [the longest x4 10.3 us: attend_forward(): total = jnp.sum(expo, axis=-1, keepdims=True)]
    slice x11 -> x7, local copies, waits for them, and re-layouts: 23.5 us -> 1.53 us  [the longest x1 0.79 us: shards(): first[:, :3 * width]]
    reshape x1 -> x13, local copies, waits for them, and re-layouts: 0.02 us -> 10.6 us  [the longest x4 8.18 us: blocks_first(): view = array.reshape(4, 16, 48, array.shape[2])]
    squeeze x4 -> x0, local copies, waits for them, and re-layouts: 8.15 us -> none  [pick(): return lax.dynamic_index_in_dim(array, index, axis, keepdims=False)]
  transfers between devices with their start and end apart: 97 -> 39, of which waited for: 27 -> 18; matrix products, arithmetic and copies ran while one was open for 16% -> 7% of each run, Pallas kernels for 1% -> 22%
where the time goes in v1:
time: 457 us; the launch traced here: 453 us
  Pallas kernels  268 us (59%)
  waiting for transfers between devices  78.8 us (17%)
  starting transfers between devices  40.3 us (9%)
  local copies, waits for them, and re-layouts  26.8 us (6%)
  other arithmetic  23.9 us (5%)
  between operations  15.2 us (3%)
    ppermute x38, waiting for transfers between devices, swap(): return lax.ppermute(value, BOTH, [(i, i ^ bits) for i in range(32)])  78.8 us
    pallas_call x2, Pallas kernels, mlp_backward(): pl.pallas_call(functools.partial(mlp_backward_kernel, earlier is not None...  68.4 us
    pallas_call x2, Pallas kernels, attention_forward(): pl.pallas_call(functools.partial(attention_forward_kernel, docs, back), g...  55.8 us
    pallas_call x4, Pallas kernels, attention_backward(): pl.pallas_call(functools.partial(attention_backward_kernel, docs, back, m...  55.1 us
    ppermute x38, starting transfers between devices, swap(): return lax.ppermute(value, BOTH, [(i, i ^ bits) for i in range(32)])  40.2 us
    pallas_call x2, Pallas kernels, mlp_forward(): pl.pallas_call(functools.partial(mlp_forward_kernel, last), grid=(hidden_...  34.2 us
    pallas_call x2, Pallas kernels, attention_terms(): pl.pallas_call(functools.partial(attention_terms_kernel, earlier is not N...  25 us
    pallas_call x2, Pallas kernels, attention_input(): pl.pallas_call(functools.partial(attention_input_kernel, earlier is not N...  21.8 us
  transfers between devices with their start and end apart: 39, of which 18 were waited for; matrix products, arithmetic and copies ran while one was open for 7% of the time, Pallas kernels for 22%

profile of v1, /device:TPU:1, one launch (start us, length us, event | category | flops | bytes accessed | tf_op | source)
XLA Modules:
  0.0 452.8 jit_solution(17648091307510152854)
XLA Ops:
  10.5 4.2 collective-permute-start.2
  15.0 3.3 collective-permute-done.2
  18.3 10.4 %collective-permute-done.1 = bf16[1,4,24,768]{3,2,1,0:T(8,128)(2,1)S(1)} collective-permute-done((bf16[1,4,24,768]{3,2,1,0:T(8,128)(2,1)S(1)}, bf16[1,4,24,768]{3,2,1,0:T(8,128)(2,1)S(1)}, u32[]{:S(2)}, u32[]{:S(2)}) %collective-permute-start.1) | collective-permute-done | bytes 147488 | tf_op jit(solution)/shard_map/ppermute | solution.py:714
  28.8 3.0 collective-permute-start.9
  31.8 1.6 collective-permute-start.8
  33.4 1.8 collective-permute-start.7
  35.6 15.1 %collective-permute-done.8.refs_2_ = bf16[4,4,24,768]{3,2,1,0:T(8,128)(2,1)S(1)} collective-permute-done((bf16[4,4,24,768]{3,2,1,0:T(8,128)(2,1)S(1)}, bf16[4,4,24,768]{3,2,1,0:T(8,128)(2,1)S(1)}, u32[]{:S(2)}, u32[]{:S(2)}) %collective-permute-start.8) | collective-permute-done | bytes 589856 | tf_op jit(solution)/shard_map/ppermute | solution.py:714
  50.6 3.3 collective-permute-done.7.refs_1_
  54.0 2.7 collective-permute-start.12
  57.3 2.3 collective-permute-start.10
  60.8 2.2 collective-permute-start.5
  63.6 2.9 collective-permute-done.10.refs_3_
  68.2 1.7 collective-permute-start.14
  70.5 3.0 collective-permute-done.6
  74.2 2.7 place_small.1
  77.0 4.9 %place.1 = bf16[4,32,24,768]{3,2,1,0:T(8,128)(2,1)} custom-call(s32[1]{0:T(128)} %bitcast.2.me_ref, bf16[4,4,24,768]{3,2,1,0:T(8,128)(2,1)} %copy-done.9, bf16[4,4,24,768]{3,2,1,0:T(8,128)(2,1)} %copy-done.8, bf16[4,4,24,768]{3,2,1,0:T(8,128)(2,1)} %copy-done.7, bf16[2,4,24,768]{3,2,1,0:T(8,128)(2,1)} %copy-done.13, bf16[2,4,24,768]{3,2,1,0:T(8,128)(2,1)} %copy-done.14, ...), custom_call_target="tpu_custom_call" | custom-call | tf_op jit(solution)/shard_map/place/pallas_call | solution.py:738
  81.9 27.9 %attention_forward.2 = (bf16[1024,768]{1,0:T(8,128)(2,1)}, bf16[1024,2304]{1,0:T(8,128)(2,1)}, bf16[1024,768]{1,0:T(8,128)(2,1)}, f32[24,1,512]{2,1,0:T(1,128)},...) custom-call(s32[2,6]{1,0:T(2,128)} %bitcast.230, bf16[1024,768]{1,0:T(8,128)(2,1)} %bitcast.213, ...), custom_call_target="tpu_custom_call" | custom-call | flops 6442450944 | bytes 18948096 | tf_op jit(solution)/shard_map/attention_forward/pallas_call | solution.py:180
  109.8 16.9 %mlp_forward.2 = (bf16[1024,3072]{1,0:T(8,128)(2,1)}, f32[1024,768]{1,0:T(8,128)}) custom-call(f32[1024,768]{1,0:T(8,128)} %get-tuple-element.119.hidden_ref, bf16[1024,768]{1,0:T(8,128)(2,1)} %get-tuple-element.120.normed_ref, bf16[16,2,4,48,768]{4,3,2,1,0:T(8,128)(2,1)} %bitcast.236, f32[1,3072]{1,0:T(1,128)} %get-tuple-element.121.fbias_ref, ...), custom_call_target="tpu_custom_call" | custom-call | flops 9663676416 | bytes 23592960 | tf_op jit(solution)/shard_map/mlp_forward/pallas_call | solution.py:262
  126.7 27.9 %attention_forward.3 = (bf16[1024,768]{1,0:T(8,128)(2,1)}, bf16[1024,2304]{1,0:T(8,128)(2,1)}, bf16[1024,768]{1,0:T(8,128)(2,1)}, f32[24,1,512]{2,1,0:T(1,128)},...) custom-call(s32[2,6]{1,0:T(2,128)} %bitcast.231, f32[1024,768]{1,0:T(8,128)} %get-tuple-element.123.state_ref, ...), custom_call_target="tpu_custom_call" | custom-call | flops 6442450944 | bytes 20520960 | tf_op jit(solution)/shard_map/attention_forward/pallas_call | solution.py:180
  154.7 17.3 %mlp_forward.3 = (bf16[1024,3072]{1,0:T(8,128)(2,1)}, bf16[1024,768]{1,0:T(8,128)(2,1)}) custom-call(f32[1024,768]{1,0:T(8,128)} %get-tuple-element.124.hidden_ref, bf16[1024,768]{1,0:T(8,128)(2,1)} %get-tuple-element.125.normed_ref, bf16[16,2,4,48,768]{4,3,2,1,0:T(8,128)(2,1)} %bitcast.238, f32[1,3072]{1,0:T(1,128)} %get-tuple-element.121.fbias_ref, ...), custom_call_target="tpu_custom_call" | custom-call | flops 9663676416 | bytes 22020096 | tf_op jit(solution)/shard_map/mlp_forward/pallas_call | solution.py:262
  171.9 33.1 %mlp_backward.2 = (f32[1024,768]{1,0:T(8,128)}, bf16[4,768,384]{2,1,0:T(8,128)(2,1)}, bf16[4,768,384]{2,1,0:T(8,128)(2,1)}, bf16[4,768,384]{2,1,0:T(8,128)(2,1)}...) custom-call(s32[1]{0:T(128)} %bitcast.12.core_ref, ...), custom_call_target="tpu_custom_call" | custom-call | flops 19327352832 | bytes 44064768 | tf_op jit(solution)/shard_map/mlp_backward/pallas_call | solution.py:431
  205.1 13.7 %attention_backward.5.rest_1_ = bf16[512,2304]{1,0:T(8,128)(2,1)} custom-call(s32[2,6]{1,0:T(2,128)} %bitcast.232, f32[1024,768]{1,0:T(8,128)} %get-tuple-element.128.dhid_ref, bf16[1024,768]{1,0:T(8,128)(2,1)} %get-tuple-element.129.att_ref, bf16[1024,2304]{1,0:T(8,128)(2,1)} %get-tuple-element.130.mixed_ref, f32[24,1,512]{2,1,0:T(1,128)} %get-tuple-element.131.lse_ref, ...), custom_call_target="tpu_custom_call" | custom-call | flops 2617245696 | bytes 4718592 | tf_op jit(solution)/shard_map/attention_backward/pallas_call | solution.py:521
  218.8 13.7 %attention_backward.4.rest_0_ = bf16[512,2304]{1,0:T(8,128)(2,1)} custom-call(s32[2,6]{1,0:T(2,128)} %bitcast.233, f32[1024,768]{1,0:T(8,128)} %get-tuple-element.128.dhid_ref, bf16[1024,768]{1,0:T(8,128)(2,1)} %get-tuple-element.129.att_ref, bf16[1024,2304]{1,0:T(8,128)(2,1)} %get-tuple-element.130.mixed_ref, f32[24,1,512]{2,1,0:T(1,128)} %get-tuple-element.131.lse_ref, ...), custom_call_target="tpu_custom_call" | custom-call | flops 2617245696 | bytes 4718592 | tf_op jit(solution)/shard_map/attention_backward/pallas_call | solution.py:521
  232.5 11.1 %attention_input.2 = (f32[1024,768]{1,0:T(8,128)}, f32[1,768]{1,0:T(1,128)}, f32[1,768]{1,0:T(1,128)}) custom-call(f32[1024,768]{1,0:T(8,128)} %get-tuple-element.128.dhid_ref, f32[1024,768]{1,0:T(8,128)} %get-tuple-element.123.state_ref, bf16[4,768,768]{2,1,0:T(8,128)(2,1)} %bitcast.185, f32[1,768]{1,0:T(1,128)} %get-tuple-element.103.gain_ref, ...), custom_call_target="tpu_custom_call" | custom-call | flops 3623878656 | bytes 18883584 | tf_op jit(solution)/shard_map/attention_input/pallas_call | solution.py:673
  243.6 35.3 %mlp_backward.3 = (f32[1024,768]{1,0:T(8,128)}, bf16[4,768,384]{2,1,0:T(8,128)(2,1)}, bf16[4,768,384]{2,1,0:T(8,128)(2,1)}, bf16[4,768,384]{2,1,0:T(8,128)(2,1)}...) custom-call(s32[1]{0:T(128)} %bitcast.12.core_ref, ...), custom_call_target="tpu_custom_call" | custom-call | flops 19327352832 | bytes 55096320 | tf_op jit(solution)/shard_map/mlp_backward/pallas_call | solution.py:431
  278.9 1.5 collective-permute-start.16
  280.4 2.0 copy.131
  282.5 13.9 %attention_backward.6.rest_0_ = bf16[512,2304]{1,0:T(8,128)(2,1)} custom-call(s32[2,6]{1,0:T(2,128)} %bitcast.234, f32[1024,768]{1,0:T(8,128)} %get-tuple-element.150.dhid_ref, bf16[1024,768]{1,0:T(8,128)(2,1)} %get-tuple-element.143.att_ref, bf16[1024,2304]{1,0:T(8,128)(2,1)} %get-tuple-element.144.mixed_ref, f32[24,1,512]{2,1,0:T(1,128)} %get-tuple-element.145.lse_ref, ...), custom_call_target="tpu_custom_call" | custom-call | flops 2617245696 | bytes 4718592 | tf_op jit(solution)/shard_map/attention_backward/pallas_call | solution.py:521
  296.4 11.7 %attention_terms.2 = (bf16[4,768,384]{2,1,0:T(8,128)(2,1)}, bf16[4,768,384]{2,1,0:T(8,128)(2,1)}, f32[4,1,768]{2,1,0:T(1,128)}) custom-call(s32[1]{0:T(128)} %bitcast.12.core_ref, bf16[1024,768]{1,0:T(8,128)(2,1)} %get-tuple-element.153.normed_ref, bf16[1024,768]{1,0:T(8,128)(2,1)} %get-tuple-element.129.att_ref, f32[1024,768]{1,0:T(8,128)} %get-tuple-element.128.dhid_ref, ...), custom_call_target="tpu_custom_call" | custom-call | flops 4831838208 | bytes 15740928 | tf_op jit(solution)/shard_map/attention_terms/pallas_call | solution.py:597
  308.2 2.0 copy.133
  310.5 1.3 copy-done.6
  311.9 1.2 fusion.5
  313.1 1.2 fusion.7
  314.3 1.2 pad_maximum_fusion.1
  315.5 1.1 pad_maximum_fusion
  318.6 1.5 add_bitcast_fusion.2
  320.0 13.7 %attention_backward.7.rest_1_ = bf16[512,2304]{1,0:T(8,128)(2,1)} custom-call(s32[2,6]{1,0:T(2,128)} %bitcast.235, f32[1024,768]{1,0:T(8,128)} %get-tuple-element.150.dhid_ref, bf16[1024,768]{1,0:T(8,128)(2,1)} %get-tuple-element.143.att_ref, bf16[1024,2304]{1,0:T(8,128)(2,1)} %get-tuple-element.144.mixed_ref, f32[24,1,512]{2,1,0:T(1,128)} %get-tuple-element.145.lse_ref, ...), custom_call_target="tpu_custom_call" | custom-call | flops 2617245696 | bytes 4718592 | tf_op jit(solution)/shard_map/attention_backward/pallas_call | solution.py:521
  333.8 13.2 %attention_terms.3 = (bf16[4,768,384]{2,1,0:T(8,128)(2,1)}, bf16[4,768,384]{2,1,0:T(8,128)(2,1)}, f32[4,1,768]{2,1,0:T(1,128)}) custom-call(s32[1]{0:T(128)} %bitcast.12.core_ref, bf16[1024,768]{1,0:T(8,128)(2,1)} %get-tuple-element.152.normed_ref, bf16[1024,768]{1,0:T(8,128)(2,1)} %get-tuple-element.143.att_ref, f32[1024,768]{1,0:T(8,128)} %get-tuple-element.150.dhid_ref, ...), custom_call_target="tpu_custom_call" | custom-call | flops 4831838208 | bytes 20471808 | tf_op jit(solution)/shard_map/attention_terms/pallas_call | solution.py:597
  347.0 2.9 fusion.3
  349.9 2.5 fusion.2
  353.1 1.7 collective-permute-start.34
  354.8 1.4 collective-permute-start.33
  356.3 2.1 copy.149
  358.4 10.4 %collective-permute-done.34 = bf16[2,384,384]{2,1,0:T(8,128)(2,1)} collective-permute-done((bf16[2,384,384]{2,1,0:T(8,128)(2,1)}, bf16[2,384,384]{2,1,0:T(8,128)(2,1)}, u32[]{:S(2)}, u32[]{:S(2)}) %collective-permute-start.34) | collective-permute-done | bytes 589856 | tf_op jit(solution)/shard_map/ppermute | solution.py:714
  368.8 1.0 add_convert_fusion.7
  369.8 1.0 add_convert_fusion.8
  370.9 2.0 copy.151
  373.2 1.1 copy-done.2
  375.3 1.3 collective-permute-start.26
  377.6 1.4 collective-permute-start.28
  379.9 1.5 collective-permute-start.35
  381.5 10.7 %attention_input.3 = (bf16[1024,768]{1,0:T(8,128)(2,1)}, f32[1,768]{1,0:T(1,128)}, f32[1,768]{1,0:T(1,128)}) custom-call(f32[1024,768]{1,0:T(8,128)} %get-tuple-element.150.dhid_ref, bf16[1024,768]{1,0:T(8,128)(2,1)} %bitcast.214, bf16[4,768,768]{2,1,0:T(8,128)(2,1)} %bitcast.188, f32[1,768]{1,0:T(1,128)} %get-tuple-element.103.gain_ref, ...), custom_call_target="tpu_custom_call" | custom-call | flops 3623878656 | bytes 15744000 | tf_op jit(solution)/shard_map/attention_input/pallas_call | solution.py:673
  393.0 1.7 collective-permute-start.20
  396.0 2.5 collective-permute-done.21
  398.6 2.9 collective-permute-done.22
  401.6 2.9 collective-permute-done.23
  405.4 3.4 collective-permute-done.24
  408.9 2.1 fusion.13
  411.5 1.2 fusion.14
  413.2 3.4 collective-permute-done.27
  417.5 6.6 %collective-permute-done.36 = bf16[384,384]{1,0:T(8,128)(2,1)S(1)} collective-permute-done((bf16[384,384]{1,0:T(8,128)(2,1)S(1)}, bf16[384,384]{1,0:T(8,128)(2,1)S(1)}, u32[]{:S(2)}, u32[]{:S(2)}) %collective-permute-start.36) | collective-permute-done | bytes 294944 | tf_op jit(solution)/shard_map/ppermute | solution.py:714
  424.1 1.2 bitcast_add_fusion
  425.3 5.3 %collective-permute-start.37 = (f32[384,384]{1,0:T(8,128)S(1)}, f32[384,384]{1,0:T(8,128)S(1)}, u32[]{:S(2)}, u32[]{:S(2)}) collective-permute-start(f32[384,384]{1,0:T(8,128)S(1)} %bitcast_add_fusion), channel_id=1, source_target_pairs={{0,1},{1,0},{2,3},{3,2},{4,5},{5,4},{6,7},{7,6},{8,9},{9,8},{10,11... | collective-permute-start | bytes 1769480 | tf_op jit(solution)/shard_map/ppermute | solution.py:714
  433.2 6.2 %collective-permute-done.31 = bf16[192,384]{1,0:T(8,128)(2,1)S(1)} collective-permute-done((bf16[192,384]{1,0:T(8,128)(2,1)S(1)}, bf16[192,384]{1,0:T(8,128)(2,1)S(1)}, u32[]{:S(2)}, u32[]{:S(2)}) %collective-permute-start.31) | collective-permute-done | bytes 147488 | tf_op jit(solution)/shard_map/ppermute | solution.py:714
  (192 shorter events, 29.4 us)
Async XLA Ops:
  7.2 3.2 copy-start.15
  7.2 3.2 copy-start.16
  7.2 28.1 %copy-start.27 = (bf16[48]{0:T(256)(128)(2,1)S(1)}, bf16[48]{0:T(256)(128)(2,1)}, u32[]{:S(2)}) copy-start(bf16[48]{0:T(256)(128)(2,1)} %param.25) | copy-start | bytes 292
  7.2 28.1 %copy-start.26 = (bf16[48]{0:T(256)(128)(2,1)S(1)}, bf16[48]{0:T(256)(128)(2,1)}, u32[]{:S(2)}) copy-start(bf16[48]{0:T(256)(128)(2,1)} %param.24) | copy-start | bytes 292
  7.2 28.0 %copy-start.25 = (bf16[48]{0:T(256)(128)(2,1)S(1)}, bf16[48]{0:T(256)(128)(2,1)}, u32[]{:S(2)}) copy-start(bf16[48]{0:T(256)(128)(2,1)} %param.23) | copy-start | bytes 292
  7.3 28.0 %copy-start.24 = (bf16[144]{0:T(256)(128)(2,1)S(1)}, bf16[144]{0:T(256)(128)(2,1)}, u32[]{:S(2)}) copy-start(bf16[144]{0:T(256)(128)(2,1)} %param.21) | copy-start | bytes 868
  7.3 27.9 %copy-start.23 = (bf16[48]{0:T(256)(128)(2,1)S(1)}, bf16[48]{0:T(256)(128)(2,1)}, u32[]{:S(2)}) copy-start(bf16[48]{0:T(256)(128)(2,1)} %param.19) | copy-start | bytes 292
  7.3 27.9 %copy-start.22 = (bf16[48]{0:T(256)(128)(2,1)S(1)}, bf16[48]{0:T(256)(128)(2,1)}, u32[]{:S(2)}) copy-start(bf16[48]{0:T(256)(128)(2,1)} %param.18) | copy-start | bytes 292
  7.3 102.5 %all-gather.3.cloned.1.call-start = ((), (), s32[]{:S(2)}) async-start(), calls=%async_computation | async-start | bytes 9732096 | tf_op jit(solution)/shard_map/all_gather | solution.py:895
  7.3 28.0 %copy-start.28 = (bf16[192]{0:T(256)(128)(2,1)S(1)}, bf16[192]{0:T(256)(128)(2,1)}, u32[]{:S(2)}) copy-start(bf16[192]{0:T(256)(128)(2,1)} %param.27) | copy-start | bytes 1156
  7.3 28.1 %copy-start.29 = (bf16[48]{0:T(256)(128)(2,1)S(1)}, bf16[48]{0:T(256)(128)(2,1)}, u32[]{:S(2)}) copy-start(bf16[48]{0:T(256)(128)(2,1)} %param.29) | copy-start | bytes 292
  10.5 7.8 %collective-permute-start.2 = (bf16[1,4,24,768]{3,2,1,0:T(8,128)(2,1)S(1)}, bf16[1,4,24,768]{3,2,1,0:T(8,128)(2,1)S(1)}, u32[]{:S(2)}, u32[]{:S(2)}) collective-permute-start(bf16[1,4,24,768]{3,2,1,0:T(8,128)(2,1)S(1)} %maximum_bitcast_fusion), channel_id=1, source_target_pairs={{0,24},{1,25},{2,26},{3,27},{4,28},{5,29},{6,30},{7,31},{8,16},{9,... | collective-permute-start | bytes 442376 | tf_op jit(solution)/shard_map/ppermute | solution.py:714
  14.7 14.0 %collective-permute-start.1 = (bf16[1,4,24,768]{3,2,1,0:T(8,128)(2,1)S(1)}, bf16[1,4,24,768]{3,2,1,0:T(8,128)(2,1)S(1)}, u32[]{:S(2)}, u32[]{:S(2)}) collective-permute-start(bf16[1,4,24,768]{3,2,1,0:T(8,128)(2,1)S(1)} %maximum_bitcast_fusion), channel_id=1, source_target_pairs={{0,16},{1,17},{2,18},{3,19},{4,20},{5,21},{6,22},{7,23},{8,24},{9,... | collective-permute-start | bytes 442376 | tf_op jit(solution)/shard_map/ppermute | solution.py:714
  14.7 14.0 %collective-permute-start = (bf16[1,4,24,768]{3,2,1,0:T(8,128)(2,1)S(1)}, bf16[1,4,24,768]{3,2,1,0:T(8,128)(2,1)S(1)}, u32[]{:S(2)}, u32[]{:S(2)}) collective-permute-start(bf16[1,4,24,768]{3,2,1,0:T(8,128)(2,1)S(1)} %maximum_bitcast_fusion), channel_id=1, source_target_pairs={{0,8},{1,9},{2,10},{3,11},{4,12},{5,13},{6,14},{7,15},{8,0},{9,1},... | collective-permute-start | bytes 442376 | tf_op jit(solution)/shard_map/ppermute | solution.py:714
  28.8 48.2 %copy-start.9 = (bf16[4,4,24,768]{3,2,1,0:T(8,128)(2,1)}, bf16[4,4,24,768]{3,2,1,0:T(8,128)(2,1)S(1)}, u32[]{:S(2)}) copy-start(bf16[4,4,24,768]{3,2,1,0:T(8,128)(2,1)S(1)} %constant_dynamic-update-slice_fusion.5.refs_0_) | copy-start | bytes 1769476
  28.8 6.8 %collective-permute-start.9 = (bf16[4,4,24,768]{3,2,1,0:T(8,128)(2,1)S(1)}, bf16[4,4,24,768]{3,2,1,0:T(8,128)(2,1)S(1)}, u32[]{:S(2)}, u32[]{:S(2)}) collective-permute-start(bf16[4,4,24,768]{3,2,1,0:T(8,128)(2,1)S(1)} %constant_dynamic-update-slice_fusion.5.refs_0_), channel_id=1, source_target_pairs={{0,1},{1,0},{2,3},{3,2},{4,5},{5,4},{6,7},{7,6},{8,9},{9,8},{10,11... | collective-permute-start | bytes 1769480 | tf_op jit(solution)/shard_map/ppermute | solution.py:714
  31.8 18.8 %collective-permute-start.8 = (bf16[4,4,24,768]{3,2,1,0:T(8,128)(2,1)S(1)}, bf16[4,4,24,768]{3,2,1,0:T(8,128)(2,1)S(1)}, u32[]{:S(2)}, u32[]{:S(2)}) collective-permute-start(bf16[4,4,24,768]{3,2,1,0:T(8,128)(2,1)S(1)} %constant_dynamic-update-slice_fusion.5.refs_0_), channel_id=1, source_target_pairs={{0,4},{1,5},{2,6},{3,7},{4,0},{5,1},{6,2},{7,3},{8,12},{9,13},{10,... | collective-permute-start | bytes 1769480 | tf_op jit(solution)/shard_map/ppermute | solution.py:714
  33.4 20.6 %collective-permute-start.7 = (bf16[4,4,24,768]{3,2,1,0:T(8,128)(2,1)S(1)}, bf16[4,4,24,768]{3,2,1,0:T(8,128)(2,1)S(1)}, u32[]{:S(2)}, u32[]{:S(2)}) collective-permute-start(bf16[4,4,24,768]{3,2,1,0:T(8,128)(2,1)S(1)} %constant_dynamic-update-slice_fusion.5.refs_0_), channel_id=1, source_target_pairs={{0,2},{1,3},{2,0},{3,1},{4,6},{5,7},{6,4},{7,5},{8,10},{9,11},{10,... | collective-permute-start | bytes 1769480 | tf_op jit(solution)/shard_map/ppermute | solution.py:714
  35.5 21.7 %collective-permute-start.3 = (bf16[1,8,256]{2,1,0:T(8,128)(2,1)S(1)}, bf16[1,8,256]{2,1,0:T(8,128)(2,1)S(1)}, u32[]{:S(2)}, u32[]{:S(2)}) collective-permute-start(bf16[1,8,256]{2,1,0:T(8,128)(2,1)S(1)} %bitcast.224), channel_id=1, source_target_pairs={{0,8},{1,9},{2,10},{3,11},{4,12},{5,13},{6,14},{7,15},{8,0},{9,1},... | collective-permute-start | bytes 12296 | tf_op jit(solution)/shard_map/ppermute | solution.py:714
  35.6 41.4 %copy-start.10 = (bf16[4,4,24,768]{3,2,1,0:T(8,128)(2,1)}, bf16[4,4,24,768]{3,2,1,0:T(8,128)(2,1)S(1)}, u32[]{:S(2)}) copy-start(bf16[4,4,24,768]{3,2,1,0:T(8,128)(2,1)S(1)} %collective-permute-done.9.refs_5_) | copy-start | bytes 1769476
  50.6 26.3 %copy-start.7 = (bf16[4,4,24,768]{3,2,1,0:T(8,128)(2,1)}, bf16[4,4,24,768]{3,2,1,0:T(8,128)(2,1)S(1)}, u32[]{:S(2)}) copy-start(bf16[4,4,24,768]{3,2,1,0:T(8,128)(2,1)S(1)} %collective-permute-done.8.refs_2_) | copy-start | bytes 1769476
  53.9 23.0 %copy-start.8 = (bf16[4,4,24,768]{3,2,1,0:T(8,128)(2,1)}, bf16[4,4,24,768]{3,2,1,0:T(8,128)(2,1)S(1)}, u32[]{:S(2)}) copy-start(bf16[4,4,24,768]{3,2,1,0:T(8,128)(2,1)S(1)} %collective-permute-done.7.refs_1_) | copy-start | bytes 1769476
  54.0 13.3 %collective-permute-start.12 = (bf16[4,4,24,768]{3,2,1,0:T(8,128)(2,1)S(1)}, bf16[4,4,24,768]{3,2,1,0:T(8,128)(2,1)S(1)}, u32[]{:S(2)}, u32[]{:S(2)}) collective-permute-start(bf16[4,4,24,768]{3,2,1,0:T(8,128)(2,1)S(1)} %collective-permute-done.7.refs_1_), channel_id=1, source_target_pairs={{0,1},{1,0},{2,3},{3,2},{4,5},{5,4},{6,7},{7,6},{8,9},{9,8},{10,11... | collective-permute-start | bytes 1769480 | tf_op jit(solution)/shard_map/ppermute | solution.py:714
  56.6 10.7 %collective-permute-start.13 = (bf16[4,4,24,768]{3,2,1,0:T(8,128)(2,1)S(1)}, bf16[4,4,24,768]{3,2,1,0:T(8,128)(2,1)S(1)}, u32[]{:S(2)}, u32[]{:S(2)}) collective-permute-start(bf16[4,4,24,768]{3,2,1,0:T(8,128)(2,1)S(1)} %collective-permute-done.8.refs_2_), channel_id=1, source_target_pairs={{0,1},{1,0},{2,3},{3,2},{4,5},{5,4},{6,7},{7,6},{8,9},{9,8},{10,11... | collective-permute-start | bytes 1769480 | tf_op jit(solution)/shard_map/ppermute | solution.py:714
  57.2 3.6 collective-permute-start.4
  57.3 9.2 %collective-permute-start.10 = (bf16[2,4,24,768]{3,2,1,0:T(8,128)(2,1)S(1)}, bf16[2,4,24,768]{3,2,1,0:T(8,128)(2,1)S(1)}, u32[]{:S(2)}, u32[]{:S(2)}) collective-permute-start(bf16[2,4,24,768]{3,2,1,0:T(8,128)(2,1)S(1)} %slice.48), channel_id=1, source_target_pairs={{0,2},{1,3},{2,0},{3,1},{4,6},{5,7},{6,4},{7,5},{8,10},{9,11},{10,... | collective-permute-start | bytes 884744 | tf_op jit(solution)/shard_map/ppermute | solution.py:714
  59.5 7.7 %collective-permute-start.11 = (bf16[2,4,24,768]{3,2,1,0:T(8,128)(2,1)S(1)}, bf16[2,4,24,768]{3,2,1,0:T(8,128)(2,1)S(1)}, u32[]{:S(2)}, u32[]{:S(2)}) collective-permute-start(bf16[2,4,24,768]{3,2,1,0:T(8,128)(2,1)S(1)} %slice.49), channel_id=1, source_target_pairs={{0,4},{1,5},{2,6},{3,7},{4,0},{5,1},{6,2},{7,3},{8,12},{9,13},{10,... | collective-permute-start | bytes 884744 | tf_op jit(solution)/shard_map/ppermute | solution.py:714
  60.8 9.1 %collective-permute-start.5 = (bf16[4,8,256]{2,1,0:T(8,128)(2,1)S(1)}, bf16[4,8,256]{2,1,0:T(8,128)(2,1)S(1)}, u32[]{:S(2)}, u32[]{:S(2)}) collective-permute-start(bf16[4,8,256]{2,1,0:T(8,128)(2,1)S(1)} %pad_maximum_fusion.6), channel_id=1, source_target_pairs={{0,2},{1,3},{2,0},{3,1},{4,6},{5,7},{6,4},{7,5},{8,10},{9,11},{10,... | collective-permute-start | bytes 49160 | tf_op jit(solution)/shard_map/ppermute | solution.py:714
  66.5 10.5 %copy-start.13 = (bf16[2,4,24,768]{3,2,1,0:T(8,128)(2,1)}, bf16[2,4,24,768]{3,2,1,0:T(8,128)(2,1)S(1)}, u32[]{:S(2)}) copy-start(bf16[2,4,24,768]{3,2,1,0:T(8,128)(2,1)S(1)} %collective-permute-done.10.refs_3_) | copy-start | bytes 884740
  67.3 9.7 %copy-start.14 = (bf16[2,4,24,768]{3,2,1,0:T(8,128)(2,1)}, bf16[2,4,24,768]{3,2,1,0:T(8,128)(2,1)S(1)}, u32[]{:S(2)}) copy-start(bf16[2,4,24,768]{3,2,1,0:T(8,128)(2,1)S(1)} %collective-permute-done.11.refs_4_) | copy-start | bytes 884740
  67.3 9.7 %copy-start.11 = (bf16[4,4,24,768]{3,2,1,0:T(8,128)(2,1)}, bf16[4,4,24,768]{3,2,1,0:T(8,128)(2,1)S(1)}, u32[]{:S(2)}) copy-start(bf16[4,4,24,768]{3,2,1,0:T(8,128)(2,1)S(1)} %collective-permute-done.12.refs_6_) | copy-start | bytes 1769476
  68.2 8.8 %collective-permute-start.14 = (bf16[2,4,24,768]{3,2,1,0:T(8,128)(2,1)S(1)}, bf16[2,4,24,768]{3,2,1,0:T(8,128)(2,1)}, u32[]{:S(2)}, u32[]{:S(2)}) collective-permute-start(bf16[2,4,24,768]{3,2,1,0:T(8,128)(2,1)S(1)} %collective-permute-done.10.refs_3_), channel_id=1, source_target_pairs={{0,1},{1,0},{2,3},{3,2},{4,5},{5,4},{6,7},{7,6},{8,9},{9,8},{10,11... | collective-permute-start | bytes 884744 | tf_op jit(solution)/shard_map/ppermute | solution.py:714
  69.8 7.1 %collective-permute-start.15 = (bf16[2,4,24,768]{3,2,1,0:T(8,128)(2,1)S(1)}, bf16[2,4,24,768]{3,2,1,0:T(8,128)(2,1)}, u32[]{:S(2)}, u32[]{:S(2)}) collective-permute-start(bf16[2,4,24,768]{3,2,1,0:T(8,128)(2,1)S(1)} %collective-permute-done.11.refs_4_), channel_id=1, source_target_pairs={{0,1},{1,0},{2,3},{3,2},{4,5},{5,4},{6,7},{7,6},{8,9},{9,8},{10,11... | collective-permute-start | bytes 884744 | tf_op jit(solution)/shard_map/ppermute | solution.py:714
  69.8 3.7 collective-permute-start.6
  278.9 29.3 %collective-permute-start.16 = (bf16[4,768,384]{2,1,0:T(8,128)(2,1)}, bf16[4,768,384]{2,1,0:T(8,128)(2,1)}, u32[]{:S(2)}, u32[]{:S(2)}) collective-permute-start(bf16[4,768,384]{2,1,0:T(8,128)(2,1)} %get-tuple-element.147), channel_id=1, source_target_pairs={{0,1},{1,0},{2,3},{3,2},{4,5},{5,4},{6,7},{7,6},{8,9},{9,8},{10,11... | collective-permute-start | bytes 7077896 | tf_op jit(solution)/shard_map/ppermute | solution.py:714
  280.4 30.2 %collective-permute-start.17 = (bf16[4,768,384]{2,1,0:T(8,128)(2,1)}, bf16[4,768,384]{2,1,0:T(8,128)(2,1)}, u32[]{:S(2)}, u32[]{:S(2)}) collective-permute-start(bf16[4,768,384]{2,1,0:T(8,128)(2,1)} %get-tuple-element.149), channel_id=1, source_target_pairs={{0,1},{1,0},{2,3},{3,2},{4,5},{5,4},{6,7},{7,6},{8,9},{9,8},{10,11... | collective-permute-start | bytes 7077896 | tf_op jit(solution)/shard_map/ppermute | solution.py:714
  315.5 31.5 %collective-permute-start.19 = (bf16[2,2,384,384]{3,2,0,1:T(8,128)(2,1)}, bf16[2,2,384,384]{3,2,0,1:T(8,128)(2,1)}, u32[]{:S(2)}, u32[]{:S(2)}) collective-permute-start(bf16[2,2,384,384]{3,2,0,1:T(8,128)(2,1)} %pad_maximum_fusion.1), channel_id=1, source_target_pairs={{0,4},{1,5},{2,6},{3,7},{4,0},{5,1},{6,2},{7,3},{8,12},{9,13},{10,... | collective-permute-start | bytes 3538952 | tf_op jit(solution)/shard_map/ppermute | solution.py:714
  316.7 33.2 %collective-permute-start.18 = (bf16[2,2,384,384]{3,2,0,1:T(8,128)(2,1)}, bf16[2,2,384,384]{3,2,0,1:T(8,128)(2,1)}, u32[]{:S(2)}, u32[]{:S(2)}) collective-permute-start(bf16[2,2,384,384]{3,2,0,1:T(8,128)(2,1)} %pad_maximum_fusion), channel_id=1, source_target_pairs={{0,2},{1,3},{2,0},{3,1},{4,6},{5,7},{6,4},{7,5},{8,10},{9,11},{10,... | collective-permute-start | bytes 3538952 | tf_op jit(solution)/shard_map/ppermute | solution.py:714
  349.9 6.4 %copy-start.17 = (f32[4,1,768]{2,1,0:T(1,128)S(1)}, f32[4,1,768]{2,1,0:T(1,128)}, u32[]{:S(2)}) copy-start(f32[4,1,768]{2,1,0:T(1,128)} %get-tuple-element.170) | copy-start | bytes 36868
  352.4 18.5 %collective-permute-start.25 = (bf16[4,768,384]{2,1,0:T(8,128)(2,1)}, bf16[4,768,384]{2,1,0:T(8,128)(2,1)}, u32[]{:S(2)}, u32[]{:S(2)}) collective-permute-start(bf16[4,768,384]{2,1,0:T(8,128)(2,1)} %get-tuple-element.173), channel_id=1, source_target_pairs={{0,1},{1,0},{2,3},{3,2},{4,5},{5,4},{6,7},{7,6},{8,9},{9,8},{10,11... | collective-permute-start | bytes 7077896 | tf_op jit(solution)/shard_map/ppermute | solution.py:714
  353.1 15.6 %collective-permute-start.34 = (bf16[2,384,384]{2,1,0:T(8,128)(2,1)}, bf16[2,384,384]{2,1,0:T(8,128)(2,1)}, u32[]{:S(2)}, u32[]{:S(2)}) collective-permute-start(bf16[2,384,384]{2,1,0:T(8,128)(2,1)} %get-tuple-element.192), channel_id=1, source_target_pairs={{0,2},{1,3},{2,0},{3,1},{4,6},{5,7},{6,4},{7,5},{8,10},{9,11},{10,... | collective-permute-start | bytes 1769480 | tf_op jit(solution)/shard_map/ppermute | solution.py:714
  354.8 15.0 %collective-permute-start.33 = (bf16[2,384,384]{2,1,0:T(8,128)(2,1)}, bf16[2,384,384]{2,1,0:T(8,128)(2,1)}, u32[]{:S(2)}, u32[]{:S(2)}) collective-permute-start(bf16[2,384,384]{2,1,0:T(8,128)(2,1)} %get-tuple-element.190), channel_id=1, source_target_pairs={{0,4},{1,5},{2,6},{3,7},{4,0},{5,1},{6,2},{7,3},{8,12},{9,13},{10,... | collective-permute-start | bytes 1769480 | tf_op jit(solution)/shard_map/ppermute | solution.py:714
  356.3 12.5 %copy-start.4 = (bf16[2,384,384]{2,1,0:T(8,128)(2,1)S(1)}, bf16[2,384,384]{2,1,0:T(8,128)(2,1)}, u32[]{:S(2)}) copy-start(bf16[2,384,384]{2,1,0:T(8,128)(2,1)} %get-tuple-element.191) | copy-start | bytes 1769476
  356.3 13.5 %copy-start.3 = (bf16[2,384,384]{2,1,0:T(8,128)(2,1)S(1)}, bf16[2,384,384]{2,1,0:T(8,128)(2,1)}, u32[]{:S(2)}) copy-start(bf16[2,384,384]{2,1,0:T(8,128)(2,1)} %get-tuple-element.189) | copy-start | bytes 1769476
  375.3 33.6 %collective-permute-start.26 = (bf16[2,2,192,384]{3,2,0,1:T(8,128)(2,1)}, bf16[2,2,192,384]{3,2,0,1:T(8,128)(2,1)}, u32[]{:S(2)}, u32[]{:S(2)}) collective-permute-start(bf16[2,2,192,384]{3,2,0,1:T(8,128)(2,1)} %fusion.8), channel_id=1, source_target_pairs={{0,2},{1,3},{2,0},{3,1},{4,6},{5,7},{6,4},{7,5},{8,10},{9,11},{10,... | collective-permute-start | bytes 1769480 | tf_op jit(solution)/shard_map/ppermute | solution.py:714
  377.6 31.3 %collective-permute-start.28 = (bf16[2,2,192,384]{3,2,0,1:T(8,128)(2,1)}, bf16[2,2,192,384]{3,2,0,1:T(8,128)(2,1)}, u32[]{:S(2)}, u32[]{:S(2)}) collective-permute-start(bf16[2,2,192,384]{3,2,0,1:T(8,128)(2,1)} %fusion.9), channel_id=1, source_target_pairs={{0,4},{1,5},{2,6},{3,7},{4,0},{5,1},{6,2},{7,3},{8,12},{9,13},{10,... | collective-permute-start | bytes 1769480 | tf_op jit(solution)/shard_map/ppermute | solution.py:714
  379.9 31.6 %collective-permute-start.35 = (bf16[2,384,384]{2,1,0:T(8,128)(2,1)}, bf16[2,384,384]{2,1,0:T(8,128)(2,1)}, u32[]{:S(2)}, u32[]{:S(2)}) collective-permute-start(bf16[2,384,384]{2,1,0:T(8,128)(2,1)} %pad_maximum_fusion.2), channel_id=1, source_target_pairs={{0,8},{1,9},{2,10},{3,11},{4,12},{5,13},{6,14},{7,15},{8,0},{9,1},... | collective-permute-start | bytes 1769480 | tf_op jit(solution)/shard_map/ppermute | solution.py:714
  381.5 10.7 %copy-start.18 = (f32[4,1,768]{2,1,0:T(1,128)S(1)}, f32[4,1,768]{2,1,0:T(1,128)}, u32[]{:S(2)}) copy-start(f32[4,1,768]{2,1,0:T(1,128)} %get-tuple-element.167) | copy-start | bytes 36868
  381.5 10.8 %copy-start.19 = (f32[1,768]{1,0:T(1,128)S(1)}, f32[1,768]{1,0:T(1,128)}, u32[]{:S(2)}) copy-start(f32[1,768]{1,0:T(1,128)} %get-tuple-element.171) | copy-start | bytes 9220
  381.5 10.8 %copy-start.20 = (f32[1,768]{1,0:T(1,128)S(1)}, f32[1,768]{1,0:T(1,128)}, u32[]{:S(2)}) copy-start(f32[1,768]{1,0:T(1,128)} %get-tuple-element.168) | copy-start | bytes 9220
  381.5 10.8 %copy-start.21 = (f32[1,768]{1,0:T(1,128)S(1)}, f32[1,768]{1,0:T(1,128)}, u32[]{:S(2)}) copy-start(f32[1,768]{1,0:T(1,128)} %get-tuple-element.169) | copy-start | bytes 9220
  393.0 2.6 collective-permute-start.20
  395.6 2.9 collective-permute-start.21
  398.5 3.0 collective-permute-start.22
  401.5 3.0 collective-permute-start.23
  404.5 4.3 collective-permute-start.24
  408.8 2.7 copy-start.5
  411.0 5.6 %collective-permute-start.27 = (bf16[2,192,384]{2,1,0:T(8,128)(2,1)S(1)}, bf16[2,192,384]{2,1,0:T(8,128)(2,1)S(1)}, u32[]{:S(2)}, u32[]{:S(2)}) collective-permute-start(bf16[2,192,384]{2,1,0:T(8,128)(2,1)S(1)} %get-tuple-element.175), channel_id=1, source_target_pairs={{0,4},{1,5},{2,6},{3,7},{4,0},{5,1},{6,2},{7,3},{8,12},{9,13},{10,... | collective-permute-start | bytes 884744 | tf_op jit(solution)/shard_map/ppermute | solution.py:714
  411.1 5.6 %collective-permute-start.29 = (bf16[2,192,384]{2,1,0:T(8,128)(2,1)S(1)}, bf16[2,192,384]{2,1,0:T(8,128)(2,1)S(1)}, u32[]{:S(2)}, u32[]{:S(2)}) collective-permute-start(bf16[2,192,384]{2,1,0:T(8,128)(2,1)S(1)} %get-tuple-element.185), channel_id=1, source_target_pairs={{0,2},{1,3},{2,0},{3,1},{4,6},{5,7},{6,4},{7,5},{8,10},{9,11},{10,... | collective-permute-start | bytes 884744 | tf_op jit(solution)/shard_map/ppermute | solution.py:714
  412.7 11.4 %collective-permute-start.36 = (bf16[384,384]{1,0:T(8,128)(2,1)S(1)}, bf16[384,384]{1,0:T(8,128)(2,1)S(1)}, u32[]{:S(2)}, u32[]{:S(2)}) collective-permute-start(bf16[384,384]{1,0:T(8,128)(2,1)S(1)} %fusion.14), channel_id=1, source_target_pairs={{0,16},{1,17},{2,18},{3,19},{4,20},{5,21},{6,22},{7,23},{8,24},{9,... | collective-permute-start | bytes 884744 | tf_op jit(solution)/shard_map/ppermute | solution.py:714
  416.8 13.8 %collective-permute-start.30 = (bf16[2,192,384]{2,1,0:T(8,128)(2,1)S(1)}, bf16[2,192,384]{2,1,0:T(8,128)(2,1)S(1)}, u32[]{:S(2)}, u32[]{:S(2)}) collective-permute-start(bf16[2,192,384]{2,1,0:T(8,128)(2,1)S(1)} %pad_maximum_fusion.4), channel_id=1, source_target_pairs={{0,8},{1,9},{2,10},{3,11},{4,12},{5,13},{6,14},{7,15},{8,0},{9,1},... | collective-permute-start | bytes 884744 | tf_op jit(solution)/shard_map/ppermute | solution.py:714
  425.3 15.1 %collective-permute-start.37 = (f32[384,384]{1,0:T(8,128)S(1)}, f32[384,384]{1,0:T(8,128)S(1)}, u32[]{:S(2)}, u32[]{:S(2)}) collective-permute-start(f32[384,384]{1,0:T(8,128)S(1)} %bitcast_add_fusion), channel_id=1, source_target_pairs={{0,1},{1,0},{2,3},{3,2},{4,5},{5,4},{6,7},{7,6},{8,9},{9,8},{10,11... | collective-permute-start | bytes 1769480 | tf_op jit(solution)/shard_map/ppermute | solution.py:714
  430.6 8.8 %collective-permute-start.31 = (bf16[192,384]{1,0:T(8,128)(2,1)S(1)}, bf16[192,384]{1,0:T(8,128)(2,1)S(1)}, u32[]{:S(2)}, u32[]{:S(2)}) collective-permute-start(bf16[192,384]{1,0:T(8,128)(2,1)S(1)} %fusion.15), channel_id=1, source_target_pairs={{0,16},{1,17},{2,18},{3,19},{4,20},{5,21},{6,22},{7,23},{8,24},{9,... | collective-permute-start | bytes 442376 | tf_op jit(solution)/shard_map/ppermute | solution.py:714
  439.4 3.8 collective-permute-start.32
  (5 other events, 7.4 us)
Sparse Core Ops, SparseCore 0:
  11.0 91.9 all-gather.2

commit v2 on v1

--- a/solution.py
+++ b/solution.py
@@ -18,11 +18,24 @@
 NORM_EPS = 1e-05
 BLOCK = 128
 FEATURES = H * HD
-VMEM_LIMIT = 60 << 20
+VMEM_LIMIT = 40 << 20
+COST_SCALE = 8
 
 
 def dot(left, right):
     return jnp.dot(left, right, preferred_element_type=jnp.float32)
+
+
+def transposed_dot(left, right):
+    return lax.dot_general(
+        left, right, (((0,), (0,)), ((), ())), preferred_element_type=jnp.float32
+    )
+
+
+def dot_transposed(left, right):
+    return lax.dot_general(
+        left, right, (((1,), (1,)), ((), ())), preferred_element_type=jnp.float32
+    )
 
 
 def norm_parts(values):
@@ -57,16 +70,23 @@
     return jnp.where(same & (key <= query), 0.0, -1e30).astype(jnp.float32)
 
 
-def head_split(pair):
-    left = lax.broadcasted_iota(jnp.int32, pair.shape, 1) < HD
-    zero = jnp.zeros_like(pair)
-    return jnp.concatenate([jnp.where(left, pair, zero), jnp.where(left, zero, pair)], axis=0)
+GROUP = 4
+LANES = GROUP * HD
+
+
+def head_split(array):
+    head = lax.broadcasted_iota(jnp.int32, array.shape, 1) // HD
+    zero = jnp.zeros_like(array)
+    return jnp.concatenate([jnp.where(head == h, array, zero) for h in range(GROUP)], axis=0)
 
 
 def head_join(stacked):
-    count = stacked.shape[0] // 2
-    left = lax.broadcasted_iota(jnp.int32, (count, 2 * HD), 1) < HD
-    return jnp.where(left, stacked[:count], stacked[count:])
+    count = stacked.shape[0] // GROUP
+    head = lax.broadcasted_iota(jnp.int32, (count, LANES), 1) // HD
+    joined = stacked[:count]
+    for h in range(1, GROUP):
+        joined = jnp.where(head == h, stacked[h * count : (h + 1) * count], joined)
+    return joined
 
 
 def attention_forward_kernel(
@@ -103,33 +123,32 @@
     bias_ref[...] = allowed_bias(count, [lengths_ref[micro, d] for d in range(docs)], docs, 0)
     lse_cols[...] = jnp.zeros_like(lse_cols)
 
-    def one_pair(pair, carry):
-        lanes = pl.multiple_of(pair * 2 * HD, 2 * HD)
+    def one_group(group, carry):
+        lanes = pl.multiple_of(group * LANES, LANES)
         for block in range(count // BLOCK):
             rows = slice(block * BLOCK, (block + 1) * BLOCK)
             low_key = max(0, block - back) * BLOCK
             keys = slice(low_key, (block + 1) * BLOCK)
-            query = head_split(mixed_ref[rows, pl.ds(lanes, 2 * HD)])
-            key = mixed_ref[keys, pl.ds(FEATURES + lanes, 2 * HD)]
-            value = mixed_ref[keys, pl.ds(2 * FEATURES + lanes, 2 * HD)]
-            scores = lax.dot_general(
-                query, key, (((1,), (1,)), ((), ())), preferred_element_type=jnp.float32
-            )
+            query = head_split(mixed_ref[rows, pl.ds(lanes, LANES)])
+            key = mixed_ref[keys, pl.ds(FEATURES + lanes, LANES)]
+            value = mixed_ref[keys, pl.ds(2 * FEATURES + lanes, LANES)]
+            scores = dot_transposed(query, key)
             bias = bias_ref[rows, keys]
-            scores = scores * 0.125 + jnp.concatenate([bias, bias], axis=0)
+            scores = scores * 0.125 + jnp.concatenate([bias] * GROUP, axis=0)
             top = jnp.max(scores, axis=-1, keepdims=True)
             expo = jnp.exp(scores - top)
-            total = jnp.sum(expo, axis=-1, keepdims=True)
-            result = dot(expo.astype(jnp.bfloat16), value) / total
-            att_ref[rows, pl.ds(lanes, 2 * HD)] = head_join(result).astype(jnp.bfloat16)
-            lse = top + jnp.log(total)
+            total_expo = jnp.sum(expo, axis=-1, keepdims=True)
+            result = dot(expo.astype(jnp.bfloat16), value) / total_expo
+            att_ref[rows, pl.ds(lanes, LANES)] = head_join(result).astype(jnp.bfloat16)
+            lse = top + jnp.log(total_expo)
             lane = lax.broadcasted_iota(jnp.int32, (BLOCK, 128), 1)
-            lse_cols[rows, :] += jnp.where(lane == 2 * pair, lse[:BLOCK], 0.0) + jnp.where(
-                lane == 2 * pair + 1, lse[BLOCK:], 0.0
-            )
+            for h in range(GROUP):
+                lse_cols[rows, :] += jnp.where(
+                    lane == GROUP * group + h, lse[h * BLOCK : (h + 1) * BLOCK], 0.0
+                )
         return carry
 
-    lax.fori_loop(0, H // 2, one_pair, 0)
+    lax.fori_loop(0, H // GROUP, one_group, 0, unroll=H // GROUP)
     lse = jnp.transpose(lse_cols[...])
     for index in range(H):
         lse_ref[index] = lse[index : index + 1]
@@ -148,18 +167,24 @@
 SMEM = pl.BlockSpec(memory_space=pltpu.SMEM)
 
 
+def in_hbm(arrays):
+    return [pltpu.with_memory_space_constraint(array, pltpu.HBM) for array in arrays]
+
+
 def rows_of(count, width):
     return pl.BlockSpec((count, width), lambda i: (i, 0))
 
 
-def params():
-    return pltpu.CompilerParams(vmem_limit_bytes=VMEM_LIMIT)
+def params(limit=VMEM_LIMIT):
+    return pltpu.CompilerParams(vmem_limit_bytes=limit)
 
 
 def cost(flops, transcendentals, *arrays):
     size = sum(math.prod(a.shape) * a.dtype.itemsize for a in arrays)
     return pl.CostEstimate(
-        flops=int(flops), transcendentals=int(transcendentals), bytes_accessed=int(size)
+        flops=int(flops) // COST_SCALE,
+        transcendentals=int(transcendentals) // COST_SCALE,
+        bytes_accessed=int(size) // COST_SCALE,
     )
 
 
@@ -167,7 +192,7 @@
     rows = state.shape[0]
     micro, docs = lengths.shape
     width = FEATURES
-    shape = jax.ShapeDtypeStruct
+    shape = pltpu.HBM
     outs = (
         shape((rows, width), jnp.bfloat16),
         shape((rows, 3 * width), jnp.bfloat16),
@@ -199,7 +224,7 @@
             8 * rows * width * width + 4 * rows * count * width, rows * count * H, state, *weights, *outs
         ),
         name="attention_forward",
-    )(lengths, state, *weights)
+    )(lengths, *in_hbm((state, *weights)))
 
 
 GELU_C = 0.7978845608028654
@@ -238,6 +263,9 @@
             final_ref[...] = state_ref[...].astype(jnp.bfloat16)
 
 
+DEVICE_GROUPS = 16
+
+
 def square_of(ref):
     return ref[...].reshape(FEATURES, FEATURES)
 
@@ -250,7 +278,7 @@
     rows, width = hidden.shape
     block = width
     hidden_units = 4 * block
-    shape = jax.ShapeDtypeStruct
+    shape = pltpu.HBM
     outs = (
         shape((rows, hidden_units), jnp.bfloat16),
         shape((rows, width), jnp.bfloat16 if last else jnp.float32),
@@ -278,19 +306,7 @@
             4 * rows * width * hidden_units, rows * hidden_units, hidden, normed, mlp, *outs
         ),
         name="mlp_forward",
-    )(hidden, normed, mlp, fbias, mlp, pbias)
-
-
-def transposed_dot(left, right):
-    return lax.dot_general(
-        left, right, (((0,), (0,)), ((), ())), preferred_element_type=jnp.float32
-    )
-
-
-def dot_transposed(left, right):
-    return lax.dot_general(
-        left, right, (((1,), (1,)), ((), ())), preferred_element_type=jnp.float32
-    )
+    )(*in_hbm((hidden, normed, mlp, fbias, mlp, pbias)))
 
 
 def transposed_dot(left, right):
@@ -310,11 +326,13 @@
     left, right = (value[:, :half], value[:, half:])
     mine = jnp.where(core == 0, left, right)
     theirs = jnp.where(core == 0, right, left)
+    shape = mine_ref.shape
+    mine, theirs = (mine.reshape(shape), theirs.reshape(shape))
     if earlier is not None:
-        mine = mine + earlier[0][0].astype(jnp.float32)
-        theirs = theirs + earlier[1][0].astype(jnp.float32)
-    mine_ref[0] = mine.astype(mine_ref.dtype)
-    theirs_ref[0] = theirs.astype(theirs_ref.dtype)
+        mine = mine + earlier[0][...].astype(jnp.float32)
+        theirs = theirs + earlier[1][...].astype(jnp.float32)
+    mine_ref[...] = mine.astype(mine_ref.dtype)
+    theirs_ref[...] = theirs.astype(theirs_ref.dtype)
 
 
 def mlp_backward_kernel(
@@ -323,21 +341,25 @@
     grad_ref,
     hidden_ref,
     normed_ref,
+    att_ref,
     expanded_ref,
     fc_ref,
     proj_ref,
     gain_ref,
     *rest,
 ):
-    earlier = rest[:8] if more else (None,) * 8
+    earlier = rest[:11] if more else (None,) * 11
     if more:
-        rest = rest[8:]
+        rest = rest[11:]
     (
         dhid_ref,
         fc_mine,
         fc_theirs,
         proj_mine,
         proj_theirs,
+        out_mine,
+        out_theirs,
+        dobias_ref,
         dfbias_ref,
         dpbias_ref,
         dgain_ref,
@@ -358,7 +380,7 @@
         low_grad = grad_ref[...].astype(jnp.bfloat16)
         low_ref[...] = low_grad
         dpbias = jnp.sum(low_grad.astype(jnp.float32), axis=0, keepdims=True)
-        dpbias_ref[...] = dpbias + earlier[5][...] if more else dpbias
+        dpbias_ref[...] = dpbias + earlier[8][...] if more else dpbias
         normed_t[...] = jnp.transpose(normed_ref[...])
         acc_ref[...] = jnp.zeros_like(acc_ref)
 
@@ -375,7 +397,7 @@
         ge_ref[part, :] = grad_exp
         bias_sum = bias_sum + jnp.sum(grad_exp.astype(jnp.float32), axis=0, keepdims=True)
         acc_ref[part, :] += dot_transposed(grad_exp, square_of(fc_ref))
-    dfbias_ref[0] = bias_sum + earlier[4][0] if more else bias_sum
+    dfbias_ref[0] = bias_sum + earlier[7][0] if more else bias_sum
     dproj = transposed_dot(act_ref[...], low_ref[...])
     store_halves(core, dproj, proj_mine, proj_theirs, earlier[2:4] if more else None)
     dfc = dot(normed_t[...], ge_ref[...])
@@ -387,44 +409,62 @@
         grad_norm = acc_ref[...]
         dgain = jnp.sum(grad_norm * normed, axis=0, keepdims=True)
         dshift = jnp.sum(grad_norm, axis=0, keepdims=True)
-        dgain_ref[...] = dgain + earlier[6][...] if more else dgain
-        dshift_ref[...] = dshift + earlier[7][...] if more else dshift
-        dhid_ref[...] = grad_ref[...].astype(jnp.float32) + norm_back(
+        dgain_ref[...] = dgain + earlier[9][...] if more else dgain
+        dshift_ref[...] = dshift + earlier[10][...] if more else dshift
+        dhid = grad_ref[...].astype(jnp.float32) + norm_back(
             normed, scale, gain_ref[...], grad_norm
         )
-
-
-def mlp_backward(core, grad, hidden, normed, expanded, mlp, gain, earlier=None):
+        dhid_ref[...] = dhid
+        low_dhid = dhid.astype(jnp.bfloat16)
+        low_ref[...] = low_dhid
+        dobias = jnp.sum(low_dhid.astype(jnp.float32), axis=0, keepdims=True)
+        dobias_ref[...] = dobias + earlier[6][...] if more else dobias
+        dout = transposed_dot(att_ref[...], low_ref[...])
+        store_halves(core, dout, out_mine, out_theirs, earlier[4:6] if more else None)
+
+
+def mlp_backward(core, grad, hidden, normed, att, expanded, mlp, gain, earlier=None):
     rows, width = hidden.shape
     blocks, block = (4, width)
-    shape = jax.ShapeDtypeStruct
-    half = shape((blocks, width, width // 2), jnp.bfloat16)
+    shape = pltpu.HBM
+    groups = DEVICE_GROUPS
+    each = width // groups
+    fc_half = shape((groups, blocks, each, width // 2), jnp.bfloat16)
+    proj_half = shape((blocks * width, width // 2), jnp.bfloat16)
+    out_half = shape((groups, each, width // 2), jnp.bfloat16)
     row = shape((1, width), jnp.float32)
     outs = (
         shape((rows, width), jnp.float32),
-        half,
-        half,
-        half,
-        half,
+        fc_half,
+        fc_half,
+        proj_half,
+        proj_half,
+        out_half,
+        out_half,
+        row,
         shape((blocks, 1, block), jnp.float32),
         row,
         row,
         row,
     )
-    halves = pl.BlockSpec((1, width, width // 2), lambda i: (i, 0, 0))
+    fc_spec = pl.BlockSpec((groups, None, each, width // 2), lambda i: (0, i, 0, 0))
+    proj_spec = pl.BlockSpec((width, width // 2), lambda i: (i, 0))
+    out_spec = pl.BlockSpec((groups, each, width // 2), lambda i: (0, 0, 0))
     bias = pl.BlockSpec((1, 1, block), lambda i: (i, 0, 0))
     vector = pl.BlockSpec((1, width), lambda i: (0, 0))
-    inputs = [grad, hidden, normed, expanded, mlp, mlp, gain]
+    inputs = [grad, hidden, normed, att, expanded, mlp, mlp, gain]
     specs = [
         whole(grad),
         whole(hidden),
         whole(normed),
+        whole(att),
         pl.BlockSpec((rows, block), lambda i: (0, i)),
         FC_BLOCK,
         PROJ_BLOCK,
         whole(gain),
     ]
-    summed = [halves, halves, halves, halves, bias, vector, vector, vector]
+    summed = [fc_spec, fc_spec, proj_spec, proj_spec, out_spec, out_spec, vector, bias]
+    summed += [vector, vector, vector]
     if earlier is not None:
         inputs += list(earlier)
         specs += summed
@@ -441,10 +481,10 @@
             pltpu.VMEM((rows, block), jnp.bfloat16),
             pltpu.VMEM((rows, block), jnp.bfloat16),
         ],
-        compiler_params=params(),
+        compiler_params=params(50 << 20),
         cost_estimate=cost(8 * rows * width * blocks * block, rows * blocks * block, *inputs, *outs),
         name="mlp_backward",
-    )(core, *inputs)
+    )(core, grad, *in_hbm(inputs[1:]))
 
 
 def attention_backward_kernel(
@@ -478,45 +518,45 @@
         delta_ref[index] = delta[index : index + 1]
     bias_ref[...] = allowed_bias(count, [lengths_ref[micro, d] for d in range(docs)], docs, 1)
 
-    def one_pair(pair, carry):
-        lanes = pl.multiple_of(pair * 2 * HD, 2 * HD)
+    def one_group(group, carry):
+        lanes = pl.multiple_of(group * LANES, LANES)
         dq_ref[...] = jnp.zeros_like(dq_ref)
         for block in range(count // BLOCK):
             keys = slice(block * BLOCK, (block + 1) * BLOCK)
             rows = slice(block * BLOCK, min(count, (block + 1 + back) * BLOCK))
-            key = head_split(mixed_ref[keys, pl.ds(FEATURES + lanes, 2 * HD)])
-            value = head_split(mixed_ref[keys, pl.ds(2 * FEATURES + lanes, 2 * HD)])
-            query = mixed_ref[rows, pl.ds(lanes, 2 * HD)]
-            datt_pair = datt_ref[rows, pl.ds(lanes, 2 * HD)]
+            key = head_split(mixed_ref[keys, pl.ds(FEATURES + lanes, LANES)])
+            value = head_split(mixed_ref[keys, pl.ds(2 * FEATURES + lanes, LANES)])
+            query = mixed_ref[rows, pl.ds(lanes, LANES)]
+            datt_group = datt_ref[rows, pl.ds(lanes, LANES)]
             scores = dot_transposed(key, query)
-            dprobs = dot_transposed(value, datt_pair)
+            dprobs = dot_transposed(value, datt_group)
             bias = bias_ref[keys, rows]
             probs_low, dscores_low = ([], [])
-            for half in range(2):
-                part = slice(half * BLOCK, (half + 1) * BLOCK)
-                lse = lse_ref[2 * pair + half, :, rows]
-                delta = delta_ref[2 * pair + half, :, rows]
+            for h in range(GROUP):
+                part = slice(h * BLOCK, (h + 1) * BLOCK)
+                lse = lse_ref[GROUP * group + h, :, rows]
+                delta = delta_ref[GROUP * group + h, :, rows]
                 probs = jnp.exp((scores[part] * 0.125 + bias) - lse)
                 dscores = probs * (dprobs[part] - delta)
                 probs_low.append(probs.astype(jnp.bfloat16))
                 dscores_low.append(dscores.astype(jnp.bfloat16))
             probs_low = jnp.concatenate(probs_low, axis=0)
             dscores_low = jnp.concatenate(dscores_low, axis=0)
-            dvalue = head_join(dot(probs_low, datt_pair))
+            dvalue = head_join(dot(probs_low, datt_group))
             dkey = head_join(dot(dscores_low, query)) * 0.125
             dq_ref[rows, :] += transposed_dot(dscores_low, key)
-            gmix_ref[keys, pl.ds(FEATURES + lanes, 2 * HD)] = dkey.astype(jnp.bfloat16)
-            gmix_ref[keys, pl.ds(2 * FEATURES + lanes, 2 * HD)] = dvalue.astype(jnp.bfloat16)
-        gmix_ref[:, pl.ds(lanes, 2 * HD)] = (dq_ref[...] * 0.125).astype(jnp.bfloat16)
+            gmix_ref[keys, pl.ds(FEATURES + lanes, LANES)] = dkey.astype(jnp.bfloat16)
+            gmix_ref[keys, pl.ds(2 * FEATURES + lanes, LANES)] = dvalue.astype(jnp.bfloat16)
+        gmix_ref[:, pl.ds(lanes, LANES)] = (dq_ref[...] * 0.125).astype(jnp.bfloat16)
         return carry
 
-    lax.fori_loop(0, H // 2, one_pair, 0)
-
-
-def attention_backward(micro, lengths, dhid, count, back, att, mixed, lse, weight):
+    lax.fori_loop(0, H // GROUP, one_group, 0, unroll=H // GROUP)
+
+
+def attention_backward(micro, lengths, dhid, count, back, att, mixed, lse, weight, shape):
     width = dhid.shape[1]
     docs = lengths.shape[1]
-    outs = jax.ShapeDtypeStruct((count, 3 * width), jnp.bfloat16)
+    outs = shape((count, 3 * width), jnp.bfloat16)
     inputs = [dhid, att, mixed, lse, weight]
     return pl.pallas_call(
         functools.partial(attention_backward_kernel, docs, back, micro),
@@ -535,79 +575,60 @@
             pltpu.VMEM((count, width), jnp.bfloat16),
             pltpu.VMEM((count, count), jnp.float32),
             pltpu.VMEM((H, 1, count), jnp.float32),
-            pltpu.VMEM((count, 2 * HD), jnp.float32),
+            pltpu.VMEM((count, LANES), jnp.float32),
         ],
         compiler_params=params(),
         cost_estimate=cost(
             2 * count * width * width + 10 * count * count * width, count * count * H, outs, outs
         ),
         name="attention_backward",
-    )(lengths, *inputs)
-
-
-def attention_terms_kernel(more, micro, core_ref, normed_ref, att_ref, dhid_ref, *rest):
+    )(lengths, *in_hbm(inputs))
+
+
+def attention_terms_kernel(more, micro, core_ref, normed_ref, *rest):
     gmix_refs, rest = (rest[:micro], rest[micro:])
     earlier = rest[:3] if more else (None,) * 3
     if more:
         rest = rest[3:]
-    mine_ref, theirs_ref, dbias_ref, left_t, right_ref = rest
-    step = pl.program_id(0)
+    mine_ref, theirs_ref, dbias_ref, right_ref = rest
     core = core_ref[0]
-
-    @pl.when(step == 0)
-    def _():
-        left_t[...] = jnp.transpose(normed_ref[...])
-
-    @pl.when(step < 3)
-    def _():
-        for index, gmix_ref in enumerate(gmix_refs):
-            count = gmix_ref.shape[0]
-            right_ref[index * count : (index + 1) * count] = gmix_ref[...]
-
-    @pl.when(step == 3)
-    def _():
-        left_t[...] = jnp.transpose(att_ref[...])
-        right_ref[...] = dhid_ref[...].astype(jnp.bfloat16)
-
+    for index, gmix_ref in enumerate(gmix_refs):
+        count = gmix_ref.shape[0]
+        right_ref[index * count : (index + 1) * count] = gmix_ref[...]
     right = right_ref[...]
     dbias = jnp.sum(right.astype(jnp.float32), axis=0, keepdims=True)
     dbias_ref[0] = dbias + earlier[2][0] if more else dbias
-    store_halves(
-        core, dot(left_t[...], right), mine_ref, theirs_ref, earlier[:2] if more else None
-    )
-
-
-def attention_terms(core, normed, att, gmix, dhid, earlier=None):
-    rows, width = dhid.shape
-    shape = jax.ShapeDtypeStruct
-    outs = (
-        shape((4, width, width // 2), jnp.bfloat16),
-        shape((4, width, width // 2), jnp.bfloat16),
-        shape((4, 1, width), jnp.float32),
-    )
-    halves = pl.BlockSpec((1, width, width // 2), lambda i: (i, 0, 0))
+    terms = transposed_dot(normed_ref[...], right)
+    store_halves(core, terms, mine_ref, theirs_ref, earlier[:2] if more else None)
+
+
+def attention_terms(core, normed, gmix, earlier=None):
+    rows, width = normed.shape
+    groups = DEVICE_GROUPS
+    each = width // groups
+    shape = pltpu.HBM
+    half = shape((groups, 3, each, width // 2), jnp.bfloat16)
+    outs = (half, half, shape((3, 1, width), jnp.float32))
+    halves = pl.BlockSpec((groups, None, each, width // 2), lambda i: (0, i, 0, 0))
     summed = [halves, halves, pl.BlockSpec((1, 1, width), lambda i: (i, 0, 0))]
-    inputs = [normed, att, dhid, *gmix]
-    specs = [whole(normed), whole(att), whole(dhid)] + [
-        pl.BlockSpec((part.shape[0], width), lambda i: (0, jnp.minimum(i, 2))) for part in gmix
+    inputs = [normed, *gmix]
+    specs = [whole(normed)] + [
+        pl.BlockSpec((part.shape[0], width), lambda i: (0, i)) for part in gmix
     ]
     if earlier is not None:
         inputs += list(earlier)
         specs += summed
     return pl.pallas_call(
         functools.partial(attention_terms_kernel, earlier is not None, len(gmix)),
-        grid=(4,),
+        grid=(3,),
         out_shape=outs,
         in_specs=[SMEM] + specs,
         out_specs=summed,
-        scratch_shapes=[
-            pltpu.VMEM((width, rows), jnp.bfloat16),
-            pltpu.VMEM((rows, width), jnp.bfloat16),
-        ],
+        scratch_shapes=[pltpu.VMEM((rows, width), jnp.bfloat16)],
         compiler_params=params(),
-        cost_estimate=cost(8 * rows * width * width, 0, *inputs, *outs),
+        cost_estimate=cost(6 * rows * width * width, 0, *inputs, *outs),
         name="attention_terms",
-    )(core, *inputs)
+    )(core, *in_hbm(inputs[:1]), *gmix, *in_hbm(inputs[1 + len(gmix) :]))
 
 
 def attention_input_kernel(more, micro, dhid_ref, state_ref, weight_ref, gain_ref, *rest):
@@ -680,7 +701,7 @@
         compiler_params=params(),
         cost_estimate=cost(6 * rows * width * width, 0, *inputs, *outs),
         name="attention_input",
-    )(*inputs)
+    )(*in_hbm(inputs[:4]), *gmix, *in_hbm(inputs[4 + len(gmix) :]))
 
 
 def place_small_kernel(sizes, me_ref, small_ref, *outs):
@@ -750,24 +771,28 @@
     return lax.optimization_barrier((values, others))[0]
 
 
-def gather_first(piece, me):
+def gather_first(piece, small, me):
     base = (0, Z1, Z2, Z3)
     pieces = lax.optimization_barrier(
-        (piece, swap(piece, Z1), swap(piece, Z2), swap(piece, Z3))
-    )
-    four = jnp.concatenate(pieces)
-    four_x, four_y = (swap(four, X), swap(four, Y))
-    four_core = swap(four, CORE)
-    four_x, four_y, four_core = lax.optimization_barrier((four_x, four_y, four_core))
-    near_xy, far_xy = (swap(four_y[:2], X), swap(four_x[2:], Y))
-    x_core, y_core = (swap(four_x, CORE), swap(four_y, CORE))
-    near_xy, far_xy, x_core, y_core = lax.optimization_barrier((near_xy, far_xy, x_core, y_core))
+        [piece] + [swap(piece, bits) for bits in base[1:]]
+        + [small] + [swap(small, bits) for bits in base[1:]]
+    )
+    four, small = (jnp.concatenate(pieces[:4]), jnp.concatenate(pieces[4:]))
+    four_x, four_y, four_core, small_x, small_y = lax.optimization_barrier(
+        (swap(four, X), swap(four, Y), swap(four, CORE), swap(small, X), swap(small, Y))
+    )
+    near_xy, far_xy, x_core, y_core, small_xy = lax.optimization_barrier(
+        (
+            swap(four_y[:2], X), swap(four_x[2:], Y), swap(four_x, CORE), swap(four_y, CORE),
+            swap(small_y, X),
+        )
+    )
     parts = [four, four_x, four_y, near_xy, far_xy]
     parts += [four_core, x_core, y_core, swap(near_xy, CORE), swap(far_xy, CORE)]
     slots = [base] + [tuple(rel ^ bits for rel in base) for bits in (X, Y)]
     slots += [(X ^ Y, X ^ Y ^ Z1), (X ^ Y ^ Z2, X ^ Y ^ Z3)]
     slots += [tuple(rel ^ CORE for rel in rels) for rels in slots]
-    return (place(me, parts, slots), pieces[1], four_x)
+    return (place(me, parts, slots), jnp.concatenate([small, small_x, small_y, small_xy]))
 
 
 def pick(array, axis, index):
@@ -789,96 +814,156 @@
     return total
 
 
+def device_at(z_pair, z_low, y, x):
+    return z_pair * 8 + z_low * 4 + y * 2 + x
+
+
+def total(*terms):
+    result = terms[0].astype(jnp.float32)
+    for term in terms[1:]:
+        result = result + term.astype(jnp.float32)
+    return result
+
+
+def first_sums_kernel(views, spot_ref, *refs):
+    mine, got = (refs[:views], refs[views : 2 * views])
+    near_sent, far_sent, near_kept, far_kept = refs[2 * views :]
+    z_pair, y, x = (spot_ref[0], spot_ref[2], spot_ref[3])
+    for low_z in range(2):
+        for other in range(2):
+            for out, device in (
+                (near_sent, device_at(z_pair, low_z, other, 1 - x)),
+                (far_sent, device_at(1 - z_pair, low_z, 1 - y, other)),
+                (near_kept, device_at(z_pair, low_z, other, x)),
+                (far_kept, device_at(1 - z_pair, low_z, y, other)),
+            ):
+                start = 0
+                for left, right in zip(mine, got):
+                    count = left.shape[1]
+                    out[low_z, other, start : start + count] = total(
+                        left[device], right[device]
+                    ).astype(jnp.bfloat16)
+                    start += count
+
+
+def second_sums_kernel(spot_ref, near, far, near_in, far_in, *outs):
+    near_sent, far_sent, near_kept, far_kept = outs
+    y, x = (spot_ref[2], spot_ref[3])
+    for low_z in range(2):
+        for out, kept, got, index in (
+            (near_sent, near, near_in, 1 - y),
+            (far_sent, far, far_in, 1 - x),
+            (near_kept, near, near_in, y),
+            (far_kept, far, far_in, x),
+        ):
+            out[low_z] = total(kept[low_z, index], got[low_z, index]).astype(jnp.bfloat16)
+
+
+def third_sums_kernel(spot_ref, near, far, near_in, far_in, sent, kept):
+    low_z = spot_ref[1]
+    sent[0] = total(near[1 - low_z], near_in[1 - low_z]).astype(jnp.bfloat16)
+    sent[1] = total(far[1 - low_z], far_in[1 - low_z]).astype(jnp.bfloat16)
+    kept[0] = total(near[low_z], near_in[low_z])
+    kept[1] = total(far[low_z], far_in[low_z])
+
+
+def assemble_kernel(layouts, core_ref, half_ref, other_ref, *outs):
+    core = core_ref[0]
+    half, other = (half_ref[...], other_ref[...])
+    left = jnp.where(core == 0, half, other)
+    right = jnp.where(core == 0, other, half)
+    start, wide_half = (0, half.shape[1])
+    for (blocks, rows), out in zip(layouts, outs):
+        for block in range(blocks):
+            part = slice(start, start + rows)
+            column = 2 * block * wide_half
+            out[:, column : column + wide_half] = left[part]
+            out[:, column + wide_half : column + 2 * wide_half] = right[part]
+            start += rows
+
+
+def in_vmem(kernel, name, outs, *args):
+    vmem = pl.BlockSpec(memory_space=pltpu.VMEM)
+    return pl.pallas_call(
+        kernel,
+        out_shape=outs,
+        in_specs=[SMEM] + [vmem] * (len(args) - 1),
+        out_specs=[vmem] * len(outs),
+        compiler_params=params(),
+        cost_estimate=cost(0, 0, *args, *outs),
+        name=name,
+    )(*args)
+
+
 class Reduction:
-    def __init__(self, spot, views, theirs):
-        self.z_pair, self.z_low, self.y, self.x, self.core = spot
-        self.views = [[self.by_device(view)] for view in views]
-        for terms, part in zip(self.views, theirs):
-            terms.append(self.by_device(swap(part[0], CORE), part[1]))
-
-    @staticmethod
-    def by_device(view, change=None):
-        view = view if change is None else change(view)
-        return view.reshape(2, 2, 2, 2, *view.shape[1:])
-
-    def sums(self, pieces, extra=None):
-        total = jnp.concatenate([add(*terms) for terms in pieces], axis=-2)
-        return total if extra is None else total + wide(extra)
-
-    def chosen(self, pieces, axis, index):
-        return [[pick(term, axis, index) for term in terms] for terms in pieces]
+    def __init__(self, spot, mine, theirs):
+        self.spot = spot
+        self.mine = list(mine)
+        self.got = [swap(part, CORE) for part in theirs]
+        self.count = sum(part.shape[1] for part in self.mine)
+        self.width = self.mine[0].shape[2]
+
+    def like(self, *lead, kind=jnp.bfloat16):
+        return jax.ShapeDtypeStruct((*lead, self.count, self.width), kind)
 
     def first(self):
-        near = self.chosen(self.views, 0, self.z_pair)
-        far = self.chosen(self.views, 0, 1 - self.z_pair)
-        near_sent = low(self.sums(self.chosen(near, 2, 1 - self.x)))
-        far_sent = low(self.sums(self.chosen(far, 1, 1 - self.y)))
-        self.near = self.chosen(near, 2, self.x)
-        self.far = self.chosen(far, 1, self.y)
-        self.near_in, self.far_in = (swap(near_sent, X), swap(far_sent, Y))
-        return (near_sent, far_sent)
+        near_sent, far_sent, *self.kept = in_vmem(
+            functools.partial(first_sums_kernel, len(self.mine)),
+            "first_sums",
+            [self.like(2, 2)] * 4,
+            self.spot,
+            *self.mine,
+            *self.got,
+        )
+        self.got = [swap(near_sent, X), swap(far_sent, Y)]
+        return self.kept
 
     def second(self):
-        near, far = (self.near, self.far)
-        near_sent = low(
-            self.sums(self.chosen(near, 1, 1 - self.y), pick(self.near_in, 1, 1 - self.y))
-        )
-        far_sent = low(
-            self.sums(self.chosen(far, 1, 1 - self.x), pick(self.far_in, 1, 1 - self.x))
-        )
-        near = self.sums(self.chosen(near, 1, self.y), pick(self.near_in, 1, self.y))
-        far = self.sums(self.chosen(far, 1, self.x), pick(self.far_in, 1, self.x))
-        self.near, self.far = (low(near), low(far))
-        self.near_in, self.far_in = (swap(near_sent, Y), swap(far_sent, X))
-        return (near_sent, far_sent)
+        near_sent, far_sent, *self.kept = in_vmem(
+            second_sums_kernel, "second_sums", [self.like(2)] * 4, self.spot, *self.kept, *self.got
+        )
+        self.got = [swap(near_sent, Y), swap(far_sent, X)]
+        return self.kept
 
     def third(self):
-        near, far = ((self.near, self.near_in), (self.far, self.far_in))
-
-        def summed(pair, index):
-            return add(*[pick(term, 0, index) for term in pair])
-
-        sent = low(jnp.stack([summed(near, 1 - self.z_low), summed(far, 1 - self.z_low)]))
-        self.kept = (summed(near, self.z_low), summed(far, self.z_low))
-        self.back = swap(sent, Z1)
-        return sent
-
-    def last(self):
-        far = low(self.kept[1] + wide(self.back[1]))
-        half = self.kept[0] + wide(self.back[0]) + wide(swap(far, Z2))
-        other = swap(half, CORE)
-        core = self.core
-        return jnp.where(core == 0, jnp.stack([half, other], -2), jnp.stack([other, half], -2))
-
-
-def blocks_first(array):
-    view = array.reshape(4, 16, 48, array.shape[2])
-    return jnp.transpose(view, (1, 0, 2, 3)).reshape(16, 192, array.shape[2])
-
-
-def rows_first(array):
-    return array.reshape(16, 192, array.shape[2])
-
-
-def reduce_small(small, dp):
-    small = jnp.concatenate([part.reshape(-1, FEATURES) for part in small])
-    for bits in (CORE, X, Y, Z1, Z2):
-        small = small + swap(small, bits)
-
+        sent, kept = in_vmem(
+            third_sums_kernel,
+            "third_sums",
+            [self.like(2), self.like(2, kind=jnp.float32)],
+            self.spot,
+            *self.kept,
+            *self.got,
+        )
+        self.kept, self.got = ([kept], [swap(sent, Z1)])
+        return self.kept
+
+    def fourth(self):
+        (kept,), (got,) = (self.kept, self.got)
+        far = low(kept[1] + wide(got[1]))
+        self.kept, self.got = ([kept, got], [swap(far, Z2)])
+
+    def fifth(self):
+        (kept, got), (far,) = (self.kept, self.got)
+        half = kept[0] + wide(got[0]) + wide(far)
+        self.kept, self.got = ([half], [swap(half, CORE)])
+
+    def whole(self, core, layouts):
+        outs = [
+            jax.ShapeDtypeStruct((rows, 2 * self.width * blocks), jnp.float32)
+            for blocks, rows in layouts
+        ]
+        return in_vmem(
+            functools.partial(assemble_kernel, layouts), "assemble", outs, core, *self.kept, *self.got
+        )
+
+
+def own_small(small, dp):
     def own(start, rows):
         vector = small[start : start + rows].reshape(-1)
         size = vector.shape[0] // 16
         return lax.dynamic_slice_in_dim(vector, dp * size, size)
 
     return [own(0, 1), own(1, 1), own(2, 3), own(5, 1), own(6, 1), own(7, 1), own(8, 4), own(12, 1)]
-
-
-def gather_small(pieces, me):
-    sizes = tuple(piece.shape[0] for piece in pieces)
-    small = jnp.stack([jnp.pad(piece, (0, 256 - piece.shape[0])) for piece in pieces])[None]
-    for bits in (Z1, Z2, X, Y):
-        small = jnp.concatenate([small, swap(small, bits)])
-    return place_small(me, small, sizes)
 
 
 def gather_all(weights, spot, me):
@@ -894,9 +979,11 @@
     across = lax.dynamic_slice_in_dim(proj, core * 96, 96, 0).reshape(2, 48, FEATURES)
     mlp = lax.all_gather(jnp.concatenate([columns, across]), BOTH)
     mlp = mlp.reshape(16, 2, 4, 48, FEATURES)
-    first, early, later = gather_first(jnp.concatenate([half(qkv), half(out)])[None], me)
     vectors = [gain_a, shift_a, qbias, obias, gain_m, shift_m, fbias, pbias]
-    return (first, mlp, *gather_small(after(vectors, early), me))
+    sizes = tuple(vector.shape[0] for vector in vectors)
+    small = jnp.stack([jnp.pad(v, (0, 256 - size)) for v, size in zip(vectors, sizes)])
+    first, small = gather_first(jnp.concatenate([half(qkv), half(out)])[None], small[None], me)
+    return (first, mlp, *place_small(me, small, sizes))
 
 
 def gather_plain(weights):
@@ -917,24 +1004,20 @@
     return (first, mlp, *rows)
 
 
-def reduce_plain(terms):
-    matrices, small = terms
-
-    def joined(pair):
-        return wide(jnp.concatenate(pair, axis=2))
-
-    def sides(blocks):
-        return jnp.transpose(blocks, (1, 0, 2)).reshape(FEATURES, -1)
-
-    first, fc, proj = [joined(pair) for pair in matrices]
-    gain_a, shift_a, bias_a, gain_m, shift_m, fbias, pbias = small
+def reduce_plain(matrices, small):
+    def joined(left, right):
+        both = jnp.concatenate([left, right], axis=-1)
+        if both.ndim == 4:
+            both = jnp.transpose(both, (0, 2, 1, 3)).reshape(FEATURES, -1)
+        return both.reshape(-1, both.shape[-1])
+
+    qkv, out, fc, proj = [joined(*pair) for pair in matrices]
+    gain_a, shift_a, qbias, obias, gain_m, shift_m, fbias, pbias = [v.reshape(-1) for v in small]
     values = (
-        gain_a.reshape(-1), shift_a.reshape(-1), sides(first[:3]), bias_a[:3].reshape(-1), first[3],
-        bias_a[3].reshape(-1), gain_m.reshape(-1), shift_m.reshape(-1), sides(fc), fbias.reshape(-1),
-        proj.reshape(-1, FEATURES), pbias.reshape(-1),
+        gain_a, shift_a, qkv, qbias, out, obias, gain_m, shift_m, fc, fbias, proj, pbias
     )
     return tuple(
-        wide(lax.psum(low(lax.psum_scatter(v, "dp", scatter_dimension=0, tiled=True)), "rep"))
+        wide(lax.psum(low(lax.psum_scatter(wide(v), "dp", scatter_dimension=0, tiled=True)), "rep"))
         for v in values
     )
 
@@ -957,6 +1040,7 @@
     dp, core = (lax.axis_index("dp"), lax.axis_index("rep"))
     spot = (dp // 8, dp // 4 % 2, dp // 2 % 2, dp % 2, core)
     me = (dp * 2 + core).astype(jnp.int32).reshape(1)
+    places = jnp.stack(spot).astype(jnp.int32)
     side = core.astype(jnp.int32).reshape(1) if custom else jnp.zeros((1,), jnp.int32)
     back = -(-(LONGEST - 1) // BLOCK)
     lengths = doc_lengths.reshape(micro, doc_lengths.shape[-1])
@@ -966,56 +1050,81 @@
     )
     weight, mlp, gain_a, gain_m = (whole_ones[0], whole_ones[1], whole_ones[2], whole_ones[6])
     grad, mlp_terms, terms, norm = (cotangent.reshape(micro * count, width), None, None, None)
+    delayed = None
     for use in range(USES - 1, -1, -1):
         before, normed_a, mixed, att, lse, hidden, normed_m, expanded = kept[use]
         dhid, *mlp_terms = mlp_backward(
-            side, grad, hidden, normed_m, expanded, mlp, gain_m, mlp_terms
+            side, grad, hidden, normed_m, att, expanded, mlp, gain_m, mlp_terms
         )
         sending = custom and use == 0
+        if delayed is not None:
+            terms = delayed()
         if sending:
-            fc_mine, fc_theirs, proj_mine, proj_theirs = mlp_terms[:4]
+            fc_mine, fc_theirs, proj_mine, proj_theirs, out_mine, out_theirs = [
+                part.reshape(16, -1, part.shape[-1]) for part in mlp_terms[:6]
+            ]
             sums = Reduction(
-                spot,
-                (blocks_first(fc_mine), rows_first(proj_mine)),
-                ((fc_theirs, blocks_first), (proj_theirs, rows_first)),
+                places, (fc_mine, proj_mine, out_mine), (fc_theirs, proj_theirs, out_theirs)
             )
-        gmix = []
-        for index in range(micro):
-            if sending and index == micro - 1:
-                dhid, *unused = after((dhid, gmix), sums.first())
-                gmix = list(unused[0])
-            gmix.append(
-                attention_backward(index, lengths, dhid, count, back, att, mixed, lse, weight)
+            sums.got, terms = lax.optimization_barrier((sums.got, terms))
+            dhid = after(dhid, sums.first())
+        gmix = [
+            attention_backward(
+                index, lengths, dhid, count, back, att, mixed, lse, weight,
+                pltpu.HBM if use else jax.ShapeDtypeStruct,
             )
-        terms = attention_terms(side, normed_a, att, gmix, dhid, terms)
+            for index in range(micro)
+        ]
+        if use:
+            delayed = functools.partial(attention_terms, side, normed_a, gmix)
+        else:
+            terms = attention_terms(side, normed_a, gmix, terms)
         if sending:
-            gmix, terms, unused = lax.optimization_barrier((gmix, terms, sums.second()))
-            attention_sums = Reduction(
-                spot, (blocks_first(terms[0]),), ((terms[1], blocks_first),)
+            qkv_sums = Reduction(
+                places, *[(part.reshape(16, -1, part.shape[-1]),) for part in terms[:2]]
             )
+            sums.got, terms = lax.optimization_barrier((sums.got, terms))
+            gmix = after(gmix, sums.second())
         kind = jnp.float32 if use else jnp.bfloat16
         grad, *norm = attention_input(dhid, before, gmix, weight, gain_a, kind, norm)
-    small = (norm[0], norm[1], terms[2], mlp_terms[6], mlp_terms[7], mlp_terms[4], mlp_terms[5])
+        if sending:
+            sums.got, qkv_sums.got, norm = lax.optimization_barrier(
+                (sums.got, qkv_sums.got, norm)
+            )
+    small = (norm[0], norm[1], terms[2], mlp_terms[6], mlp_terms[9], mlp_terms[10])
+    small += (mlp_terms[7], mlp_terms[8])
     if custom:
+        small = jnp.concatenate([part.reshape(-1, width) for part in small])
+        qkv_sums.first()
         sums.third()
-        attention_sums.first()
-        attention_sums.second()
-        attention_sums.third()
-        fc, proj = jnp.split(sums.last(), 2)
-        first = attention_sums.last()
-
-        def columns(array):
-            return jnp.transpose(array.reshape(4, 48, width), (1, 0, 2)).reshape(48, 4 * width)
-
-        first = columns(first)
-        gain_a, shift_a, qbias, obias, gain_m, shift_m, fbias, pbias = reduce_small(small, dp)
+        small = small + swap(small, CORE)
+        got = swap(small, X)
+        sums.got, qkv_sums.got, got = lax.optimization_barrier((sums.got, qkv_sums.got, got))
+        qkv_sums.second()
+        sums.fourth()
+        small = small + got
+        got = swap(small, Y)
+        sums.got, qkv_sums.got, got = lax.optimization_barrier((sums.got, qkv_sums.got, got))
+        qkv_sums.third()
+        sums.fifth()
+        small = small + got
+        got = swap(small, Z1)
+        sums.got, qkv_sums.got, got = lax.optimization_barrier((sums.got, qkv_sums.got, got))
+        qkv_sums.fourth()
+        small = small + got
+        got = swap(small, Z2)
+        qkv_sums.got, got = lax.optimization_barrier((qkv_sums.got, got))
+        qkv_sums.fifth()
+        fc, proj, out = sums.whole(side, ((4, 48), (1, 192), (1, 48)))
+        (qkv,) = qkv_sums.whole(side, ((3, 48),))
+        small = own_small(small + got, dp)
+        gain_a, shift_a, qbias, obias, gain_m, shift_m, fbias, pbias = small
         final = (
-            gain_a, shift_a, first[:, : 3 * width], qbias, first[:, 3 * width :], obias,
-            gain_m, shift_m, columns(fc), fbias, proj.reshape(192, width), pbias,
+            gain_a, shift_a, qkv, qbias, out, obias, gain_m, shift_m, fc, fbias, proj, pbias
         )
     else:
-        matrices = (terms[:2], mlp_terms[:2], mlp_terms[2:4])
-        final = reduce_plain((matrices, small))
+        matrices = (terms[:2], mlp_terms[4:6], mlp_terms[:2], mlp_terms[2:4])
+        final = reduce_plain(matrices, small)
     return (state.reshape(tokens.shape), grad.reshape(tokens.shape), *final)
 
 

time: 457 us -> 399 us (0.87)
  Pallas kernels: 268 us -> 246 us
  other arithmetic: 23.9 us -> 2.56 us
  waiting for transfers between devices: 78.8 us -> 60.3 us
  starting transfers between devices: 40.3 us -> 54 us
  local copies, waits for them, and re-layouts: 26.8 us -> 17.4 us
    ppermute x38 -> x41, waiting for transfers between devices: 78.8 us -> 58.7 us  [swap(): return lax.ppermute(value, BOTH, [(i, i ^ bits) for i in range(32)])]
    pallas_call x2, Pallas kernels: 55.8 us -> 40.5 us  [attention_forward(): pl.pallas_call(functools.partial(attention_forward_kernel, docs, back), g...]
    ppermute x38 -> x41, starting transfers between devices: 40.2 us -> 53.9 us  [swap(): return lax.ppermute(value, BOTH, [(i, i ^ bits) for i in range(32)])]
    pallas_call x0 -> x8, Pallas kernels: none -> 11.6 us  [in_vmem(): pl.pallas_call(kernel, out_shape=outs, in_specs=[SMEM] + [vmem] * (len(ar...]
    reshape x8 -> x0, local copies, waits for them, and re-layouts: 10.4 us -> none  [the longest x4 8.18 us: blocks_first(): view = array.reshape(4, 16, 48, array.shape[2])]
    pallas_call x4, Pallas kernels: 55.1 us -> 44.7 us  [attention_backward(): pl.pallas_call(functools.partial(attention_backward_kernel, docs, back, m...]
    pallas_call x2, Pallas kernels: 25 us -> 15.1 us  [attention_terms(): pl.pallas_call(functools.partial(attention_terms_kernel, earlier is not N...]
    convert_element_type x7 -> x2, other arithmetic: 10.6 us -> 1.07 us  [low(): return value.astype(jnp.bfloat16)]
  transfers between devices with their start and end apart: 39 -> 42, of which waited for: 18 -> 16; matrix products, arithmetic and copies ran while one was open for 7% -> 3% of each run, Pallas kernels for 22% -> 20%
where the time goes in v2:
time: 399 us; the launch traced here: 395 us
  Pallas kernels  246 us (62%)
  waiting for transfers between devices  60.3 us (15%)
  starting transfers between devices  54 us (14%)
  local copies, waits for them, and re-layouts  17.4 us (4%)
  between operations  15.1 us (4%)
    pallas_call x2, Pallas kernels, mlp_backward(): pl.pallas_call(functools.partial(mlp_backward_kernel, earlier is not None...  73.9 us
    ppermute x41, waiting for transfers between devices, swap(): return lax.ppermute(value, BOTH, [(i, i ^ bits) for i in range(32)])  58.7 us
    ppermute x41, starting transfers between devices, swap(): return lax.ppermute(value, BOTH, [(i, i ^ bits) for i in range(32)])  53.9 us
    pallas_call x4, Pallas kernels, attention_backward(): pl.pallas_call(functools.partial(attention_backward_kernel, docs, back, m...  44.7 us
    pallas_call x2, Pallas kernels, attention_forward(): pl.pallas_call(functools.partial(attention_forward_kernel, docs, back), g...  40.5 us
    pallas_call x2, Pallas kernels, mlp_forward(): pl.pallas_call(functools.partial(mlp_forward_kernel, last), grid=(hidden_...  33.9 us
    pallas_call x2, Pallas kernels, attention_input(): pl.pallas_call(functools.partial(attention_input_kernel, earlier is not N...  18.1 us
    pallas_call x2, Pallas kernels, attention_terms(): pl.pallas_call(functools.partial(attention_terms_kernel, earlier is not N...  15.1 us
  transfers between devices with their start and end apart: 42, of which 16 were waited for; matrix products, arithmetic and copies ran while one was open for 3% of the time, Pallas kernels for 20%

profile of v2, /device:TPU:1, one launch (start us, length us, event | category | flops | bytes accessed | tf_op | source)
XLA Modules:
  0.0 394.9 jit_solution(6308749299872277806)
XLA Ops:
  8.3 0.9 constant_dynamic-slice_fusion.7
  10.5 2.2 collective-permute-start
  12.7 2.3 collective-permute-start.1
  15.7 3.2 collective-permute-start.4
  18.9 3.1 collective-permute-done.3
  21.9 1.9 collective-permute-start.5
  23.8 6.9 %collective-permute-done.4 = bf16[1,8,256]{2,1,0:T(8,128)(2,1)S(1)} collective-permute-done((bf16[1,8,256]{2,1,0:T(8,128)(2,1)S(1)}, bf16[1,8,256]{2,1,0:T(8,128)(2,1)S(1)}, u32[]{:S(2)}, u32[]{:S(2)}) %collective-permute-start.4) | collective-permute-done | bytes 4128 | tf_op jit(solution)/shard_map/ppermute | solution.py:735
  30.9 1.3 collective-permute-start.6
  32.2 1.7 collective-permute-start.7
  33.9 4.8 %collective-permute-start.8 = (bf16[4,4,24,768]{3,2,1,0:T(8,128)(2,1)S(1)}, bf16[4,4,24,768]{3,2,1,0:T(8,128)(2,1)S(1)}, u32[]{:S(2)}, u32[]{:S(2)}) collective-permute-start(bf16[4,4,24,768]{3,2,1,0:T(8,128)(2,1)S(1)} %constant_dynamic-update-slice_fusion.refs_0_), channel_id=1, source_target_pairs={{0,1},{1,0},{2,3},{3,2},{4,5},{5,4},{6,7},{7,6},{8,9},{9,8},{10,11... | collective-permute-start | bytes 1769480 | tf_op jit(solution)/shard_map/ppermute | solution.py:735
  41.4 3.1 collective-permute-done.9
  44.5 9.6 %collective-permute-start.13 = (bf16[4,4,24,768]{3,2,1,0:T(8,128)(2,1)S(1)}, bf16[4,4,24,768]{3,2,1,0:T(8,128)(2,1)S(1)}, u32[]{:S(2)}, u32[]{:S(2)}) collective-permute-start(bf16[4,4,24,768]{3,2,1,0:T(8,128)(2,1)S(1)} %collective-permute-done.6.refs_1_), channel_id=1, source_target_pairs={{0,1},{1,0},{2,3},{3,2},{4,5},{5,4},{6,7},{7,6},{8,9},{9,8},{10,11... | collective-permute-start | bytes 1769480 | tf_op jit(solution)/shard_map/ppermute | solution.py:735
  55.7 2.3 collective-permute-start.11
  58.1 2.1 collective-permute-start.12
  60.2 5.5 %collective-permute-done.15 = bf16[4,8,256]{2,1,0:T(8,128)(2,1)} collective-permute-done((bf16[4,8,256]{2,1,0:T(8,128)(2,1)}, bf16[4,8,256]{2,1,0:T(8,128)(2,1)}, u32[]{:S(2)}, u32[]{:S(2)}) %collective-permute-start.15) | collective-permute-done | bytes 16416 | tf_op jit(solution)/shard_map/ppermute | solution.py:735
  65.7 1.5 collective-permute-done.12.refs_4_
  67.2 1.3 collective-permute-start.16
  68.6 1.3 constant_dynamic-update-slice_fusion.10
  70.0 1.3 constant_dynamic-update-slice_fusion.9
  71.3 1.3 constant_dynamic-update-slice_fusion.8.small_ref
  72.6 2.7 place_small.1
  75.4 5.0 %place.1 = bf16[4,32,24,768]{3,2,1,0:T(8,128)(2,1)} custom-call(s32[1]{0:T(128)} %bitcast.2.me_ref, bf16[4,4,24,768]{3,2,1,0:T(8,128)(2,1)} %copy-done.15, bf16[4,4,24,768]{3,2,1,0:T(8,128)(2,1)} %copy-done.13, bf16[4,4,24,768]{3,2,1,0:T(8,128)(2,1)} %copy-done.14, bf16[2,4,24,768]{3,2,1,0:T(8,128)(2,1)} %collective-permute-done.11.refs_3_, ...), custom_call_target="tpu_custom_call" | custom-call | tf_op jit(solution)/shard_map/place/pallas_call | solution.py:759
  80.4 19.7 %attention_forward.2 = (bf16[1024,768]{1,0:T(8,128)(2,1)}, bf16[1024,2304]{1,0:T(8,128)(2,1)}, bf16[1024,768]{1,0:T(8,128)(2,1)}, f32[24,1,512]{2,1,0:T(1,128)},...) custom-call(s32[2,6]{1,0:T(2,128)S(1)} %bitcast.63, bf16[1024,768]{1,0:T(8,128)(2,1)} %bitcast.85, ...), custom_call_target="tpu_custom_call" | custom-call | flops 805306368 | bytes 2368512 | tf_op jit(solution)/shard_map/attention_forward/pallas_call | solution.py:205
  100.1 1.6 all-gather.3.cloned.1.call-done
  101.7 16.9 %mlp_forward.2 = (bf16[1024,3072]{1,0:T(8,128)(2,1)}, f32[1024,768]{1,0:T(8,128)}) custom-call(f32[1024,768]{1,0:T(8,128)} %get-tuple-element.169.hidden_ref, bf16[1024,768]{1,0:T(8,128)(2,1)} %get-tuple-element.170.normed_ref, bf16[16,2,4,48,768]{4,3,2,1,0:T(8,128)(2,1)} %bitcast.69, f32[1,3072]{1,0:T(1,128)} %get-tuple-element.171.fbias_ref, ...), custom_call_target="tpu_custom_call" | custom-call | flops 1207959552 | bytes 2949120 | tf_op jit(solution)/shard_map/mlp_forward/pallas_call | solution.py:290
  118.6 20.8 %attention_forward.3 = (bf16[1024,768]{1,0:T(8,128)(2,1)}, bf16[1024,2304]{1,0:T(8,128)(2,1)}, bf16[1024,768]{1,0:T(8,128)(2,1)}, f32[24,1,512]{2,1,0:T(1,128)},...) custom-call(s32[2,6]{1,0:T(2,128)S(1)} %bitcast.64, f32[1024,768]{1,0:T(8,128)} %get-tuple-element.173.state_ref, ...), custom_call_target="tpu_custom_call" | custom-call | flops 805306368 | bytes 2565120 | tf_op jit(solution)/shard_map/attention_forward/pallas_call | solution.py:205
  139.4 17.0 %mlp_forward.3 = (bf16[1024,3072]{1,0:T(8,128)(2,1)}, bf16[1024,768]{1,0:T(8,128)(2,1)}) custom-call(f32[1024,768]{1,0:T(8,128)} %get-tuple-element.174.hidden_ref, bf16[1024,768]{1,0:T(8,128)(2,1)} %get-tuple-element.175.normed_ref, bf16[16,2,4,48,768]{4,3,2,1,0:T(8,128)(2,1)} %bitcast.71, f32[1,3072]{1,0:T(1,128)} %get-tuple-element.171.fbias_ref, ...), custom_call_target="tpu_custom_call" | custom-call | flops 1207959552 | bytes 2752512 | tf_op jit(solution)/shard_map/mlp_forward/pallas_call | solution.py:290
  156.4 36.1 %mlp_backward.2 = (f32[1024,768]{1,0:T(8,128)}, bf16[16,4,48,384]{3,2,1,0:T(8,128)(2,1)}, bf16[16,4,48,384]{3,2,1,0:T(8,128)(2,1)}, bf16[3072,384]{1,0:T(8,128)(...) custom-call(s32[1]{0:T(128)} %bitcast.12.core_ref, ...), custom_call_target="tpu_custom_call" | custom-call | flops 2415919104 | bytes 5852544 | tf_op jit(solution)/shard_map/mlp_backward/pallas_call | solution.py:471
  192.5 11.8 %attention_backward.4.rest_0_ = bf16[512,2304]{1,0:T(8,128)(2,1)} custom-call(s32[2,6]{1,0:T(2,128)S(1)} %bitcast.65, f32[1024,768]{1,0:T(8,128)} %get-tuple-element.179.dhid_ref, bf16[1024,768]{1,0:T(8,128)(2,1)} %get-tuple-element.177.att_ref, bf16[1024,2304]{1,0:T(8,128)(2,1)} %get-tuple-element.180.mixed_ref, f32[24,1,512]{2,1,0:T(1,128)} %get-tuple-element.181.lse_ref, ...), custom_call_target="tpu_custom_call" | custom-call | flops 327155712 | bytes 589824 | tf_op jit(solution)/shard_map/attention_backward/pallas_call | solution.py:561
  204.3 11.9 %attention_backward.5.rest_1_ = bf16[512,2304]{1,0:T(8,128)(2,1)} custom-call(s32[2,6]{1,0:T(2,128)S(1)} %bitcast.66, f32[1024,768]{1,0:T(8,128)} %get-tuple-element.179.dhid_ref, bf16[1024,768]{1,0:T(8,128)(2,1)} %get-tuple-element.177.att_ref, bf16[1024,2304]{1,0:T(8,128)(2,1)} %get-tuple-element.180.mixed_ref, f32[24,1,512]{2,1,0:T(1,128)} %get-tuple-element.181.lse_ref, ...), custom_call_target="tpu_custom_call" | custom-call | flops 327155712 | bytes 589824 | tf_op jit(solution)/shard_map/attention_backward/pallas_call | solution.py:561
  216.2 1.7 copy-done.3
  217.9 8.7 %attention_input.2 = (f32[1024,768]{1,0:T(8,128)S(1)}, f32[1,768]{1,0:T(1,128)S(1)}, f32[1,768]{1,0:T(1,128)S(1)}) custom-call(f32[1024,768]{1,0:T(8,128)} %get-tuple-element.179.dhid_ref, f32[1024,768]{1,0:T(8,128)} %get-tuple-element.173.state_ref, bf16[4,768,768]{2,1,0:T(8,128)(2,1)} %bitcast.81, f32[1,768]{1,0:T(1,128)} %get-tuple-element.158.gain_ref, ...), custom_call_target="tpu_custom_call" | custom-call | flops 452984832 | bytes 2360448 | tf_op jit(solution)/shard_map/attention_input/pallas_call | solution.py:694
  226.6 37.8 %mlp_backward.3 = (f32[1024,768]{1,0:T(8,128)}, bf16[16,4,48,384]{3,2,1,0:T(8,128)(2,1)}, bf16[16,4,48,384]{3,2,1,0:T(8,128)(2,1)}, bf16[3072,384]{1,0:T(8,128)(...) custom-call(s32[1]{0:T(128)} %bitcast.12.core_ref, ...), custom_call_target="tpu_custom_call" | custom-call | flops 2415919104 | bytes 7379328 | tf_op jit(solution)/shard_map/mlp_backward/pallas_call | solution.py:471
  265.4 1.7 copy-done.4
  267.1 7.3 %attention_terms.2 = (bf16[16,3,48,384]{3,2,1,0:T(8,128)(2,1)}, bf16[16,3,48,384]{3,2,1,0:T(8,128)(2,1)}, f32[3,1,768]{2,1,0:T(1,128)}) custom-call(s32[1]{0:T(128)} %bitcast.12.core_ref, bf16[1024,768]{1,0:T(8,128)(2,1)} %get-tuple-element.203.normed_ref, bf16[512,2304]{1,0:T(8,128)(2,1)S(1)} %copy-done.2, bf16[512,2304]{1,0:T(8,128)(2,1)S(1)} %copy-done.4), custom_call_target="tpu_custom_call" | custom-call | flops 452984832 | bytes 1229952 | tf_op jit(solution)/shard_map/attention_terms/pallas_call | solution.py:621
  274.4 3.8 first_sums.2
  278.2 1.2 collective-permute-start.21
  279.7 10.4 %attention_backward.6.rest_0_ = bf16[512,2304]{1,0:T(8,128)(2,1)S(1)} custom-call(s32[2,6]{1,0:T(2,128)S(1)} %bitcast.67, f32[1024,768]{1,0:T(8,128)} %get-tuple-element.212.dhid_ref, bf16[1024,768]{1,0:T(8,128)(2,1)} %get-tuple-element.183.att_ref, bf16[1024,2304]{1,0:T(8,128)(2,1)} %get-tuple-element.213.mixed_ref, ...), custom_call_target="tpu_custom_call" | custom-call | flops 327155712 | bytes 589824 | tf_op jit(solution)/shard_map/attention_backward/pallas_call | solution.py:561
  290.1 10.6 %attention_backward.7.rest_1_ = bf16[512,2304]{1,0:T(8,128)(2,1)S(1)} custom-call(s32[2,6]{1,0:T(2,128)S(1)} %bitcast.68, f32[1024,768]{1,0:T(8,128)} %get-tuple-element.212.dhid_ref, bf16[1024,768]{1,0:T(8,128)(2,1)} %get-tuple-element.183.att_ref, bf16[1024,2304]{1,0:T(8,128)(2,1)} %get-tuple-element.213.mixed_ref, ...), custom_call_target="tpu_custom_call" | custom-call | flops 327155712 | bytes 589824 | tf_op jit(solution)/shard_map/attention_backward/pallas_call | solution.py:561
  300.8 7.8 %attention_terms.3 = (bf16[16,3,48,384]{3,2,1,0:T(8,128)(2,1)}, bf16[16,3,48,384]{3,2,1,0:T(8,128)(2,1)}, f32[3,1,768]{2,1,0:T(1,128)}) custom-call(s32[1]{0:T(128)} %bitcast.12.core_ref, bf16[1024,768]{1,0:T(8,128)(2,1)} %get-tuple-element.217.normed_ref, bf16[512,2304]{1,0:T(8,128)(2,1)S(1)} %attention_backward.6.rest_0_, ...), custom_call_target="tpu_custom_call" | custom-call | flops 452984832 | bytes 1673472 | tf_op jit(solution)/shard_map/attention_terms/pallas_call | solution.py:621
  309.6 1.2 second_sums.2
  310.8 1.0 collective-permute-start.23
  312.3 9.4 %attention_input.3 = (bf16[1024,768]{1,0:T(8,128)(2,1)}, f32[1,768]{1,0:T(1,128)S(1)}, f32[1,768]{1,0:T(1,128)S(1)}) custom-call(f32[1024,768]{1,0:T(8,128)} %get-tuple-element.212.dhid_ref, bf16[1024,768]{1,0:T(8,128)(2,1)} %bitcast.86, bf16[4,768,768]{2,1,0:T(8,128)(2,1)} %bitcast.84, f32[1,768]{1,0:T(1,128)} %get-tuple-element.158.gain_ref, ...), custom_call_target="tpu_custom_call" | custom-call | flops 452984832 | bytes 1968000 | tf_op jit(solution)/shard_map/attention_input/pallas_call | solution.py:694
  321.7 4.1 %collective-permute-done.23.near_in = bf16[2,432,384]{2,1,0:T(8,128)(2,1)S(1)} collective-permute-done((bf16[2,432,384]{2,1,0:T(8,128)(2,1)S(1)}, bf16[2,432,384]{2,1,0:T(8,128)(2,1)S(1)}, u32[]{:S(2)}, u32[]{:S(2)}) %collective-permute-start.23) | collective-permute-done | bytes 663584 | tf_op jit(solution)/shard_map/ppermute | solution.py:735
  325.9 1.3 collective-permute-done.24.far_in
  327.1 1.6 third_sums.2
  328.8 1.2 collective-permute-start.27
  330.0 1.6 first_sums.3
  332.1 1.1 collective-permute-start.29
  333.4 2.8 collective-permute-start.26
  337.5 4.9 %collective-permute-done.30 = f32[13,768]{1,0:T(8,128)S(1)} collective-permute-done((f32[13,768]{1,0:T(8,128)S(1)}, f32[13,768]{1,0:T(8,128)S(1)}, u32[]{:S(2)}, u32[]{:S(2)}) %collective-permute-start.30) | collective-permute-done | bytes 39968 | tf_op jit(solution)/shard_map/ppermute | solution.py:735
  342.5 1.2 collective-permute-done.27
  343.6 1.1 fusion
  344.7 1.4 collective-permute-start.31
  347.0 1.8 collective-permute-start.33
  348.9 3.3 collective-permute-done.34
  352.2 9.3 %collective-permute-done.31 = bf16[432,384]{1,0:T(8,128)(2,1)S(1)} collective-permute-done((bf16[432,384]{1,0:T(8,128)(2,1)S(1)}, bf16[432,384]{1,0:T(8,128)(2,1)S(1)}, u32[]{:S(2)}, u32[]{:S(2)}) %collective-permute-start.31) | collective-permute-done | bytes 331808 | tf_op jit(solution)/shard_map/ppermute | solution.py:735
  361.5 1.1 bitcast_add_fusion.half_ref
  362.6 1.5 collective-permute-start.35
  364.9 1.4 collective-permute-start.37
  366.3 6.6 %collective-permute-done.37 = f32[13,768]{1,0:T(8,128)S(1)} collective-permute-done((f32[13,768]{1,0:T(8,128)S(1)}, f32[13,768]{1,0:T(8,128)S(1)}, u32[]{:S(2)}, u32[]{:S(2)}) %collective-permute-start.37) | collective-permute-done | bytes 39968 | tf_op jit(solution)/shard_map/ppermute | solution.py:735
  373.3 2.1 collective-permute-start.39
  375.4 1.1 assemble.3
  376.6 6.8 %collective-permute-done.39 = f32[13,768]{1,0:T(8,128)S(1)} collective-permute-done((f32[13,768]{1,0:T(8,128)S(1)}, f32[13,768]{1,0:T(8,128)S(1)}, u32[]{:S(2)}, u32[]{:S(2)}) %collective-permute-start.39) | collective-permute-done | bytes 39968 | tf_op jit(solution)/shard_map/ppermute | solution.py:735
  (178 shorter events, 18.5 us)
Async XLA Ops:
  7.2 7.8 %copy-start.27 = (bf16[48]{0:T(256)(128)(2,1)S(1)}, bf16[48]{0:T(256)(128)(2,1)}, u32[]{:S(2)}) copy-start(bf16[48]{0:T(256)(128)(2,1)} %param.18) | copy-start | bytes 292
  7.2 7.8 %copy-start.28 = (bf16[48]{0:T(256)(128)(2,1)S(1)}, bf16[48]{0:T(256)(128)(2,1)}, u32[]{:S(2)}) copy-start(bf16[48]{0:T(256)(128)(2,1)} %param.19) | copy-start | bytes 292
  7.2 7.8 %copy-start.29 = (bf16[144]{0:T(256)(128)(2,1)S(1)}, bf16[144]{0:T(256)(128)(2,1)}, u32[]{:S(2)}) copy-start(bf16[144]{0:T(256)(128)(2,1)} %param.21) | copy-start | bytes 868
  7.3 7.8 %copy-start.30 = (bf16[48]{0:T(256)(128)(2,1)S(1)}, bf16[48]{0:T(256)(128)(2,1)}, u32[]{:S(2)}) copy-start(bf16[48]{0:T(256)(128)(2,1)} %param.23) | copy-start | bytes 292
  7.3 7.8 %copy-start.31 = (bf16[48]{0:T(256)(128)(2,1)S(1)}, bf16[48]{0:T(256)(128)(2,1)}, u32[]{:S(2)}) copy-start(bf16[48]{0:T(256)(128)(2,1)} %param.24) | copy-start | bytes 292
  7.3 7.9 %copy-start.32 = (bf16[48]{0:T(256)(128)(2,1)S(1)}, bf16[48]{0:T(256)(128)(2,1)}, u32[]{:S(2)}) copy-start(bf16[48]{0:T(256)(128)(2,1)} %param.25) | copy-start | bytes 292
  7.3 7.9 %copy-start.33 = (bf16[192]{0:T(256)(128)(2,1)S(1)}, bf16[192]{0:T(256)(128)(2,1)}, u32[]{:S(2)}) copy-start(bf16[192]{0:T(256)(128)(2,1)} %param.27) | copy-start | bytes 1156
  7.3 7.9 %copy-start.34 = (bf16[48]{0:T(256)(128)(2,1)S(1)}, bf16[48]{0:T(256)(128)(2,1)}, u32[]{:S(2)}) copy-start(bf16[48]{0:T(256)(128)(2,1)} %param.29) | copy-start | bytes 292
  7.3 94.4 %all-gather.3.cloned.1.call-start = ((), (), s32[]{:S(2)}) async-start(), calls=%async_computation | async-start | bytes 9732096 | tf_op jit(solution)/shard_map/all_gather | solution.py:980
  10.5 20.3 %collective-permute-start = (bf16[1,4,24,768]{3,2,1,0:T(8,128)(2,1)S(1)}, bf16[1,4,24,768]{3,2,1,0:T(8,128)(2,1)S(1)}, u32[]{:S(2)}, u32[]{:S(2)}) collective-permute-start(bf16[1,4,24,768]{3,2,1,0:T(8,128)(2,1)S(1)} %maximum_bitcast_fusion), channel_id=1, source_target_pairs={{0,8},{1,9},{2,10},{3,11},{4,12},{5,13},{6,14},{7,15},{8,0},{9,1},... | collective-permute-start | bytes 442376 | tf_op jit(solution)/shard_map/ppermute | solution.py:735
  12.7 18.1 %collective-permute-start.1 = (bf16[1,4,24,768]{3,2,1,0:T(8,128)(2,1)S(1)}, bf16[1,4,24,768]{3,2,1,0:T(8,128)(2,1)S(1)}, u32[]{:S(2)}, u32[]{:S(2)}) collective-permute-start(bf16[1,4,24,768]{3,2,1,0:T(8,128)(2,1)S(1)} %maximum_bitcast_fusion), channel_id=1, source_target_pairs={{0,16},{1,17},{2,18},{3,19},{4,20},{5,21},{6,22},{7,23},{8,24},{9,... | collective-permute-start | bytes 442376 | tf_op jit(solution)/shard_map/ppermute | solution.py:735
  15.0 15.8 %collective-permute-start.2 = (bf16[1,4,24,768]{3,2,1,0:T(8,128)(2,1)S(1)}, bf16[1,4,24,768]{3,2,1,0:T(8,128)(2,1)S(1)}, u32[]{:S(2)}, u32[]{:S(2)}) collective-permute-start(bf16[1,4,24,768]{3,2,1,0:T(8,128)(2,1)S(1)} %maximum_bitcast_fusion), channel_id=1, source_target_pairs={{0,24},{1,25},{2,26},{3,27},{4,28},{5,29},{6,30},{7,31},{8,16},{9,... | collective-permute-start | bytes 442376 | tf_op jit(solution)/shard_map/ppermute | solution.py:735
  15.3 6.7 %collective-permute-start.3 = (bf16[1,8,256]{2,1,0:T(8,128)(2,1)S(1)}, bf16[1,8,256]{2,1,0:T(8,128)(2,1)S(1)}, u32[]{:S(2)}, u32[]{:S(2)}) collective-permute-start(bf16[1,8,256]{2,1,0:T(8,128)(2,1)S(1)} %bitcast.93), channel_id=1, source_target_pairs={{0,8},{1,9},{2,10},{3,11},{4,12},{5,13},{6,14},{7,15},{8,0},{9,1},... | collective-permute-start | bytes 12296 | tf_op jit(solution)/shard_map/ppermute | solution.py:735
  15.7 15.1 %collective-permute-start.4 = (bf16[1,8,256]{2,1,0:T(8,128)(2,1)S(1)}, bf16[1,8,256]{2,1,0:T(8,128)(2,1)S(1)}, u32[]{:S(2)}, u32[]{:S(2)}) collective-permute-start(bf16[1,8,256]{2,1,0:T(8,128)(2,1)S(1)} %bitcast.94), channel_id=1, source_target_pairs={{0,16},{1,17},{2,18},{3,19},{4,20},{5,21},{6,22},{7,23},{8,24},{9,... | collective-permute-start | bytes 12296 | tf_op jit(solution)/shard_map/ppermute | solution.py:735
  21.9 8.8 %collective-permute-start.5 = (bf16[1,8,256]{2,1,0:T(8,128)(2,1)S(1)}, bf16[1,8,256]{2,1,0:T(8,128)(2,1)S(1)}, u32[]{:S(2)}, u32[]{:S(2)}) collective-permute-start(bf16[1,8,256]{2,1,0:T(8,128)(2,1)S(1)} %bitcast.95), channel_id=1, source_target_pairs={{0,24},{1,25},{2,26},{3,27},{4,28},{5,29},{6,30},{7,31},{8,16},{9,... | collective-permute-start | bytes 12296 | tf_op jit(solution)/shard_map/ppermute | solution.py:735
  30.9 44.5 %copy-start.15 = (bf16[4,4,24,768]{3,2,1,0:T(8,128)(2,1)}, bf16[4,4,24,768]{3,2,1,0:T(8,128)(2,1)S(1)}, u32[]{:S(2)}) copy-start(bf16[4,4,24,768]{3,2,1,0:T(8,128)(2,1)S(1)} %constant_dynamic-update-slice_fusion.refs_0_) | copy-start | bytes 1769476
  30.9 13.6 %collective-permute-start.6 = (bf16[4,4,24,768]{3,2,1,0:T(8,128)(2,1)S(1)}, bf16[4,4,24,768]{3,2,1,0:T(8,128)(2,1)S(1)}, u32[]{:S(2)}, u32[]{:S(2)}) collective-permute-start(bf16[4,4,24,768]{3,2,1,0:T(8,128)(2,1)S(1)} %constant_dynamic-update-slice_fusion.refs_0_), channel_id=1, source_target_pairs={{0,2},{1,3},{2,0},{3,1},{4,6},{5,7},{6,4},{7,5},{8,10},{9,11},{10,... | collective-permute-start | bytes 1769480 | tf_op jit(solution)/shard_map/ppermute | solution.py:735
  32.2 12.3 %collective-permute-start.7 = (bf16[4,4,24,768]{3,2,1,0:T(8,128)(2,1)S(1)}, bf16[4,4,24,768]{3,2,1,0:T(8,128)(2,1)S(1)}, u32[]{:S(2)}, u32[]{:S(2)}) collective-permute-start(bf16[4,4,24,768]{3,2,1,0:T(8,128)(2,1)S(1)} %constant_dynamic-update-slice_fusion.refs_0_), channel_id=1, source_target_pairs={{0,4},{1,5},{2,6},{3,7},{4,0},{5,1},{6,2},{7,3},{8,12},{9,13},{10,... | collective-permute-start | bytes 1769480 | tf_op jit(solution)/shard_map/ppermute | solution.py:735
  33.9 10.6 %collective-permute-start.8 = (bf16[4,4,24,768]{3,2,1,0:T(8,128)(2,1)S(1)}, bf16[4,4,24,768]{3,2,1,0:T(8,128)(2,1)S(1)}, u32[]{:S(2)}, u32[]{:S(2)}) collective-permute-start(bf16[4,4,24,768]{3,2,1,0:T(8,128)(2,1)S(1)} %constant_dynamic-update-slice_fusion.refs_0_), channel_id=1, source_target_pairs={{0,1},{1,0},{2,3},{3,2},{4,5},{5,4},{6,7},{7,6},{8,9},{9,8},{10,11... | collective-permute-start | bytes 1769480 | tf_op jit(solution)/shard_map/ppermute | solution.py:735
  41.0 3.5 collective-permute-start.9
  41.2 3.3 collective-permute-start.10
  44.5 30.9 %copy-start.13 = (bf16[4,4,24,768]{3,2,1,0:T(8,128)(2,1)}, bf16[4,4,24,768]{3,2,1,0:T(8,128)(2,1)S(1)}, u32[]{:S(2)}) copy-start(bf16[4,4,24,768]{3,2,1,0:T(8,128)(2,1)S(1)} %collective-permute-done.6.refs_1_) | copy-start | bytes 1769476
  44.5 30.9 %copy-start.14 = (bf16[4,4,24,768]{3,2,1,0:T(8,128)(2,1)}, bf16[4,4,24,768]{3,2,1,0:T(8,128)(2,1)S(1)}, u32[]{:S(2)}) copy-start(bf16[4,4,24,768]{3,2,1,0:T(8,128)(2,1)S(1)} %collective-permute-done.7.refs_2_) | copy-start | bytes 1769476
  44.5 30.9 %copy-start.16 = (bf16[4,4,24,768]{3,2,1,0:T(8,128)(2,1)}, bf16[4,4,24,768]{3,2,1,0:T(8,128)(2,1)S(1)}, u32[]{:S(2)}) copy-start(bf16[4,4,24,768]{3,2,1,0:T(8,128)(2,1)S(1)} %collective-permute-done.8.refs_5_) | copy-start | bytes 1769476
  44.5 22.7 %collective-permute-start.13 = (bf16[4,4,24,768]{3,2,1,0:T(8,128)(2,1)S(1)}, bf16[4,4,24,768]{3,2,1,0:T(8,128)(2,1)S(1)}, u32[]{:S(2)}, u32[]{:S(2)}) collective-permute-start(bf16[4,4,24,768]{3,2,1,0:T(8,128)(2,1)S(1)} %collective-permute-done.6.refs_1_), channel_id=1, source_target_pairs={{0,1},{1,0},{2,3},{3,2},{4,5},{5,4},{6,7},{7,6},{8,9},{9,8},{10,11... | collective-permute-start | bytes 1769480 | tf_op jit(solution)/shard_map/ppermute | solution.py:735
  54.2 13.0 %collective-permute-start.14 = (bf16[4,4,24,768]{3,2,1,0:T(8,128)(2,1)S(1)}, bf16[4,4,24,768]{3,2,1,0:T(8,128)(2,1)S(1)}, u32[]{:S(2)}, u32[]{:S(2)}) collective-permute-start(bf16[4,4,24,768]{3,2,1,0:T(8,128)(2,1)S(1)} %collective-permute-done.7.refs_2_), channel_id=1, source_target_pairs={{0,1},{1,0},{2,3},{3,2},{4,5},{5,4},{6,7},{7,6},{8,9},{9,8},{10,11... | collective-permute-start | bytes 1769480 | tf_op jit(solution)/shard_map/ppermute | solution.py:735
  55.7 10.0 %collective-permute-start.11 = (bf16[2,4,24,768]{3,2,1,0:T(8,128)(2,1)}, bf16[2,4,24,768]{3,2,1,0:T(8,128)(2,1)}, u32[]{:S(2)}, u32[]{:S(2)}) collective-permute-start(bf16[2,4,24,768]{3,2,1,0:T(8,128)(2,1)} %slice.54), channel_id=1, source_target_pairs={{0,2},{1,3},{2,0},{3,1},{4,6},{5,7},{6,4},{7,5},{8,10},{9,11},{10,... | collective-permute-start | bytes 884744 | tf_op jit(solution)/shard_map/ppermute | solution.py:735
  58.1 9.1 %collective-permute-start.12 = (bf16[2,4,24,768]{3,2,1,0:T(8,128)(2,1)}, bf16[2,4,24,768]{3,2,1,0:T(8,128)(2,1)}, u32[]{:S(2)}, u32[]{:S(2)}) collective-permute-start(bf16[2,4,24,768]{3,2,1,0:T(8,128)(2,1)} %slice.55), channel_id=1, source_target_pairs={{0,4},{1,5},{2,6},{3,7},{4,0},{5,1},{6,2},{7,3},{8,12},{9,13},{10,... | collective-permute-start | bytes 884744 | tf_op jit(solution)/shard_map/ppermute | solution.py:735
  60.2 5.5 %collective-permute-start.15 = (bf16[4,8,256]{2,1,0:T(8,128)(2,1)}, bf16[4,8,256]{2,1,0:T(8,128)(2,1)}, u32[]{:S(2)}, u32[]{:S(2)}) collective-permute-start(bf16[4,8,256]{2,1,0:T(8,128)(2,1)} %collective-permute-done.10), channel_id=1, source_target_pairs={{0,2},{1,3},{2,0},{3,1},{4,6},{5,7},{6,4},{7,5},{8,10},{9,11},{10,... | collective-permute-start | bytes 49160 | tf_op jit(solution)/shard_map/ppermute | solution.py:735
  67.2 8.2 %copy-start.17 = (bf16[4,4,24,768]{3,2,1,0:T(8,128)(2,1)}, bf16[4,4,24,768]{3,2,1,0:T(8,128)(2,1)S(1)}, u32[]{:S(2)}) copy-start(bf16[4,4,24,768]{3,2,1,0:T(8,128)(2,1)S(1)} %collective-permute-done.13.refs_6_) | copy-start | bytes 1769476
  67.2 8.2 %copy-start.18 = (bf16[4,4,24,768]{3,2,1,0:T(8,128)(2,1)}, bf16[4,4,24,768]{3,2,1,0:T(8,128)(2,1)S(1)}, u32[]{:S(2)}) copy-start(bf16[4,4,24,768]{3,2,1,0:T(8,128)(2,1)S(1)} %collective-permute-done.14.refs_7_) | copy-start | bytes 1769476
  67.2 8.1 %collective-permute-start.16 = (bf16[2,4,24,768]{3,2,1,0:T(8,128)(2,1)}, bf16[2,4,24,768]{3,2,1,0:T(8,128)(2,1)}, u32[]{:S(2)}, u32[]{:S(2)}) collective-permute-start(bf16[2,4,24,768]{3,2,1,0:T(8,128)(2,1)} %collective-permute-done.11.refs_3_), channel_id=1, source_target_pairs={{0,1},{1,0},{2,3},{3,2},{4,5},{5,4},{6,7},{7,6},{8,9},{9,8},{10,11... | collective-permute-start | bytes 884744 | tf_op jit(solution)/shard_map/ppermute | solution.py:735
  68.5 6.8 %collective-permute-start.17 = (bf16[2,4,24,768]{3,2,1,0:T(8,128)(2,1)}, bf16[2,4,24,768]{3,2,1,0:T(8,128)(2,1)}, u32[]{:S(2)}, u32[]{:S(2)}) collective-permute-start(bf16[2,4,24,768]{3,2,1,0:T(8,128)(2,1)} %collective-permute-done.12.refs_4_), channel_id=1, source_target_pairs={{0,1},{1,0},{2,3},{3,2},{4,5},{5,4},{6,7},{7,6},{8,9},{9,8},{10,11... | collective-permute-start | bytes 884744 | tf_op jit(solution)/shard_map/ppermute | solution.py:735
  139.4 17.0 %copy-start.8 = (bf16[2,512,768]{2,1,0:T(8,128)(2,1)S(1)}, bf16[2,512,768]{2,1,0:T(8,128)(2,1)}, u32[]{:S(2)}) copy-start(bf16[2,512,768]{2,1,0:T(8,128)(2,1)} %param.17) | copy-start | bytes 4718596
  204.3 11.9 %copy-start.2 = (bf16[512,2304]{1,0:T(8,128)(2,1)S(1)}, bf16[512,2304]{1,0:T(8,128)(2,1)}, u32[]{:S(2)}) copy-start(bf16[512,2304]{1,0:T(8,128)(2,1)} %attention_backward.4.rest_0_) | copy-start | bytes 7077892
  226.6 37.8 %copy-start.11 = (f32[1,768]{1,0:T(1,128)}, f32[1,768]{1,0:T(1,128)S(1)}, u32[]{:S(2)}) copy-start(f32[1,768]{1,0:T(1,128)S(1)} %get-tuple-element.230.rest_2_) | copy-start | bytes 9220
  226.6 37.8 %copy-start.12 = (f32[1,768]{1,0:T(1,128)}, f32[1,768]{1,0:T(1,128)S(1)}, u32[]{:S(2)}) copy-start(f32[1,768]{1,0:T(1,128)S(1)} %get-tuple-element.231.rest_3_) | copy-start | bytes 9220
  264.5 9.9 %collective-permute-start.18 = (bf16[16,192,384]{2,1,0:T(8,128)(2,1)}, bf16[16,192,384]{2,1,0:T(8,128)(2,1)}, u32[]{:S(2)}, u32[]{:S(2)}) collective-permute-start(bf16[16,192,384]{2,1,0:T(8,128)(2,1)} %bitcast.98), channel_id=1, source_target_pairs={{0,1},{1,0},{2,3},{3,2},{4,5},{5,4},{6,7},{7,6},{8,9},{9,8},{10,11... | collective-permute-start | bytes 7077896 | tf_op jit(solution)/shard_map/ppermute | solution.py:735
  264.8 9.6 %collective-permute-start.19 = (bf16[16,192,384]{2,1,0:T(8,128)(2,1)}, bf16[16,192,384]{2,1,0:T(8,128)(2,1)}, u32[]{:S(2)}, u32[]{:S(2)}) collective-permute-start(bf16[16,192,384]{2,1,0:T(8,128)(2,1)} %bitcast.97), channel_id=1, source_target_pairs={{0,1},{1,0},{2,3},{3,2},{4,5},{5,4},{6,7},{7,6},{8,9},{9,8},{10,11... | collective-permute-start | bytes 7077896 | tf_op jit(solution)/shard_map/ppermute | solution.py:735
  265.0 9.3 %collective-permute-start.20 = (bf16[16,48,384]{2,1,0:T(8,128)(2,1)}, bf16[16,48,384]{2,1,0:T(8,128)(2,1)S(1)}, u32[]{:S(2)}, u32[]{:S(2)}) collective-permute-start(bf16[16,48,384]{2,1,0:T(8,128)(2,1)} %get-tuple-element.202), channel_id=1, source_target_pairs={{0,1},{1,0},{2,3},{3,2},{4,5},{5,4},{6,7},{7,6},{8,9},{9,8},{10,11... | collective-permute-start | bytes 1769480 | tf_op jit(solution)/shard_map/ppermute | solution.py:735
  267.1 7.4 %copy-start.6 = (bf16[3072,384]{1,0:T(8,128)(2,1)S(1)}, bf16[3072,384]{1,0:T(8,128)(2,1)}, u32[]{:S(2)}) copy-start(bf16[3072,384]{1,0:T(8,128)(2,1)} %get-tuple-element.198) | copy-start | bytes 7077892
  267.1 7.4 %copy-start.9 = (bf16[16,48,384]{2,1,0:T(8,128)(2,1)S(1)}, bf16[16,48,384]{2,1,0:T(8,128)(2,1)}, u32[]{:S(2)}) copy-start(bf16[16,48,384]{2,1,0:T(8,128)(2,1)} %get-tuple-element.199.refs_2_) | copy-start | bytes 1769476
  278.2 31.2 %collective-permute-start.21 = (bf16[2,2,432,384]{3,2,1,0:T(8,128)(2,1)S(1)}, bf16[2,2,432,384]{3,2,1,0:T(8,128)(2,1)S(1)}, u32[]{:S(2)}, u32[]{:S(2)}) collective-permute-start(bf16[2,2,432,384]{3,2,1,0:T(8,128)(2,1)S(1)} %get-tuple-element.215), channel_id=1, source_target_pairs={{0,2},{1,3},{2,0},{3,1},{4,6},{5,7},{6,4},{7,5},{8,10},{9,11},{10,... | collective-permute-start | bytes 3981320 | tf_op jit(solution)/shard_map/ppermute | solution.py:735
  279.4 30.2 %collective-permute-start.22 = (bf16[2,2,432,384]{3,2,1,0:T(8,128)(2,1)S(1)}, bf16[2,2,432,384]{3,2,1,0:T(8,128)(2,1)S(1)}, u32[]{:S(2)}, u32[]{:S(2)}) collective-permute-start(bf16[2,2,432,384]{3,2,1,0:T(8,128)(2,1)S(1)} %get-tuple-element.216), channel_id=1, source_target_pairs={{0,4},{1,5},{2,6},{3,7},{4,0},{5,1},{6,2},{7,3},{8,12},{9,13},{10,... | collective-permute-start | bytes 3981320 | tf_op jit(solution)/shard_map/ppermute | solution.py:735
  308.6 13.2 %collective-permute-start.25 = (bf16[16,144,384]{2,1,0:T(8,128)(2,1)}, bf16[16,144,384]{2,1,0:T(8,128)(2,1)S(1)}, u32[]{:S(2)}, u32[]{:S(2)}) collective-permute-start(bf16[16,144,384]{2,1,0:T(8,128)(2,1)} %bitcast.99), channel_id=1, source_target_pairs={{0,1},{1,0},{2,3},{3,2},{4,5},{5,4},{6,7},{7,6},{8,9},{9,8},{10,11... | collective-permute-start | bytes 5308424 | tf_op jit(solution)/shard_map/ppermute | solution.py:735
  310.8 15.1 %collective-permute-start.23 = (bf16[2,432,384]{2,1,0:T(8,128)(2,1)S(1)}, bf16[2,432,384]{2,1,0:T(8,128)(2,1)S(1)}, u32[]{:S(2)}, u32[]{:S(2)}) collective-permute-start(bf16[2,432,384]{2,1,0:T(8,128)(2,1)S(1)} %get-tuple-element.233), channel_id=1, source_target_pairs={{0,4},{1,5},{2,6},{3,7},{4,0},{5,1},{6,2},{7,3},{8,12},{9,13},{10,... | collective-permute-start | bytes 1990664 | tf_op jit(solution)/shard_map/ppermute | solution.py:735
  311.8 15.4 %collective-permute-start.24 = (bf16[2,432,384]{2,1,0:T(8,128)(2,1)S(1)}, bf16[2,432,384]{2,1,0:T(8,128)(2,1)S(1)}, u32[]{:S(2)}, u32[]{:S(2)}) collective-permute-start(bf16[2,432,384]{2,1,0:T(8,128)(2,1)S(1)} %get-tuple-element.234), channel_id=1, source_target_pairs={{0,2},{1,3},{2,0},{3,1},{4,6},{5,7},{6,4},{7,5},{8,10},{9,11},{10,... | collective-permute-start | bytes 1990664 | tf_op jit(solution)/shard_map/ppermute | solution.py:735
  321.7 8.3 %copy-start.7 = (bf16[16,3,48,384]{3,2,1,0:T(8,128)(2,1)S(1)}, bf16[16,3,48,384]{3,2,1,0:T(8,128)(2,1)}, u32[]{:S(2)}) copy-start(bf16[16,3,48,384]{3,2,1,0:T(8,128)(2,1)} %get-tuple-element.221) | copy-start | bytes 5308420
  328.8 14.8 %collective-permute-start.27 = (bf16[2,432,384]{2,1,0:T(8,128)(2,1)}, bf16[2,432,384]{2,1,0:T(8,128)(2,1)}, u32[]{:S(2)}, u32[]{:S(2)}) collective-permute-start(bf16[2,432,384]{2,1,0:T(8,128)(2,1)} %get-tuple-element.247), channel_id=1, source_target_pairs={{0,8},{1,9},{2,10},{3,11},{4,12},{5,13},{6,14},{7,15},{8,0},{9,1},... | collective-permute-start | bytes 1990664 | tf_op jit(solution)/shard_map/ppermute | solution.py:735
  331.7 10.8 %collective-permute-start.28 = (bf16[2,2,144,384]{3,2,1,0:T(8,128)(2,1)}, bf16[2,2,144,384]{3,2,1,0:T(8,128)(2,1)S(1)}, u32[]{:S(2)}, u32[]{:S(2)}) collective-permute-start(bf16[2,2,144,384]{3,2,1,0:T(8,128)(2,1)} %get-tuple-element.249), channel_id=1, source_target_pairs={{0,2},{1,3},{2,0},{3,1},{4,6},{5,7},{6,4},{7,5},{8,10},{9,11},{10,... | collective-permute-start | bytes 1327112 | tf_op jit(solution)/shard_map/ppermute | solution.py:735
  332.1 10.4 %collective-permute-start.29 = (bf16[2,2,144,384]{3,2,1,0:T(8,128)(2,1)}, bf16[2,2,144,384]{3,2,1,0:T(8,128)(2,1)S(1)}, u32[]{:S(2)}, u32[]{:S(2)}) collective-permute-start(bf16[2,2,144,384]{3,2,1,0:T(8,128)(2,1)} %get-tuple-element.250), channel_id=1, source_target_pairs={{0,4},{1,5},{2,6},{3,7},{4,0},{5,1},{6,2},{7,3},{8,12},{9,13},{10,... | collective-permute-start | bytes 1327112 | tf_op jit(solution)/shard_map/ppermute | solution.py:735
  333.4 3.7 collective-permute-start.26
  337.1 5.4 %collective-permute-start.30 = (f32[13,768]{1,0:T(8,128)S(1)}, f32[13,768]{1,0:T(8,128)S(1)}, u32[]{:S(2)}, u32[]{:S(2)}) collective-permute-start(f32[13,768]{1,0:T(8,128)S(1)} %add.104), channel_id=1, source_target_pairs={{0,2},{1,3},{2,0},{3,1},{4,6},{5,7},{6,4},{7,5},{8,10},{9,11},{10,... | collective-permute-start | bytes 119816 | tf_op jit(solution)/shard_map/ppermute | solution.py:735
  344.7 16.9 %collective-permute-start.31 = (bf16[432,384]{1,0:T(8,128)(2,1)S(1)}, bf16[432,384]{1,0:T(8,128)(2,1)S(1)}, u32[]{:S(2)}, u32[]{:S(2)}) collective-permute-start(bf16[432,384]{1,0:T(8,128)(2,1)S(1)} %fusion), channel_id=1, source_target_pairs={{0,16},{1,17},{2,18},{3,19},{4,20},{5,21},{6,22},{7,23},{8,24},{9,... | collective-permute-start | bytes 995336 | tf_op jit(solution)/shard_map/ppermute | solution.py:735
  346.9 5.4 %collective-permute-start.32 = (bf16[2,144,384]{2,1,0:T(8,128)(2,1)S(1)}, bf16[2,144,384]{2,1,0:T(8,128)(2,1)S(1)}, u32[]{:S(2)}, u32[]{:S(2)}) collective-permute-start(bf16[2,144,384]{2,1,0:T(8,128)(2,1)S(1)} %get-tuple-element.258), channel_id=1, source_target_pairs={{0,4},{1,5},{2,6},{3,7},{4,0},{5,1},{6,2},{7,3},{8,12},{9,13},{10,... | collective-permute-start | bytes 663560 | tf_op jit(solution)/shard_map/ppermute | solution.py:735
  347.0 5.2 %collective-permute-start.33 = (bf16[2,144,384]{2,1,0:T(8,128)(2,1)S(1)}, bf16[2,144,384]{2,1,0:T(8,128)(2,1)S(1)}, u32[]{:S(2)}, u32[]{:S(2)}) collective-permute-start(bf16[2,144,384]{2,1,0:T(8,128)(2,1)S(1)} %get-tuple-element.259), channel_id=1, source_target_pairs={{0,2},{1,3},{2,0},{3,1},{4,6},{5,7},{6,4},{7,5},{8,10},{9,11},{10,... | collective-permute-start | bytes 663560 | tf_op jit(solution)/shard_map/ppermute | solution.py:735
  348.8 3.4 collective-permute-start.34
  362.6 10.3 %collective-permute-start.35 = (f32[432,384]{1,0:T(8,128)S(1)}, f32[432,384]{1,0:T(8,128)S(1)}, u32[]{:S(2)}, u32[]{:S(2)}) collective-permute-start(f32[432,384]{1,0:T(8,128)S(1)} %bitcast_add_fusion.half_ref), channel_id=1, source_target_pairs={{0,1},{1,0},{2,3},{3,2},{4,5},{5,4},{6,7},{7,6},{8,9},{9,8},{10,11... | collective-permute-start | bytes 1990664 | tf_op jit(solution)/shard_map/ppermute | solution.py:735
  364.1 23.7 %copy-start.1 = (bf16[192,768]{1,0:T(8,128)(2,1)S(1)}, bf16[192,768]{1,0:T(8,128)(2,1)}, u32[]{:S(2)}) copy-start(bf16[192,768]{1,0:T(8,128)(2,1)} %param.28) | copy-start | bytes 884740
  364.8 8.2 %collective-permute-start.36 = (bf16[2,144,384]{2,1,0:T(8,128)(2,1)S(1)}, bf16[2,144,384]{2,1,0:T(8,128)(2,1)S(1)}, u32[]{:S(2)}, u32[]{:S(2)}) collective-permute-start(bf16[2,144,384]{2,1,0:T(8,128)(2,1)S(1)} %get-tuple-element.266), channel_id=1, source_target_pairs={{0,8},{1,9},{2,10},{3,11},{4,12},{5,13},{6,14},{7,15},{8,0},{9,1},... | collective-permute-start | bytes 663560 | tf_op jit(solution)/shard_map/ppermute | solution.py:735
  364.9 8.1 %collective-permute-start.37 = (f32[13,768]{1,0:T(8,128)S(1)}, f32[13,768]{1,0:T(8,128)S(1)}, u32[]{:S(2)}, u32[]{:S(2)}) collective-permute-start(f32[13,768]{1,0:T(8,128)S(1)} %add.107), channel_id=1, source_target_pairs={{0,8},{1,9},{2,10},{3,11},{4,12},{5,13},{6,14},{7,15},{8,0},{9,1},... | collective-permute-start | bytes 119816 | tf_op jit(solution)/shard_map/ppermute | solution.py:735
  373.0 10.3 %collective-permute-start.38 = (bf16[144,384]{1,0:T(8,128)(2,1)S(1)}, bf16[144,384]{1,0:T(8,128)(2,1)S(1)}, u32[]{:S(2)}, u32[]{:S(2)}) collective-permute-start(bf16[144,384]{1,0:T(8,128)(2,1)S(1)} %fusion.1), channel_id=1, source_target_pairs={{0,16},{1,17},{2,18},{3,19},{4,20},{5,21},{6,22},{7,23},{8,24},{9,... | collective-permute-start | bytes 331784 | tf_op jit(solution)/shard_map/ppermute | solution.py:735
  373.3 10.0 %collective-permute-start.39 = (f32[13,768]{1,0:T(8,128)S(1)}, f32[13,768]{1,0:T(8,128)S(1)}, u32[]{:S(2)}, u32[]{:S(2)}) collective-permute-start(f32[13,768]{1,0:T(8,128)S(1)} %add.111), channel_id=1, source_target_pairs={{0,16},{1,17},{2,18},{3,19},{4,20},{5,21},{6,22},{7,23},{8,24},{9,... | collective-permute-start | bytes 119816 | tf_op jit(solution)/shard_map/ppermute | solution.py:735
  383.4 3.6 collective-permute-start.40
  (13 other events, 50.1 us)
Sparse Core Ops, SparseCore 0:
  11.0 90.6 all-gather.2

commit v3 on v2

--- a/solution.py
+++ b/solution.py
@@ -238,9 +238,8 @@
 
 
 def mlp_forward_kernel(
-    last, hidden_ref, normed_ref, fc_ref, fbias_ref, proj_ref, pbias_ref, expanded_ref, *rest
+    hidden_ref, normed_ref, fc_ref, fbias_ref, proj_ref, pbias_ref, expanded_ref, state_ref
 ):
-    final_ref, state_ref = rest if last else (None, rest[0])
     step = pl.program_id(0)
     chunk = 256
 
@@ -256,12 +255,6 @@
         activated = (expanded * gate).astype(jnp.bfloat16)
         state_ref[rows, :] += dot(activated, square_of(proj_ref))
 
-    if last:
-
-        @pl.when(step == pl.num_programs(0) - 1)
-        def _():
-            final_ref[...] = state_ref[...].astype(jnp.bfloat16)
-
 
 DEVICE_GROUPS = 16
 
@@ -270,25 +263,29 @@
     return ref[...].reshape(FEATURES, FEATURES)
 
 
-FC_BLOCK = pl.BlockSpec((16, 1, 1, 48, FEATURES), lambda i: (0, i // 2, i % 2, 0, 0))
-PROJ_BLOCK = pl.BlockSpec((4, 2, 2, 48, FEATURES), lambda i: (i, 0, 1, 0, 0))
-
-
-def mlp_forward(hidden, normed, mlp, fbias, pbias, last):
+def fc_at(step):
+    return jnp.minimum(step, 3)
+
+
+FC_BLOCK = pl.BlockSpec((16, 1, 1, 48, FEATURES), lambda i: (0, fc_at(i) // 2, fc_at(i) % 2, 0, 0))
+PROJ_BLOCK = pl.BlockSpec((4, 2, 2, 48, FEATURES), lambda i: (fc_at(i), 0, 1, 0, 0))
+
+
+def mlp_forward(hidden, normed, mlp, fbias, pbias):
     rows, width = hidden.shape
     block = width
     hidden_units = 4 * block
     shape = pltpu.HBM
     outs = (
         shape((rows, hidden_units), jnp.bfloat16),
-        shape((rows, width), jnp.bfloat16 if last else jnp.float32),
+        shape((rows, width), jnp.float32),
     )
     specs = (
         pl.BlockSpec((rows, block), lambda i: (0, i)),
         pl.BlockSpec((rows, width), lambda i: (0, 0)),
     )
     return pl.pallas_call(
-        functools.partial(mlp_forward_kernel, last),
+        mlp_forward_kernel,
         grid=(hidden_units // block,),
         out_shape=outs,
         in_specs=[
@@ -300,7 +297,6 @@
             whole(pbias),
         ],
         out_specs=specs,
-        scratch_shapes=[pltpu.VMEM((rows, width), jnp.float32)] if last else [],
         compiler_params=params(),
         cost_estimate=cost(
             4 * rows * width * hidden_units, rows * hidden_units, hidden, normed, mlp, *outs
@@ -337,20 +333,23 @@
 
 def mlp_backward_kernel(
     more,
+    forward,
     core_ref,
     grad_ref,
     hidden_ref,
     normed_ref,
     att_ref,
-    expanded_ref,
-    fc_ref,
-    proj_ref,
-    gain_ref,
     *rest,
 ):
+    if forward:
+        fbias_ref, pbias_ref, fc_ref, proj_ref, gain_ref, *rest = rest
+    else:
+        expanded_ref, fc_ref, proj_ref, gain_ref, *rest = rest
     earlier = rest[:11] if more else (None,) * 11
     if more:
         rest = rest[11:]
+    if forward:
+        final_ref, *rest, state_ref = rest
     (
         dhid_ref,
         fc_mine,
@@ -369,61 +368,99 @@
         acc_ref,
         act_ref,
         ge_ref,
+        hidden_buf,
+        att_buf,
+        sems,
     ) = rest
     step = pl.program_id(0)
     core = core_ref[0]
     rows = grad_ref.shape[0]
+    blocks = pl.num_programs(0) - 1
     chunk = 256
+    chunks = [slice(start, start + chunk) for start in range(0, rows, chunk)]
+    late = [
+        pltpu.make_async_copy(hidden_ref, hidden_buf, sems.at[0]),
+        pltpu.make_async_copy(att_ref, att_buf, sems.at[1]),
+    ]
 
     @pl.when(step == 0)
     def _():
+        for copy in late:
+            copy.start()
         low_grad = grad_ref[...].astype(jnp.bfloat16)
         low_ref[...] = low_grad
         dpbias = jnp.sum(low_grad.astype(jnp.float32), axis=0, keepdims=True)
         dpbias_ref[...] = dpbias + earlier[8][...] if more else dpbias
         normed_t[...] = jnp.transpose(normed_ref[...])
         acc_ref[...] = jnp.zeros_like(acc_ref)
-
-    bias_sum = jnp.zeros(dfbias_ref.shape[1:], jnp.float32)
-    for start in range(0, rows, chunk):
-        part = slice(start, start + chunk)
-        grad_act = dot_transposed(low_ref[part, :], square_of(proj_ref))
-        value = expanded_ref[part, :].astype(jnp.float32)
-        gate, square = gelu_gate(value)
-        act = value * gate
-        slope = gate + act * (1.0 - gate) * (2 * GELU_C + 6 * GELU_K * square)
-        act_ref[part, :] = act.astype(jnp.bfloat16)
-        grad_exp = (grad_act * slope).astype(jnp.bfloat16)
-        ge_ref[part, :] = grad_exp
-        bias_sum = bias_sum + jnp.sum(grad_exp.astype(jnp.float32), axis=0, keepdims=True)
-        acc_ref[part, :] += dot_transposed(grad_exp, square_of(fc_ref))
-    dfbias_ref[0] = bias_sum + earlier[7][0] if more else bias_sum
-    dproj = transposed_dot(act_ref[...], low_ref[...])
-    store_halves(core, dproj, proj_mine, proj_theirs, earlier[2:4] if more else None)
-    dfc = dot(normed_t[...], ge_ref[...])
-    store_halves(core, dfc, fc_mine, fc_theirs, earlier[:2] if more else None)
-
-    @pl.when(step == pl.num_programs(0) - 1)
+        if forward:
+            state_ref[...] = jnp.zeros_like(state_ref)
+
+    @pl.when(step < blocks)
     def _():
-        normed, scale = norm_parts(hidden_ref[...])
-        grad_norm = acc_ref[...]
-        dgain = jnp.sum(grad_norm * normed, axis=0, keepdims=True)
-        dshift = jnp.sum(grad_norm, axis=0, keepdims=True)
+        bias_sum = jnp.zeros(dfbias_ref.shape[1:], jnp.float32)
+        for part in chunks:
+            grad_act = dot_transposed(low_ref[part, :], square_of(proj_ref))
+            if forward:
+                value = dot(normed_ref[part, :], square_of(fc_ref)) + fbias_ref[...]
+            else:
+                value = expanded_ref[part, :].astype(jnp.float32)
+            gate, square = gelu_gate(value)
+            act = value * gate
+            slope = gate + act * (1.0 - gate) * (2 * GELU_C + 6 * GELU_K * square)
+            activated = act.astype(jnp.bfloat16)
+            act_ref[part, :] = activated
+            if forward:
+                state_ref[part, :] += dot(activated, square_of(proj_ref))
+            grad_exp = (grad_act * slope).astype(jnp.bfloat16)
+            ge_ref[part, :] = grad_exp
+            bias_sum = bias_sum + jnp.sum(grad_exp.astype(jnp.float32), axis=0, keepdims=True)
+            acc_ref[part, :] += dot_transposed(grad_exp, square_of(fc_ref))
+        dfbias_ref[0] = bias_sum + earlier[7][0] if more else bias_sum
+        dproj = transposed_dot(act_ref[...], low_ref[...])
+        store_halves(core, dproj, proj_mine, proj_theirs, earlier[2:4] if more else None)
+        dfc = dot(normed_t[...], ge_ref[...])
+        store_halves(core, dfc, fc_mine, fc_theirs, earlier[:2] if more else None)
+
+    @pl.when(step == blocks)
+    def _():
+        for copy in late:
+            copy.wait()
+        dgain = jnp.zeros(dgain_ref.shape, jnp.float32)
+        dshift, dobias = (dgain, dgain)
+        copies = []
+        for index, part in enumerate(chunks):
+            hidden = hidden_buf[part, :]
+            if forward:
+                final = hidden + (state_ref[part, :] + pbias_ref[...])
+                final_ref[part, :] = final.astype(jnp.bfloat16)
+            normed, scale = norm_parts(hidden)
+            grad_norm = acc_ref[part, :]
+            dgain = dgain + jnp.sum(grad_norm * normed, axis=0, keepdims=True)
+            dshift = dshift + jnp.sum(grad_norm, axis=0, keepdims=True)
+            dhid = grad_ref[part, :].astype(jnp.float32) + norm_back(
+                normed, scale, gain_ref[...], grad_norm
+            )
+            hidden_buf[part, :] = dhid
+            copies.append(
+                pltpu.make_async_copy(
+                    hidden_buf.at[part, :], dhid_ref.at[part, :], sems.at[2 + index]
+                )
+            )
+            copies[-1].start()
+            low_dhid = dhid.astype(jnp.bfloat16)
+            low_ref[part, :] = low_dhid
+            dobias = dobias + jnp.sum(low_dhid.astype(jnp.float32), axis=0, keepdims=True)
         dgain_ref[...] = dgain + earlier[9][...] if more else dgain
         dshift_ref[...] = dshift + earlier[10][...] if more else dshift
-        dhid = grad_ref[...].astype(jnp.float32) + norm_back(
-            normed, scale, gain_ref[...], grad_norm
-        )
-        dhid_ref[...] = dhid
-        low_dhid = dhid.astype(jnp.bfloat16)
-        low_ref[...] = low_dhid
-        dobias = jnp.sum(low_dhid.astype(jnp.float32), axis=0, keepdims=True)
         dobias_ref[...] = dobias + earlier[6][...] if more else dobias
-        dout = transposed_dot(att_ref[...], low_ref[...])
+        dout = transposed_dot(att_buf[...], low_ref[...])
         store_halves(core, dout, out_mine, out_theirs, earlier[4:6] if more else None)
-
-
-def mlp_backward(core, grad, hidden, normed, att, expanded, mlp, gain, earlier=None):
+        for copy in copies:
+            copy.wait()
+
+
+def mlp_backward(core, grad, hidden, normed, att, expanded, mlp, gain, earlier=None, biases=None):
     rows, width = hidden.shape
     blocks, block = (4, width)
     shape = pltpu.HBM
@@ -447,44 +484,80 @@
         row,
         row,
     )
-    fc_spec = pl.BlockSpec((groups, None, each, width // 2), lambda i: (0, i, 0, 0))
-    proj_spec = pl.BlockSpec((width, width // 2), lambda i: (i, 0))
+    fc_spec = pl.BlockSpec((groups, None, each, width // 2), lambda i: (0, jnp.minimum(i, 3), 0, 0))
+    proj_spec = pl.BlockSpec((width, width // 2), lambda i: (jnp.minimum(i, 3), 0))
     out_spec = pl.BlockSpec((groups, each, width // 2), lambda i: (0, 0, 0))
-    bias = pl.BlockSpec((1, 1, block), lambda i: (i, 0, 0))
+    bias = pl.BlockSpec((1, 1, block), lambda i: (jnp.minimum(i, 3), 0, 0))
     vector = pl.BlockSpec((1, width), lambda i: (0, 0))
-    inputs = [grad, hidden, normed, att, expanded, mlp, mlp, gain]
-    specs = [
-        whole(grad),
-        whole(hidden),
-        whole(normed),
-        whole(att),
-        pl.BlockSpec((rows, block), lambda i: (0, i)),
-        FC_BLOCK,
-        PROJ_BLOCK,
-        whole(gain),
-    ]
+    inputs = [grad, hidden, normed, att]
+    raw = pl.BlockSpec(memory_space=pltpu.HBM)
+    specs = [whole(grad), raw, whole(normed), raw]
+    out_specs = [raw]
+    scratch = []
+    if biases is None:
+        inputs.append(expanded)
+        specs.append(pl.BlockSpec((rows, block), lambda i: (0, jnp.minimum(i, 3))))
+    else:
+        inputs += list(biases)
+        specs += [pl.BlockSpec((1, block), lambda i: (0, jnp.minimum(i, 3))), whole(biases[1])]
+        outs = (shape((rows, width), jnp.bfloat16), *outs)
+        out_specs = [pl.BlockSpec((rows, width), lambda i: (0, 0)), raw]
+        scratch = [pltpu.VMEM((rows, width), jnp.float32)]
+    inputs += [mlp, mlp, gain]
+    specs += [FC_BLOCK, PROJ_BLOCK, whole(gain)]
     summed = [fc_spec, fc_spec, proj_spec, proj_spec, out_spec, out_spec, vector, bias]
     summed += [vector, vector, vector]
     if earlier is not None:
         inputs += list(earlier)
         specs += summed
     return pl.pallas_call(
-        functools.partial(mlp_backward_kernel, earlier is not None),
-        grid=(blocks,),
+        functools.partial(mlp_backward_kernel, earlier is not None, biases is not None),
+        grid=(blocks + 1,),
         out_shape=outs,
         in_specs=[SMEM] + specs,
-        out_specs=[pl.BlockSpec((rows, width), lambda i: (0, 0))] + summed,
+        out_specs=out_specs + summed,
         scratch_shapes=[
             pltpu.VMEM((rows, width), jnp.bfloat16),
             pltpu.VMEM((width, rows), jnp.bfloat16),
             pltpu.VMEM((rows, width), jnp.float32),
             pltpu.VMEM((rows, block), jnp.bfloat16),
             pltpu.VMEM((rows, block), jnp.bfloat16),
+            pltpu.VMEM((rows, width), jnp.float32),
+            pltpu.VMEM((rows, width), jnp.bfloat16),
+            pltpu.SemaphoreType.DMA((2 + rows // 256,)),
+            *scratch,
         ],
-        compiler_params=params(50 << 20),
+        compiler_params=params(54 << 20),
         cost_estimate=cost(8 * rows * width * blocks * block, rows * blocks * block, *inputs, *outs),
         name="mlp_backward",
     )(core, grad, *in_hbm(inputs[1:]))
+
+
+def input_gradient(
+    dhid_ref, state_ref, gmix_ref, weight_ref, gain_ref, earlier, grad_ref, dgain_ref, dshift_ref
+):
+    step = pl.program_id(0)
+    grad_norm = dot_transposed(gmix_ref[:, :FEATURES], weight_ref[0])
+    for part in range(1, 3):
+        grad_norm = grad_norm + dot_transposed(
+            gmix_ref[:, part * FEATURES : (part + 1) * FEATURES], weight_ref[part]
+        )
+    normed, scale = norm_parts(state_ref[...].astype(jnp.float32))
+    dgain = jnp.sum(grad_norm * normed, axis=0, keepdims=True)
+    dshift = jnp.sum(grad_norm, axis=0, keepdims=True)
+
+    @pl.when(step == 0)
+    def _():
+        dgain_ref[...] = dgain if earlier is None else dgain + earlier[0][...]
+        dshift_ref[...] = dshift if earlier is None else dshift + earlier[1][...]
+
+    @pl.when(step > 0)
+    def _():
+        dgain_ref[...] += dgain
+        dshift_ref[...] += dshift
+
+    grad = dhid_ref[...] + norm_back(normed, scale, gain_ref[...], grad_norm)
+    grad_ref[...] = grad.astype(grad_ref.dtype)
 
 
 def attention_backward_kernel(
@@ -497,15 +570,22 @@
     mixed_ref,
     lse_ref,
     out_ref,
-    gmix_ref,
-    datt_ref,
-    bias_ref,
-    delta_ref,
-    dq_ref,
+    *rest,
 ):
+    if micro is None:
+        micro = pl.program_id(0)
+        state_ref, gain_ref, gmix_ref, grad_ref, dgain_ref, dshift_ref, *rest = rest
+        finish = functools.partial(
+            input_gradient, dhid_ref, state_ref, gmix_ref, out_ref, gain_ref, None,
+            grad_ref, dgain_ref, dshift_ref,
+        )
+    else:
+        gmix_ref, *rest = rest
+        finish = None
+    datt_ref, bias_ref, delta_ref, dq_ref = rest
     count = dhid_ref.shape[0]
     low_grad = dhid_ref[...].astype(jnp.bfloat16)
-    datt = dot_transposed(low_grad, out_ref[0]).astype(jnp.bfloat16)
+    datt = dot_transposed(low_grad, out_ref[out_ref.shape[0] - 1]).astype(jnp.bfloat16)
     datt_ref[...] = datt
     product = datt.astype(jnp.float32) * att_ref[...].astype(jnp.float32)
     high = product.astype(jnp.bfloat16)
@@ -551,12 +631,14 @@
         return carry
 
     lax.fori_loop(0, H // GROUP, one_group, 0, unroll=H // GROUP)
-
-
-def attention_backward(micro, lengths, dhid, count, back, att, mixed, lse, weight, shape):
+    if finish is not None:
+        finish()
+
+
+def attention_backward(micro, lengths, dhid, count, back, att, mixed, lse, weight):
     width = dhid.shape[1]
     docs = lengths.shape[1]
-    outs = shape((count, 3 * width), jnp.bfloat16)
+    outs = jax.ShapeDtypeStruct((count, 3 * width), jnp.bfloat16)
     inputs = [dhid, att, mixed, lse, weight]
     return pl.pallas_call(
         functools.partial(attention_backward_kernel, docs, back, micro),
@@ -582,6 +664,46 @@
             2 * count * width * width + 10 * count * count * width, count * count * H, outs, outs
         ),
         name="attention_backward",
+    )(lengths, *in_hbm(inputs))
+
+
+def attention_backward_all(lengths, dhid, count, back, att, mixed, lse, weight, state, gain):
+    rows, width = dhid.shape
+    micro, docs = lengths.shape
+    vector = pl.BlockSpec((1, width), lambda i: (0, 0))
+    outs = (
+        pltpu.HBM((rows, 3 * width), jnp.bfloat16),
+        jax.ShapeDtypeStruct((rows, width), jnp.float32),
+        jax.ShapeDtypeStruct((1, width), jnp.float32),
+        jax.ShapeDtypeStruct((1, width), jnp.float32),
+    )
+    inputs = [dhid, att, mixed, lse, weight, state, gain]
+    return pl.pallas_call(
+        functools.partial(attention_backward_kernel, docs, back, None),
+        grid=(micro,),
+        out_shape=outs,
+        in_specs=[
+            SMEM,
+            rows_of(count, width),
+            rows_of(count, width),
+            rows_of(count, 3 * width),
+            pl.BlockSpec((H, 1, count), lambda i: (i, 0, 0)),
+            whole(weight),
+            rows_of(count, width),
+            whole(gain),
+        ],
+        out_specs=[rows_of(count, 3 * width), rows_of(count, width), vector, vector],
+        scratch_shapes=[
+            pltpu.VMEM((count, width), jnp.bfloat16),
+            pltpu.VMEM((count, count), jnp.float32),
+            pltpu.VMEM((H, 1, count), jnp.float32),
+            pltpu.VMEM((count, LANES), jnp.float32),
+        ],
+        compiler_params=params(44 << 20),
+        cost_estimate=cost(
+            8 * rows * width * width + 10 * rows * count * width, rows * count * H, *inputs, *outs
+        ),
+        name="attention_backward_all",
     )(lengths, *in_hbm(inputs))
 
 
@@ -637,35 +759,16 @@
     if more:
         rest = rest[2:]
     grad_ref, dgain_ref, dshift_ref, gmix_ref = rest
-    step = pl.program_id(0)
     each = pl.num_programs(0) // micro
     for index, part_ref in enumerate(gmix_refs):
 
-        @pl.when(step // each == index)
+        @pl.when(pl.program_id(0) // each == index)
         def _(part_ref=part_ref):
             gmix_ref[...] = part_ref[...]
 
-    grad_norm = dot_transposed(gmix_ref[:, :FEATURES], weight_ref[0])
-    for part in range(1, 3):
-        grad_norm = grad_norm + dot_transposed(
-            gmix_ref[:, part * FEATURES : (part + 1) * FEATURES], weight_ref[part]
-        )
-    normed, scale = norm_parts(state_ref[...].astype(jnp.float32))
-    dgain = jnp.sum(grad_norm * normed, axis=0, keepdims=True)
-    dshift = jnp.sum(grad_norm, axis=0, keepdims=True)
-
-    @pl.when(step == 0)
-    def _():
-        dgain_ref[...] = dgain + earlier[0][...] if more else dgain
-        dshift_ref[...] = dshift + earlier[1][...] if more else dshift
-
-    @pl.when(step > 0)
-    def _():
-        dgain_ref[...] += dgain
-        dshift_ref[...] += dshift
-
-    grad = dhid_ref[...] + norm_back(normed, scale, gain_ref[...], grad_norm)
-    grad_ref[...] = grad.astype(grad_ref.dtype)
+    input_gradient(
+        dhid_ref, state_ref, gmix_ref, weight_ref, gain_ref, earlier, grad_ref, dgain_ref, dshift_ref
+    )
 
 
 def attention_input(dhid, state, gmix, weight, gain, kind, earlier=None, chunk=256):
@@ -704,7 +807,8 @@
     )(*in_hbm(inputs[:4]), *gmix, *in_hbm(inputs[4 + len(gmix) :]))
 
 
-def place_small_kernel(sizes, me_ref, small_ref, *outs):
+def place_small_kernel(sizes, me_ref, *refs):
+    smalls, outs = (refs[:4], refs[4:])
     dp = me_ref[0] // 2
     slot = lax.broadcasted_iota(jnp.int32, (16, 1), 0)
     owner = ((slot % 4) * 4 + (slot // 8) * 2 + slot // 4 % 2) ^ dp
@@ -713,7 +817,7 @@
         lane = lax.broadcasted_iota(jnp.int32, (256, width), 0)
         column = lax.broadcasted_iota(jnp.int32, (256, width), 1)
         spread = (column % size == lane).astype(jnp.bfloat16)
-        rows = jnp.concatenate([small_ref[d, index : index + 1] for d in range(16)], axis=0)
+        rows = jnp.concatenate([ref[z, index : index + 1] for ref in smalls for z in range(4)], axis=0)
         spread_rows = dot(rows, spread)
         column = lax.broadcasted_iota(jnp.int32, (1, width), 1)
         out_ref[...] = jnp.sum(
@@ -721,14 +825,14 @@
         )
 
 
-def place_small(me, small, sizes):
+def place_small(me, smalls, sizes):
     return pl.pallas_call(
         functools.partial(place_small_kernel, sizes),
         out_shape=[jax.ShapeDtypeStruct((1, 16 * size), jnp.float32) for size in sizes],
-        in_specs=[SMEM, pl.BlockSpec(memory_space=pltpu.VMEM)],
+        in_specs=[SMEM] + [pl.BlockSpec(memory_space=pltpu.VMEM)] * len(smalls),
         out_specs=[pl.BlockSpec(memory_space=pltpu.VMEM)] * len(sizes),
         name="place_small",
-    )(me, small)
+    )(me, *smalls)
 
 
 def swap(value, bits):
@@ -792,7 +896,7 @@
     slots = [base] + [tuple(rel ^ bits for rel in base) for bits in (X, Y)]
     slots += [(X ^ Y, X ^ Y ^ Z1), (X ^ Y ^ Z2, X ^ Y ^ Z3)]
     slots += [tuple(rel ^ CORE for rel in rels) for rels in slots]
-    return (place(me, parts, slots), jnp.concatenate([small, small_x, small_y, small_xy]))
+    return (place(me, parts, slots), (small, small_x, small_y, small_xy))
 
 
 def pick(array, axis, index):
@@ -859,12 +963,12 @@
             out[low_z] = total(kept[low_z, index], got[low_z, index]).astype(jnp.bfloat16)
 
 
-def third_sums_kernel(spot_ref, near, far, near_in, far_in, sent, kept):
+def third_sums_kernel(spot_ref, near, far, near_in, far_in, first, second, third, kept):
     low_z = spot_ref[1]
-    sent[0] = total(near[1 - low_z], near_in[1 - low_z]).astype(jnp.bfloat16)
-    sent[1] = total(far[1 - low_z], far_in[1 - low_z]).astype(jnp.bfloat16)
-    kept[0] = total(near[low_z], near_in[low_z])
-    kept[1] = total(far[low_z], far_in[low_z])
+    first[...] = total(near[1 - low_z], near_in[1 - low_z]).astype(jnp.bfloat16)
+    second[...] = total(far[low_z], far_in[low_z]).astype(jnp.bfloat16)
+    third[...] = total(far[1 - low_z], far_in[1 - low_z]).astype(jnp.bfloat16)
+    kept[...] = total(near[low_z], near_in[low_z])
 
 
 def assemble_kernel(layouts, core_ref, half_ref, other_ref, *outs):
@@ -882,6 +986,19 @@
             start += rows
 
 
+def pack_rows_kernel(unused_ref, *refs):
+    *parts, out = refs
+    start = 0
+    for part in parts:
+        if len(part.shape) == 2:
+            out[start : start + 1] = part[...]
+            start += 1
+        else:
+            for index in range(part.shape[0]):
+                out[start : start + 1] = part[index]
+                start += 1
+
+
 def in_vmem(kernel, name, outs, *args):
     vmem = pl.BlockSpec(memory_space=pltpu.VMEM)
     return pl.pallas_call(
@@ -926,25 +1043,20 @@
         return self.kept
 
     def third(self):
-        sent, kept = in_vmem(
+        *sent, kept = in_vmem(
             third_sums_kernel,
             "third_sums",
-            [self.like(2), self.like(2, kind=jnp.float32)],
+            [self.like()] * 3 + [self.like(kind=jnp.float32)],
             self.spot,
             *self.kept,
             *self.got,
         )
-        self.kept, self.got = ([kept], [swap(sent, Z1)])
+        self.kept = [kept]
+        self.got = [swap(part, bits) for part, bits in zip(sent, (Z1, Z2, Z3))]
         return self.kept
 
     def fourth(self):
-        (kept,), (got,) = (self.kept, self.got)
-        far = low(kept[1] + wide(got[1]))
-        self.kept, self.got = ([kept, got], [swap(far, Z2)])
-
-    def fifth(self):
-        (kept, got), (far,) = (self.kept, self.got)
-        half = kept[0] + wide(got[0]) + wide(far)
+        half = total(*self.kept, *self.got)
         self.kept, self.got = ([half], [swap(half, CORE)])
 
     def whole(self, core, layouts):
@@ -982,8 +1094,8 @@
     vectors = [gain_a, shift_a, qbias, obias, gain_m, shift_m, fbias, pbias]
     sizes = tuple(vector.shape[0] for vector in vectors)
     small = jnp.stack([jnp.pad(v, (0, 256 - size)) for v, size in zip(vectors, sizes)])
-    first, small = gather_first(jnp.concatenate([half(qkv), half(out)])[None], small[None], me)
-    return (first, mlp, *place_small(me, small, sizes))
+    first, smalls = gather_first(jnp.concatenate([half(qkv), half(out)])[None], small[None], me)
+    return (first, mlp, *place_small(me, smalls, sizes))
 
 
 def gather_plain(weights):
@@ -1029,10 +1141,12 @@
         normed_a, mixed, att, lse, hidden, normed_m = attention_forward(
             lengths, state, count, back, gain_a, shift_a, weight, qbias, obias, gain_m, shift_m
         )
-        expanded, after_mlp = mlp_forward(hidden, normed_m, mlp, fbias, pbias, use == USES - 1)
+        expanded, after_mlp = (None, None)
+        if use < USES - 1:
+            expanded, after_mlp = mlp_forward(hidden, normed_m, mlp, fbias, pbias)
         kept.append((state, normed_a, mixed, att, lse, hidden, normed_m, expanded))
         state = after_mlp
-    return (state, kept)
+    return kept
 
 
 def shards(custom, tokens, doc_lengths, cotangent, *weights):
@@ -1045,17 +1159,19 @@
     back = -(-(LONGEST - 1) // BLOCK)
     lengths = doc_lengths.reshape(micro, doc_lengths.shape[-1])
     whole_ones = gather_all(weights, spot, me) if custom else gather_plain(weights)
-    state, kept = forward(
-        tokens.reshape(micro * count, width), lengths, count, back, whole_ones
-    )
+    kept = forward(tokens.reshape(micro * count, width), lengths, count, back, whole_ones)
     weight, mlp, gain_a, gain_m = (whole_ones[0], whole_ones[1], whole_ones[2], whole_ones[6])
     grad, mlp_terms, terms, norm = (cotangent.reshape(micro * count, width), None, None, None)
     delayed = None
     for use in range(USES - 1, -1, -1):
         before, normed_a, mixed, att, lse, hidden, normed_m, expanded = kept[use]
+        last = use == USES - 1
         dhid, *mlp_terms = mlp_backward(
-            side, grad, hidden, normed_m, att, expanded, mlp, gain_m, mlp_terms
-        )
+            side, grad, hidden, normed_m, att, expanded, mlp, gain_m, mlp_terms,
+            whole_ones[-2:] if last else None,
+        )
+        if last:
+            state, (dhid, *mlp_terms) = (dhid, mlp_terms)
         sending = custom and use == 0
         if delayed is not None:
             terms = delayed()
@@ -1068,25 +1184,24 @@
             )
             sums.got, terms = lax.optimization_barrier((sums.got, terms))
             dhid = after(dhid, sums.first())
+        if use:
+            gmix, grad, *norm = attention_backward_all(
+                lengths, dhid, count, back, att, mixed, lse, weight, before, gain_a
+            )
+            delayed = functools.partial(attention_terms, side, normed_a, [gmix])
+            continue
         gmix = [
-            attention_backward(
-                index, lengths, dhid, count, back, att, mixed, lse, weight,
-                pltpu.HBM if use else jax.ShapeDtypeStruct,
-            )
+            attention_backward(index, lengths, dhid, count, back, att, mixed, lse, weight)
             for index in range(micro)
         ]
-        if use:
-            delayed = functools.partial(attention_terms, side, normed_a, gmix)
-        else:
-            terms = attention_terms(side, normed_a, gmix, terms)
+        terms = attention_terms(side, normed_a, gmix, terms)
         if sending:
             qkv_sums = Reduction(
                 places, *[(part.reshape(16, -1, part.shape[-1]),) for part in terms[:2]]
             )
             sums.got, terms = lax.optimization_barrier((sums.got, terms))
             gmix = after(gmix, sums.second())
-        kind = jnp.float32 if use else jnp.bfloat16
-        grad, *norm = attention_input(dhid, before, gmix, weight, gain_a, kind, norm)
+        grad, *norm = attention_input(dhid, before, gmix, weight, gain_a, jnp.bfloat16, norm)
         if sending:
             sums.got, qkv_sums.got, norm = lax.optimization_barrier(
                 (sums.got, qkv_sums.got, norm)
@@ -1094,30 +1209,27 @@
     small = (norm[0], norm[1], terms[2], mlp_terms[6], mlp_terms[9], mlp_terms[10])
     small += (mlp_terms[7], mlp_terms[8])
     if custom:
-        small = jnp.concatenate([part.reshape(-1, width) for part in small])
+        (small,) = in_vmem(
+            pack_rows_kernel, "pack_rows", [jax.ShapeDtypeStruct((13, width), jnp.float32)], side, *small
+        )
         qkv_sums.first()
         sums.third()
         small = small + swap(small, CORE)
         got = swap(small, X)
-        sums.got, qkv_sums.got, got = lax.optimization_barrier((sums.got, qkv_sums.got, got))
+        qkv_sums.got, got = lax.optimization_barrier((qkv_sums.got, got))
         qkv_sums.second()
-        sums.fourth()
         small = small + got
         got = swap(small, Y)
-        sums.got, qkv_sums.got, got = lax.optimization_barrier((sums.got, qkv_sums.got, got))
+        qkv_sums.got, got = lax.optimization_barrier((qkv_sums.got, got))
         qkv_sums.third()
-        sums.fifth()
         small = small + got
-        got = swap(small, Z1)
-        sums.got, qkv_sums.got, got = lax.optimization_barrier((sums.got, qkv_sums.got, got))
+        got = [swap(small, bits) for bits in (Z1, Z2, Z3)]
+        sums.fourth()
+        qkv_sums.got, got = lax.optimization_barrier((qkv_sums.got, got))
         qkv_sums.fourth()
-        small = small + got
-        got = swap(small, Z2)
-        qkv_sums.got, got = lax.optimization_barrier((qkv_sums.got, got))
-        qkv_sums.fifth()
         fc, proj, out = sums.whole(side, ((4, 48), (1, 192), (1, 48)))
         (qkv,) = qkv_sums.whole(side, ((3, 48),))
-        small = own_small(small + got, dp)
+        small = own_small(total(small, *got), dp)
         gain_a, shift_a, qbias, obias, gain_m, shift_m, fbias, pbias = small
         final = (
             gain_a, shift_a, qkv, qbias, out, obias, gain_m, shift_m, fc, fbias, proj, pbias

time: 399 us -> 383 us (0.960)
  starting transfers between devices: 54 us -> 72.3 us
  Pallas kernels: 246 us -> 230 us
  waiting for transfers between devices: 60.3 us -> 49.2 us
  local copies, waits for them, and re-layouts: 17.4 us -> 11.3 us
    pallas_call x4 -> x2, Pallas kernels: 44.7 us -> 21 us  [attention_backward(): pl.pallas_call(functools.partial(attention_backward_kernel, docs, back, m...]
    ppermute x41 -> x44, waiting for transfers between devices: 58.7 us -> 40 us  [swap(): return lax.ppermute(value, BOTH, [(i, i ^ bits) for i in range(32)])]
    ppermute x41 -> x44, starting transfers between devices: 53.9 us -> 72.3 us  [swap(): return lax.ppermute(value, BOTH, [(i, i ^ bits) for i in range(32)])]
    pallas_call x2, Pallas kernels: 33.9 us -> 44.3 us  [the longest x1 27.3 us: attention_backward_all(): pl.pallas_call(functools.partial(attention_backward_kernel, docs, back, N...]
    pallas_call x2 -> x1, Pallas kernels: 18.1 us -> 9.52 us  [attention_input(): pl.pallas_call(functools.partial(attention_input_kernel, earlier is not N...]
    all_gather x1, waiting for transfers between devices: 1.59 us -> 9.15 us  [gather_all(): mlp = lax.all_gather(jnp.concatenate([columns, across]), BOTH)]
    pallas_call x2, Pallas kernels: 73.9 us -> 81.4 us  [mlp_backward(): pl.pallas_call(functools.partial(mlp_backward_kernel, earlier is not None...]
    pallas_call x8 -> x9, Pallas kernels: 11.6 us -> 9.44 us  [in_vmem(): pl.pallas_call(kernel, out_shape=outs, in_specs=[SMEM] + [vmem] * (len(ar...]
  transfers between devices with their start and end apart: 42 -> 45, of which waited for: 16 -> 15; matrix products, arithmetic and copies ran while one was open for 3% -> 1% of each run, Pallas kernels for 20% -> 21%
where the time goes in v3:
time: 383 us; the launch traced here: 379 us
  Pallas kernels  230 us (60%)
  starting transfers between devices  72.3 us (19%)
  waiting for transfers between devices  49.2 us (13%)
  between operations  15.1 us (4%)
  local copies, waits for them, and re-layouts  11.3 us (3%)
    pallas_call x2, Pallas kernels, mlp_backward(): pl.pallas_call(functools.partial(mlp_backward_kernel, earlier is not None...  81.4 us
    ppermute x44, starting transfers between devices, swap(): return lax.ppermute(value, BOTH, [(i, i ^ bits) for i in range(32)])  72.3 us
    pallas_call x2, Pallas kernels, attention_forward(): pl.pallas_call(functools.partial(attention_forward_kernel, docs, back), g...  40.5 us
    ppermute x44, waiting for transfers between devices, swap(): return lax.ppermute(value, BOTH, [(i, i ^ bits) for i in range(32)])  40 us
    pallas_call x1, Pallas kernels, attention_backward_all(): pl.pallas_call(functools.partial(attention_backward_kernel, docs, back, N...  27.3 us
    pallas_call x2, Pallas kernels, attention_backward(): pl.pallas_call(functools.partial(attention_backward_kernel, docs, back, m...  21 us
    pallas_call x1, Pallas kernels, mlp_forward(): pl.pallas_call(mlp_forward_kernel, grid=(hidden_units // block,), out_sha...  17 us
    pallas_call x2, Pallas kernels, attention_terms(): pl.pallas_call(functools.partial(attention_terms_kernel, earlier is not N...  15.4 us
  transfers between devices with their start and end apart: 45, of which 15 were waited for; matrix products, arithmetic and copies ran while one was open for 1% of the time, Pallas kernels for 21%

profile of v3, /device:TPU:1, one launch (start us, length us, event | category | flops | bytes accessed | tf_op | source)
XLA Modules:
  0.0 379.5 jit_solution(10382992263059893191)
XLA Ops:
  7.4 0.8 copy-done
  8.2 0.9 constant_dynamic-slice_fusion.6
  9.6 0.7 copy.36
  10.5 2.2 collective-permute-start
  12.7 2.3 collective-permute-start.1
  15.7 3.2 collective-permute-start.4
  18.9 3.1 collective-permute-done.3
  21.9 1.9 collective-permute-start.5
  23.8 6.2 %collective-permute-done.4 = bf16[1,8,256]{2,1,0:T(8,128)(2,1)S(1)} collective-permute-done((bf16[1,8,256]{2,1,0:T(8,128)(2,1)S(1)}, bf16[1,8,256]{2,1,0:T(8,128)(2,1)S(1)}, u32[]{:S(2)}, u32[]{:S(2)}) %collective-permute-start.4) | collective-permute-done | bytes 4128 | tf_op jit(solution)/shard_map/ppermute | solution.py:839
  30.1 1.3 collective-permute-start.6
  31.4 1.3 collective-permute-start.7
  32.7 5.3 %collective-permute-start.8 = (bf16[4,4,24,768]{3,2,1,0:T(8,128)(2,1)S(1)}, bf16[4,4,24,768]{3,2,1,0:T(8,128)(2,1)S(1)}, u32[]{:S(2)}, u32[]{:S(2)}) collective-permute-start(bf16[4,4,24,768]{3,2,1,0:T(8,128)(2,1)S(1)} %constant_dynamic-update-slice_fusion.4.refs_0_), channel_id=1, source_target_pairs={{0,1},{1,0},{2,3},{3,2},{4,5},{5,4},{6,7},{7,6},{8,9},{9,8},{10,11... | collective-permute-start | bytes 1769480 | tf_op jit(solution)/shard_map/ppermute | solution.py:839
  38.4 3.4 collective-permute-done.10.refs_2_
  41.9 9.9 %collective-permute-start.13 = (bf16[4,4,24,768]{3,2,1,0:T(8,128)(2,1)S(1)}, bf16[4,4,24,768]{3,2,1,0:T(8,128)(2,1)S(1)}, u32[]{:S(2)}, u32[]{:S(2)}) collective-permute-start(bf16[4,4,24,768]{3,2,1,0:T(8,128)(2,1)S(1)} %collective-permute-done.6.refs_1_), channel_id=1, source_target_pairs={{0,1},{1,0},{2,3},{3,2},{4,5},{5,4},{6,7},{7,6},{8,9},{9,8},{10,11... | collective-permute-start | bytes 1769480 | tf_op jit(solution)/shard_map/ppermute | solution.py:839
  52.3 2.1 collective-permute-start.11
  54.4 1.1 collective-permute-start.12
  55.6 6.6 %collective-permute-done.15.refs_3_ = bf16[4,8,256]{2,1,0:T(8,128)(2,1)S(1)} collective-permute-done((bf16[4,8,256]{2,1,0:T(8,128)(2,1)S(1)}, bf16[4,8,256]{2,1,0:T(8,128)(2,1)S(1)}, u32[]{:S(2)}, u32[]{:S(2)}) %collective-permute-start.15) | collective-permute-done | bytes 16416 | tf_op jit(solution)/shard_map/ppermute | solution.py:839
  62.8 1.2 collective-permute-start.16
  64.1 2.7 place_small.1
  66.8 5.5 %place.1 = bf16[4,32,24,768]{3,2,1,0:T(8,128)(2,1)} custom-call(s32[1]{0:T(128)} %bitcast.4.me_ref, bf16[4,4,24,768]{3,2,1,0:T(8,128)(2,1)} %copy-done.19, bf16[4,4,24,768]{3,2,1,0:T(8,128)(2,1)} %copy-done.17, bf16[4,4,24,768]{3,2,1,0:T(8,128)(2,1)} %copy-done.18, bf16[2,4,24,768]{3,2,1,0:T(8,128)(2,1)} %collective-permute-done.11.refs_3_, ...), custom_call_target="tpu_custom_call" | custom-call | tf_op jit(solution)/shard_map/place/pallas_call | solution.py:863
  72.3 19.7 %attention_forward.2 = (bf16[1024,768]{1,0:T(8,128)(2,1)}, bf16[1024,2304]{1,0:T(8,128)(2,1)}, bf16[1024,768]{1,0:T(8,128)(2,1)}, f32[24,1,512]{2,1,0:T(1,128)},...) custom-call(s32[2,6]{1,0:T(2,128)S(1)} %bitcast.48, bf16[1024,768]{1,0:T(8,128)(2,1)} %bitcast.65, ...), custom_call_target="tpu_custom_call" | custom-call | flops 805306368 | bytes 2368512 | tf_op jit(solution)/shard_map/attention_forward/pallas_call | solution.py:205
  92.1 9.2 %all-gather.3.cloned.1.call-done = bf16[128,48,768]{2,1,0:T(8,128)(2,1)} async-done(((bf16[4,48,768]{2,1,0:T(8,128)(2,1)}), bf16[128,48,768]{2,1,0:T(8,128)(2,1)}) %all-gather.3.cloned.1.call-update) | async-done | bytes 9437200 | tf_op jit(solution)/shard_map/all_gather | solution.py:1092
  101.2 17.0 %mlp_forward.1 = (bf16[1024,3072]{1,0:T(8,128)(2,1)}, f32[1024,768]{1,0:T(8,128)}) custom-call(f32[1024,768]{1,0:T(8,128)} %get-tuple-element.172.hidden_ref, bf16[1024,768]{1,0:T(8,128)(2,1)} %get-tuple-element.173.normed_ref, bf16[16,2,4,48,768]{4,3,2,1,0:T(8,128)(2,1)} %bitcast.53, f32[1,3072]{1,0:T(1,128)} %get-tuple-element.174.fbias_ref.rest_0_, ...), custom_call_target="tpu_custom_call" | custom-call | flops 1207959552 | bytes 2949120 | tf_op jit(solution)/shard_map/mlp_forward/pallas_call | solution.py:287
  118.3 20.8 %attention_forward.3 = (bf16[1024,768]{1,0:T(8,128)(2,1)}, bf16[1024,2304]{1,0:T(8,128)(2,1)}, bf16[1024,768]{1,0:T(8,128)(2,1)}, f32[24,1,512]{2,1,0:T(1,128)},...) custom-call(s32[2,6]{1,0:T(2,128)S(1)} %bitcast.49, f32[1024,768]{1,0:T(8,128)} %get-tuple-element.176.state_ref.rest_0_, ...), custom_call_target="tpu_custom_call" | custom-call | flops 805306368 | bytes 2565120 | tf_op jit(solution)/shard_map/attention_forward/pallas_call | solution.py:205
  139.1 45.0 %mlp_backward.2 = (bf16[1024,768]{1,0:T(8,128)(2,1)}, f32[1024,768]{1,0:T(8,128)}, bf16[16,4,48,384]{3,2,1,0:T(8,128)(2,1)}, bf16[16,4,48,384]{3,2,1,0:T(8,128)(...) custom-call(s32[1]{0:T(128)} %bitcast.core_ref.unused_ref, ...), custom_call_target="tpu_custom_call" | custom-call | flops 2415919104 | bytes 5264640 | tf_op jit(solution)/shard_map/mlp_backward/pallas_call | solution.py:513
  184.0 27.3 %attention_backward_all.1 = (bf16[1024,2304]{1,0:T(8,128)(2,1)}, f32[1024,768]{1,0:T(8,128)S(1)}, f32[1,768]{1,0:T(1,128)S(1)}, f32[1,768]{1,0:T(1,128)S(1)}) custom-call(s32[2,6]{1,0:T(2,128)S(1)} %bitcast.50, f32[1024,768]{1,0:T(8,128)} %get-tuple-element.181.dhid_ref, bf16[1024,768]{1,0:T(8,128)(2,1)} %get-tuple-element.179.att_ref, ...), custom_call_target="tpu_custom_call" | custom-call | flops 1107296256 | bytes 3153024 | tf_op jit(solution)/shard_map/attention_backward_all/pallas_call | solution.py:681
  211.3 1.6 copy-done.3
  214.1 36.5 %mlp_backward.3 = (f32[1024,768]{1,0:T(8,128)}, bf16[16,4,48,384]{3,2,1,0:T(8,128)(2,1)}, bf16[16,4,48,384]{3,2,1,0:T(8,128)(2,1)}, bf16[3072,384]{1,0:T(8,128)(...) custom-call(s32[1]{0:T(128)} %bitcast.core_ref.unused_ref, ...), custom_call_target="tpu_custom_call" | custom-call | flops 2415919104 | bytes 7379328 | tf_op jit(solution)/shard_map/mlp_backward/pallas_call | solution.py:513
  251.5 2.3 copy-done.2
  253.9 7.6 %attention_terms.2 = (bf16[16,3,48,384]{3,2,1,0:T(8,128)(2,1)}, bf16[16,3,48,384]{3,2,1,0:T(8,128)(2,1)}, f32[3,1,768]{2,1,0:T(1,128)}) custom-call(s32[1]{0:T(128)} %bitcast.core_ref.unused_ref, bf16[1024,768]{1,0:T(8,128)(2,1)} %get-tuple-element.205.normed_ref, bf16[1024,2304]{1,0:T(8,128)(2,1)S(1)} %copy-done.2), custom_call_target="tpu_custom_call" | custom-call | flops 452984832 | bytes 1229952 | tf_op jit(solution)/shard_map/attention_terms/pallas_call | solution.py:743
  261.5 3.1 first_sums.2
  264.6 1.2 collective-permute-start.21
  266.1 10.4 %attention_backward.3.rest_1_ = bf16[512,2304]{1,0:T(8,128)(2,1)S(1)} custom-call(s32[2,6]{1,0:T(2,128)S(1)} %bitcast.51, f32[1024,768]{1,0:T(8,128)} %get-tuple-element.215.dhid_ref, bf16[1024,768]{1,0:T(8,128)(2,1)} %get-tuple-element.185.att_ref, bf16[1024,2304]{1,0:T(8,128)(2,1)} %get-tuple-element.216.mixed_ref, ...), custom_call_target="tpu_custom_call" | custom-call | flops 327155712 | bytes 589824 | tf_op jit(solution)/shard_map/attention_backward/pallas_call | solution.py:643
  276.5 10.6 %attention_backward.2.rest_0_ = bf16[512,2304]{1,0:T(8,128)(2,1)S(1)} custom-call(s32[2,6]{1,0:T(2,128)S(1)} %bitcast.52, f32[1024,768]{1,0:T(8,128)} %get-tuple-element.215.dhid_ref, bf16[1024,768]{1,0:T(8,128)(2,1)} %get-tuple-element.185.att_ref, bf16[1024,2304]{1,0:T(8,128)(2,1)} %get-tuple-element.216.mixed_ref, ...), custom_call_target="tpu_custom_call" | custom-call | flops 327155712 | bytes 589824 | tf_op jit(solution)/shard_map/attention_backward/pallas_call | solution.py:643
  287.1 7.8 %attention_terms.3 = (bf16[16,3,48,384]{3,2,1,0:T(8,128)(2,1)}, bf16[16,3,48,384]{3,2,1,0:T(8,128)(2,1)}, f32[3,1,768]{2,1,0:T(1,128)}) custom-call(s32[1]{0:T(128)} %bitcast.core_ref.unused_ref, bf16[1024,768]{1,0:T(8,128)(2,1)} %get-tuple-element.220.normed_ref, bf16[512,2304]{1,0:T(8,128)(2,1)S(1)} %attention_backward.2.rest_0_, ...), custom_call_target="tpu_custom_call" | custom-call | flops 452984832 | bytes 1673472 | tf_op jit(solution)/shard_map/attention_terms/pallas_call | solution.py:743
  294.9 0.8 collective-permute-start.25
  295.9 1.2 second_sums.2
  297.1 1.0 collective-permute-start.23
  298.7 9.5 %attention_input.1 = (bf16[1024,768]{1,0:T(8,128)(2,1)}, f32[1,768]{1,0:T(1,128)S(1)}, f32[1,768]{1,0:T(1,128)S(1)}) custom-call(f32[1024,768]{1,0:T(8,128)} %get-tuple-element.215.dhid_ref, bf16[1024,768]{1,0:T(8,128)(2,1)} %bitcast.66, bf16[4,768,768]{2,1,0:T(8,128)(2,1)} %bitcast.64, f32[1,768]{1,0:T(1,128)} %get-tuple-element.161.gain_ref.rest_1_, ...), custom_call_target="tpu_custom_call" | custom-call | flops 452984832 | bytes 1968000 | tf_op jit(solution)/shard_map/attention_input/pallas_call | solution.py:797
  308.3 3.9 %collective-permute-done.23.near_in = bf16[2,432,384]{2,1,0:T(8,128)(2,1)S(1)} collective-permute-done((bf16[2,432,384]{2,1,0:T(8,128)(2,1)S(1)}, bf16[2,432,384]{2,1,0:T(8,128)(2,1)S(1)}, u32[]{:S(2)}, u32[]{:S(2)}) %collective-permute-start.23) | collective-permute-done | bytes 663584 | tf_op jit(solution)/shard_map/ppermute | solution.py:839
  312.2 1.2 collective-permute-done.24.far_in
  313.4 1.0 first_sums.3
  314.9 1.1 collective-permute-start.28
  316.1 2.6 collective-permute-start.26
  318.7 0.9 collective-permute-done.26
  320.1 0.8 third_sums.3
  320.9 1.3 collective-permute-start.40
  322.9 2.3 collective-permute-done.29
  325.2 1.7 collective-permute-start.42
  327.0 0.8 second_sums.3
  327.7 1.5 collective-permute-start.30
  329.2 1.0 collective-permute-done.32
  330.5 2.5 collective-permute-done.30.near_in
  333.0 2.5 collective-permute-done.31.far_in
  335.9 1.5 collective-permute-start.37
  338.1 1.7 collective-permute-start.38
  339.8 5.6 %collective-permute-done.42 = bf16[432,384]{1,0:T(8,128)(2,1)} collective-permute-done((bf16[432,384]{1,0:T(8,128)(2,1)S(1)}, bf16[432,384]{1,0:T(8,128)(2,1)}, u32[]{:S(2)}, u32[]{:S(2)}) %collective-permute-start.42) | collective-permute-done | bytes 331808 | tf_op jit(solution)/shard_map/ppermute | solution.py:839
  345.4 10.4 %collective-permute-start.34 = (bf16[144,384]{1,0:T(8,128)(2,1)S(1)}, bf16[144,384]{1,0:T(8,128)(2,1)S(1)}, u32[]{:S(2)}, u32[]{:S(2)}) collective-permute-start(bf16[144,384]{1,0:T(8,128)(2,1)S(1)} %get-tuple-element.264), channel_id=1, source_target_pairs={{0,16},{1,17},{2,18},{3,19},{4,20},{5,21},{6,22},{7,23},{8,24},{9,... | collective-permute-start | bytes 331784 | tf_op jit(solution)/shard_map/ppermute | solution.py:839
  355.8 1.6 collective-permute-start.35
  357.5 1.4 convert_add_fusion.half_ref
  358.9 3.9 %collective-permute-start.43 = (f32[432,384]{1,0:T(8,128)S(1)}, f32[432,384]{1,0:T(8,128)S(1)}, u32[]{:S(2)}, u32[]{:S(2)}) collective-permute-start(f32[432,384]{1,0:T(8,128)S(1)} %convert_add_fusion.half_ref), channel_id=1, source_target_pairs={{0,1},{1,0},{2,3},{3,2},{4,5},{5,4},{6,7},{7,6},{8,9},{9,8},{10,11... | collective-permute-start | bytes 1990664 | tf_op jit(solution)/shard_map/ppermute | solution.py:839
  362.9 4.5 %collective-permute-start.39 = (f32[144,384]{1,0:T(8,128)S(1)}, f32[144,384]{1,0:T(8,128)S(1)}, u32[]{:S(2)}, u32[]{:S(2)}) collective-permute-start(f32[144,384]{1,0:T(8,128)S(1)} %convert_add_fusion.1.half_ref), channel_id=1, source_target_pairs={{0,1},{1,0},{2,3},{3,2},{4,5},{5,4},{6,7},{7,6},{8,9},{9,8},{10,11... | collective-permute-start | bytes 663560 | tf_op jit(solution)/shard_map/ppermute | solution.py:839
  370.5 1.1 assemble.3
  371.7 0.8 assemble.2
  (177 shorter events, 12.5 us)
Async XLA Ops:
  7.3 7.8 %copy-start.32 = (bf16[48]{0:T(256)(128)(2,1)S(1)}, bf16[48]{0:T(256)(128)(2,1)}, u32[]{:S(2)}) copy-start(bf16[48]{0:T(256)(128)(2,1)} %param.23) | copy-start | bytes 292
  7.3 7.8 %copy-start.33 = (bf16[48]{0:T(256)(128)(2,1)S(1)}, bf16[48]{0:T(256)(128)(2,1)}, u32[]{:S(2)}) copy-start(bf16[48]{0:T(256)(128)(2,1)} %param.24) | copy-start | bytes 292
  7.3 7.9 %copy-start.34 = (bf16[48]{0:T(256)(128)(2,1)S(1)}, bf16[48]{0:T(256)(128)(2,1)}, u32[]{:S(2)}) copy-start(bf16[48]{0:T(256)(128)(2,1)} %param.25) | copy-start | bytes 292
  7.3 7.9 %copy-start.35 = (bf16[192]{0:T(256)(128)(2,1)S(1)}, bf16[192]{0:T(256)(128)(2,1)}, u32[]{:S(2)}) copy-start(bf16[192]{0:T(256)(128)(2,1)} %param.27) | copy-start | bytes 1156
  7.3 7.9 %copy-start.36 = (bf16[48]{0:T(256)(128)(2,1)S(1)}, bf16[48]{0:T(256)(128)(2,1)}, u32[]{:S(2)}) copy-start(bf16[48]{0:T(256)(128)(2,1)} %param.29) | copy-start | bytes 292
  7.3 93.9 %all-gather.3.cloned.1.call-start = ((), (), s32[]{:S(2)}) async-start(), calls=%async_computation | async-start | bytes 9732096 | tf_op jit(solution)/shard_map/all_gather | solution.py:1092
  10.5 19.5 %collective-permute-start = (bf16[1,4,24,768]{3,2,1,0:T(8,128)(2,1)S(1)}, bf16[1,4,24,768]{3,2,1,0:T(8,128)(2,1)S(1)}, u32[]{:S(2)}, u32[]{:S(2)}) collective-permute-start(bf16[1,4,24,768]{3,2,1,0:T(8,128)(2,1)S(1)} %maximum_bitcast_fusion), channel_id=1, source_target_pairs={{0,8},{1,9},{2,10},{3,11},{4,12},{5,13},{6,14},{7,15},{8,0},{9,1},... | collective-permute-start | bytes 442376 | tf_op jit(solution)/shard_map/ppermute | solution.py:839
  12.7 17.3 %collective-permute-start.1 = (bf16[1,4,24,768]{3,2,1,0:T(8,128)(2,1)S(1)}, bf16[1,4,24,768]{3,2,1,0:T(8,128)(2,1)S(1)}, u32[]{:S(2)}, u32[]{:S(2)}) collective-permute-start(bf16[1,4,24,768]{3,2,1,0:T(8,128)(2,1)S(1)} %maximum_bitcast_fusion), channel_id=1, source_target_pairs={{0,16},{1,17},{2,18},{3,19},{4,20},{5,21},{6,22},{7,23},{8,24},{9,... | collective-permute-start | bytes 442376 | tf_op jit(solution)/shard_map/ppermute | solution.py:839
  15.0 15.0 %collective-permute-start.2 = (bf16[1,4,24,768]{3,2,1,0:T(8,128)(2,1)S(1)}, bf16[1,4,24,768]{3,2,1,0:T(8,128)(2,1)S(1)}, u32[]{:S(2)}, u32[]{:S(2)}) collective-permute-start(bf16[1,4,24,768]{3,2,1,0:T(8,128)(2,1)S(1)} %maximum_bitcast_fusion), channel_id=1, source_target_pairs={{0,24},{1,25},{2,26},{3,27},{4,28},{5,29},{6,30},{7,31},{8,16},{9,... | collective-permute-start | bytes 442376 | tf_op jit(solution)/shard_map/ppermute | solution.py:839
  15.3 6.7 %collective-permute-start.3 = (bf16[1,8,256]{2,1,0:T(8,128)(2,1)S(1)}, bf16[1,8,256]{2,1,0:T(8,128)(2,1)S(1)}, u32[]{:S(2)}, u32[]{:S(2)}) collective-permute-start(bf16[1,8,256]{2,1,0:T(8,128)(2,1)S(1)} %bitcast.72), channel_id=1, source_target_pairs={{0,8},{1,9},{2,10},{3,11},{4,12},{5,13},{6,14},{7,15},{8,0},{9,1},... | collective-permute-start | bytes 12296 | tf_op jit(solution)/shard_map/ppermute | solution.py:839
  15.7 14.3 %collective-permute-start.4 = (bf16[1,8,256]{2,1,0:T(8,128)(2,1)S(1)}, bf16[1,8,256]{2,1,0:T(8,128)(2,1)S(1)}, u32[]{:S(2)}, u32[]{:S(2)}) collective-permute-start(bf16[1,8,256]{2,1,0:T(8,128)(2,1)S(1)} %bitcast.73), channel_id=1, source_target_pairs={{0,16},{1,17},{2,18},{3,19},{4,20},{5,21},{6,22},{7,23},{8,24},{9,... | collective-permute-start | bytes 12296 | tf_op jit(solution)/shard_map/ppermute | solution.py:839
  21.9 8.0 %collective-permute-start.5 = (bf16[1,8,256]{2,1,0:T(8,128)(2,1)S(1)}, bf16[1,8,256]{2,1,0:T(8,128)(2,1)S(1)}, u32[]{:S(2)}, u32[]{:S(2)}) collective-permute-start(bf16[1,8,256]{2,1,0:T(8,128)(2,1)S(1)} %bitcast.74), channel_id=1, source_target_pairs={{0,24},{1,25},{2,26},{3,27},{4,28},{5,29},{6,30},{7,31},{8,16},{9,... | collective-permute-start | bytes 12296 | tf_op jit(solution)/shard_map/ppermute | solution.py:839
  30.1 36.7 %copy-start.19 = (bf16[4,4,24,768]{3,2,1,0:T(8,128)(2,1)}, bf16[4,4,24,768]{3,2,1,0:T(8,128)(2,1)S(1)}, u32[]{:S(2)}) copy-start(bf16[4,4,24,768]{3,2,1,0:T(8,128)(2,1)S(1)} %constant_dynamic-update-slice_fusion.4.refs_0_) | copy-start | bytes 1769476
  30.1 11.7 %collective-permute-start.6 = (bf16[4,4,24,768]{3,2,1,0:T(8,128)(2,1)S(1)}, bf16[4,4,24,768]{3,2,1,0:T(8,128)(2,1)S(1)}, u32[]{:S(2)}, u32[]{:S(2)}) collective-permute-start(bf16[4,4,24,768]{3,2,1,0:T(8,128)(2,1)S(1)} %constant_dynamic-update-slice_fusion.4.refs_0_), channel_id=1, source_target_pairs={{0,2},{1,3},{2,0},{3,1},{4,6},{5,7},{6,4},{7,5},{8,10},{9,11},{10,... | collective-permute-start | bytes 1769480 | tf_op jit(solution)/shard_map/ppermute | solution.py:839
  31.4 10.5 %collective-permute-start.7 = (bf16[4,4,24,768]{3,2,1,0:T(8,128)(2,1)S(1)}, bf16[4,4,24,768]{3,2,1,0:T(8,128)(2,1)S(1)}, u32[]{:S(2)}, u32[]{:S(2)}) collective-permute-start(bf16[4,4,24,768]{3,2,1,0:T(8,128)(2,1)S(1)} %constant_dynamic-update-slice_fusion.4.refs_0_), channel_id=1, source_target_pairs={{0,4},{1,5},{2,6},{3,7},{4,0},{5,1},{6,2},{7,3},{8,12},{9,13},{10,... | collective-permute-start | bytes 1769480 | tf_op jit(solution)/shard_map/ppermute | solution.py:839
  32.7 9.2 %collective-permute-start.8 = (bf16[4,4,24,768]{3,2,1,0:T(8,128)(2,1)S(1)}, bf16[4,4,24,768]{3,2,1,0:T(8,128)(2,1)S(1)}, u32[]{:S(2)}, u32[]{:S(2)}) collective-permute-start(bf16[4,4,24,768]{3,2,1,0:T(8,128)(2,1)S(1)} %constant_dynamic-update-slice_fusion.4.refs_0_), channel_id=1, source_target_pairs={{0,1},{1,0},{2,3},{3,2},{4,5},{5,4},{6,7},{7,6},{8,9},{9,8},{10,11... | collective-permute-start | bytes 1769480 | tf_op jit(solution)/shard_map/ppermute | solution.py:839
  38.0 13.8 %copy-start.24 = (bf16[4,8,256]{2,1,0:T(8,128)(2,1)}, bf16[4,8,256]{2,1,0:T(8,128)(2,1)S(1)}, u32[]{:S(2)}) copy-start(bf16[4,8,256]{2,1,0:T(8,128)(2,1)S(1)} %constant_dynamic-update-slice_fusion.refs_0_) | copy-start | bytes 49156
  38.0 3.8 %collective-permute-start.10 = (bf16[4,8,256]{2,1,0:T(8,128)(2,1)S(1)}, bf16[4,8,256]{2,1,0:T(8,128)(2,1)S(1)}, u32[]{:S(2)}, u32[]{:S(2)}) collective-permute-start(bf16[4,8,256]{2,1,0:T(8,128)(2,1)S(1)} %constant_dynamic-update-slice_fusion.refs_0_), channel_id=1, source_target_pairs={{0,4},{1,5},{2,6},{3,7},{4,0},{5,1},{6,2},{7,3},{8,12},{9,13},{10,... | collective-permute-start | bytes 49160 | tf_op jit(solution)/shard_map/ppermute | solution.py:839
  38.1 3.7 collective-permute-start.9
  41.8 21.0 %copy-start.26 = (bf16[4,8,256]{2,1,0:T(8,128)(2,1)}, bf16[4,8,256]{2,1,0:T(8,128)(2,1)S(1)}, u32[]{:S(2)}) copy-start(bf16[4,8,256]{2,1,0:T(8,128)(2,1)S(1)} %collective-permute-done.10.refs_2_) | copy-start | bytes 49156
  41.8 10.0 %copy-start.27 = (bf16[4,8,256]{2,1,0:T(8,128)(2,1)}, bf16[4,8,256]{2,1,0:T(8,128)(2,1)S(1)}, u32[]{:S(2)}) copy-start(bf16[4,8,256]{2,1,0:T(8,128)(2,1)S(1)} %collective-permute-done.9.refs_1_) | copy-start | bytes 49156
  41.8 25.0 %copy-start.17 = (bf16[4,4,24,768]{3,2,1,0:T(8,128)(2,1)}, bf16[4,4,24,768]{3,2,1,0:T(8,128)(2,1)S(1)}, u32[]{:S(2)}) copy-start(bf16[4,4,24,768]{3,2,1,0:T(8,128)(2,1)S(1)} %collective-permute-done.6.refs_1_) | copy-start | bytes 1769476
  41.8 25.0 %copy-start.18 = (bf16[4,4,24,768]{3,2,1,0:T(8,128)(2,1)}, bf16[4,4,24,768]{3,2,1,0:T(8,128)(2,1)S(1)}, u32[]{:S(2)}) copy-start(bf16[4,4,24,768]{3,2,1,0:T(8,128)(2,1)S(1)} %collective-permute-done.7.refs_2_) | copy-start | bytes 1769476
  41.9 24.9 %copy-start.20 = (bf16[4,4,24,768]{3,2,1,0:T(8,128)(2,1)}, bf16[4,4,24,768]{3,2,1,0:T(8,128)(2,1)S(1)}, u32[]{:S(2)}) copy-start(bf16[4,4,24,768]{3,2,1,0:T(8,128)(2,1)S(1)} %collective-permute-done.8.refs_5_) | copy-start | bytes 1769476
  41.9 20.9 %collective-permute-start.13 = (bf16[4,4,24,768]{3,2,1,0:T(8,128)(2,1)S(1)}, bf16[4,4,24,768]{3,2,1,0:T(8,128)(2,1)S(1)}, u32[]{:S(2)}, u32[]{:S(2)}) collective-permute-start(bf16[4,4,24,768]{3,2,1,0:T(8,128)(2,1)S(1)} %collective-permute-done.6.refs_1_), channel_id=1, source_target_pairs={{0,1},{1,0},{2,3},{3,2},{4,5},{5,4},{6,7},{7,6},{8,9},{9,8},{10,11... | collective-permute-start | bytes 1769480 | tf_op jit(solution)/shard_map/ppermute | solution.py:839
  51.8 11.0 %collective-permute-start.14 = (bf16[4,4,24,768]{3,2,1,0:T(8,128)(2,1)S(1)}, bf16[4,4,24,768]{3,2,1,0:T(8,128)(2,1)S(1)}, u32[]{:S(2)}, u32[]{:S(2)}) collective-permute-start(bf16[4,4,24,768]{3,2,1,0:T(8,128)(2,1)S(1)} %collective-permute-done.7.refs_2_), channel_id=1, source_target_pairs={{0,1},{1,0},{2,3},{3,2},{4,5},{5,4},{6,7},{7,6},{8,9},{9,8},{10,11... | collective-permute-start | bytes 1769480 | tf_op jit(solution)/shard_map/ppermute | solution.py:839
  52.3 9.9 %collective-permute-start.11 = (bf16[2,4,24,768]{3,2,1,0:T(8,128)(2,1)S(1)}, bf16[2,4,24,768]{3,2,1,0:T(8,128)(2,1)}, u32[]{:S(2)}, u32[]{:S(2)}) collective-permute-start(bf16[2,4,24,768]{3,2,1,0:T(8,128)(2,1)S(1)} %slice.30), channel_id=1, source_target_pairs={{0,2},{1,3},{2,0},{3,1},{4,6},{5,7},{6,4},{7,5},{8,10},{9,11},{10,... | collective-permute-start | bytes 884744 | tf_op jit(solution)/shard_map/ppermute | solution.py:839
  54.4 8.4 %collective-permute-start.12 = (bf16[2,4,24,768]{3,2,1,0:T(8,128)(2,1)S(1)}, bf16[2,4,24,768]{3,2,1,0:T(8,128)(2,1)}, u32[]{:S(2)}, u32[]{:S(2)}) collective-permute-start(bf16[2,4,24,768]{3,2,1,0:T(8,128)(2,1)S(1)} %slice.31), channel_id=1, source_target_pairs={{0,4},{1,5},{2,6},{3,7},{4,0},{5,1},{6,2},{7,3},{8,12},{9,13},{10,... | collective-permute-start | bytes 884744 | tf_op jit(solution)/shard_map/ppermute | solution.py:839
  55.5 6.7 %collective-permute-start.15 = (bf16[4,8,256]{2,1,0:T(8,128)(2,1)S(1)}, bf16[4,8,256]{2,1,0:T(8,128)(2,1)S(1)}, u32[]{:S(2)}, u32[]{:S(2)}) collective-permute-start(bf16[4,8,256]{2,1,0:T(8,128)(2,1)S(1)} %collective-permute-done.10.refs_2_), channel_id=1, source_target_pairs={{0,2},{1,3},{2,0},{3,1},{4,6},{5,7},{6,4},{7,5},{8,10},{9,11},{10,... | collective-permute-start | bytes 49160 | tf_op jit(solution)/shard_map/ppermute | solution.py:839
  62.8 3.9 %collective-permute-start.16 = (bf16[2,4,24,768]{3,2,1,0:T(8,128)(2,1)}, bf16[2,4,24,768]{3,2,1,0:T(8,128)(2,1)}, u32[]{:S(2)}, u32[]{:S(2)}) collective-permute-start(bf16[2,4,24,768]{3,2,1,0:T(8,128)(2,1)} %collective-permute-done.11.refs_3_), channel_id=1, source_target_pairs={{0,1},{1,0},{2,3},{3,2},{4,5},{5,4},{6,7},{7,6},{8,9},{9,8},{10,11... | collective-permute-start | bytes 884744 | tf_op jit(solution)/shard_map/ppermute | solution.py:839
  64.0 2.8 collective-permute-start.17
  250.6 10.9 %collective-permute-start.18 = (bf16[16,192,384]{2,1,0:T(8,128)(2,1)}, bf16[16,192,384]{2,1,0:T(8,128)(2,1)S(1)}, u32[]{:S(2)}, u32[]{:S(2)}) collective-permute-start(bf16[16,192,384]{2,1,0:T(8,128)(2,1)} %bitcast.77), channel_id=1, source_target_pairs={{0,1},{1,0},{2,3},{3,2},{4,5},{5,4},{6,7},{7,6},{8,9},{9,8},{10,11... | collective-permute-start | bytes 7077896 | tf_op jit(solution)/shard_map/ppermute | solution.py:839
  250.9 10.6 %collective-permute-start.19 = (bf16[16,192,384]{2,1,0:T(8,128)(2,1)}, bf16[16,192,384]{2,1,0:T(8,128)(2,1)}, u32[]{:S(2)}, u32[]{:S(2)}) collective-permute-start(bf16[16,192,384]{2,1,0:T(8,128)(2,1)} %bitcast.76), channel_id=1, source_target_pairs={{0,1},{1,0},{2,3},{3,2},{4,5},{5,4},{6,7},{7,6},{8,9},{9,8},{10,11... | collective-permute-start | bytes 7077896 | tf_op jit(solution)/shard_map/ppermute | solution.py:839
  251.2 10.3 %collective-permute-start.20 = (bf16[16,48,384]{2,1,0:T(8,128)(2,1)}, bf16[16,48,384]{2,1,0:T(8,128)(2,1)S(1)}, u32[]{:S(2)}, u32[]{:S(2)}) collective-permute-start(bf16[16,48,384]{2,1,0:T(8,128)(2,1)} %get-tuple-element.204), channel_id=1, source_target_pairs={{0,1},{1,0},{2,3},{3,2},{4,5},{5,4},{6,7},{7,6},{8,9},{9,8},{10,11... | collective-permute-start | bytes 1769480 | tf_op jit(solution)/shard_map/ppermute | solution.py:839
  264.6 31.1 %collective-permute-start.21 = (bf16[2,2,432,384]{3,2,1,0:T(8,128)(2,1)S(1)}, bf16[2,2,432,384]{3,2,1,0:T(8,128)(2,1)S(1)}, u32[]{:S(2)}, u32[]{:S(2)}) collective-permute-start(bf16[2,2,432,384]{3,2,1,0:T(8,128)(2,1)S(1)} %get-tuple-element.218), channel_id=1, source_target_pairs={{0,2},{1,3},{2,0},{3,1},{4,6},{5,7},{6,4},{7,5},{8,10},{9,11},{10,... | collective-permute-start | bytes 3981320 | tf_op jit(solution)/shard_map/ppermute | solution.py:839
  265.8 30.1 %collective-permute-start.22 = (bf16[2,2,432,384]{3,2,1,0:T(8,128)(2,1)S(1)}, bf16[2,2,432,384]{3,2,1,0:T(8,128)(2,1)S(1)}, u32[]{:S(2)}, u32[]{:S(2)}) collective-permute-start(bf16[2,2,432,384]{3,2,1,0:T(8,128)(2,1)S(1)} %get-tuple-element.219), channel_id=1, source_target_pairs={{0,4},{1,5},{2,6},{3,7},{4,0},{5,1},{6,2},{7,3},{8,12},{9,13},{10,... | collective-permute-start | bytes 3981320 | tf_op jit(solution)/shard_map/ppermute | solution.py:839
  294.9 13.4 %collective-permute-start.25 = (bf16[16,144,384]{2,1,0:T(8,128)(2,1)}, bf16[16,144,384]{2,1,0:T(8,128)(2,1)S(1)}, u32[]{:S(2)}, u32[]{:S(2)}) collective-permute-start(bf16[16,144,384]{2,1,0:T(8,128)(2,1)} %bitcast.78), channel_id=1, source_target_pairs={{0,1},{1,0},{2,3},{3,2},{4,5},{5,4},{6,7},{7,6},{8,9},{9,8},{10,11... | collective-permute-start | bytes 5308424 | tf_op jit(solution)/shard_map/ppermute | solution.py:839
  297.1 15.1 %collective-permute-start.23 = (bf16[2,432,384]{2,1,0:T(8,128)(2,1)S(1)}, bf16[2,432,384]{2,1,0:T(8,128)(2,1)S(1)}, u32[]{:S(2)}, u32[]{:S(2)}) collective-permute-start(bf16[2,432,384]{2,1,0:T(8,128)(2,1)S(1)} %get-tuple-element.236), channel_id=1, source_target_pairs={{0,4},{1,5},{2,6},{3,7},{4,0},{5,1},{6,2},{7,3},{8,12},{9,13},{10,... | collective-permute-start | bytes 1990664 | tf_op jit(solution)/shard_map/ppermute | solution.py:839
  298.1 15.3 %collective-permute-start.24 = (bf16[2,432,384]{2,1,0:T(8,128)(2,1)S(1)}, bf16[2,432,384]{2,1,0:T(8,128)(2,1)S(1)}, u32[]{:S(2)}, u32[]{:S(2)}) collective-permute-start(bf16[2,432,384]{2,1,0:T(8,128)(2,1)S(1)} %get-tuple-element.237), channel_id=1, source_target_pairs={{0,2},{1,3},{2,0},{3,1},{4,6},{5,7},{6,4},{7,5},{8,10},{9,11},{10,... | collective-permute-start | bytes 1990664 | tf_op jit(solution)/shard_map/ppermute | solution.py:839
  298.7 14.7 %copy-start.6 = (bf16[16,3,48,384]{3,2,1,0:T(8,128)(2,1)S(1)}, bf16[16,3,48,384]{3,2,1,0:T(8,128)(2,1)}, u32[]{:S(2)}) copy-start(bf16[16,3,48,384]{3,2,1,0:T(8,128)(2,1)} %get-tuple-element.224) | copy-start | bytes 5308420
  308.2 7.8 %copy-start.9 = (f32[4,1,768]{2,1,0:T(1,128)S(1)}, f32[4,1,768]{2,1,0:T(1,128)}, u32[]{:S(2)}) copy-start(f32[4,1,768]{2,1,0:T(1,128)} %get-tuple-element.246.refs_6_) | copy-start | bytes 36868
  308.2 7.8 %copy-start.10 = (f32[3,1,768]{2,1,0:T(1,128)S(1)}, f32[3,1,768]{2,1,0:T(1,128)}, u32[]{:S(2)}) copy-start(f32[3,1,768]{2,1,0:T(1,128)} %get-tuple-element.242.refs_2_) | copy-start | bytes 27652
  308.2 7.8 %copy-start.13 = (f32[1,768]{1,0:T(1,128)S(1)}, f32[1,768]{1,0:T(1,128)}, u32[]{:S(2)}) copy-start(f32[1,768]{1,0:T(1,128)} %get-tuple-element.243.refs_3_) | copy-start | bytes 9220
  308.2 7.8 %copy-start.14 = (f32[1,768]{1,0:T(1,128)S(1)}, f32[1,768]{1,0:T(1,128)}, u32[]{:S(2)}) copy-start(f32[1,768]{1,0:T(1,128)} %get-tuple-element.247.refs_7_) | copy-start | bytes 9220
  308.3 7.8 %copy-start.15 = (f32[1,768]{1,0:T(1,128)S(1)}, f32[1,768]{1,0:T(1,128)}, u32[]{:S(2)}) copy-start(f32[1,768]{1,0:T(1,128)} %get-tuple-element.244.refs_4_) | copy-start | bytes 9220
  314.4 12.5 %collective-permute-start.27 = (bf16[2,2,144,384]{3,2,1,0:T(8,128)(2,1)S(1)}, bf16[2,2,144,384]{3,2,1,0:T(8,128)(2,1)S(1)}, u32[]{:S(2)}, u32[]{:S(2)}) collective-permute-start(bf16[2,2,144,384]{3,2,1,0:T(8,128)(2,1)S(1)} %get-tuple-element.249), channel_id=1, source_target_pairs={{0,2},{1,3},{2,0},{3,1},{4,6},{5,7},{6,4},{7,5},{8,10},{9,11},{10,... | collective-permute-start | bytes 1327112 | tf_op jit(solution)/shard_map/ppermute | solution.py:839
  314.9 12.0 %collective-permute-start.28 = (bf16[2,2,144,384]{3,2,1,0:T(8,128)(2,1)S(1)}, bf16[2,2,144,384]{3,2,1,0:T(8,128)(2,1)S(1)}, u32[]{:S(2)}, u32[]{:S(2)}) collective-permute-start(bf16[2,2,144,384]{3,2,1,0:T(8,128)(2,1)S(1)} %get-tuple-element.250), channel_id=1, source_target_pairs={{0,4},{1,5},{2,6},{3,7},{4,0},{5,1},{6,2},{7,3},{8,12},{9,13},{10,... | collective-permute-start | bytes 1327112 | tf_op jit(solution)/shard_map/ppermute | solution.py:839
  316.1 3.5 collective-permute-start.26
  319.6 5.6 %collective-permute-start.29 = (f32[13,768]{1,0:T(8,128)S(1)}, f32[13,768]{1,0:T(8,128)S(1)}, u32[]{:S(2)}, u32[]{:S(2)}) collective-permute-start(f32[13,768]{1,0:T(8,128)S(1)} %add.99), channel_id=1, source_target_pairs={{0,2},{1,3},{2,0},{3,1},{4,6},{5,7},{6,4},{7,5},{8,10},{9,11},{10,... | collective-permute-start | bytes 119816 | tf_op jit(solution)/shard_map/ppermute | solution.py:839
  320.9 17.1 %collective-permute-start.40 = (bf16[432,384]{1,0:T(8,128)(2,1)S(1)}, bf16[432,384]{1,0:T(8,128)(2,1)}, u32[]{:S(2)}, u32[]{:S(2)}) collective-permute-start(bf16[432,384]{1,0:T(8,128)(2,1)S(1)} %get-tuple-element.276), channel_id=1, source_target_pairs={{0,8},{1,9},{2,10},{3,11},{4,12},{5,13},{6,14},{7,15},{8,0},{9,1},... | collective-permute-start | bytes 995336 | tf_op jit(solution)/shard_map/ppermute | solution.py:839
  322.2 17.6 %collective-permute-start.41 = (bf16[432,384]{1,0:T(8,128)(2,1)S(1)}, bf16[432,384]{1,0:T(8,128)(2,1)}, u32[]{:S(2)}, u32[]{:S(2)}) collective-permute-start(bf16[432,384]{1,0:T(8,128)(2,1)S(1)} %get-tuple-element.277), channel_id=1, source_target_pairs={{0,16},{1,17},{2,18},{3,19},{4,20},{5,21},{6,22},{7,23},{8,24},{9,... | collective-permute-start | bytes 995336 | tf_op jit(solution)/shard_map/ppermute | solution.py:839
  325.2 20.3 %collective-permute-start.42 = (bf16[432,384]{1,0:T(8,128)(2,1)S(1)}, bf16[432,384]{1,0:T(8,128)(2,1)}, u32[]{:S(2)}, u32[]{:S(2)}) collective-permute-start(bf16[432,384]{1,0:T(8,128)(2,1)S(1)} %get-tuple-element.278), channel_id=1, source_target_pairs={{0,24},{1,25},{2,26},{3,27},{4,28},{5,29},{6,30},{7,31},{8,16},{9,... | collective-permute-start | bytes 995336 | tf_op jit(solution)/shard_map/ppermute | solution.py:839
  326.9 3.4 collective-permute-start.32
  327.7 5.2 %collective-permute-start.30 = (bf16[2,144,384]{2,1,0:T(8,128)(2,1)S(1)}, bf16[2,144,384]{2,1,0:T(8,128)(2,1)S(1)}, u32[]{:S(2)}, u32[]{:S(2)}) collective-permute-start(bf16[2,144,384]{2,1,0:T(8,128)(2,1)S(1)} %get-tuple-element.256), channel_id=1, source_target_pairs={{0,4},{1,5},{2,6},{3,7},{4,0},{5,1},{6,2},{7,3},{8,12},{9,13},{10,... | collective-permute-start | bytes 663560 | tf_op jit(solution)/shard_map/ppermute | solution.py:839
  330.3 5.2 %collective-permute-start.31 = (bf16[2,144,384]{2,1,0:T(8,128)(2,1)S(1)}, bf16[2,144,384]{2,1,0:T(8,128)(2,1)S(1)}, u32[]{:S(2)}, u32[]{:S(2)}) collective-permute-start(bf16[2,144,384]{2,1,0:T(8,128)(2,1)S(1)} %get-tuple-element.257), channel_id=1, source_target_pairs={{0,2},{1,3},{2,0},{3,1},{4,6},{5,7},{6,4},{7,5},{8,10},{9,11},{10,... | collective-permute-start | bytes 663560 | tf_op jit(solution)/shard_map/ppermute | solution.py:839
  335.5 20.4 %collective-permute-start.36 = (f32[13,768]{1,0:T(8,128)S(1)}, f32[13,768]{1,0:T(8,128)S(1)}, u32[]{:S(2)}, u32[]{:S(2)}) collective-permute-start(f32[13,768]{1,0:T(8,128)S(1)} %add.101), channel_id=1, source_target_pairs={{0,8},{1,9},{2,10},{3,11},{4,12},{5,13},{6,14},{7,15},{8,0},{9,1},... | collective-permute-start | bytes 119816 | tf_op jit(solution)/shard_map/ppermute | solution.py:839
  335.9 23.0 %collective-permute-start.37 = (f32[13,768]{1,0:T(8,128)S(1)}, f32[13,768]{1,0:T(8,128)S(1)}, u32[]{:S(2)}, u32[]{:S(2)}) collective-permute-start(f32[13,768]{1,0:T(8,128)S(1)} %add.101), channel_id=1, source_target_pairs={{0,16},{1,17},{2,18},{3,19},{4,20},{5,21},{6,22},{7,23},{8,24},{9,... | collective-permute-start | bytes 119816 | tf_op jit(solution)/shard_map/ppermute | solution.py:839
  338.1 24.7 %collective-permute-start.38 = (f32[13,768]{1,0:T(8,128)S(1)}, f32[13,768]{1,0:T(8,128)S(1)}, u32[]{:S(2)}, u32[]{:S(2)}) collective-permute-start(f32[13,768]{1,0:T(8,128)S(1)} %add.101), channel_id=1, source_target_pairs={{0,24},{1,25},{2,26},{3,27},{4,28},{5,29},{6,30},{7,31},{8,16},{9,... | collective-permute-start | bytes 119816 | tf_op jit(solution)/shard_map/ppermute | solution.py:839
  339.8 23.0 %collective-permute-start.33 = (bf16[144,384]{1,0:T(8,128)(2,1)S(1)}, bf16[144,384]{1,0:T(8,128)(2,1)S(1)}, u32[]{:S(2)}, u32[]{:S(2)}) collective-permute-start(bf16[144,384]{1,0:T(8,128)(2,1)S(1)} %get-tuple-element.263), channel_id=1, source_target_pairs={{0,8},{1,9},{2,10},{3,11},{4,12},{5,13},{6,14},{7,15},{8,0},{9,1},... | collective-permute-start | bytes 331784 | tf_op jit(solution)/shard_map/ppermute | solution.py:839
  345.4 17.3 %collective-permute-start.34 = (bf16[144,384]{1,0:T(8,128)(2,1)S(1)}, bf16[144,384]{1,0:T(8,128)(2,1)S(1)}, u32[]{:S(2)}, u32[]{:S(2)}) collective-permute-start(bf16[144,384]{1,0:T(8,128)(2,1)S(1)} %get-tuple-element.264), channel_id=1, source_target_pairs={{0,16},{1,17},{2,18},{3,19},{4,20},{5,21},{6,22},{7,23},{8,24},{9,... | collective-permute-start | bytes 331784 | tf_op jit(solution)/shard_map/ppermute | solution.py:839
  355.8 7.0 %collective-permute-start.35 = (bf16[144,384]{1,0:T(8,128)(2,1)S(1)}, bf16[144,384]{1,0:T(8,128)(2,1)S(1)}, u32[]{:S(2)}, u32[]{:S(2)}) collective-permute-start(bf16[144,384]{1,0:T(8,128)(2,1)S(1)} %get-tuple-element.265), channel_id=1, source_target_pairs={{0,24},{1,25},{2,26},{3,27},{4,28},{5,29},{6,30},{7,31},{8,16},{9,... | collective-permute-start | bytes 331784 | tf_op jit(solution)/shard_map/ppermute | solution.py:839
  357.5 15.0 %copy-start.1 = (bf16[48,3072]{1,0:T(8,128)(2,1)S(1)}, bf16[48,3072]{1,0:T(8,128)(2,1)}, u32[]{:S(2)}) copy-start(bf16[48,3072]{1,0:T(8,128)(2,1)} %param.26) | copy-start | bytes 884740
  358.9 11.6 %collective-permute-start.43 = (f32[432,384]{1,0:T(8,128)S(1)}, f32[432,384]{1,0:T(8,128)S(1)}, u32[]{:S(2)}, u32[]{:S(2)}) collective-permute-start(f32[432,384]{1,0:T(8,128)S(1)} %convert_add_fusion.half_ref), channel_id=1, source_target_pairs={{0,1},{1,0},{2,3},{3,2},{4,5},{5,4},{6,7},{7,6},{8,9},{9,8},{10,11... | collective-permute-start | bytes 1990664 | tf_op jit(solution)/shard_map/ppermute | solution.py:839
  362.9 8.7 %collective-permute-start.39 = (f32[144,384]{1,0:T(8,128)S(1)}, f32[144,384]{1,0:T(8,128)S(1)}, u32[]{:S(2)}, u32[]{:S(2)}) collective-permute-start(f32[144,384]{1,0:T(8,128)S(1)} %convert_add_fusion.1.half_ref), channel_id=1, source_target_pairs={{0,1},{1,0},{2,3},{3,2},{4,5},{5,4},{6,7},{7,6},{8,9},{9,8},{10,11... | collective-permute-start | bytes 663560 | tf_op jit(solution)/shard_map/ppermute | solution.py:839
  (18 other events, 81.9 us)
Sparse Core Ops, SparseCore 0:
  11.6 89.5 all-gather.2

commit v4 on v3

--- a/solution.py
+++ b/solution.py
@@ -240,10 +240,9 @@
 def mlp_forward_kernel(
     hidden_ref, normed_ref, fc_ref, fbias_ref, proj_ref, pbias_ref, expanded_ref, state_ref
 ):
-    step = pl.program_id(0)
     chunk = 256
 
-    @pl.when(step == 0)
+    @pl.when(pl.program_id(0) == 0)
     def _():
         state_ref[...] = hidden_ref[...] + pbias_ref[...]
 
@@ -530,7 +529,7 @@
         compiler_params=params(54 << 20),
         cost_estimate=cost(8 * rows * width * blocks * block, rows * blocks * block, *inputs, *outs),
         name="mlp_backward",
-    )(core, grad, *in_hbm(inputs[1:]))
+    )(core, *in_hbm(inputs))
 
 
 def input_gradient(
@@ -673,7 +672,7 @@
     vector = pl.BlockSpec((1, width), lambda i: (0, 0))
     outs = (
         pltpu.HBM((rows, 3 * width), jnp.bfloat16),
-        jax.ShapeDtypeStruct((rows, width), jnp.float32),
+        pltpu.HBM((rows, width), jnp.float32),
         jax.ShapeDtypeStruct((1, width), jnp.float32),
         jax.ShapeDtypeStruct((1, width), jnp.float32),
     )
@@ -712,15 +711,16 @@
     earlier = rest[:3] if more else (None,) * 3
     if more:
         rest = rest[3:]
-    mine_ref, theirs_ref, dbias_ref, right_ref = rest
+    mine_ref, theirs_ref, dbias_ref = rest
     core = core_ref[0]
-    for index, gmix_ref in enumerate(gmix_refs):
-        count = gmix_ref.shape[0]
-        right_ref[index * count : (index + 1) * count] = gmix_ref[...]
-    right = right_ref[...]
-    dbias = jnp.sum(right.astype(jnp.float32), axis=0, keepdims=True)
+    terms, dbias, start = (0.0, 0.0, 0)
+    for gmix_ref in gmix_refs:
+        right = gmix_ref[...]
+        stop = start + right.shape[0]
+        terms = terms + transposed_dot(normed_ref[start:stop], right)
+        dbias = dbias + jnp.sum(right.astype(jnp.float32), axis=0, keepdims=True)
+        start = stop
     dbias_ref[0] = dbias + earlier[2][0] if more else dbias
-    terms = transposed_dot(normed_ref[...], right)
     store_halves(core, terms, mine_ref, theirs_ref, earlier[:2] if more else None)
 
 
@@ -746,7 +746,6 @@
         out_shape=outs,
         in_specs=[SMEM] + specs,
         out_specs=summed,
-        scratch_shapes=[pltpu.VMEM((rows, width), jnp.bfloat16)],
         compiler_params=params(),
         cost_estimate=cost(6 * rows * width * width, 0, *inputs, *outs),
         name="attention_terms",
@@ -930,8 +929,8 @@
 
 
 def first_sums_kernel(views, spot_ref, *refs):
-    mine, got = (refs[:views], refs[views : 2 * views])
-    near_sent, far_sent, near_kept, far_kept = refs[2 * views :]
+    mine, got, alone = (refs[:views], refs[views : 2 * views], refs[2 * views : -4])
+    near_sent, far_sent, near_kept, far_kept = refs[-4:]
     z_pair, y, x = (spot_ref[0], spot_ref[2], spot_ref[3])
     for low_z in range(2):
         for other in range(2):
@@ -948,6 +947,8 @@
                         left[device], right[device]
                     ).astype(jnp.bfloat16)
                     start += count
+                for only in alone:
+                    out[low_z, other, start:] = only[device]
 
 
 def second_sums_kernel(spot_ref, near, far, near_in, far_in, *outs):
@@ -972,6 +973,8 @@
 
 
 def assemble_kernel(layouts, core_ref, half_ref, other_ref, *outs):
+    if len(outs) > len(layouts):
+        outs[-1][...] = half_ref[-16:] + other_ref[-16:]
     core = core_ref[0]
     half, other = (half_ref[...], other_ref[...])
     left = jnp.where(core == 0, half, other)
@@ -986,17 +989,33 @@
             start += rows
 
 
-def pack_rows_kernel(unused_ref, *refs):
-    *parts, out = refs
-    start = 0
-    for part in parts:
-        if len(part.shape) == 2:
-            out[start : start + 1] = part[...]
-            start += 1
-        else:
-            for index in range(part.shape[0]):
-                out[start : start + 1] = part[index]
-                start += 1
+SMALL_ROWS = ((48, 48, 144, 48, 48, 48), (192, 48))
+
+
+def pack_small_kernel(unused_ref, *refs):
+    *vectors, out = refs
+    width = out.shape[2]
+    device = lax.broadcasted_iota(jnp.int32, (16, 1), 0)
+    rows, vectors = ([], iter(vectors))
+    for sizes in SMALL_ROWS:
+        row, start = (jnp.zeros((16, width), jnp.float32), 0)
+        for size, ref in zip(sizes, vectors):
+            if len(ref.shape) == 2:
+                vector = ref[...]
+            else:
+                vector = jnp.concatenate([ref[i] for i in range(ref.shape[0])], axis=1)
+            column = lax.broadcasted_iota(jnp.int32, (1, 16 * size), 1)
+            parts = jnp.where(column // size == device, vector, 0.0).astype(jnp.bfloat16)
+            place_in = lax.broadcasted_iota(jnp.int32, (16 * size, width), 0) % size + start
+            lane = lax.broadcasted_iota(jnp.int32, (16 * size, width), 1)
+            row = row + dot(parts, (place_in == lane).astype(jnp.bfloat16))
+            start += size
+        rows.append(row)
+    line = lax.broadcasted_iota(jnp.int32, out.shape[1:], 0)
+    for d in range(16):
+        first, second = (rows[0][d : d + 1], rows[1][d : d + 1])
+        value = jnp.where(line == 0, first, jnp.where(line == 1, second, 0.0))
+        out[d] = value.astype(jnp.bfloat16)
 
 
 def in_vmem(kernel, name, outs, *args):
@@ -1017,11 +1036,12 @@
         self.spot = spot
         self.mine = list(mine)
         self.got = [swap(part, CORE) for part in theirs]
-        self.count = sum(part.shape[1] for part in self.mine)
+        self.alone = []
         self.width = self.mine[0].shape[2]
 
     def like(self, *lead, kind=jnp.bfloat16):
-        return jax.ShapeDtypeStruct((*lead, self.count, self.width), kind)
+        count = sum(part.shape[1] for part in (*self.mine, *self.alone))
+        return jax.ShapeDtypeStruct((*lead, count, self.width), kind)
 
     def first(self):
         near_sent, far_sent, *self.kept = in_vmem(
@@ -1031,6 +1051,7 @@
             self.spot,
             *self.mine,
             *self.got,
+            *self.alone,
         )
         self.got = [swap(near_sent, X), swap(far_sent, Y)]
         return self.kept
@@ -1064,18 +1085,11 @@
             jax.ShapeDtypeStruct((rows, 2 * self.width * blocks), jnp.float32)
             for blocks, rows in layouts
         ]
+        if self.alone:
+            outs.append(jax.ShapeDtypeStruct((16, self.width), jnp.float32))
         return in_vmem(
             functools.partial(assemble_kernel, layouts), "assemble", outs, core, *self.kept, *self.got
         )
-
-
-def own_small(small, dp):
-    def own(start, rows):
-        vector = small[start : start + rows].reshape(-1)
-        size = vector.shape[0] // 16
-        return lax.dynamic_slice_in_dim(vector, dp * size, size)
-
-    return [own(0, 1), own(1, 1), own(2, 3), own(5, 1), own(6, 1), own(7, 1), own(8, 4), own(12, 1)]
 
 
 def gather_all(weights, spot, me):
@@ -1188,7 +1202,7 @@
             gmix, grad, *norm = attention_backward_all(
                 lengths, dhid, count, back, att, mixed, lse, weight, before, gain_a
             )
-            delayed = functools.partial(attention_terms, side, normed_a, [gmix])
+            delayed = functools.partial(attention_terms, side, normed_a, in_hbm([gmix]))
             continue
         gmix = [
             attention_backward(index, lengths, dhid, count, back, att, mixed, lse, weight)
@@ -1203,34 +1217,28 @@
             gmix = after(gmix, sums.second())
         grad, *norm = attention_input(dhid, before, gmix, weight, gain_a, jnp.bfloat16, norm)
         if sending:
-            sums.got, qkv_sums.got, norm = lax.optimization_barrier(
-                (sums.got, qkv_sums.got, norm)
-            )
+            sums.got, qkv_sums.got = after((sums.got, qkv_sums.got), norm)
     small = (norm[0], norm[1], terms[2], mlp_terms[6], mlp_terms[9], mlp_terms[10])
     small += (mlp_terms[7], mlp_terms[8])
     if custom:
-        (small,) = in_vmem(
-            pack_rows_kernel, "pack_rows", [jax.ShapeDtypeStruct((13, width), jnp.float32)], side, *small
-        )
+        packed = jax.ShapeDtypeStruct((16, 16, width // 2), jnp.bfloat16)
+        qkv_sums.alone = in_vmem(pack_small_kernel, "pack_small", [packed], side, *small)
+        sums.got = after(sums.got, qkv_sums.alone)
+        qkv_sums.got = after(qkv_sums.got, sums.third())
         qkv_sums.first()
-        sums.third()
-        small = small + swap(small, CORE)
-        got = swap(small, X)
-        qkv_sums.got, got = lax.optimization_barrier((qkv_sums.got, got))
         qkv_sums.second()
-        small = small + got
-        got = swap(small, Y)
-        qkv_sums.got, got = lax.optimization_barrier((qkv_sums.got, got))
-        qkv_sums.third()
-        small = small + got
-        got = [swap(small, bits) for bits in (Z1, Z2, Z3)]
+        sums.got = after(sums.got, qkv_sums.third())
         sums.fourth()
-        qkv_sums.got, got = lax.optimization_barrier((qkv_sums.got, got))
         qkv_sums.fourth()
         fc, proj, out = sums.whole(side, ((4, 48), (1, 192), (1, 48)))
-        (qkv,) = qkv_sums.whole(side, ((3, 48),))
-        small = own_small(total(small, *got), dp)
-        gain_a, shift_a, qbias, obias, gain_m, shift_m, fbias, pbias = small
+        qkv, small = qkv_sums.whole(side, ((3, 48),))
+        parts = []
+        for row, sizes in enumerate(SMALL_ROWS):
+            start = 0
+            for size in sizes:
+                parts.append(small[row, start : start + size])
+                start += size
+        gain_a, shift_a, qbias, obias, gain_m, shift_m, fbias, pbias = parts
         final = (
             gain_a, shift_a, qkv, qbias, out, obias, gain_m, shift_m, fc, fbias, proj, pbias
         )

time: 383 us -> 374 us (0.977)
  starting transfers between devices: 72.3 us -> 65.2 us
  local copies, waits for them, and re-layouts: 11.3 us -> 6.09 us
  Pallas kernels: 230 us -> 234 us
    ppermute x44 -> x38, starting transfers between devices: 72.3 us -> 65.1 us  [swap(): return lax.ppermute(value, BOTH, [(i, i ^ bits) for i in range(32)])]
    unnamed x80 -> x76, local copies, waits for them, and re-layouts: 6.13 us -> 2.16 us
    ppermute x44 -> x38, waiting for transfers between devices: 40 us -> 39.9 us  [swap(): return lax.ppermute(value, BOTH, [(i, i ^ bits) for i in range(32)])]
  transfers between devices with their start and end apart: 45 -> 39, of which waited for: 15 -> 15; matrix products, arithmetic and copies ran while one was open for 1% -> 1% of each run, Pallas kernels for 21% -> 22%
where the time goes in v4:
time: 374 us; the launch traced here: 370 us
  Pallas kernels  234 us (63%)
  starting transfers between devices  65.2 us (17%)
  waiting for transfers between devices  49.1 us (13%)
  between operations  15.1 us (4%)
  local copies, waits for them, and re-layouts  6.09 us (2%)
    pallas_call x2, Pallas kernels, mlp_backward(): pl.pallas_call(functools.partial(mlp_backward_kernel, earlier is not None...  81.4 us
    ppermute x38, starting transfers between devices, swap(): return lax.ppermute(value, BOTH, [(i, i ^ bits) for i in range(32)])  65.1 us
    pallas_call x2, Pallas kernels, attention_forward(): pl.pallas_call(functools.partial(attention_forward_kernel, docs, back), g...  40.5 us
    ppermute x38, waiting for transfers between devices, swap(): return lax.ppermute(value, BOTH, [(i, i ^ bits) for i in range(32)])  39.9 us
    pallas_call x1, Pallas kernels, attention_backward_all(): pl.pallas_call(functools.partial(attention_backward_kernel, docs, back, N...  27.9 us
    pallas_call x2, Pallas kernels, attention_backward(): pl.pallas_call(functools.partial(attention_backward_kernel, docs, back, m...  21 us
    pallas_call x1, Pallas kernels, mlp_forward(): pl.pallas_call(mlp_forward_kernel, grid=(hidden_units // block,), out_sha...  17.1 us
    pallas_call x2, Pallas kernels, attention_terms(): pl.pallas_call(functools.partial(attention_terms_kernel, earlier is not N...  16 us
  transfers between devices with their start and end apart: 39, of which 15 were waited for; matrix products, arithmetic and copies ran while one was open for 1% of the time, Pallas kernels for 22%

profile of v4, /device:TPU:1, one launch (start us, length us, event | category | flops | bytes accessed | tf_op | source)
XLA Modules:
  0.0 369.7 jit_solution(3663097491573314569)
XLA Ops:
  7.4 0.8 copy-done
  8.2 0.9 constant_dynamic-slice_fusion
  9.6 0.7 copy.36
  10.5 2.2 collective-permute-start
  12.7 2.3 collective-permute-start.1
  15.7 3.2 collective-permute-start.4
  18.9 3.1 collective-permute-done.3
  21.9 1.9 collective-permute-start.5
  23.8 6.2 %collective-permute-done.4 = bf16[1,8,256]{2,1,0:T(8,128)(2,1)S(1)} collective-permute-done((bf16[1,8,256]{2,1,0:T(8,128)(2,1)S(1)}, bf16[1,8,256]{2,1,0:T(8,128)(2,1)S(1)}, u32[]{:S(2)}, u32[]{:S(2)}) %collective-permute-start.4) | collective-permute-done | bytes 4128 | tf_op jit(solution)/shard_map/ppermute | solution.py:838
  30.1 1.3 collective-permute-start.6
  31.4 1.3 collective-permute-start.7
  32.7 5.3 %collective-permute-start.8 = (bf16[4,4,24,768]{3,2,1,0:T(8,128)(2,1)S(1)}, bf16[4,4,24,768]{3,2,1,0:T(8,128)(2,1)S(1)}, u32[]{:S(2)}, u32[]{:S(2)}) collective-permute-start(bf16[4,4,24,768]{3,2,1,0:T(8,128)(2,1)S(1)} %constant_dynamic-update-slice_fusion.4.refs_0_), channel_id=1, source_target_pairs={{0,1},{1,0},{2,3},{3,2},{4,5},{5,4},{6,7},{7,6},{8,9},{9,8},{10,11... | collective-permute-start | bytes 1769480 | tf_op jit(solution)/shard_map/ppermute | solution.py:838
  38.4 3.4 collective-permute-done.10.refs_2_
  41.9 9.9 %collective-permute-start.13 = (bf16[4,4,24,768]{3,2,1,0:T(8,128)(2,1)S(1)}, bf16[4,4,24,768]{3,2,1,0:T(8,128)(2,1)S(1)}, u32[]{:S(2)}, u32[]{:S(2)}) collective-permute-start(bf16[4,4,24,768]{3,2,1,0:T(8,128)(2,1)S(1)} %collective-permute-done.6.refs_1_), channel_id=1, source_target_pairs={{0,1},{1,0},{2,3},{3,2},{4,5},{5,4},{6,7},{7,6},{8,9},{9,8},{10,11... | collective-permute-start | bytes 1769480 | tf_op jit(solution)/shard_map/ppermute | solution.py:838
  52.3 2.1 collective-permute-start.11
  54.4 1.1 collective-permute-start.12
  55.6 6.6 %collective-permute-done.15.refs_3_ = bf16[4,8,256]{2,1,0:T(8,128)(2,1)S(1)} collective-permute-done((bf16[4,8,256]{2,1,0:T(8,128)(2,1)S(1)}, bf16[4,8,256]{2,1,0:T(8,128)(2,1)S(1)}, u32[]{:S(2)}, u32[]{:S(2)}) %collective-permute-start.15) | collective-permute-done | bytes 16416 | tf_op jit(solution)/shard_map/ppermute | solution.py:838
  62.8 1.2 collective-permute-start.16
  64.1 2.7 place_small.1
  66.8 5.5 %place.1 = bf16[4,32,24,768]{3,2,1,0:T(8,128)(2,1)} custom-call(s32[1]{0:T(128)} %bitcast.4.me_ref, bf16[4,4,24,768]{3,2,1,0:T(8,128)(2,1)} %copy-done.17, bf16[4,4,24,768]{3,2,1,0:T(8,128)(2,1)} %copy-done.15, bf16[4,4,24,768]{3,2,1,0:T(8,128)(2,1)} %copy-done.16, bf16[2,4,24,768]{3,2,1,0:T(8,128)(2,1)} %collective-permute-done.11.refs_3_, ...), custom_call_target="tpu_custom_call" | custom-call | tf_op jit(solution)/shard_map/place/pallas_call | solution.py:862
  72.3 19.7 %attention_forward.2 = (bf16[1024,768]{1,0:T(8,128)(2,1)}, bf16[1024,2304]{1,0:T(8,128)(2,1)}, bf16[1024,768]{1,0:T(8,128)(2,1)}, f32[24,1,512]{2,1,0:T(1,128)},...) custom-call(s32[2,6]{1,0:T(2,128)S(1)} %bitcast.50, bf16[1024,768]{1,0:T(8,128)(2,1)} %bitcast.67, ...), custom_call_target="tpu_custom_call" | custom-call | flops 805306368 | bytes 2368512 | tf_op jit(solution)/shard_map/attention_forward/pallas_call | solution.py:205
  92.0 9.2 %all-gather.3.cloned.1.call-done = bf16[128,48,768]{2,1,0:T(8,128)(2,1)} async-done(((bf16[4,48,768]{2,1,0:T(8,128)(2,1)}), bf16[128,48,768]{2,1,0:T(8,128)(2,1)}) %all-gather.3.cloned.1.call-update) | async-done | bytes 9437200 | tf_op jit(solution)/shard_map/all_gather | solution.py:1106
  101.2 17.1 %mlp_forward.1 = (bf16[1024,3072]{1,0:T(8,128)(2,1)}, f32[1024,768]{1,0:T(8,128)}) custom-call(f32[1024,768]{1,0:T(8,128)} %get-tuple-element.166.hidden_ref, bf16[1024,768]{1,0:T(8,128)(2,1)} %get-tuple-element.167.normed_ref, bf16[16,2,4,48,768]{4,3,2,1,0:T(8,128)(2,1)} %bitcast.55, f32[1,3072]{1,0:T(1,128)} %get-tuple-element.168.fbias_ref.rest_0_, ...), custom_call_target="tpu_custom_call" | custom-call | flops 1207959552 | bytes 2949120 | tf_op jit(solution)/shard_map/mlp_forward/pallas_call | solution.py:286
  118.3 20.8 %attention_forward.3 = (bf16[1024,768]{1,0:T(8,128)(2,1)}, bf16[1024,2304]{1,0:T(8,128)(2,1)}, bf16[1024,768]{1,0:T(8,128)(2,1)}, f32[24,1,512]{2,1,0:T(1,128)},...) custom-call(s32[2,6]{1,0:T(2,128)S(1)} %bitcast.51, f32[1024,768]{1,0:T(8,128)} %get-tuple-element.170.state_ref.rest_0_, ...), custom_call_target="tpu_custom_call" | custom-call | flops 805306368 | bytes 2565120 | tf_op jit(solution)/shard_map/attention_forward/pallas_call | solution.py:205
  139.1 45.0 %mlp_backward.2 = (bf16[1024,768]{1,0:T(8,128)(2,1)}, f32[1024,768]{1,0:T(8,128)}, bf16[16,4,48,384]{3,2,1,0:T(8,128)(2,1)}, bf16[16,4,48,384]{3,2,1,0:T(8,128)(...) custom-call(s32[1]{0:T(128)} %bitcast.core_ref.unused_ref, ...), custom_call_target="tpu_custom_call" | custom-call | flops 2415919104 | bytes 5264640 | tf_op jit(solution)/shard_map/mlp_backward/pallas_call | solution.py:512
  184.1 27.9 %attention_backward_all.1 = (bf16[1024,2304]{1,0:T(8,128)(2,1)}, f32[1024,768]{1,0:T(8,128)}, f32[1,768]{1,0:T(1,128)S(1)}, f32[1,768]{1,0:T(1,128)S(1)}) custom-call(s32[2,6]{1,0:T(2,128)S(1)} %bitcast.52, f32[1024,768]{1,0:T(8,128)} %get-tuple-element.175.dhid_ref, bf16[1024,768]{1,0:T(8,128)(2,1)} %get-tuple-element.173.att_ref, ...), custom_call_target="tpu_custom_call" | custom-call | flops 1107296256 | bytes 3153024 | tf_op jit(solution)/shard_map/attention_backward_all/pallas_call | solution.py:680
  213.1 36.5 %mlp_backward.3 = (f32[1024,768]{1,0:T(8,128)}, bf16[16,4,48,384]{3,2,1,0:T(8,128)(2,1)}, bf16[16,4,48,384]{3,2,1,0:T(8,128)(2,1)}, bf16[3072,384]{1,0:T(8,128)(...) custom-call(s32[1]{0:T(128)} %bitcast.core_ref.unused_ref, ...), custom_call_target="tpu_custom_call" | custom-call | flops 2415919104 | bytes 7379328 | tf_op jit(solution)/shard_map/mlp_backward/pallas_call | solution.py:512
  250.5 8.2 %attention_terms.2 = (bf16[16,3,48,384]{3,2,1,0:T(8,128)(2,1)}, bf16[16,3,48,384]{3,2,1,0:T(8,128)(2,1)}, f32[3,1,768]{2,1,0:T(1,128)}) custom-call(s32[1]{0:T(128)} %bitcast.core_ref.unused_ref, bf16[1024,768]{1,0:T(8,128)(2,1)} %get-tuple-element.199.normed_ref, bf16[1024,2304]{1,0:T(8,128)(2,1)} %get-tuple-element.200.rest_0_), custom_call_target="tpu_custom_call" | custom-call | flops 452984832 | bytes 1229952 | tf_op jit(solution)/shard_map/attention_terms/pallas_call | solution.py:743
  258.8 3.1 first_sums.2
  261.8 1.2 collective-permute-start.21
  263.4 10.4 %attention_backward.3.rest_1_ = bf16[512,2304]{1,0:T(8,128)(2,1)S(1)} custom-call(s32[2,6]{1,0:T(2,128)S(1)} %bitcast.53, f32[1024,768]{1,0:T(8,128)} %get-tuple-element.209.dhid_ref, bf16[1024,768]{1,0:T(8,128)(2,1)} %get-tuple-element.179.att_ref, bf16[1024,2304]{1,0:T(8,128)(2,1)} %get-tuple-element.210.mixed_ref, ...), custom_call_target="tpu_custom_call" | custom-call | flops 327155712 | bytes 589824 | tf_op jit(solution)/shard_map/attention_backward/pallas_call | solution.py:642
  273.8 10.6 %attention_backward.2.rest_0_ = bf16[512,2304]{1,0:T(8,128)(2,1)S(1)} custom-call(s32[2,6]{1,0:T(2,128)S(1)} %bitcast.54, f32[1024,768]{1,0:T(8,128)} %get-tuple-element.209.dhid_ref, bf16[1024,768]{1,0:T(8,128)(2,1)} %get-tuple-element.179.att_ref, bf16[1024,2304]{1,0:T(8,128)(2,1)} %get-tuple-element.210.mixed_ref, ...), custom_call_target="tpu_custom_call" | custom-call | flops 327155712 | bytes 589824 | tf_op jit(solution)/shard_map/attention_backward/pallas_call | solution.py:642
  284.4 7.8 %attention_terms.3 = (bf16[16,3,48,384]{3,2,1,0:T(8,128)(2,1)}, bf16[16,3,48,384]{3,2,1,0:T(8,128)(2,1)}, f32[3,1,768]{2,1,0:T(1,128)}) custom-call(s32[1]{0:T(128)} %bitcast.core_ref.unused_ref, bf16[1024,768]{1,0:T(8,128)(2,1)} %get-tuple-element.214.normed_ref, bf16[512,2304]{1,0:T(8,128)(2,1)S(1)} %attention_backward.2.rest_0_, ...), custom_call_target="tpu_custom_call" | custom-call | flops 452984832 | bytes 1673472 | tf_op jit(solution)/shard_map/attention_terms/pallas_call | solution.py:743
  292.1 0.8 collective-permute-start.25
  293.2 1.2 second_sums.2
  294.4 0.9 collective-permute-start.23
  295.3 0.7 collective-permute-start.24
  296.0 9.6 %attention_input.1 = (bf16[1024,768]{1,0:T(8,128)(2,1)}, f32[1,768]{1,0:T(1,128)S(1)}, f32[1,768]{1,0:T(1,128)S(1)}) custom-call(f32[1024,768]{1,0:T(8,128)} %get-tuple-element.209.dhid_ref, bf16[1024,768]{1,0:T(8,128)(2,1)} %bitcast.68, bf16[4,768,768]{2,1,0:T(8,128)(2,1)} %bitcast.66, f32[1,768]{1,0:T(1,128)} %get-tuple-element.155.gain_ref.rest_1_, ...), custom_call_target="tpu_custom_call" | custom-call | flops 452984832 | bytes 1968000 | tf_op jit(solution)/shard_map/attention_input/pallas_call | solution.py:796
  305.7 2.7 pack_small.1.refs_2_
  308.4 1.1 collective-permute-done.23.near_in
  309.5 1.1 collective-permute-done.24.far_in
  310.6 0.9 third_sums.2
  311.5 1.0 first_sums.3
  313.0 1.1 collective-permute-start.27
  314.1 1.2 collective-permute-start.34
  315.3 0.7 collective-permute-start.35
  316.0 1.7 collective-permute-start.36
  317.7 5.5 %collective-permute-done.26.near_in = bf16[2,2,160,384]{3,2,1,0:T(8,128)(2,1)S(1)} collective-permute-done((bf16[2,2,160,384]{3,2,1,0:T(8,128)(2,1)S(1)}, bf16[2,2,160,384]{3,2,1,0:T(8,128)(2,1)S(1)}, u32[]{:S(2)}, u32[]{:S(2)}) %collective-permute-start.26) | collective-permute-done | bytes 491552 | tf_op jit(solution)/shard_map/ppermute | solution.py:838
  323.2 0.8 second_sums.3
  324.0 1.4 collective-permute-start.28
  325.7 3.7 collective-permute-done.28.near_in
  329.4 1.4 collective-permute-done.29.far_in
  330.8 0.7 third_sums.3
  331.4 5.0 %collective-permute-done.36 = bf16[432,384]{1,0:T(8,128)(2,1)S(1)} collective-permute-done((bf16[432,384]{1,0:T(8,128)(2,1)S(1)}, bf16[432,384]{1,0:T(8,128)(2,1)S(1)}, u32[]{:S(2)}, u32[]{:S(2)}) %collective-permute-start.36) | collective-permute-done | bytes 331808 | tf_op jit(solution)/shard_map/ppermute | solution.py:838
  336.4 7.9 %collective-permute-start.30 = (bf16[160,384]{1,0:T(8,128)(2,1)S(1)}, bf16[160,384]{1,0:T(8,128)(2,1)S(1)}, u32[]{:S(2)}, u32[]{:S(2)}) collective-permute-start(bf16[160,384]{1,0:T(8,128)(2,1)S(1)} %get-tuple-element.256), channel_id=1, source_target_pairs={{0,8},{1,9},{2,10},{3,11},{4,12},{5,13},{6,14},{7,15},{8,0},{9,1},... | collective-permute-start | bytes 368648 | tf_op jit(solution)/shard_map/ppermute | solution.py:838
  344.8 1.6 collective-permute-start.32
  346.6 4.3 %collective-permute-start.37 = (f32[432,384]{1,0:T(8,128)S(1)}, f32[432,384]{1,0:T(8,128)S(1)}, u32[]{:S(2)}, u32[]{:S(2)}) collective-permute-start(f32[432,384]{1,0:T(8,128)S(1)} %convert_add_fusion.half_ref), channel_id=1, source_target_pairs={{0,1},{1,0},{2,3},{3,2},{4,5},{5,4},{6,7},{7,6},{8,9},{9,8},{10,11... | collective-permute-start | bytes 1990664 | tf_op jit(solution)/shard_map/ppermute | solution.py:838
  350.9 0.8 collective-permute-done.31
  351.8 6.0 %collective-permute-start.33 = (f32[160,384]{1,0:T(8,128)S(1)}, f32[160,384]{1,0:T(8,128)S(1)}, u32[]{:S(2)}, u32[]{:S(2)}) collective-permute-start(f32[160,384]{1,0:T(8,128)S(1)} %convert_add_fusion.1.half_ref), channel_id=1, source_target_pairs={{0,1},{1,0},{2,3},{3,2},{4,5},{5,4},{6,7},{7,6},{8,9},{9,8},{10,11... | collective-permute-start | bytes 737288 | tf_op jit(solution)/shard_map/ppermute | solution.py:838
  357.7 1.1 collective-permute-done.33.other_ref
  358.9 0.8 assemble.2
  359.6 0.6 slice.34
  360.8 0.6 slice_bitcast_fusion
  361.4 1.1 assemble.3
  (150 shorter events, 7.7 us)
Async XLA Ops:
  7.2 7.7 %copy-start.27 = (bf16[48]{0:T(256)(128)(2,1)S(1)}, bf16[48]{0:T(256)(128)(2,1)}, u32[]{:S(2)}) copy-start(bf16[48]{0:T(256)(128)(2,1)} %param.18) | copy-start | bytes 292
  7.2 7.8 %copy-start.28 = (bf16[48]{0:T(256)(128)(2,1)S(1)}, bf16[48]{0:T(256)(128)(2,1)}, u32[]{:S(2)}) copy-start(bf16[48]{0:T(256)(128)(2,1)} %param.19) | copy-start | bytes 292
  7.2 7.8 %copy-start.29 = (bf16[144]{0:T(256)(128)(2,1)S(1)}, bf16[144]{0:T(256)(128)(2,1)}, u32[]{:S(2)}) copy-start(bf16[144]{0:T(256)(128)(2,1)} %param.21) | copy-start | bytes 868
  7.3 7.8 %copy-start.30 = (bf16[48]{0:T(256)(128)(2,1)S(1)}, bf16[48]{0:T(256)(128)(2,1)}, u32[]{:S(2)}) copy-start(bf16[48]{0:T(256)(128)(2,1)} %param.23) | copy-start | bytes 292
  7.3 7.8 %copy-start.31 = (bf16[48]{0:T(256)(128)(2,1)S(1)}, bf16[48]{0:T(256)(128)(2,1)}, u32[]{:S(2)}) copy-start(bf16[48]{0:T(256)(128)(2,1)} %param.24) | copy-start | bytes 292
  7.3 7.9 %copy-start.32 = (bf16[48]{0:T(256)(128)(2,1)S(1)}, bf16[48]{0:T(256)(128)(2,1)}, u32[]{:S(2)}) copy-start(bf16[48]{0:T(256)(128)(2,1)} %param.25) | copy-start | bytes 292
  7.3 7.9 %copy-start.33 = (bf16[192]{0:T(256)(128)(2,1)S(1)}, bf16[192]{0:T(256)(128)(2,1)}, u32[]{:S(2)}) copy-start(bf16[192]{0:T(256)(128)(2,1)} %param.27) | copy-start | bytes 1156
  7.3 7.9 %copy-start.34 = (bf16[48]{0:T(256)(128)(2,1)S(1)}, bf16[48]{0:T(256)(128)(2,1)}, u32[]{:S(2)}) copy-start(bf16[48]{0:T(256)(128)(2,1)} %param.29) | copy-start | bytes 292
  7.3 93.9 %all-gather.3.cloned.1.call-start = ((), (), s32[]{:S(2)}) async-start(), calls=%async_computation | async-start | bytes 9732096 | tf_op jit(solution)/shard_map/all_gather | solution.py:1106
  10.5 19.5 %collective-permute-start = (bf16[1,4,24,768]{3,2,1,0:T(8,128)(2,1)S(1)}, bf16[1,4,24,768]{3,2,1,0:T(8,128)(2,1)S(1)}, u32[]{:S(2)}, u32[]{:S(2)}) collective-permute-start(bf16[1,4,24,768]{3,2,1,0:T(8,128)(2,1)S(1)} %maximum_bitcast_fusion), channel_id=1, source_target_pairs={{0,8},{1,9},{2,10},{3,11},{4,12},{5,13},{6,14},{7,15},{8,0},{9,1},... | collective-permute-start | bytes 442376 | tf_op jit(solution)/shard_map/ppermute | solution.py:838
  12.7 17.3 %collective-permute-start.1 = (bf16[1,4,24,768]{3,2,1,0:T(8,128)(2,1)S(1)}, bf16[1,4,24,768]{3,2,1,0:T(8,128)(2,1)S(1)}, u32[]{:S(2)}, u32[]{:S(2)}) collective-permute-start(bf16[1,4,24,768]{3,2,1,0:T(8,128)(2,1)S(1)} %maximum_bitcast_fusion), channel_id=1, source_target_pairs={{0,16},{1,17},{2,18},{3,19},{4,20},{5,21},{6,22},{7,23},{8,24},{9,... | collective-permute-start | bytes 442376 | tf_op jit(solution)/shard_map/ppermute | solution.py:838
  15.0 15.0 %collective-permute-start.2 = (bf16[1,4,24,768]{3,2,1,0:T(8,128)(2,1)S(1)}, bf16[1,4,24,768]{3,2,1,0:T(8,128)(2,1)S(1)}, u32[]{:S(2)}, u32[]{:S(2)}) collective-permute-start(bf16[1,4,24,768]{3,2,1,0:T(8,128)(2,1)S(1)} %maximum_bitcast_fusion), channel_id=1, source_target_pairs={{0,24},{1,25},{2,26},{3,27},{4,28},{5,29},{6,30},{7,31},{8,16},{9,... | collective-permute-start | bytes 442376 | tf_op jit(solution)/shard_map/ppermute | solution.py:838
  15.3 6.7 %collective-permute-start.3 = (bf16[1,8,256]{2,1,0:T(8,128)(2,1)S(1)}, bf16[1,8,256]{2,1,0:T(8,128)(2,1)S(1)}, u32[]{:S(2)}, u32[]{:S(2)}) collective-permute-start(bf16[1,8,256]{2,1,0:T(8,128)(2,1)S(1)} %bitcast.74), channel_id=1, source_target_pairs={{0,8},{1,9},{2,10},{3,11},{4,12},{5,13},{6,14},{7,15},{8,0},{9,1},... | collective-permute-start | bytes 12296 | tf_op jit(solution)/shard_map/ppermute | solution.py:838
  15.7 14.3 %collective-permute-start.4 = (bf16[1,8,256]{2,1,0:T(8,128)(2,1)S(1)}, bf16[1,8,256]{2,1,0:T(8,128)(2,1)S(1)}, u32[]{:S(2)}, u32[]{:S(2)}) collective-permute-start(bf16[1,8,256]{2,1,0:T(8,128)(2,1)S(1)} %bitcast.75), channel_id=1, source_target_pairs={{0,16},{1,17},{2,18},{3,19},{4,20},{5,21},{6,22},{7,23},{8,24},{9,... | collective-permute-start | bytes 12296 | tf_op jit(solution)/shard_map/ppermute | solution.py:838
  21.9 8.0 %collective-permute-start.5 = (bf16[1,8,256]{2,1,0:T(8,128)(2,1)S(1)}, bf16[1,8,256]{2,1,0:T(8,128)(2,1)S(1)}, u32[]{:S(2)}, u32[]{:S(2)}) collective-permute-start(bf16[1,8,256]{2,1,0:T(8,128)(2,1)S(1)} %bitcast.76), channel_id=1, source_target_pairs={{0,24},{1,25},{2,26},{3,27},{4,28},{5,29},{6,30},{7,31},{8,16},{9,... | collective-permute-start | bytes 12296 | tf_op jit(solution)/shard_map/ppermute | solution.py:838
  30.1 36.7 %copy-start.17 = (bf16[4,4,24,768]{3,2,1,0:T(8,128)(2,1)}, bf16[4,4,24,768]{3,2,1,0:T(8,128)(2,1)S(1)}, u32[]{:S(2)}) copy-start(bf16[4,4,24,768]{3,2,1,0:T(8,128)(2,1)S(1)} %constant_dynamic-update-slice_fusion.4.refs_0_) | copy-start | bytes 1769476
  30.1 11.7 %collective-permute-start.6 = (bf16[4,4,24,768]{3,2,1,0:T(8,128)(2,1)S(1)}, bf16[4,4,24,768]{3,2,1,0:T(8,128)(2,1)S(1)}, u32[]{:S(2)}, u32[]{:S(2)}) collective-permute-start(bf16[4,4,24,768]{3,2,1,0:T(8,128)(2,1)S(1)} %constant_dynamic-update-slice_fusion.4.refs_0_), channel_id=1, source_target_pairs={{0,2},{1,3},{2,0},{3,1},{4,6},{5,7},{6,4},{7,5},{8,10},{9,11},{10,... | collective-permute-start | bytes 1769480 | tf_op jit(solution)/shard_map/ppermute | solution.py:838
  31.4 10.5 %collective-permute-start.7 = (bf16[4,4,24,768]{3,2,1,0:T(8,128)(2,1)S(1)}, bf16[4,4,24,768]{3,2,1,0:T(8,128)(2,1)S(1)}, u32[]{:S(2)}, u32[]{:S(2)}) collective-permute-start(bf16[4,4,24,768]{3,2,1,0:T(8,128)(2,1)S(1)} %constant_dynamic-update-slice_fusion.4.refs_0_), channel_id=1, source_target_pairs={{0,4},{1,5},{2,6},{3,7},{4,0},{5,1},{6,2},{7,3},{8,12},{9,13},{10,... | collective-permute-start | bytes 1769480 | tf_op jit(solution)/shard_map/ppermute | solution.py:838
  32.7 9.2 %collective-permute-start.8 = (bf16[4,4,24,768]{3,2,1,0:T(8,128)(2,1)S(1)}, bf16[4,4,24,768]{3,2,1,0:T(8,128)(2,1)S(1)}, u32[]{:S(2)}, u32[]{:S(2)}) collective-permute-start(bf16[4,4,24,768]{3,2,1,0:T(8,128)(2,1)S(1)} %constant_dynamic-update-slice_fusion.4.refs_0_), channel_id=1, source_target_pairs={{0,1},{1,0},{2,3},{3,2},{4,5},{5,4},{6,7},{7,6},{8,9},{9,8},{10,11... | collective-permute-start | bytes 1769480 | tf_op jit(solution)/shard_map/ppermute | solution.py:838
  38.0 13.8 %copy-start.22 = (bf16[4,8,256]{2,1,0:T(8,128)(2,1)}, bf16[4,8,256]{2,1,0:T(8,128)(2,1)S(1)}, u32[]{:S(2)}) copy-start(bf16[4,8,256]{2,1,0:T(8,128)(2,1)S(1)} %constant_dynamic-update-slice_fusion.refs_0_) | copy-start | bytes 49156
  38.0 3.8 %collective-permute-start.10 = (bf16[4,8,256]{2,1,0:T(8,128)(2,1)S(1)}, bf16[4,8,256]{2,1,0:T(8,128)(2,1)S(1)}, u32[]{:S(2)}, u32[]{:S(2)}) collective-permute-start(bf16[4,8,256]{2,1,0:T(8,128)(2,1)S(1)} %constant_dynamic-update-slice_fusion.refs_0_), channel_id=1, source_target_pairs={{0,4},{1,5},{2,6},{3,7},{4,0},{5,1},{6,2},{7,3},{8,12},{9,13},{10,... | collective-permute-start | bytes 49160 | tf_op jit(solution)/shard_map/ppermute | solution.py:838
  38.1 3.7 %collective-permute-start.9 = (bf16[4,8,256]{2,1,0:T(8,128)(2,1)S(1)}, bf16[4,8,256]{2,1,0:T(8,128)(2,1)S(1)}, u32[]{:S(2)}, u32[]{:S(2)}) collective-permute-start(bf16[4,8,256]{2,1,0:T(8,128)(2,1)S(1)} %constant_dynamic-update-slice_fusion.refs_0_), channel_id=1, source_target_pairs={{0,2},{1,3},{2,0},{3,1},{4,6},{5,7},{6,4},{7,5},{8,10},{9,11},{10,... | collective-permute-start | bytes 49160 | tf_op jit(solution)/shard_map/ppermute | solution.py:838
  41.8 21.0 %copy-start.24 = (bf16[4,8,256]{2,1,0:T(8,128)(2,1)}, bf16[4,8,256]{2,1,0:T(8,128)(2,1)S(1)}, u32[]{:S(2)}) copy-start(bf16[4,8,256]{2,1,0:T(8,128)(2,1)S(1)} %collective-permute-done.10.refs_2_) | copy-start | bytes 49156
  41.8 10.0 %copy-start.25 = (bf16[4,8,256]{2,1,0:T(8,128)(2,1)}, bf16[4,8,256]{2,1,0:T(8,128)(2,1)S(1)}, u32[]{:S(2)}) copy-start(bf16[4,8,256]{2,1,0:T(8,128)(2,1)S(1)} %collective-permute-done.9.refs_1_) | copy-start | bytes 49156
  41.8 25.0 %copy-start.15 = (bf16[4,4,24,768]{3,2,1,0:T(8,128)(2,1)}, bf16[4,4,24,768]{3,2,1,0:T(8,128)(2,1)S(1)}, u32[]{:S(2)}) copy-start(bf16[4,4,24,768]{3,2,1,0:T(8,128)(2,1)S(1)} %collective-permute-done.6.refs_1_) | copy-start | bytes 1769476
  41.8 24.9 %copy-start.16 = (bf16[4,4,24,768]{3,2,1,0:T(8,128)(2,1)}, bf16[4,4,24,768]{3,2,1,0:T(8,128)(2,1)S(1)}, u32[]{:S(2)}) copy-start(bf16[4,4,24,768]{3,2,1,0:T(8,128)(2,1)S(1)} %collective-permute-done.7.refs_2_) | copy-start | bytes 1769476
  41.9 24.9 %copy-start.18 = (bf16[4,4,24,768]{3,2,1,0:T(8,128)(2,1)}, bf16[4,4,24,768]{3,2,1,0:T(8,128)(2,1)S(1)}, u32[]{:S(2)}) copy-start(bf16[4,4,24,768]{3,2,1,0:T(8,128)(2,1)S(1)} %collective-permute-done.8.refs_5_) | copy-start | bytes 1769476
  41.9 20.9 %collective-permute-start.13 = (bf16[4,4,24,768]{3,2,1,0:T(8,128)(2,1)S(1)}, bf16[4,4,24,768]{3,2,1,0:T(8,128)(2,1)S(1)}, u32[]{:S(2)}, u32[]{:S(2)}) collective-permute-start(bf16[4,4,24,768]{3,2,1,0:T(8,128)(2,1)S(1)} %collective-permute-done.6.refs_1_), channel_id=1, source_target_pairs={{0,1},{1,0},{2,3},{3,2},{4,5},{5,4},{6,7},{7,6},{8,9},{9,8},{10,11... | collective-permute-start | bytes 1769480 | tf_op jit(solution)/shard_map/ppermute | solution.py:838
  51.8 11.0 %collective-permute-start.14 = (bf16[4,4,24,768]{3,2,1,0:T(8,128)(2,1)S(1)}, bf16[4,4,24,768]{3,2,1,0:T(8,128)(2,1)S(1)}, u32[]{:S(2)}, u32[]{:S(2)}) collective-permute-start(bf16[4,4,24,768]{3,2,1,0:T(8,128)(2,1)S(1)} %collective-permute-done.7.refs_2_), channel_id=1, source_target_pairs={{0,1},{1,0},{2,3},{3,2},{4,5},{5,4},{6,7},{7,6},{8,9},{9,8},{10,11... | collective-permute-start | bytes 1769480 | tf_op jit(solution)/shard_map/ppermute | solution.py:838
  52.3 9.9 %collective-permute-start.11 = (bf16[2,4,24,768]{3,2,1,0:T(8,128)(2,1)S(1)}, bf16[2,4,24,768]{3,2,1,0:T(8,128)(2,1)}, u32[]{:S(2)}, u32[]{:S(2)}) collective-permute-start(bf16[2,4,24,768]{3,2,1,0:T(8,128)(2,1)S(1)} %slice.30), channel_id=1, source_target_pairs={{0,2},{1,3},{2,0},{3,1},{4,6},{5,7},{6,4},{7,5},{8,10},{9,11},{10,... | collective-permute-start | bytes 884744 | tf_op jit(solution)/shard_map/ppermute | solution.py:838
  54.4 8.4 %collective-permute-start.12 = (bf16[2,4,24,768]{3,2,1,0:T(8,128)(2,1)S(1)}, bf16[2,4,24,768]{3,2,1,0:T(8,128)(2,1)}, u32[]{:S(2)}, u32[]{:S(2)}) collective-permute-start(bf16[2,4,24,768]{3,2,1,0:T(8,128)(2,1)S(1)} %slice.31), channel_id=1, source_target_pairs={{0,4},{1,5},{2,6},{3,7},{4,0},{5,1},{6,2},{7,3},{8,12},{9,13},{10,... | collective-permute-start | bytes 884744 | tf_op jit(solution)/shard_map/ppermute | solution.py:838
  55.5 6.7 %collective-permute-start.15 = (bf16[4,8,256]{2,1,0:T(8,128)(2,1)S(1)}, bf16[4,8,256]{2,1,0:T(8,128)(2,1)S(1)}, u32[]{:S(2)}, u32[]{:S(2)}) collective-permute-start(bf16[4,8,256]{2,1,0:T(8,128)(2,1)S(1)} %collective-permute-done.10.refs_2_), channel_id=1, source_target_pairs={{0,2},{1,3},{2,0},{3,1},{4,6},{5,7},{6,4},{7,5},{8,10},{9,11},{10,... | collective-permute-start | bytes 49160 | tf_op jit(solution)/shard_map/ppermute | solution.py:838
  62.8 3.9 %collective-permute-start.16 = (bf16[2,4,24,768]{3,2,1,0:T(8,128)(2,1)}, bf16[2,4,24,768]{3,2,1,0:T(8,128)(2,1)}, u32[]{:S(2)}, u32[]{:S(2)}) collective-permute-start(bf16[2,4,24,768]{3,2,1,0:T(8,128)(2,1)} %collective-permute-done.11.refs_3_), channel_id=1, source_target_pairs={{0,1},{1,0},{2,3},{3,2},{4,5},{5,4},{6,7},{7,6},{8,9},{9,8},{10,11... | collective-permute-start | bytes 884744 | tf_op jit(solution)/shard_map/ppermute | solution.py:838
  64.0 2.7 collective-permute-start.17
  249.6 9.1 %collective-permute-start.18 = (bf16[16,192,384]{2,1,0:T(8,128)(2,1)}, bf16[16,192,384]{2,1,0:T(8,128)(2,1)S(1)}, u32[]{:S(2)}, u32[]{:S(2)}) collective-permute-start(bf16[16,192,384]{2,1,0:T(8,128)(2,1)} %bitcast.81), channel_id=1, source_target_pairs={{0,1},{1,0},{2,3},{3,2},{4,5},{5,4},{6,7},{7,6},{8,9},{9,8},{10,11... | collective-permute-start | bytes 7077896 | tf_op jit(solution)/shard_map/ppermute | solution.py:838
  249.9 8.9 %collective-permute-start.19 = (bf16[16,192,384]{2,1,0:T(8,128)(2,1)}, bf16[16,192,384]{2,1,0:T(8,128)(2,1)}, u32[]{:S(2)}, u32[]{:S(2)}) collective-permute-start(bf16[16,192,384]{2,1,0:T(8,128)(2,1)} %bitcast.80), channel_id=1, source_target_pairs={{0,1},{1,0},{2,3},{3,2},{4,5},{5,4},{6,7},{7,6},{8,9},{9,8},{10,11... | collective-permute-start | bytes 7077896 | tf_op jit(solution)/shard_map/ppermute | solution.py:838
  250.2 8.5 %collective-permute-start.20 = (bf16[16,48,384]{2,1,0:T(8,128)(2,1)}, bf16[16,48,384]{2,1,0:T(8,128)(2,1)S(1)}, u32[]{:S(2)}, u32[]{:S(2)}) collective-permute-start(bf16[16,48,384]{2,1,0:T(8,128)(2,1)} %get-tuple-element.198), channel_id=1, source_target_pairs={{0,1},{1,0},{2,3},{3,2},{4,5},{5,4},{6,7},{7,6},{8,9},{9,8},{10,11... | collective-permute-start | bytes 1769480 | tf_op jit(solution)/shard_map/ppermute | solution.py:838
  250.5 8.3 %copy-start.2 = (bf16[16,4,48,384]{3,2,1,0:T(8,128)(2,1)S(1)}, bf16[16,4,48,384]{3,2,1,0:T(8,128)(2,1)}, u32[]{:S(2)}) copy-start(bf16[16,4,48,384]{3,2,1,0:T(8,128)(2,1)} %get-tuple-element.193) | copy-start | bytes 7077892
  250.5 8.3 %copy-start.3 = (bf16[3072,384]{1,0:T(8,128)(2,1)S(1)}, bf16[3072,384]{1,0:T(8,128)(2,1)}, u32[]{:S(2)}) copy-start(bf16[3072,384]{1,0:T(8,128)(2,1)} %get-tuple-element.194) | copy-start | bytes 7077892
  250.5 8.3 %copy-start.5 = (bf16[16,48,384]{2,1,0:T(8,128)(2,1)S(1)}, bf16[16,48,384]{2,1,0:T(8,128)(2,1)}, u32[]{:S(2)}) copy-start(bf16[16,48,384]{2,1,0:T(8,128)(2,1)} %get-tuple-element.195.refs_2_) | copy-start | bytes 1769476
  261.8 31.1 %collective-permute-start.21 = (bf16[2,2,432,384]{3,2,1,0:T(8,128)(2,1)S(1)}, bf16[2,2,432,384]{3,2,1,0:T(8,128)(2,1)S(1)}, u32[]{:S(2)}, u32[]{:S(2)}) collective-permute-start(bf16[2,2,432,384]{3,2,1,0:T(8,128)(2,1)S(1)} %get-tuple-element.212), channel_id=1, source_target_pairs={{0,2},{1,3},{2,0},{3,1},{4,6},{5,7},{6,4},{7,5},{8,10},{9,11},{10,... | collective-permute-start | bytes 3981320 | tf_op jit(solution)/shard_map/ppermute | solution.py:838
  263.1 30.2 %collective-permute-start.22 = (bf16[2,2,432,384]{3,2,1,0:T(8,128)(2,1)S(1)}, bf16[2,2,432,384]{3,2,1,0:T(8,128)(2,1)S(1)}, u32[]{:S(2)}, u32[]{:S(2)}) collective-permute-start(bf16[2,2,432,384]{3,2,1,0:T(8,128)(2,1)S(1)} %get-tuple-element.213), channel_id=1, source_target_pairs={{0,4},{1,5},{2,6},{3,7},{4,0},{5,1},{6,2},{7,3},{8,12},{9,13},{10,... | collective-permute-start | bytes 3981320 | tf_op jit(solution)/shard_map/ppermute | solution.py:838
  292.1 16.3 %collective-permute-start.25 = (bf16[16,144,384]{2,1,0:T(8,128)(2,1)}, bf16[16,144,384]{2,1,0:T(8,128)(2,1)S(1)}, u32[]{:S(2)}, u32[]{:S(2)}) collective-permute-start(bf16[16,144,384]{2,1,0:T(8,128)(2,1)} %bitcast.82), channel_id=1, source_target_pairs={{0,1},{1,0},{2,3},{3,2},{4,5},{5,4},{6,7},{7,6},{8,9},{9,8},{10,11... | collective-permute-start | bytes 5308424 | tf_op jit(solution)/shard_map/ppermute | solution.py:838
  294.4 15.1 %collective-permute-start.23 = (bf16[2,432,384]{2,1,0:T(8,128)(2,1)S(1)}, bf16[2,432,384]{2,1,0:T(8,128)(2,1)S(1)}, u32[]{:S(2)}, u32[]{:S(2)}) collective-permute-start(bf16[2,432,384]{2,1,0:T(8,128)(2,1)S(1)} %get-tuple-element.230), channel_id=1, source_target_pairs={{0,4},{1,5},{2,6},{3,7},{4,0},{5,1},{6,2},{7,3},{8,12},{9,13},{10,... | collective-permute-start | bytes 1990664 | tf_op jit(solution)/shard_map/ppermute | solution.py:838
  295.3 15.3 %collective-permute-start.24 = (bf16[2,432,384]{2,1,0:T(8,128)(2,1)S(1)}, bf16[2,432,384]{2,1,0:T(8,128)(2,1)S(1)}, u32[]{:S(2)}, u32[]{:S(2)}) collective-permute-start(bf16[2,432,384]{2,1,0:T(8,128)(2,1)S(1)} %get-tuple-element.231), channel_id=1, source_target_pairs={{0,2},{1,3},{2,0},{3,1},{4,6},{5,7},{6,4},{7,5},{8,10},{9,11},{10,... | collective-permute-start | bytes 1990664 | tf_op jit(solution)/shard_map/ppermute | solution.py:838
  296.0 9.7 %copy-start.7 = (f32[4,1,768]{2,1,0:T(1,128)S(1)}, f32[4,1,768]{2,1,0:T(1,128)}, u32[]{:S(2)}) copy-start(f32[4,1,768]{2,1,0:T(1,128)} %get-tuple-element.241.refs_6_) | copy-start | bytes 36868
  296.0 9.7 %copy-start.8 = (f32[3,1,768]{2,1,0:T(1,128)S(1)}, f32[3,1,768]{2,1,0:T(1,128)}, u32[]{:S(2)}) copy-start(f32[3,1,768]{2,1,0:T(1,128)} %get-tuple-element.237.refs_2_) | copy-start | bytes 27652
  296.0 9.7 %copy-start.11 = (f32[1,768]{1,0:T(1,128)S(1)}, f32[1,768]{1,0:T(1,128)}, u32[]{:S(2)}) copy-start(f32[1,768]{1,0:T(1,128)} %get-tuple-element.238.refs_3_) | copy-start | bytes 9220
  296.0 9.7 %copy-start.12 = (f32[1,768]{1,0:T(1,128)S(1)}, f32[1,768]{1,0:T(1,128)}, u32[]{:S(2)}) copy-start(f32[1,768]{1,0:T(1,128)} %get-tuple-element.242.refs_7_) | copy-start | bytes 9220
  296.0 9.7 %copy-start.13 = (f32[1,768]{1,0:T(1,128)S(1)}, f32[1,768]{1,0:T(1,128)}, u32[]{:S(2)}) copy-start(f32[1,768]{1,0:T(1,128)} %get-tuple-element.239.refs_4_) | copy-start | bytes 9220
  296.0 9.7 %copy-start.14 = (f32[1,768]{1,0:T(1,128)S(1)}, f32[1,768]{1,0:T(1,128)}, u32[]{:S(2)}) copy-start(f32[1,768]{1,0:T(1,128)} %get-tuple-element.240.refs_5_) | copy-start | bytes 9220
  312.4 10.7 %collective-permute-start.26 = (bf16[2,2,160,384]{3,2,1,0:T(8,128)(2,1)S(1)}, bf16[2,2,160,384]{3,2,1,0:T(8,128)(2,1)S(1)}, u32[]{:S(2)}, u32[]{:S(2)}) collective-permute-start(bf16[2,2,160,384]{3,2,1,0:T(8,128)(2,1)S(1)} %get-tuple-element.249), channel_id=1, source_target_pairs={{0,2},{1,3},{2,0},{3,1},{4,6},{5,7},{6,4},{7,5},{8,10},{9,11},{10,... | collective-permute-start | bytes 1474568 | tf_op jit(solution)/shard_map/ppermute | solution.py:838
  313.0 10.2 %collective-permute-start.27 = (bf16[2,2,160,384]{3,2,1,0:T(8,128)(2,1)S(1)}, bf16[2,2,160,384]{3,2,1,0:T(8,128)(2,1)S(1)}, u32[]{:S(2)}, u32[]{:S(2)}) collective-permute-start(bf16[2,2,160,384]{3,2,1,0:T(8,128)(2,1)S(1)} %get-tuple-element.250), channel_id=1, source_target_pairs={{0,4},{1,5},{2,6},{3,7},{4,0},{5,1},{6,2},{7,3},{8,12},{9,13},{10,... | collective-permute-start | bytes 1474568 | tf_op jit(solution)/shard_map/ppermute | solution.py:838
  314.1 17.3 %collective-permute-start.34 = (bf16[432,384]{1,0:T(8,128)(2,1)S(1)}, bf16[432,384]{1,0:T(8,128)(2,1)S(1)}, u32[]{:S(2)}, u32[]{:S(2)}) collective-permute-start(bf16[432,384]{1,0:T(8,128)(2,1)S(1)} %get-tuple-element.261), channel_id=1, source_target_pairs={{0,8},{1,9},{2,10},{3,11},{4,12},{5,13},{6,14},{7,15},{8,0},{9,1},... | collective-permute-start | bytes 995336 | tf_op jit(solution)/shard_map/ppermute | solution.py:838
  315.3 16.2 %collective-permute-start.35 = (bf16[432,384]{1,0:T(8,128)(2,1)S(1)}, bf16[432,384]{1,0:T(8,128)(2,1)S(1)}, u32[]{:S(2)}, u32[]{:S(2)}) collective-permute-start(bf16[432,384]{1,0:T(8,128)(2,1)S(1)} %get-tuple-element.262), channel_id=1, source_target_pairs={{0,16},{1,17},{2,18},{3,19},{4,20},{5,21},{6,22},{7,23},{8,24},{9,... | collective-permute-start | bytes 995336 | tf_op jit(solution)/shard_map/ppermute | solution.py:838
  316.0 20.4 %collective-permute-start.36 = (bf16[432,384]{1,0:T(8,128)(2,1)S(1)}, bf16[432,384]{1,0:T(8,128)(2,1)S(1)}, u32[]{:S(2)}, u32[]{:S(2)}) collective-permute-start(bf16[432,384]{1,0:T(8,128)(2,1)S(1)} %get-tuple-element.263), channel_id=1, source_target_pairs={{0,24},{1,25},{2,26},{3,27},{4,28},{5,29},{6,30},{7,31},{8,16},{9,... | collective-permute-start | bytes 995336 | tf_op jit(solution)/shard_map/ppermute | solution.py:838
  324.0 5.4 %collective-permute-start.28 = (bf16[2,160,384]{2,1,0:T(8,128)(2,1)S(1)}, bf16[2,160,384]{2,1,0:T(8,128)(2,1)S(1)}, u32[]{:S(2)}, u32[]{:S(2)}) collective-permute-start(bf16[2,160,384]{2,1,0:T(8,128)(2,1)S(1)} %get-tuple-element.253), channel_id=1, source_target_pairs={{0,4},{1,5},{2,6},{3,7},{4,0},{5,1},{6,2},{7,3},{8,12},{9,13},{10,... | collective-permute-start | bytes 737288 | tf_op jit(solution)/shard_map/ppermute | solution.py:838
  325.4 5.3 %collective-permute-start.29 = (bf16[2,160,384]{2,1,0:T(8,128)(2,1)S(1)}, bf16[2,160,384]{2,1,0:T(8,128)(2,1)S(1)}, u32[]{:S(2)}, u32[]{:S(2)}) collective-permute-start(bf16[2,160,384]{2,1,0:T(8,128)(2,1)S(1)} %get-tuple-element.254), channel_id=1, source_target_pairs={{0,2},{1,3},{2,0},{3,1},{4,6},{5,7},{6,4},{7,5},{8,10},{9,11},{10,... | collective-permute-start | bytes 737288 | tf_op jit(solution)/shard_map/ppermute | solution.py:838
  336.4 14.5 %collective-permute-start.30 = (bf16[160,384]{1,0:T(8,128)(2,1)S(1)}, bf16[160,384]{1,0:T(8,128)(2,1)S(1)}, u32[]{:S(2)}, u32[]{:S(2)}) collective-permute-start(bf16[160,384]{1,0:T(8,128)(2,1)S(1)} %get-tuple-element.256), channel_id=1, source_target_pairs={{0,8},{1,9},{2,10},{3,11},{4,12},{5,13},{6,14},{7,15},{8,0},{9,1},... | collective-permute-start | bytes 368648 | tf_op jit(solution)/shard_map/ppermute | solution.py:838
  344.3 7.4 %collective-permute-start.31 = (bf16[160,384]{1,0:T(8,128)(2,1)S(1)}, bf16[160,384]{1,0:T(8,128)(2,1)S(1)}, u32[]{:S(2)}, u32[]{:S(2)}) collective-permute-start(bf16[160,384]{1,0:T(8,128)(2,1)S(1)} %get-tuple-element.257), channel_id=1, source_target_pairs={{0,16},{1,17},{2,18},{3,19},{4,20},{5,21},{6,22},{7,23},{8,24},{9,... | collective-permute-start | bytes 368648 | tf_op jit(solution)/shard_map/ppermute | solution.py:838
  344.8 17.8 %copy-start.1 = (bf16[48,3072]{1,0:T(8,128)(2,1)S(1)}, bf16[48,3072]{1,0:T(8,128)(2,1)}, u32[]{:S(2)}) copy-start(bf16[48,3072]{1,0:T(8,128)(2,1)} %param.26) | copy-start | bytes 884740
  344.8 6.9 %collective-permute-start.32 = (bf16[160,384]{1,0:T(8,128)(2,1)S(1)}, bf16[160,384]{1,0:T(8,128)(2,1)S(1)}, u32[]{:S(2)}, u32[]{:S(2)}) collective-permute-start(bf16[160,384]{1,0:T(8,128)(2,1)S(1)} %get-tuple-element.258), channel_id=1, source_target_pairs={{0,24},{1,25},{2,26},{3,27},{4,28},{5,29},{6,30},{7,31},{8,16},{9,... | collective-permute-start | bytes 368648 | tf_op jit(solution)/shard_map/ppermute | solution.py:838
  346.6 14.9 %collective-permute-start.37 = (f32[432,384]{1,0:T(8,128)S(1)}, f32[432,384]{1,0:T(8,128)S(1)}, u32[]{:S(2)}, u32[]{:S(2)}) collective-permute-start(f32[432,384]{1,0:T(8,128)S(1)} %convert_add_fusion.half_ref), channel_id=1, source_target_pairs={{0,1},{1,0},{2,3},{3,2},{4,5},{5,4},{6,7},{7,6},{8,9},{9,8},{10,11... | collective-permute-start | bytes 1990664 | tf_op jit(solution)/shard_map/ppermute | solution.py:838
  351.8 7.1 %collective-permute-start.33 = (f32[160,384]{1,0:T(8,128)S(1)}, f32[160,384]{1,0:T(8,128)S(1)}, u32[]{:S(2)}, u32[]{:S(2)}) collective-permute-start(f32[160,384]{1,0:T(8,128)S(1)} %convert_add_fusion.1.half_ref), channel_id=1, source_target_pairs={{0,1},{1,0},{2,3},{3,2},{4,5},{5,4},{6,7},{7,6},{8,9},{9,8},{10,11... | collective-permute-start | bytes 737288 | tf_op jit(solution)/shard_map/ppermute | solution.py:838
  (10 other events, 29.8 us)
Sparse Core Ops, SparseCore 0:
  11.6 89.5 all-gather.2

commit v5 on v4

--- a/solution.py
+++ b/solution.py
@@ -964,12 +964,11 @@
             out[low_z] = total(kept[low_z, index], got[low_z, index]).astype(jnp.bfloat16)
 
 
-def third_sums_kernel(spot_ref, near, far, near_in, far_in, first, second, third, kept):
+def third_sums_kernel(spot_ref, near, far, near_in, far_in, sent, kept):
     low_z = spot_ref[1]
-    first[...] = total(near[1 - low_z], near_in[1 - low_z]).astype(jnp.bfloat16)
-    second[...] = total(far[low_z], far_in[low_z]).astype(jnp.bfloat16)
-    third[...] = total(far[1 - low_z], far_in[1 - low_z]).astype(jnp.bfloat16)
-    kept[...] = total(near[low_z], near_in[low_z])
+    for index, (left, right) in enumerate(((near, near_in), (far, far_in))):
+        sent[index] = total(left[1 - low_z], right[1 - low_z]).astype(jnp.bfloat16)
+        kept[index] = total(left[low_z], right[low_z])
 
 
 def assemble_kernel(layouts, core_ref, half_ref, other_ref, *outs):
@@ -1064,19 +1063,24 @@
         return self.kept
 
     def third(self):
-        *sent, kept = in_vmem(
+        sent, kept = in_vmem(
             third_sums_kernel,
             "third_sums",
-            [self.like()] * 3 + [self.like(kind=jnp.float32)],
+            [self.like(2), self.like(2, kind=jnp.float32)],
             self.spot,
             *self.kept,
             *self.got,
         )
-        self.kept = [kept]
-        self.got = [swap(part, bits) for part, bits in zip(sent, (Z1, Z2, Z3))]
+        self.kept, self.got = ([kept], [swap(sent, Z1)])
         return self.kept
 
     def fourth(self):
+        (kept,), (got,) = (self.kept, self.got)
+        far = low(kept[1] + wide(got[1]))
+        self.kept, self.got = ([kept[0], got[0]], [swap(far, Z2)])
+        return far
+
+    def fifth(self):
         half = total(*self.kept, *self.got)
         self.kept, self.got = ([half], [swap(half, CORE)])
 
@@ -1227,9 +1231,11 @@
         qkv_sums.got = after(qkv_sums.got, sums.third())
         qkv_sums.first()
         qkv_sums.second()
-        sums.got = after(sums.got, qkv_sums.third())
-        sums.fourth()
+        qkv_sums.got = after(qkv_sums.got, sums.fourth())
+        qkv_sums.third()
         qkv_sums.fourth()
+        sums.fifth()
+        qkv_sums.fifth()
         fc, proj, out = sums.whole(side, ((4, 48), (1, 192), (1, 48)))
         qkv, small = qkv_sums.whole(side, ((3, 48),))
         parts = []

time: 374 us -> 372 us (level)
  starting transfers between devices: 65.2 us -> 51.4 us
  waiting for transfers between devices: 49.1 us -> 61.3 us
    ppermute x38 -> x36, starting transfers between devices: 65.1 us -> 51.3 us  [swap(): return lax.ppermute(value, BOTH, [(i, i ^ bits) for i in range(32)])]
    ppermute x38 -> x36, waiting for transfers between devices: 39.9 us -> 52 us  [swap(): return lax.ppermute(value, BOTH, [(i, i ^ bits) for i in range(32)])]
  transfers between devices with their start and end apart: 39 -> 37, of which waited for: 15 -> 15; matrix products, arithmetic and copies ran while one was open for 1% -> 1% of each run, Pallas kernels for 22% -> 22%
where the time goes in v5:
time: 372 us; the launch traced here: 368 us
  Pallas kernels  234 us (63%)
  waiting for transfers between devices  61.3 us (16%)
  starting transfers between devices  51.4 us (14%)
  between operations  15.1 us (4%)
  local copies, waits for them, and re-layouts  6.08 us (2%)
    pallas_call x2, Pallas kernels, mlp_backward(): pl.pallas_call(functools.partial(mlp_backward_kernel, earlier is not None...  81.4 us
    ppermute x36, waiting for transfers between devices, swap(): return lax.ppermute(value, BOTH, [(i, i ^ bits) for i in range(32)])  52 us
    ppermute x36, starting transfers between devices, swap(): return lax.ppermute(value, BOTH, [(i, i ^ bits) for i in range(32)])  51.3 us
    pallas_call x2, Pallas kernels, attention_forward(): pl.pallas_call(functools.partial(attention_forward_kernel, docs, back), g...  40.5 us
    pallas_call x1, Pallas kernels, attention_backward_all(): pl.pallas_call(functools.partial(attention_backward_kernel, docs, back, N...  27.9 us
    pallas_call x2, Pallas kernels, attention_backward(): pl.pallas_call(functools.partial(attention_backward_kernel, docs, back, m...  21 us
    pallas_call x1, Pallas kernels, mlp_forward(): pl.pallas_call(mlp_forward_kernel, grid=(hidden_units // block,), out_sha...  17 us
    pallas_call x2, Pallas kernels, attention_terms(): pl.pallas_call(functools.partial(attention_terms_kernel, earlier is not N...  16 us
  transfers between devices with their start and end apart: 37, of which 15 were waited for; matrix products, arithmetic and copies ran while one was open for 1% of the time, Pallas kernels for 22%

profile of v5, /device:TPU:1, one launch (start us, length us, event | category | flops | bytes accessed | tf_op | source)
XLA Modules:
  0.0 367.9 jit_solution(6879974714848625736)
XLA Ops:
  7.4 0.8 copy-done
  8.2 0.9 constant_dynamic-slice_fusion
  9.6 0.7 copy.36
  10.5 2.2 collective-permute-start
  12.7 2.3 collective-permute-start.1
  15.7 3.2 collective-permute-start.4
  18.9 3.1 collective-permute-done.3
  21.9 1.9 collective-permute-start.5
  23.8 6.2 %collective-permute-done.4 = bf16[1,8,256]{2,1,0:T(8,128)(2,1)S(1)} collective-permute-done((bf16[1,8,256]{2,1,0:T(8,128)(2,1)S(1)}, bf16[1,8,256]{2,1,0:T(8,128)(2,1)S(1)}, u32[]{:S(2)}, u32[]{:S(2)}) %collective-permute-start.4) | collective-permute-done | bytes 4128 | tf_op jit(solution)/shard_map/ppermute | solution.py:838
  30.1 1.3 collective-permute-start.6
  31.4 1.3 collective-permute-start.7
  32.7 5.3 %collective-permute-start.8 = (bf16[4,4,24,768]{3,2,1,0:T(8,128)(2,1)S(1)}, bf16[4,4,24,768]{3,2,1,0:T(8,128)(2,1)S(1)}, u32[]{:S(2)}, u32[]{:S(2)}) collective-permute-start(bf16[4,4,24,768]{3,2,1,0:T(8,128)(2,1)S(1)} %constant_dynamic-update-slice_fusion.4.refs_0_), channel_id=1, source_target_pairs={{0,1},{1,0},{2,3},{3,2},{4,5},{5,4},{6,7},{7,6},{8,9},{9,8},{10,11... | collective-permute-start | bytes 1769480 | tf_op jit(solution)/shard_map/ppermute | solution.py:838
  38.4 3.4 collective-permute-done.10.refs_2_
  41.9 9.9 %collective-permute-start.13 = (bf16[4,4,24,768]{3,2,1,0:T(8,128)(2,1)S(1)}, bf16[4,4,24,768]{3,2,1,0:T(8,128)(2,1)S(1)}, u32[]{:S(2)}, u32[]{:S(2)}) collective-permute-start(bf16[4,4,24,768]{3,2,1,0:T(8,128)(2,1)S(1)} %collective-permute-done.6.refs_1_), channel_id=1, source_target_pairs={{0,1},{1,0},{2,3},{3,2},{4,5},{5,4},{6,7},{7,6},{8,9},{9,8},{10,11... | collective-permute-start | bytes 1769480 | tf_op jit(solution)/shard_map/ppermute | solution.py:838
  52.3 2.1 collective-permute-start.11
  54.4 1.1 collective-permute-start.12
  55.6 6.6 %collective-permute-done.15.refs_3_ = bf16[4,8,256]{2,1,0:T(8,128)(2,1)S(1)} collective-permute-done((bf16[4,8,256]{2,1,0:T(8,128)(2,1)S(1)}, bf16[4,8,256]{2,1,0:T(8,128)(2,1)S(1)}, u32[]{:S(2)}, u32[]{:S(2)}) %collective-permute-start.15) | collective-permute-done | bytes 16416 | tf_op jit(solution)/shard_map/ppermute | solution.py:838
  62.2 0.6 collective-permute-done.12.refs_4_
  62.8 1.2 collective-permute-start.16
  64.1 2.6 place_small.1
  66.8 5.5 %place.1 = bf16[4,32,24,768]{3,2,1,0:T(8,128)(2,1)} custom-call(s32[1]{0:T(128)} %bitcast.4.me_ref, bf16[4,4,24,768]{3,2,1,0:T(8,128)(2,1)} %copy-done.17, bf16[4,4,24,768]{3,2,1,0:T(8,128)(2,1)} %copy-done.15, bf16[4,4,24,768]{3,2,1,0:T(8,128)(2,1)} %copy-done.16, bf16[2,4,24,768]{3,2,1,0:T(8,128)(2,1)} %collective-permute-done.11.refs_3_, ...), custom_call_target="tpu_custom_call" | custom-call | tf_op jit(solution)/shard_map/place/pallas_call | solution.py:862
  72.3 19.7 %attention_forward.2 = (bf16[1024,768]{1,0:T(8,128)(2,1)}, bf16[1024,2304]{1,0:T(8,128)(2,1)}, bf16[1024,768]{1,0:T(8,128)(2,1)}, f32[24,1,512]{2,1,0:T(1,128)},...) custom-call(s32[2,6]{1,0:T(2,128)S(1)} %bitcast.58, bf16[1024,768]{1,0:T(8,128)(2,1)} %bitcast.75, ...), custom_call_target="tpu_custom_call" | custom-call | flops 805306368 | bytes 2368512 | tf_op jit(solution)/shard_map/attention_forward/pallas_call | solution.py:205
  92.0 9.2 %all-gather.3.cloned.1.call-done = bf16[128,48,768]{2,1,0:T(8,128)(2,1)} async-done(((bf16[4,48,768]{2,1,0:T(8,128)(2,1)}), bf16[128,48,768]{2,1,0:T(8,128)(2,1)}) %all-gather.3.cloned.1.call-update) | async-done | bytes 9437200 | tf_op jit(solution)/shard_map/all_gather | solution.py:1110
  101.2 17.0 %mlp_forward.1 = (bf16[1024,3072]{1,0:T(8,128)(2,1)}, f32[1024,768]{1,0:T(8,128)}) custom-call(f32[1024,768]{1,0:T(8,128)} %get-tuple-element.161.hidden_ref, bf16[1024,768]{1,0:T(8,128)(2,1)} %get-tuple-element.162.normed_ref, bf16[16,2,4,48,768]{4,3,2,1,0:T(8,128)(2,1)} %bitcast.63, f32[1,3072]{1,0:T(1,128)} %get-tuple-element.163.fbias_ref.rest_0_, ...), custom_call_target="tpu_custom_call" | custom-call | flops 1207959552 | bytes 2949120 | tf_op jit(solution)/shard_map/mlp_forward/pallas_call | solution.py:286
  118.2 20.8 %attention_forward.3 = (bf16[1024,768]{1,0:T(8,128)(2,1)}, bf16[1024,2304]{1,0:T(8,128)(2,1)}, bf16[1024,768]{1,0:T(8,128)(2,1)}, f32[24,1,512]{2,1,0:T(1,128)},...) custom-call(s32[2,6]{1,0:T(2,128)S(1)} %bitcast.59, f32[1024,768]{1,0:T(8,128)} %get-tuple-element.165.state_ref.rest_0_, ...), custom_call_target="tpu_custom_call" | custom-call | flops 805306368 | bytes 2565120 | tf_op jit(solution)/shard_map/attention_forward/pallas_call | solution.py:205
  139.0 44.9 %mlp_backward.2 = (bf16[1024,768]{1,0:T(8,128)(2,1)}, f32[1024,768]{1,0:T(8,128)}, bf16[16,4,48,384]{3,2,1,0:T(8,128)(2,1)}, bf16[16,4,48,384]{3,2,1,0:T(8,128)(...) custom-call(s32[1]{0:T(128)} %bitcast.core_ref.unused_ref, ...), custom_call_target="tpu_custom_call" | custom-call | flops 2415919104 | bytes 5264640 | tf_op jit(solution)/shard_map/mlp_backward/pallas_call | solution.py:512
  184.0 27.9 %attention_backward_all.1 = (bf16[1024,2304]{1,0:T(8,128)(2,1)}, f32[1024,768]{1,0:T(8,128)}, f32[1,768]{1,0:T(1,128)S(1)}, f32[1,768]{1,0:T(1,128)S(1)}) custom-call(s32[2,6]{1,0:T(2,128)S(1)} %bitcast.60, f32[1024,768]{1,0:T(8,128)} %get-tuple-element.170.dhid_ref, bf16[1024,768]{1,0:T(8,128)(2,1)} %get-tuple-element.168.att_ref, ...), custom_call_target="tpu_custom_call" | custom-call | flops 1107296256 | bytes 3153024 | tf_op jit(solution)/shard_map/attention_backward_all/pallas_call | solution.py:680
  211.8 0.6 copy-done.9
  212.4 0.6 copy-done.10
  213.0 36.4 %mlp_backward.3 = (f32[1024,768]{1,0:T(8,128)}, bf16[16,4,48,384]{3,2,1,0:T(8,128)(2,1)}, bf16[16,4,48,384]{3,2,1,0:T(8,128)(2,1)}, bf16[3072,384]{1,0:T(8,128)(...) custom-call(s32[1]{0:T(128)} %bitcast.core_ref.unused_ref, ...), custom_call_target="tpu_custom_call" | custom-call | flops 2415919104 | bytes 7379328 | tf_op jit(solution)/shard_map/mlp_backward/pallas_call | solution.py:512
  250.4 8.2 %attention_terms.2 = (bf16[16,3,48,384]{3,2,1,0:T(8,128)(2,1)}, bf16[16,3,48,384]{3,2,1,0:T(8,128)(2,1)}, f32[3,1,768]{2,1,0:T(1,128)}) custom-call(s32[1]{0:T(128)} %bitcast.core_ref.unused_ref, bf16[1024,768]{1,0:T(8,128)(2,1)} %get-tuple-element.194.normed_ref, bf16[1024,2304]{1,0:T(8,128)(2,1)} %get-tuple-element.195.rest_0_), custom_call_target="tpu_custom_call" | custom-call | flops 452984832 | bytes 1229952 | tf_op jit(solution)/shard_map/attention_terms/pallas_call | solution.py:743
  258.7 3.1 first_sums.2
  261.7 1.2 collective-permute-start.21
  263.3 10.4 %attention_backward.3.rest_1_ = bf16[512,2304]{1,0:T(8,128)(2,1)S(1)} custom-call(s32[2,6]{1,0:T(2,128)S(1)} %bitcast.61, f32[1024,768]{1,0:T(8,128)} %get-tuple-element.204.dhid_ref, bf16[1024,768]{1,0:T(8,128)(2,1)} %get-tuple-element.174.att_ref, bf16[1024,2304]{1,0:T(8,128)(2,1)} %get-tuple-element.205.mixed_ref, ...), custom_call_target="tpu_custom_call" | custom-call | flops 327155712 | bytes 589824 | tf_op jit(solution)/shard_map/attention_backward/pallas_call | solution.py:642
  273.7 10.6 %attention_backward.2.rest_0_ = bf16[512,2304]{1,0:T(8,128)(2,1)S(1)} custom-call(s32[2,6]{1,0:T(2,128)S(1)} %bitcast.62, f32[1024,768]{1,0:T(8,128)} %get-tuple-element.204.dhid_ref, bf16[1024,768]{1,0:T(8,128)(2,1)} %get-tuple-element.174.att_ref, bf16[1024,2304]{1,0:T(8,128)(2,1)} %get-tuple-element.205.mixed_ref, ...), custom_call_target="tpu_custom_call" | custom-call | flops 327155712 | bytes 589824 | tf_op jit(solution)/shard_map/attention_backward/pallas_call | solution.py:642
  284.3 7.8 %attention_terms.3 = (bf16[16,3,48,384]{3,2,1,0:T(8,128)(2,1)}, bf16[16,3,48,384]{3,2,1,0:T(8,128)(2,1)}, f32[3,1,768]{2,1,0:T(1,128)}) custom-call(s32[1]{0:T(128)} %bitcast.core_ref.unused_ref, bf16[1024,768]{1,0:T(8,128)(2,1)} %get-tuple-element.209.normed_ref, bf16[512,2304]{1,0:T(8,128)(2,1)S(1)} %attention_backward.2.rest_0_, ...), custom_call_target="tpu_custom_call" | custom-call | flops 452984832 | bytes 1673472 | tf_op jit(solution)/shard_map/attention_terms/pallas_call | solution.py:743
  292.0 0.8 collective-permute-start.25
  293.1 1.2 second_sums.2
  294.2 1.0 collective-permute-start.23
  295.2 0.6 collective-permute-start.24
  295.9 9.6 %attention_input.1 = (bf16[1024,768]{1,0:T(8,128)(2,1)}, f32[1,768]{1,0:T(1,128)S(1)}, f32[1,768]{1,0:T(1,128)S(1)}) custom-call(f32[1024,768]{1,0:T(8,128)} %get-tuple-element.204.dhid_ref, bf16[1024,768]{1,0:T(8,128)(2,1)} %bitcast.76, bf16[4,768,768]{2,1,0:T(8,128)(2,1)} %bitcast.74, f32[1,768]{1,0:T(1,128)} %get-tuple-element.150.gain_ref.rest_1_, ...), custom_call_target="tpu_custom_call" | custom-call | flops 452984832 | bytes 1968000 | tf_op jit(solution)/shard_map/attention_input/pallas_call | solution.py:796
  305.6 2.7 pack_small.1.refs_2_
  308.2 1.1 collective-permute-done.23.near_in
  309.3 1.2 collective-permute-done.24.far_in
  310.5 0.9 third_sums.2
  311.4 1.3 collective-permute-start.30
  312.6 1.0 first_sums.3
  314.1 1.1 collective-permute-start.27
  315.2 8.8 %collective-permute-done.26.near_in = bf16[2,2,160,384]{3,2,1,0:T(8,128)(2,1)S(1)} collective-permute-done((bf16[2,2,160,384]{3,2,1,0:T(8,128)(2,1)S(1)}, bf16[2,2,160,384]{3,2,1,0:T(8,128)(2,1)S(1)}, u32[]{:S(2)}, u32[]{:S(2)}) %collective-permute-start.26) | collective-permute-done | bytes 491552 | tf_op jit(solution)/shard_map/ppermute | solution.py:838
  324.1 0.8 second_sums.3
  324.9 1.4 collective-permute-start.28
  326.6 3.4 collective-permute-done.28.near_in
  330.0 1.3 collective-permute-done.29.far_in
  331.3 0.7 third_sums.3
  332.3 1.6 collective-permute-start.34
  333.9 5.1 %collective-permute-done.31 = bf16[2,160,384]{2,1,0:T(8,128)(2,1)S(1)} collective-permute-done((bf16[2,160,384]{2,1,0:T(8,128)(2,1)S(1)}, bf16[2,160,384]{2,1,0:T(8,128)(2,1)S(1)}, u32[]{:S(2)}, u32[]{:S(2)}) %collective-permute-start.31) | collective-permute-done | bytes 245792 | tf_op jit(solution)/shard_map/ppermute | solution.py:838
  339.2 9.9 %collective-permute-done.34 = bf16[432,384]{1,0:T(8,128)(2,1)S(1)} collective-permute-done((bf16[432,384]{1,0:T(8,128)(2,1)S(1)}, bf16[432,384]{1,0:T(8,128)(2,1)S(1)}, u32[]{:S(2)}, u32[]{:S(2)}) %collective-permute-start.34) | collective-permute-done | bytes 331808 | tf_op jit(solution)/shard_map/ppermute | solution.py:838
  349.2 5.5 %collective-permute-start.35 = (f32[432,384]{1,0:T(8,128)S(1)}, f32[432,384]{1,0:T(8,128)S(1)}, u32[]{:S(2)}, u32[]{:S(2)}) collective-permute-start(f32[432,384]{1,0:T(8,128)S(1)} %bitcast_add_fusion.half_ref), channel_id=1, source_target_pairs={{0,1},{1,0},{2,3},{3,2},{4,5},{5,4},{6,7},{7,6},{8,9},{9,8},{10,11... | collective-permute-start | bytes 1990664 | tf_op jit(solution)/shard_map/ppermute | solution.py:838
  354.8 1.2 collective-permute-start.33
  356.0 1.1 collective-permute-done.33.other_ref
  357.1 0.8 assemble.2
  357.9 0.6 slice.64
  359.1 0.6 slice_bitcast_fusion
  359.7 1.1 assemble.3
  (148 shorter events, 5.9 us)
Async XLA Ops:
  7.2 7.7 %copy-start.27 = (bf16[48]{0:T(256)(128)(2,1)S(1)}, bf16[48]{0:T(256)(128)(2,1)}, u32[]{:S(2)}) copy-start(bf16[48]{0:T(256)(128)(2,1)} %param.18) | copy-start | bytes 292
  7.2 7.8 %copy-start.28 = (bf16[48]{0:T(256)(128)(2,1)S(1)}, bf16[48]{0:T(256)(128)(2,1)}, u32[]{:S(2)}) copy-start(bf16[48]{0:T(256)(128)(2,1)} %param.19) | copy-start | bytes 292
  7.2 7.8 %copy-start.29 = (bf16[144]{0:T(256)(128)(2,1)S(1)}, bf16[144]{0:T(256)(128)(2,1)}, u32[]{:S(2)}) copy-start(bf16[144]{0:T(256)(128)(2,1)} %param.21) | copy-start | bytes 868
  7.3 7.8 %copy-start.30 = (bf16[48]{0:T(256)(128)(2,1)S(1)}, bf16[48]{0:T(256)(128)(2,1)}, u32[]{:S(2)}) copy-start(bf16[48]{0:T(256)(128)(2,1)} %param.23) | copy-start | bytes 292
  7.3 7.8 %copy-start.31 = (bf16[48]{0:T(256)(128)(2,1)S(1)}, bf16[48]{0:T(256)(128)(2,1)}, u32[]{:S(2)}) copy-start(bf16[48]{0:T(256)(128)(2,1)} %param.24) | copy-start | bytes 292
  7.3 7.9 %copy-start.32 = (bf16[48]{0:T(256)(128)(2,1)S(1)}, bf16[48]{0:T(256)(128)(2,1)}, u32[]{:S(2)}) copy-start(bf16[48]{0:T(256)(128)(2,1)} %param.25) | copy-start | bytes 292
  7.3 7.9 %copy-start.33 = (bf16[192]{0:T(256)(128)(2,1)S(1)}, bf16[192]{0:T(256)(128)(2,1)}, u32[]{:S(2)}) copy-start(bf16[192]{0:T(256)(128)(2,1)} %param.27) | copy-start | bytes 1156
  7.3 7.9 %copy-start.34 = (bf16[48]{0:T(256)(128)(2,1)S(1)}, bf16[48]{0:T(256)(128)(2,1)}, u32[]{:S(2)}) copy-start(bf16[48]{0:T(256)(128)(2,1)} %param.29) | copy-start | bytes 292
  7.3 93.9 %all-gather.3.cloned.1.call-start = ((), (), s32[]{:S(2)}) async-start(), calls=%async_computation | async-start | bytes 9732096 | tf_op jit(solution)/shard_map/all_gather | solution.py:1110
  10.5 19.5 %collective-permute-start = (bf16[1,4,24,768]{3,2,1,0:T(8,128)(2,1)S(1)}, bf16[1,4,24,768]{3,2,1,0:T(8,128)(2,1)S(1)}, u32[]{:S(2)}, u32[]{:S(2)}) collective-permute-start(bf16[1,4,24,768]{3,2,1,0:T(8,128)(2,1)S(1)} %maximum_bitcast_fusion), channel_id=1, source_target_pairs={{0,8},{1,9},{2,10},{3,11},{4,12},{5,13},{6,14},{7,15},{8,0},{9,1},... | collective-permute-start | bytes 442376 | tf_op jit(solution)/shard_map/ppermute | solution.py:838
  12.7 17.3 %collective-permute-start.1 = (bf16[1,4,24,768]{3,2,1,0:T(8,128)(2,1)S(1)}, bf16[1,4,24,768]{3,2,1,0:T(8,128)(2,1)S(1)}, u32[]{:S(2)}, u32[]{:S(2)}) collective-permute-start(bf16[1,4,24,768]{3,2,1,0:T(8,128)(2,1)S(1)} %maximum_bitcast_fusion), channel_id=1, source_target_pairs={{0,16},{1,17},{2,18},{3,19},{4,20},{5,21},{6,22},{7,23},{8,24},{9,... | collective-permute-start | bytes 442376 | tf_op jit(solution)/shard_map/ppermute | solution.py:838
  15.0 15.0 %collective-permute-start.2 = (bf16[1,4,24,768]{3,2,1,0:T(8,128)(2,1)S(1)}, bf16[1,4,24,768]{3,2,1,0:T(8,128)(2,1)S(1)}, u32[]{:S(2)}, u32[]{:S(2)}) collective-permute-start(bf16[1,4,24,768]{3,2,1,0:T(8,128)(2,1)S(1)} %maximum_bitcast_fusion), channel_id=1, source_target_pairs={{0,24},{1,25},{2,26},{3,27},{4,28},{5,29},{6,30},{7,31},{8,16},{9,... | collective-permute-start | bytes 442376 | tf_op jit(solution)/shard_map/ppermute | solution.py:838
  15.3 6.7 %collective-permute-start.3 = (bf16[1,8,256]{2,1,0:T(8,128)(2,1)S(1)}, bf16[1,8,256]{2,1,0:T(8,128)(2,1)S(1)}, u32[]{:S(2)}, u32[]{:S(2)}) collective-permute-start(bf16[1,8,256]{2,1,0:T(8,128)(2,1)S(1)} %bitcast.82), channel_id=1, source_target_pairs={{0,8},{1,9},{2,10},{3,11},{4,12},{5,13},{6,14},{7,15},{8,0},{9,1},... | collective-permute-start | bytes 12296 | tf_op jit(solution)/shard_map/ppermute | solution.py:838
  15.7 14.3 %collective-permute-start.4 = (bf16[1,8,256]{2,1,0:T(8,128)(2,1)S(1)}, bf16[1,8,256]{2,1,0:T(8,128)(2,1)S(1)}, u32[]{:S(2)}, u32[]{:S(2)}) collective-permute-start(bf16[1,8,256]{2,1,0:T(8,128)(2,1)S(1)} %bitcast.83), channel_id=1, source_target_pairs={{0,16},{1,17},{2,18},{3,19},{4,20},{5,21},{6,22},{7,23},{8,24},{9,... | collective-permute-start | bytes 12296 | tf_op jit(solution)/shard_map/ppermute | solution.py:838
  21.9 8.0 %collective-permute-start.5 = (bf16[1,8,256]{2,1,0:T(8,128)(2,1)S(1)}, bf16[1,8,256]{2,1,0:T(8,128)(2,1)S(1)}, u32[]{:S(2)}, u32[]{:S(2)}) collective-permute-start(bf16[1,8,256]{2,1,0:T(8,128)(2,1)S(1)} %bitcast.84), channel_id=1, source_target_pairs={{0,24},{1,25},{2,26},{3,27},{4,28},{5,29},{6,30},{7,31},{8,16},{9,... | collective-permute-start | bytes 12296 | tf_op jit(solution)/shard_map/ppermute | solution.py:838
  30.1 36.7 %copy-start.17 = (bf16[4,4,24,768]{3,2,1,0:T(8,128)(2,1)}, bf16[4,4,24,768]{3,2,1,0:T(8,128)(2,1)S(1)}, u32[]{:S(2)}) copy-start(bf16[4,4,24,768]{3,2,1,0:T(8,128)(2,1)S(1)} %constant_dynamic-update-slice_fusion.4.refs_0_) | copy-start | bytes 1769476
  30.1 11.7 %collective-permute-start.6 = (bf16[4,4,24,768]{3,2,1,0:T(8,128)(2,1)S(1)}, bf16[4,4,24,768]{3,2,1,0:T(8,128)(2,1)S(1)}, u32[]{:S(2)}, u32[]{:S(2)}) collective-permute-start(bf16[4,4,24,768]{3,2,1,0:T(8,128)(2,1)S(1)} %constant_dynamic-update-slice_fusion.4.refs_0_), channel_id=1, source_target_pairs={{0,2},{1,3},{2,0},{3,1},{4,6},{5,7},{6,4},{7,5},{8,10},{9,11},{10,... | collective-permute-start | bytes 1769480 | tf_op jit(solution)/shard_map/ppermute | solution.py:838
  31.4 10.5 %collective-permute-start.7 = (bf16[4,4,24,768]{3,2,1,0:T(8,128)(2,1)S(1)}, bf16[4,4,24,768]{3,2,1,0:T(8,128)(2,1)S(1)}, u32[]{:S(2)}, u32[]{:S(2)}) collective-permute-start(bf16[4,4,24,768]{3,2,1,0:T(8,128)(2,1)S(1)} %constant_dynamic-update-slice_fusion.4.refs_0_), channel_id=1, source_target_pairs={{0,4},{1,5},{2,6},{3,7},{4,0},{5,1},{6,2},{7,3},{8,12},{9,13},{10,... | collective-permute-start | bytes 1769480 | tf_op jit(solution)/shard_map/ppermute | solution.py:838
  32.7 9.2 %collective-permute-start.8 = (bf16[4,4,24,768]{3,2,1,0:T(8,128)(2,1)S(1)}, bf16[4,4,24,768]{3,2,1,0:T(8,128)(2,1)S(1)}, u32[]{:S(2)}, u32[]{:S(2)}) collective-permute-start(bf16[4,4,24,768]{3,2,1,0:T(8,128)(2,1)S(1)} %constant_dynamic-update-slice_fusion.4.refs_0_), channel_id=1, source_target_pairs={{0,1},{1,0},{2,3},{3,2},{4,5},{5,4},{6,7},{7,6},{8,9},{9,8},{10,11... | collective-permute-start | bytes 1769480 | tf_op jit(solution)/shard_map/ppermute | solution.py:838
  38.0 13.8 %copy-start.22 = (bf16[4,8,256]{2,1,0:T(8,128)(2,1)}, bf16[4,8,256]{2,1,0:T(8,128)(2,1)S(1)}, u32[]{:S(2)}) copy-start(bf16[4,8,256]{2,1,0:T(8,128)(2,1)S(1)} %constant_dynamic-update-slice_fusion.refs_0_) | copy-start | bytes 49156
  38.0 3.8 %collective-permute-start.10 = (bf16[4,8,256]{2,1,0:T(8,128)(2,1)S(1)}, bf16[4,8,256]{2,1,0:T(8,128)(2,1)S(1)}, u32[]{:S(2)}, u32[]{:S(2)}) collective-permute-start(bf16[4,8,256]{2,1,0:T(8,128)(2,1)S(1)} %constant_dynamic-update-slice_fusion.refs_0_), channel_id=1, source_target_pairs={{0,4},{1,5},{2,6},{3,7},{4,0},{5,1},{6,2},{7,3},{8,12},{9,13},{10,... | collective-permute-start | bytes 49160 | tf_op jit(solution)/shard_map/ppermute | solution.py:838
  38.1 3.7 %collective-permute-start.9 = (bf16[4,8,256]{2,1,0:T(8,128)(2,1)S(1)}, bf16[4,8,256]{2,1,0:T(8,128)(2,1)S(1)}, u32[]{:S(2)}, u32[]{:S(2)}) collective-permute-start(bf16[4,8,256]{2,1,0:T(8,128)(2,1)S(1)} %constant_dynamic-update-slice_fusion.refs_0_), channel_id=1, source_target_pairs={{0,2},{1,3},{2,0},{3,1},{4,6},{5,7},{6,4},{7,5},{8,10},{9,11},{10,... | collective-permute-start | bytes 49160 | tf_op jit(solution)/shard_map/ppermute | solution.py:838
  41.8 21.0 %copy-start.24 = (bf16[4,8,256]{2,1,0:T(8,128)(2,1)}, bf16[4,8,256]{2,1,0:T(8,128)(2,1)S(1)}, u32[]{:S(2)}) copy-start(bf16[4,8,256]{2,1,0:T(8,128)(2,1)S(1)} %collective-permute-done.10.refs_2_) | copy-start | bytes 49156
  41.8 10.0 %copy-start.25 = (bf16[4,8,256]{2,1,0:T(8,128)(2,1)}, bf16[4,8,256]{2,1,0:T(8,128)(2,1)S(1)}, u32[]{:S(2)}) copy-start(bf16[4,8,256]{2,1,0:T(8,128)(2,1)S(1)} %collective-permute-done.9.refs_1_) | copy-start | bytes 49156
  41.8 24.9 %copy-start.15 = (bf16[4,4,24,768]{3,2,1,0:T(8,128)(2,1)}, bf16[4,4,24,768]{3,2,1,0:T(8,128)(2,1)S(1)}, u32[]{:S(2)}) copy-start(bf16[4,4,24,768]{3,2,1,0:T(8,128)(2,1)S(1)} %collective-permute-done.6.refs_1_) | copy-start | bytes 1769476
  41.8 24.9 %copy-start.16 = (bf16[4,4,24,768]{3,2,1,0:T(8,128)(2,1)}, bf16[4,4,24,768]{3,2,1,0:T(8,128)(2,1)S(1)}, u32[]{:S(2)}) copy-start(bf16[4,4,24,768]{3,2,1,0:T(8,128)(2,1)S(1)} %collective-permute-done.7.refs_2_) | copy-start | bytes 1769476
  41.9 24.9 %copy-start.18 = (bf16[4,4,24,768]{3,2,1,0:T(8,128)(2,1)}, bf16[4,4,24,768]{3,2,1,0:T(8,128)(2,1)S(1)}, u32[]{:S(2)}) copy-start(bf16[4,4,24,768]{3,2,1,0:T(8,128)(2,1)S(1)} %collective-permute-done.8.refs_5_) | copy-start | bytes 1769476
  41.9 20.9 %collective-permute-start.13 = (bf16[4,4,24,768]{3,2,1,0:T(8,128)(2,1)S(1)}, bf16[4,4,24,768]{3,2,1,0:T(8,128)(2,1)S(1)}, u32[]{:S(2)}, u32[]{:S(2)}) collective-permute-start(bf16[4,4,24,768]{3,2,1,0:T(8,128)(2,1)S(1)} %collective-permute-done.6.refs_1_), channel_id=1, source_target_pairs={{0,1},{1,0},{2,3},{3,2},{4,5},{5,4},{6,7},{7,6},{8,9},{9,8},{10,11... | collective-permute-start | bytes 1769480 | tf_op jit(solution)/shard_map/ppermute | solution.py:838
  51.8 11.0 %collective-permute-start.14 = (bf16[4,4,24,768]{3,2,1,0:T(8,128)(2,1)S(1)}, bf16[4,4,24,768]{3,2,1,0:T(8,128)(2,1)S(1)}, u32[]{:S(2)}, u32[]{:S(2)}) collective-permute-start(bf16[4,4,24,768]{3,2,1,0:T(8,128)(2,1)S(1)} %collective-permute-done.7.refs_2_), channel_id=1, source_target_pairs={{0,1},{1,0},{2,3},{3,2},{4,5},{5,4},{6,7},{7,6},{8,9},{9,8},{10,11... | collective-permute-start | bytes 1769480 | tf_op jit(solution)/shard_map/ppermute | solution.py:838
  52.3 9.9 %collective-permute-start.11 = (bf16[2,4,24,768]{3,2,1,0:T(8,128)(2,1)S(1)}, bf16[2,4,24,768]{3,2,1,0:T(8,128)(2,1)}, u32[]{:S(2)}, u32[]{:S(2)}) collective-permute-start(bf16[2,4,24,768]{3,2,1,0:T(8,128)(2,1)S(1)} %slice.54), channel_id=1, source_target_pairs={{0,2},{1,3},{2,0},{3,1},{4,6},{5,7},{6,4},{7,5},{8,10},{9,11},{10,... | collective-permute-start | bytes 884744 | tf_op jit(solution)/shard_map/ppermute | solution.py:838
  54.4 8.4 %collective-permute-start.12 = (bf16[2,4,24,768]{3,2,1,0:T(8,128)(2,1)S(1)}, bf16[2,4,24,768]{3,2,1,0:T(8,128)(2,1)}, u32[]{:S(2)}, u32[]{:S(2)}) collective-permute-start(bf16[2,4,24,768]{3,2,1,0:T(8,128)(2,1)S(1)} %slice.55), channel_id=1, source_target_pairs={{0,4},{1,5},{2,6},{3,7},{4,0},{5,1},{6,2},{7,3},{8,12},{9,13},{10,... | collective-permute-start | bytes 884744 | tf_op jit(solution)/shard_map/ppermute | solution.py:838
  55.5 6.7 %collective-permute-start.15 = (bf16[4,8,256]{2,1,0:T(8,128)(2,1)S(1)}, bf16[4,8,256]{2,1,0:T(8,128)(2,1)S(1)}, u32[]{:S(2)}, u32[]{:S(2)}) collective-permute-start(bf16[4,8,256]{2,1,0:T(8,128)(2,1)S(1)} %collective-permute-done.10.refs_2_), channel_id=1, source_target_pairs={{0,2},{1,3},{2,0},{3,1},{4,6},{5,7},{6,4},{7,5},{8,10},{9,11},{10,... | collective-permute-start | bytes 49160 | tf_op jit(solution)/shard_map/ppermute | solution.py:838
  62.8 3.9 %collective-permute-start.16 = (bf16[2,4,24,768]{3,2,1,0:T(8,128)(2,1)}, bf16[2,4,24,768]{3,2,1,0:T(8,128)(2,1)}, u32[]{:S(2)}, u32[]{:S(2)}) collective-permute-start(bf16[2,4,24,768]{3,2,1,0:T(8,128)(2,1)} %collective-permute-done.11.refs_3_), channel_id=1, source_target_pairs={{0,1},{1,0},{2,3},{3,2},{4,5},{5,4},{6,7},{7,6},{8,9},{9,8},{10,11... | collective-permute-start | bytes 884744 | tf_op jit(solution)/shard_map/ppermute | solution.py:838
  64.0 2.7 collective-permute-start.17
  66.7 5.5 %copy-start.6 = (s32[2,1,6]{2,1,0:T(1,128)S(1)}, s32[2,1,6]{2,1,0:T(1,128)}, u32[]{:S(2)}) copy-start(s32[2,1,6]{2,1,0:T(1,128)} %param.16) | copy-start | bytes 148
  249.4 9.2 %collective-permute-start.18 = (bf16[16,192,384]{2,1,0:T(8,128)(2,1)}, bf16[16,192,384]{2,1,0:T(8,128)(2,1)S(1)}, u32[]{:S(2)}, u32[]{:S(2)}) collective-permute-start(bf16[16,192,384]{2,1,0:T(8,128)(2,1)} %bitcast.89), channel_id=1, source_target_pairs={{0,1},{1,0},{2,3},{3,2},{4,5},{5,4},{6,7},{7,6},{8,9},{9,8},{10,11... | collective-permute-start | bytes 7077896 | tf_op jit(solution)/shard_map/ppermute | solution.py:838
  249.8 8.9 %collective-permute-start.19 = (bf16[16,192,384]{2,1,0:T(8,128)(2,1)}, bf16[16,192,384]{2,1,0:T(8,128)(2,1)}, u32[]{:S(2)}, u32[]{:S(2)}) collective-permute-start(bf16[16,192,384]{2,1,0:T(8,128)(2,1)} %bitcast.88), channel_id=1, source_target_pairs={{0,1},{1,0},{2,3},{3,2},{4,5},{5,4},{6,7},{7,6},{8,9},{9,8},{10,11... | collective-permute-start | bytes 7077896 | tf_op jit(solution)/shard_map/ppermute | solution.py:838
  250.0 8.6 %collective-permute-start.20 = (bf16[16,48,384]{2,1,0:T(8,128)(2,1)}, bf16[16,48,384]{2,1,0:T(8,128)(2,1)S(1)}, u32[]{:S(2)}, u32[]{:S(2)}) collective-permute-start(bf16[16,48,384]{2,1,0:T(8,128)(2,1)} %get-tuple-element.193), channel_id=1, source_target_pairs={{0,1},{1,0},{2,3},{3,2},{4,5},{5,4},{6,7},{7,6},{8,9},{9,8},{10,11... | collective-permute-start | bytes 1769480 | tf_op jit(solution)/shard_map/ppermute | solution.py:838
  250.4 8.3 %copy-start.2 = (bf16[16,4,48,384]{3,2,1,0:T(8,128)(2,1)S(1)}, bf16[16,4,48,384]{3,2,1,0:T(8,128)(2,1)}, u32[]{:S(2)}) copy-start(bf16[16,4,48,384]{3,2,1,0:T(8,128)(2,1)} %get-tuple-element.188) | copy-start | bytes 7077892
  250.4 8.3 %copy-start.3 = (bf16[3072,384]{1,0:T(8,128)(2,1)S(1)}, bf16[3072,384]{1,0:T(8,128)(2,1)}, u32[]{:S(2)}) copy-start(bf16[3072,384]{1,0:T(8,128)(2,1)} %get-tuple-element.189) | copy-start | bytes 7077892
  250.4 8.3 %copy-start.5 = (bf16[16,48,384]{2,1,0:T(8,128)(2,1)S(1)}, bf16[16,48,384]{2,1,0:T(8,128)(2,1)}, u32[]{:S(2)}) copy-start(bf16[16,48,384]{2,1,0:T(8,128)(2,1)} %get-tuple-element.190.refs_2_) | copy-start | bytes 1769476
  261.7 31.1 %collective-permute-start.21 = (bf16[2,2,432,384]{3,2,1,0:T(8,128)(2,1)S(1)}, bf16[2,2,432,384]{3,2,1,0:T(8,128)(2,1)S(1)}, u32[]{:S(2)}, u32[]{:S(2)}) collective-permute-start(bf16[2,2,432,384]{3,2,1,0:T(8,128)(2,1)S(1)} %get-tuple-element.207), channel_id=1, source_target_pairs={{0,2},{1,3},{2,0},{3,1},{4,6},{5,7},{6,4},{7,5},{8,10},{9,11},{10,... | collective-permute-start | bytes 3981320 | tf_op jit(solution)/shard_map/ppermute | solution.py:838
  262.9 30.1 %collective-permute-start.22 = (bf16[2,2,432,384]{3,2,1,0:T(8,128)(2,1)S(1)}, bf16[2,2,432,384]{3,2,1,0:T(8,128)(2,1)S(1)}, u32[]{:S(2)}, u32[]{:S(2)}) collective-permute-start(bf16[2,2,432,384]{3,2,1,0:T(8,128)(2,1)S(1)} %get-tuple-element.208), channel_id=1, source_target_pairs={{0,4},{1,5},{2,6},{3,7},{4,0},{5,1},{6,2},{7,3},{8,12},{9,13},{10,... | collective-permute-start | bytes 3981320 | tf_op jit(solution)/shard_map/ppermute | solution.py:838
  292.0 16.2 %collective-permute-start.25 = (bf16[16,144,384]{2,1,0:T(8,128)(2,1)}, bf16[16,144,384]{2,1,0:T(8,128)(2,1)S(1)}, u32[]{:S(2)}, u32[]{:S(2)}) collective-permute-start(bf16[16,144,384]{2,1,0:T(8,128)(2,1)} %bitcast.90), channel_id=1, source_target_pairs={{0,1},{1,0},{2,3},{3,2},{4,5},{5,4},{6,7},{7,6},{8,9},{9,8},{10,11... | collective-permute-start | bytes 5308424 | tf_op jit(solution)/shard_map/ppermute | solution.py:838
  294.2 15.1 %collective-permute-start.23 = (bf16[2,432,384]{2,1,0:T(8,128)(2,1)S(1)}, bf16[2,432,384]{2,1,0:T(8,128)(2,1)S(1)}, u32[]{:S(2)}, u32[]{:S(2)}) collective-permute-start(bf16[2,432,384]{2,1,0:T(8,128)(2,1)S(1)} %get-tuple-element.225), channel_id=1, source_target_pairs={{0,4},{1,5},{2,6},{3,7},{4,0},{5,1},{6,2},{7,3},{8,12},{9,13},{10,... | collective-permute-start | bytes 1990664 | tf_op jit(solution)/shard_map/ppermute | solution.py:838
  295.2 15.3 %collective-permute-start.24 = (bf16[2,432,384]{2,1,0:T(8,128)(2,1)S(1)}, bf16[2,432,384]{2,1,0:T(8,128)(2,1)S(1)}, u32[]{:S(2)}, u32[]{:S(2)}) collective-permute-start(bf16[2,432,384]{2,1,0:T(8,128)(2,1)S(1)} %get-tuple-element.226), channel_id=1, source_target_pairs={{0,2},{1,3},{2,0},{3,1},{4,6},{5,7},{6,4},{7,5},{8,10},{9,11},{10,... | collective-permute-start | bytes 1990664 | tf_op jit(solution)/shard_map/ppermute | solution.py:838
  295.8 9.7 %copy-start.7 = (f32[4,1,768]{2,1,0:T(1,128)S(1)}, f32[4,1,768]{2,1,0:T(1,128)}, u32[]{:S(2)}) copy-start(f32[4,1,768]{2,1,0:T(1,128)} %get-tuple-element.236.refs_6_) | copy-start | bytes 36868
  295.8 9.7 %copy-start.8 = (f32[3,1,768]{2,1,0:T(1,128)S(1)}, f32[3,1,768]{2,1,0:T(1,128)}, u32[]{:S(2)}) copy-start(f32[3,1,768]{2,1,0:T(1,128)} %get-tuple-element.232.refs_2_) | copy-start | bytes 27652
  295.8 9.7 %copy-start.11 = (f32[1,768]{1,0:T(1,128)S(1)}, f32[1,768]{1,0:T(1,128)}, u32[]{:S(2)}) copy-start(f32[1,768]{1,0:T(1,128)} %get-tuple-element.233.refs_3_) | copy-start | bytes 9220
  295.8 9.7 %copy-start.12 = (f32[1,768]{1,0:T(1,128)S(1)}, f32[1,768]{1,0:T(1,128)}, u32[]{:S(2)}) copy-start(f32[1,768]{1,0:T(1,128)} %get-tuple-element.237.refs_7_) | copy-start | bytes 9220
  295.8 9.7 %copy-start.13 = (f32[1,768]{1,0:T(1,128)S(1)}, f32[1,768]{1,0:T(1,128)}, u32[]{:S(2)}) copy-start(f32[1,768]{1,0:T(1,128)} %get-tuple-element.234.refs_4_) | copy-start | bytes 9220
  295.9 9.7 %copy-start.14 = (f32[1,768]{1,0:T(1,128)S(1)}, f32[1,768]{1,0:T(1,128)}, u32[]{:S(2)}) copy-start(f32[1,768]{1,0:T(1,128)} %get-tuple-element.235.refs_5_) | copy-start | bytes 9220
  305.5 7.1 %copy-start.4 = (bf16[16,3,48,384]{3,2,1,0:T(8,128)(2,1)S(1)}, bf16[16,3,48,384]{3,2,1,0:T(8,128)(2,1)}, u32[]{:S(2)}) copy-start(bf16[16,3,48,384]{3,2,1,0:T(8,128)(2,1)} %get-tuple-element.213) | copy-start | bytes 5308420
  311.4 15.2 %collective-permute-start.30 = (bf16[2,432,384]{2,1,0:T(8,128)(2,1)S(1)}, bf16[2,432,384]{2,1,0:T(8,128)(2,1)S(1)}, u32[]{:S(2)}, u32[]{:S(2)}) collective-permute-start(bf16[2,432,384]{2,1,0:T(8,128)(2,1)S(1)} %get-tuple-element.250), channel_id=1, source_target_pairs={{0,8},{1,9},{2,10},{3,11},{4,12},{5,13},{6,14},{7,15},{8,0},{9,1},... | collective-permute-start | bytes 1990664 | tf_op jit(solution)/shard_map/ppermute | solution.py:838
  313.6 10.5 %collective-permute-start.26 = (bf16[2,2,160,384]{3,2,1,0:T(8,128)(2,1)S(1)}, bf16[2,2,160,384]{3,2,1,0:T(8,128)(2,1)S(1)}, u32[]{:S(2)}, u32[]{:S(2)}) collective-permute-start(bf16[2,2,160,384]{3,2,1,0:T(8,128)(2,1)S(1)} %get-tuple-element.244), channel_id=1, source_target_pairs={{0,2},{1,3},{2,0},{3,1},{4,6},{5,7},{6,4},{7,5},{8,10},{9,11},{10,... | collective-permute-start | bytes 1474568 | tf_op jit(solution)/shard_map/ppermute | solution.py:838
  314.1 10.0 %collective-permute-start.27 = (bf16[2,2,160,384]{3,2,1,0:T(8,128)(2,1)S(1)}, bf16[2,2,160,384]{3,2,1,0:T(8,128)(2,1)S(1)}, u32[]{:S(2)}, u32[]{:S(2)}) collective-permute-start(bf16[2,2,160,384]{3,2,1,0:T(8,128)(2,1)S(1)} %get-tuple-element.245), channel_id=1, source_target_pairs={{0,4},{1,5},{2,6},{3,7},{4,0},{5,1},{6,2},{7,3},{8,12},{9,13},{10,... | collective-permute-start | bytes 1474568 | tf_op jit(solution)/shard_map/ppermute | solution.py:838
  324.9 5.1 %collective-permute-start.28 = (bf16[2,160,384]{2,1,0:T(8,128)(2,1)S(1)}, bf16[2,160,384]{2,1,0:T(8,128)(2,1)S(1)}, u32[]{:S(2)}, u32[]{:S(2)}) collective-permute-start(bf16[2,160,384]{2,1,0:T(8,128)(2,1)S(1)} %get-tuple-element.248), channel_id=1, source_target_pairs={{0,4},{1,5},{2,6},{3,7},{4,0},{5,1},{6,2},{7,3},{8,12},{9,13},{10,... | collective-permute-start | bytes 737288 | tf_op jit(solution)/shard_map/ppermute | solution.py:838
  326.2 5.0 %collective-permute-start.29 = (bf16[2,160,384]{2,1,0:T(8,128)(2,1)S(1)}, bf16[2,160,384]{2,1,0:T(8,128)(2,1)S(1)}, u32[]{:S(2)}, u32[]{:S(2)}) collective-permute-start(bf16[2,160,384]{2,1,0:T(8,128)(2,1)S(1)} %get-tuple-element.249), channel_id=1, source_target_pairs={{0,2},{1,3},{2,0},{3,1},{4,6},{5,7},{6,4},{7,5},{8,10},{9,11},{10,... | collective-permute-start | bytes 737288 | tf_op jit(solution)/shard_map/ppermute | solution.py:838
  331.9 7.0 %collective-permute-start.31 = (bf16[2,160,384]{2,1,0:T(8,128)(2,1)S(1)}, bf16[2,160,384]{2,1,0:T(8,128)(2,1)S(1)}, u32[]{:S(2)}, u32[]{:S(2)}) collective-permute-start(bf16[2,160,384]{2,1,0:T(8,128)(2,1)S(1)} %get-tuple-element.254), channel_id=1, source_target_pairs={{0,8},{1,9},{2,10},{3,11},{4,12},{5,13},{6,14},{7,15},{8,0},{9,1},... | collective-permute-start | bytes 737288 | tf_op jit(solution)/shard_map/ppermute | solution.py:838
  332.3 16.8 %collective-permute-start.34 = (bf16[432,384]{1,0:T(8,128)(2,1)S(1)}, bf16[432,384]{1,0:T(8,128)(2,1)S(1)}, u32[]{:S(2)}, u32[]{:S(2)}) collective-permute-start(bf16[432,384]{1,0:T(8,128)(2,1)S(1)} %fusion), channel_id=1, source_target_pairs={{0,16},{1,17},{2,18},{3,19},{4,20},{5,21},{6,22},{7,23},{8,24},{9,... | collective-permute-start | bytes 995336 | tf_op jit(solution)/shard_map/ppermute | solution.py:838
  339.0 21.9 %copy-start.1 = (bf16[48,3072]{1,0:T(8,128)(2,1)S(1)}, bf16[48,3072]{1,0:T(8,128)(2,1)}, u32[]{:S(2)}) copy-start(bf16[48,3072]{1,0:T(8,128)(2,1)} %param.26) | copy-start | bytes 884740
  339.0 15.7 %collective-permute-start.32 = (bf16[160,384]{1,0:T(8,128)(2,1)S(1)}, bf16[160,384]{1,0:T(8,128)(2,1)S(1)}, u32[]{:S(2)}, u32[]{:S(2)}) collective-permute-start(bf16[160,384]{1,0:T(8,128)(2,1)S(1)} %fusion.1), channel_id=1, source_target_pairs={{0,16},{1,17},{2,18},{3,19},{4,20},{5,21},{6,22},{7,23},{8,24},{9,... | collective-permute-start | bytes 368648 | tf_op jit(solution)/shard_map/ppermute | solution.py:838
  349.2 10.5 %collective-permute-start.35 = (f32[432,384]{1,0:T(8,128)S(1)}, f32[432,384]{1,0:T(8,128)S(1)}, u32[]{:S(2)}, u32[]{:S(2)}) collective-permute-start(f32[432,384]{1,0:T(8,128)S(1)} %bitcast_add_fusion.half_ref), channel_id=1, source_target_pairs={{0,1},{1,0},{2,3},{3,2},{4,5},{5,4},{6,7},{7,6},{8,9},{9,8},{10,11... | collective-permute-start | bytes 1990664 | tf_op jit(solution)/shard_map/ppermute | solution.py:838
  354.8 2.3 collective-permute-start.33
  (8 other events, 18.3 us)
Sparse Core Ops, SparseCore 0:
  11.6 89.5 all-gather.2

commit v6 on v5

--- a/solution.py
+++ b/solution.py
@@ -573,18 +573,31 @@
 ):
     if micro is None:
         micro = pl.program_id(0)
-        state_ref, gain_ref, gmix_ref, grad_ref, dgain_ref, dshift_ref, *rest = rest
-        finish = functools.partial(
-            input_gradient, dhid_ref, state_ref, gmix_ref, out_ref, gain_ref, None,
-            grad_ref, dgain_ref, dshift_ref,
-        )
+        weight_ref, state_ref, gain_ref, gmix_ref, grad_ref, dgain_ref, dshift_ref, *rest = rest
+        *rest, weight_buf, sem = rest
+        late = pltpu.make_async_copy(weight_ref.at[pl.ds(0, 3)], weight_buf, sem.at[0])
+
+        @pl.when(micro == 0)
+        def _():
+            late.start()
+
+        def finish():
+            @pl.when(micro == 0)
+            def _():
+                late.wait()
+
+            input_gradient(
+                dhid_ref, state_ref, gmix_ref, weight_buf, gain_ref, None,
+                grad_ref, dgain_ref, dshift_ref,
+            )
+
     else:
         gmix_ref, *rest = rest
         finish = None
     datt_ref, bias_ref, delta_ref, dq_ref = rest
     count = dhid_ref.shape[0]
     low_grad = dhid_ref[...].astype(jnp.bfloat16)
-    datt = dot_transposed(low_grad, out_ref[out_ref.shape[0] - 1]).astype(jnp.bfloat16)
+    datt = dot_transposed(low_grad, out_ref[0]).astype(jnp.bfloat16)
     datt_ref[...] = datt
     product = datt.astype(jnp.float32) * att_ref[...].astype(jnp.float32)
     high = product.astype(jnp.bfloat16)
@@ -676,7 +689,7 @@
         jax.ShapeDtypeStruct((1, width), jnp.float32),
         jax.ShapeDtypeStruct((1, width), jnp.float32),
     )
-    inputs = [dhid, att, mixed, lse, weight, state, gain]
+    inputs = [dhid, att, mixed, lse, weight, weight, state, gain]
     return pl.pallas_call(
         functools.partial(attention_backward_kernel, docs, back, None),
         grid=(micro,),
@@ -687,7 +700,8 @@
             rows_of(count, width),
             rows_of(count, 3 * width),
             pl.BlockSpec((H, 1, count), lambda i: (i, 0, 0)),
-            whole(weight),
+            pl.BlockSpec((1, width, width), lambda i: (3, 0, 0), pipeline_mode=pl.Buffered(1)),
+            pl.BlockSpec(memory_space=pltpu.HBM),
             rows_of(count, width),
             whole(gain),
         ],
@@ -697,6 +711,8 @@
             pltpu.VMEM((count, count), jnp.float32),
             pltpu.VMEM((H, 1, count), jnp.float32),
             pltpu.VMEM((count, LANES), jnp.float32),
+            pltpu.VMEM((3, width, width), jnp.bfloat16),
+            pltpu.SemaphoreType.DMA((1,)),
         ],
         compiler_params=params(44 << 20),
         cost_estimate=cost(
@@ -1104,10 +1120,12 @@
         part = lax.dynamic_slice_in_dim(weight, core * 24, 24, 0)
         return jnp.transpose(part.reshape(24, -1, FEATURES), (1, 0, 2))
 
-    columns = lax.dynamic_slice_in_dim(fc, core * 2 * FEATURES, 2 * FEATURES, 1)
-    columns = jnp.transpose(columns.reshape(48, 2, FEATURES), (1, 0, 2))
+    columns = [
+        lax.dynamic_slice_in_dim(fc, core * 2 * FEATURES + part * FEATURES, FEATURES, 1)
+        for part in range(2)
+    ]
     across = lax.dynamic_slice_in_dim(proj, core * 96, 96, 0).reshape(2, 48, FEATURES)
-    mlp = lax.all_gather(jnp.concatenate([columns, across]), BOTH)
+    mlp = lax.all_gather(jnp.stack([*columns, across[0], across[1]]), BOTH)
     mlp = mlp.reshape(16, 2, 4, 48, FEATURES)
     vectors = [gain_a, shift_a, qbias, obias, gain_m, shift_m, fbias, pbias]
     sizes = tuple(vector.shape[0] for vector in vectors)

time: 372 us -> 372 us (level)
  no operation moved by 1% of the time
where the time goes in v6:
time: 372 us; the launch traced here: 368 us
  Pallas kernels  234 us (63%)
  waiting for transfers between devices  59.9 us (16%)
  starting transfers between devices  50.8 us (14%)
  between operations  15 us (4%)
  local copies, waits for them, and re-layouts  7.25 us (2%)
    pallas_call x2, Pallas kernels, mlp_backward(): pl.pallas_call(functools.partial(mlp_backward_kernel, earlier is not None...  81.4 us
    ppermute x36, starting transfers between devices, swap(): return lax.ppermute(value, BOTH, [(i, i ^ bits) for i in range(32)])  50.8 us
    ppermute x36, waiting for transfers between devices, swap(): return lax.ppermute(value, BOTH, [(i, i ^ bits) for i in range(32)])  49.4 us
    pallas_call x2, Pallas kernels, attention_forward(): pl.pallas_call(functools.partial(attention_forward_kernel, docs, back), g...  40.6 us
    pallas_call x1, Pallas kernels, attention_backward_all(): pl.pallas_call(functools.partial(attention_backward_kernel, docs, back, N...  28.9 us
    pallas_call x2, Pallas kernels, attention_backward(): pl.pallas_call(functools.partial(attention_backward_kernel, docs, back, m...  21 us
    pallas_call x1, Pallas kernels, mlp_forward(): pl.pallas_call(mlp_forward_kernel, grid=(hidden_units // block,), out_sha...  17 us
    pallas_call x2, Pallas kernels, attention_terms(): pl.pallas_call(functools.partial(attention_terms_kernel, earlier is not N...  16.1 us
  transfers between devices with their start and end apart: 37, of which 15 were waited for; matrix products, arithmetic and copies ran while one was open for 1% of the time, Pallas kernels for 22%

profile of v6, /device:TPU:1, one launch (start us, length us, event | category | flops | bytes accessed | tf_op | source)
XLA Modules:
  0.0 368.2 jit_solution(6502048149143319627)
XLA Ops:
  7.3 1.1 dynamic-slice_bitcast_fusion.1
  8.4 0.8 pad_maximum_fusion
  9.2 0.8 dynamic-slice_bitcast_fusion.4
  10.0 2.2 collective-permute-start
  12.2 2.3 collective-permute-start.1
  14.5 0.7 pad.27
  15.2 0.7 pad.28
  15.9 0.7 pad.29
  17.1 3.2 collective-permute-start.4
  20.3 1.2 collective-permute-done.3
  21.5 1.9 collective-permute-start.5
  23.4 5.8 %collective-permute-done.4 = bf16[1,8,256]{2,1,0:T(8,128)(2,1)S(1)} collective-permute-done((bf16[1,8,256]{2,1,0:T(8,128)(2,1)S(1)}, bf16[1,8,256]{2,1,0:T(8,128)(2,1)S(1)}, u32[]{:S(2)}, u32[]{:S(2)}) %collective-permute-start.4) | collective-permute-done | bytes 4128 | tf_op jit(solution)/shard_map/ppermute | solution.py:854
  29.3 1.3 collective-permute-start.6
  30.6 1.5 collective-permute-start.7
  32.1 5.0 %collective-permute-start.8 = (bf16[4,4,24,768]{3,2,1,0:T(8,128)(2,1)S(1)}, bf16[4,4,24,768]{3,2,1,0:T(8,128)(2,1)S(1)}, u32[]{:S(2)}, u32[]{:S(2)}) collective-permute-start(bf16[4,4,24,768]{3,2,1,0:T(8,128)(2,1)S(1)} %constant_dynamic-update-slice_fusion.4.refs_0_), channel_id=1, source_target_pairs={{0,1},{1,0},{2,3},{3,2},{4,5},{5,4},{6,7},{7,6},{8,9},{9,8},{10,11... | collective-permute-start | bytes 1769480 | tf_op jit(solution)/shard_map/ppermute | solution.py:854
  37.6 3.6 collective-permute-done.10.refs_2_
  41.2 9.9 %collective-permute-start.13 = (bf16[4,4,24,768]{3,2,1,0:T(8,128)(2,1)S(1)}, bf16[4,4,24,768]{3,2,1,0:T(8,128)(2,1)S(1)}, u32[]{:S(2)}, u32[]{:S(2)}) collective-permute-start(bf16[4,4,24,768]{3,2,1,0:T(8,128)(2,1)S(1)} %collective-permute-done.6.refs_1_), channel_id=1, source_target_pairs={{0,1},{1,0},{2,3},{3,2},{4,5},{5,4},{6,7},{7,6},{8,9},{9,8},{10,11... | collective-permute-start | bytes 1769480 | tf_op jit(solution)/shard_map/ppermute | solution.py:854
  51.6 0.7 collective-permute-start.11
  52.4 1.7 collective-permute-start.12
  54.6 6.1 %collective-permute-done.15.refs_3_ = bf16[4,8,256]{2,1,0:T(8,128)(2,1)S(1)} collective-permute-done((bf16[4,8,256]{2,1,0:T(8,128)(2,1)S(1)}, bf16[4,8,256]{2,1,0:T(8,128)(2,1)S(1)}, u32[]{:S(2)}, u32[]{:S(2)}) %collective-permute-start.15) | collective-permute-done | bytes 16416 | tf_op jit(solution)/shard_map/ppermute | solution.py:854
  61.3 0.9 collective-permute-start.16
  62.3 2.7 place_small.1
  65.0 4.9 %place.1 = bf16[4,32,24,768]{3,2,1,0:T(8,128)(2,1)} custom-call(s32[1]{0:T(128)} %bitcast.4.me_ref, bf16[4,4,24,768]{3,2,1,0:T(8,128)(2,1)} %copy-done.17, bf16[4,4,24,768]{3,2,1,0:T(8,128)(2,1)} %copy-done.15, bf16[4,4,24,768]{3,2,1,0:T(8,128)(2,1)} %copy-done.16, bf16[2,4,24,768]{3,2,1,0:T(8,128)(2,1)} %collective-permute-done.11.refs_3_, ...), custom_call_target="tpu_custom_call" | custom-call | tf_op jit(solution)/shard_map/place/pallas_call | solution.py:878
  69.9 19.7 %attention_forward.2 = (bf16[1024,768]{1,0:T(8,128)(2,1)}, bf16[1024,2304]{1,0:T(8,128)(2,1)}, bf16[1024,768]{1,0:T(8,128)(2,1)}, f32[24,1,512]{2,1,0:T(1,128)},...) custom-call(s32[2,6]{1,0:T(2,128)S(1)} %bitcast.64, bf16[1024,768]{1,0:T(8,128)(2,1)} %bitcast.82, ...), custom_call_target="tpu_custom_call" | custom-call | flops 805306368 | bytes 2368512 | tf_op jit(solution)/shard_map/attention_forward/pallas_call | solution.py:205
  89.7 10.5 %all-gather.3.cloned.1.call-done = bf16[128,48,768]{2,1,0:T(8,128)(2,1)} async-done(((bf16[4,48,768]{2,1,0:T(8,128)(2,1)}), bf16[128,48,768]{2,1,0:T(8,128)(2,1)}) %all-gather.3.cloned.1.call-update) | async-done | bytes 9437200 | tf_op jit(solution)/shard_map/all_gather | solution.py:1128
  100.2 17.0 %mlp_forward.1 = (bf16[1024,3072]{1,0:T(8,128)(2,1)}, f32[1024,768]{1,0:T(8,128)}) custom-call(f32[1024,768]{1,0:T(8,128)} %get-tuple-element.161.hidden_ref, bf16[1024,768]{1,0:T(8,128)(2,1)} %get-tuple-element.162.normed_ref, bf16[16,2,4,48,768]{4,3,2,1,0:T(8,128)(2,1)} %bitcast.69, f32[1,3072]{1,0:T(1,128)} %get-tuple-element.163.fbias_ref.rest_0_, ...), custom_call_target="tpu_custom_call" | custom-call | flops 1207959552 | bytes 2949120 | tf_op jit(solution)/shard_map/mlp_forward/pallas_call | solution.py:286
  117.3 20.8 %attention_forward.3 = (bf16[1024,768]{1,0:T(8,128)(2,1)}, bf16[1024,2304]{1,0:T(8,128)(2,1)}, bf16[1024,768]{1,0:T(8,128)(2,1)}, f32[24,1,512]{2,1,0:T(1,128)},...) custom-call(s32[2,6]{1,0:T(2,128)S(1)} %bitcast.65, f32[1024,768]{1,0:T(8,128)} %get-tuple-element.165.state_ref.rest_1_, ...), custom_call_target="tpu_custom_call" | custom-call | flops 805306368 | bytes 2565120 | tf_op jit(solution)/shard_map/attention_forward/pallas_call | solution.py:205
  138.1 45.0 %mlp_backward.2 = (bf16[1024,768]{1,0:T(8,128)(2,1)}, f32[1024,768]{1,0:T(8,128)}, bf16[16,4,48,384]{3,2,1,0:T(8,128)(2,1)}, bf16[16,4,48,384]{3,2,1,0:T(8,128)(...) custom-call(s32[1]{0:T(128)} %bitcast.core_ref.unused_ref, ...), custom_call_target="tpu_custom_call" | custom-call | flops 2415919104 | bytes 5264640 | tf_op jit(solution)/shard_map/mlp_backward/pallas_call | solution.py:512
  183.0 28.9 %attention_backward_all.1 = (bf16[1024,2304]{1,0:T(8,128)(2,1)}, f32[1024,768]{1,0:T(8,128)}, f32[1,768]{1,0:T(1,128)S(1)}, f32[1,768]{1,0:T(1,128)S(1)}) custom-call(s32[2,6]{1,0:T(2,128)S(1)} %bitcast.66, f32[1024,768]{1,0:T(8,128)} %get-tuple-element.170.dhid_ref, bf16[1024,768]{1,0:T(8,128)(2,1)} %get-tuple-element.168.att_ref, ...), custom_call_target="tpu_custom_call" | custom-call | flops 1107296256 | bytes 3742848 | tf_op jit(solution)/shard_map/attention_backward_all/pallas_call | solution.py:693
  213.2 36.5 %mlp_backward.3 = (f32[1024,768]{1,0:T(8,128)}, bf16[16,4,48,384]{3,2,1,0:T(8,128)(2,1)}, bf16[16,4,48,384]{3,2,1,0:T(8,128)(2,1)}, bf16[3072,384]{1,0:T(8,128)(...) custom-call(s32[1]{0:T(128)} %bitcast.core_ref.unused_ref, ...), custom_call_target="tpu_custom_call" | custom-call | flops 2415919104 | bytes 7379328 | tf_op jit(solution)/shard_map/mlp_backward/pallas_call | solution.py:512
  250.6 8.3 %attention_terms.2 = (bf16[16,3,48,384]{3,2,1,0:T(8,128)(2,1)}, bf16[16,3,48,384]{3,2,1,0:T(8,128)(2,1)}, f32[3,1,768]{2,1,0:T(1,128)}) custom-call(s32[1]{0:T(128)} %bitcast.core_ref.unused_ref, bf16[1024,768]{1,0:T(8,128)(2,1)} %get-tuple-element.194.normed_ref, bf16[1024,2304]{1,0:T(8,128)(2,1)} %get-tuple-element.195.rest_0_), custom_call_target="tpu_custom_call" | custom-call | flops 452984832 | bytes 1229952 | tf_op jit(solution)/shard_map/attention_terms/pallas_call | solution.py:759
  258.9 3.1 first_sums.2
  262.0 1.2 collective-permute-start.21
  263.5 10.4 %attention_backward.3.rest_1_ = bf16[512,2304]{1,0:T(8,128)(2,1)S(1)} custom-call(s32[2,6]{1,0:T(2,128)S(1)} %bitcast.67, f32[1024,768]{1,0:T(8,128)} %get-tuple-element.204.dhid_ref, bf16[1024,768]{1,0:T(8,128)(2,1)} %get-tuple-element.174.att_ref, bf16[1024,2304]{1,0:T(8,128)(2,1)} %get-tuple-element.205.mixed_ref, ...), custom_call_target="tpu_custom_call" | custom-call | flops 327155712 | bytes 589824 | tf_op jit(solution)/shard_map/attention_backward/pallas_call | solution.py:655
  273.9 10.6 %attention_backward.2.rest_0_ = bf16[512,2304]{1,0:T(8,128)(2,1)S(1)} custom-call(s32[2,6]{1,0:T(2,128)S(1)} %bitcast.68, f32[1024,768]{1,0:T(8,128)} %get-tuple-element.204.dhid_ref, bf16[1024,768]{1,0:T(8,128)(2,1)} %get-tuple-element.174.att_ref, bf16[1024,2304]{1,0:T(8,128)(2,1)} %get-tuple-element.205.mixed_ref, ...), custom_call_target="tpu_custom_call" | custom-call | flops 327155712 | bytes 589824 | tf_op jit(solution)/shard_map/attention_backward/pallas_call | solution.py:655
  284.5 7.8 %attention_terms.3 = (bf16[16,3,48,384]{3,2,1,0:T(8,128)(2,1)}, bf16[16,3,48,384]{3,2,1,0:T(8,128)(2,1)}, f32[3,1,768]{2,1,0:T(1,128)}) custom-call(s32[1]{0:T(128)} %bitcast.core_ref.unused_ref, bf16[1024,768]{1,0:T(8,128)(2,1)} %get-tuple-element.209.normed_ref, bf16[512,2304]{1,0:T(8,128)(2,1)S(1)} %attention_backward.2.rest_0_, ...), custom_call_target="tpu_custom_call" | custom-call | flops 452984832 | bytes 1673472 | tf_op jit(solution)/shard_map/attention_terms/pallas_call | solution.py:759
  292.2 0.8 collective-permute-start.25
  293.3 1.2 second_sums.2
  294.5 1.0 collective-permute-start.23
  295.5 0.6 collective-permute-start.24
  296.2 9.6 %attention_input.1 = (bf16[1024,768]{1,0:T(8,128)(2,1)}, f32[1,768]{1,0:T(1,128)S(1)}, f32[1,768]{1,0:T(1,128)S(1)}) custom-call(f32[1024,768]{1,0:T(8,128)} %get-tuple-element.204.dhid_ref, bf16[1024,768]{1,0:T(8,128)(2,1)} %bitcast.83, bf16[4,768,768]{2,1,0:T(8,128)(2,1)} %bitcast.81, f32[1,768]{1,0:T(1,128)} %get-tuple-element.150.gain_ref.rest_2_, ...), custom_call_target="tpu_custom_call" | custom-call | flops 452984832 | bytes 1968000 | tf_op jit(solution)/shard_map/attention_input/pallas_call | solution.py:812
  305.9 2.7 pack_small.1.refs_2_
  308.5 1.1 collective-permute-done.23.near_in
  309.6 1.2 collective-permute-done.24.far_in
  310.8 0.9 third_sums.2
  311.7 1.2 collective-permute-start.30
  312.9 1.0 first_sums.3
  314.3 1.1 collective-permute-start.27
  315.5 8.8 %collective-permute-done.26.near_in = bf16[2,2,160,384]{3,2,1,0:T(8,128)(2,1)S(1)} collective-permute-done((bf16[2,2,160,384]{3,2,1,0:T(8,128)(2,1)S(1)}, bf16[2,2,160,384]{3,2,1,0:T(8,128)(2,1)S(1)}, u32[]{:S(2)}, u32[]{:S(2)}) %collective-permute-start.26) | collective-permute-done | bytes 491552 | tf_op jit(solution)/shard_map/ppermute | solution.py:854
  324.3 0.8 second_sums.3
  325.1 1.4 collective-permute-start.28
  326.9 3.3 collective-permute-done.28.near_in
  330.2 1.4 collective-permute-done.29.far_in
  331.6 0.7 third_sums.3
  332.6 1.6 collective-permute-start.34
  334.2 5.1 %collective-permute-done.31 = bf16[2,160,384]{2,1,0:T(8,128)(2,1)S(1)} collective-permute-done((bf16[2,160,384]{2,1,0:T(8,128)(2,1)S(1)}, bf16[2,160,384]{2,1,0:T(8,128)(2,1)S(1)}, u32[]{:S(2)}, u32[]{:S(2)}) %collective-permute-start.31) | collective-permute-done | bytes 245792 | tf_op jit(solution)/shard_map/ppermute | solution.py:854
  339.4 9.9 %collective-permute-done.34 = bf16[432,384]{1,0:T(8,128)(2,1)S(1)} collective-permute-done((bf16[432,384]{1,0:T(8,128)(2,1)S(1)}, bf16[432,384]{1,0:T(8,128)(2,1)S(1)}, u32[]{:S(2)}, u32[]{:S(2)}) %collective-permute-start.34) | collective-permute-done | bytes 331808 | tf_op jit(solution)/shard_map/ppermute | solution.py:854
  349.4 5.5 %collective-permute-start.35 = (f32[432,384]{1,0:T(8,128)S(1)}, f32[432,384]{1,0:T(8,128)S(1)}, u32[]{:S(2)}, u32[]{:S(2)}) collective-permute-start(f32[432,384]{1,0:T(8,128)S(1)} %bitcast_add_fusion.half_ref), channel_id=1, source_target_pairs={{0,1},{1,0},{2,3},{3,2},{4,5},{5,4},{6,7},{7,6},{8,9},{9,8},{10,11... | collective-permute-start | bytes 1990664 | tf_op jit(solution)/shard_map/ppermute | solution.py:854
  355.0 1.2 collective-permute-start.33
  356.2 1.1 collective-permute-done.33.other_ref
  357.4 0.8 assemble.2
  358.2 0.6 slice.80
  359.4 0.6 slice_bitcast_fusion
  360.0 1.1 assemble.3
  (134 shorter events, 7.7 us)
Async XLA Ops:
  7.2 2.0 copy-start
  7.2 9.3 %copy-start.25 = (bf16[48]{0:T(256)(128)(2,1)S(1)}, bf16[48]{0:T(256)(128)(2,1)}, u32[]{:S(2)}) copy-start(bf16[48]{0:T(256)(128)(2,1)} %param.23) | copy-start | bytes 292
  7.2 9.3 %copy-start.26 = (bf16[48]{0:T(256)(128)(2,1)S(1)}, bf16[48]{0:T(256)(128)(2,1)}, u32[]{:S(2)}) copy-start(bf16[48]{0:T(256)(128)(2,1)} %param.24) | copy-start | bytes 292
  7.2 9.4 %copy-start.27 = (bf16[48]{0:T(256)(128)(2,1)S(1)}, bf16[48]{0:T(256)(128)(2,1)}, u32[]{:S(2)}) copy-start(bf16[48]{0:T(256)(128)(2,1)} %param.25) | copy-start | bytes 292
  7.2 9.4 %copy-start.28 = (bf16[192]{0:T(256)(128)(2,1)S(1)}, bf16[192]{0:T(256)(128)(2,1)}, u32[]{:S(2)}) copy-start(bf16[192]{0:T(256)(128)(2,1)} %param.27) | copy-start | bytes 1156
  7.2 9.4 %copy-start.29 = (bf16[48]{0:T(256)(128)(2,1)S(1)}, bf16[48]{0:T(256)(128)(2,1)}, u32[]{:S(2)}) copy-start(bf16[48]{0:T(256)(128)(2,1)} %param.29) | copy-start | bytes 292
  7.2 93.0 %all-gather.3.cloned.1.call-start = ((), (), s32[]{:S(2)}) async-start(), calls=%async_computation | async-start | bytes 9732096 | tf_op jit(solution)/shard_map/all_gather | solution.py:1128
  10.0 19.2 %collective-permute-start = (bf16[1,4,24,768]{3,2,1,0:T(8,128)(2,1)S(1)}, bf16[1,4,24,768]{3,2,1,0:T(8,128)(2,1)S(1)}, u32[]{:S(2)}, u32[]{:S(2)}) collective-permute-start(bf16[1,4,24,768]{3,2,1,0:T(8,128)(2,1)S(1)} %maximum_bitcast_fusion), channel_id=1, source_target_pairs={{0,8},{1,9},{2,10},{3,11},{4,12},{5,13},{6,14},{7,15},{8,0},{9,1},... | collective-permute-start | bytes 442376 | tf_op jit(solution)/shard_map/ppermute | solution.py:854
  12.2 17.0 %collective-permute-start.1 = (bf16[1,4,24,768]{3,2,1,0:T(8,128)(2,1)S(1)}, bf16[1,4,24,768]{3,2,1,0:T(8,128)(2,1)S(1)}, u32[]{:S(2)}, u32[]{:S(2)}) collective-permute-start(bf16[1,4,24,768]{3,2,1,0:T(8,128)(2,1)S(1)} %maximum_bitcast_fusion), channel_id=1, source_target_pairs={{0,16},{1,17},{2,18},{3,19},{4,20},{5,21},{6,22},{7,23},{8,24},{9,... | collective-permute-start | bytes 442376 | tf_op jit(solution)/shard_map/ppermute | solution.py:854
  14.5 14.7 %collective-permute-start.2 = (bf16[1,4,24,768]{3,2,1,0:T(8,128)(2,1)S(1)}, bf16[1,4,24,768]{3,2,1,0:T(8,128)(2,1)S(1)}, u32[]{:S(2)}, u32[]{:S(2)}) collective-permute-start(bf16[1,4,24,768]{3,2,1,0:T(8,128)(2,1)S(1)} %maximum_bitcast_fusion), channel_id=1, source_target_pairs={{0,24},{1,25},{2,26},{3,27},{4,28},{5,29},{6,30},{7,31},{8,16},{9,... | collective-permute-start | bytes 442376 | tf_op jit(solution)/shard_map/ppermute | solution.py:854
  16.7 4.8 %collective-permute-start.3 = (bf16[1,8,256]{2,1,0:T(8,128)(2,1)S(1)}, bf16[1,8,256]{2,1,0:T(8,128)(2,1)S(1)}, u32[]{:S(2)}, u32[]{:S(2)}) collective-permute-start(bf16[1,8,256]{2,1,0:T(8,128)(2,1)S(1)} %bitcast.87), channel_id=1, source_target_pairs={{0,8},{1,9},{2,10},{3,11},{4,12},{5,13},{6,14},{7,15},{8,0},{9,1},... | collective-permute-start | bytes 12296 | tf_op jit(solution)/shard_map/ppermute | solution.py:854
  17.1 12.1 %collective-permute-start.4 = (bf16[1,8,256]{2,1,0:T(8,128)(2,1)S(1)}, bf16[1,8,256]{2,1,0:T(8,128)(2,1)S(1)}, u32[]{:S(2)}, u32[]{:S(2)}) collective-permute-start(bf16[1,8,256]{2,1,0:T(8,128)(2,1)S(1)} %bitcast.88), channel_id=1, source_target_pairs={{0,16},{1,17},{2,18},{3,19},{4,20},{5,21},{6,22},{7,23},{8,24},{9,... | collective-permute-start | bytes 12296 | tf_op jit(solution)/shard_map/ppermute | solution.py:854
  21.5 7.7 %collective-permute-start.5 = (bf16[1,8,256]{2,1,0:T(8,128)(2,1)S(1)}, bf16[1,8,256]{2,1,0:T(8,128)(2,1)S(1)}, u32[]{:S(2)}, u32[]{:S(2)}) collective-permute-start(bf16[1,8,256]{2,1,0:T(8,128)(2,1)S(1)} %bitcast.89), channel_id=1, source_target_pairs={{0,24},{1,25},{2,26},{3,27},{4,28},{5,29},{6,30},{7,31},{8,16},{9,... | collective-permute-start | bytes 12296 | tf_op jit(solution)/shard_map/ppermute | solution.py:854
  29.3 35.7 %copy-start.17 = (bf16[4,4,24,768]{3,2,1,0:T(8,128)(2,1)}, bf16[4,4,24,768]{3,2,1,0:T(8,128)(2,1)S(1)}, u32[]{:S(2)}) copy-start(bf16[4,4,24,768]{3,2,1,0:T(8,128)(2,1)S(1)} %constant_dynamic-update-slice_fusion.4.refs_0_) | copy-start | bytes 1769476
  29.3 11.9 %collective-permute-start.6 = (bf16[4,4,24,768]{3,2,1,0:T(8,128)(2,1)S(1)}, bf16[4,4,24,768]{3,2,1,0:T(8,128)(2,1)S(1)}, u32[]{:S(2)}, u32[]{:S(2)}) collective-permute-start(bf16[4,4,24,768]{3,2,1,0:T(8,128)(2,1)S(1)} %constant_dynamic-update-slice_fusion.4.refs_0_), channel_id=1, source_target_pairs={{0,2},{1,3},{2,0},{3,1},{4,6},{5,7},{6,4},{7,5},{8,10},{9,11},{10,... | collective-permute-start | bytes 1769480 | tf_op jit(solution)/shard_map/ppermute | solution.py:854
  30.6 10.6 %collective-permute-start.7 = (bf16[4,4,24,768]{3,2,1,0:T(8,128)(2,1)S(1)}, bf16[4,4,24,768]{3,2,1,0:T(8,128)(2,1)S(1)}, u32[]{:S(2)}, u32[]{:S(2)}) collective-permute-start(bf16[4,4,24,768]{3,2,1,0:T(8,128)(2,1)S(1)} %constant_dynamic-update-slice_fusion.4.refs_0_), channel_id=1, source_target_pairs={{0,4},{1,5},{2,6},{3,7},{4,0},{5,1},{6,2},{7,3},{8,12},{9,13},{10,... | collective-permute-start | bytes 1769480 | tf_op jit(solution)/shard_map/ppermute | solution.py:854
  32.1 9.1 %collective-permute-start.8 = (bf16[4,4,24,768]{3,2,1,0:T(8,128)(2,1)S(1)}, bf16[4,4,24,768]{3,2,1,0:T(8,128)(2,1)S(1)}, u32[]{:S(2)}, u32[]{:S(2)}) collective-permute-start(bf16[4,4,24,768]{3,2,1,0:T(8,128)(2,1)S(1)} %constant_dynamic-update-slice_fusion.4.refs_0_), channel_id=1, source_target_pairs={{0,1},{1,0},{2,3},{3,2},{4,5},{5,4},{6,7},{7,6},{8,9},{9,8},{10,11... | collective-permute-start | bytes 1769480 | tf_op jit(solution)/shard_map/ppermute | solution.py:854
  37.1 14.0 %copy-start.21 = (bf16[4,8,256]{2,1,0:T(8,128)(2,1)}, bf16[4,8,256]{2,1,0:T(8,128)(2,1)S(1)}, u32[]{:S(2)}) copy-start(bf16[4,8,256]{2,1,0:T(8,128)(2,1)S(1)} %constant_dynamic-update-slice_fusion.refs_0_) | copy-start | bytes 49156
  37.2 4.0 %collective-permute-start.10 = (bf16[4,8,256]{2,1,0:T(8,128)(2,1)S(1)}, bf16[4,8,256]{2,1,0:T(8,128)(2,1)S(1)}, u32[]{:S(2)}, u32[]{:S(2)}) collective-permute-start(bf16[4,8,256]{2,1,0:T(8,128)(2,1)S(1)} %constant_dynamic-update-slice_fusion.refs_0_), channel_id=1, source_target_pairs={{0,4},{1,5},{2,6},{3,7},{4,0},{5,1},{6,2},{7,3},{8,12},{9,13},{10,... | collective-permute-start | bytes 49160 | tf_op jit(solution)/shard_map/ppermute | solution.py:854
  37.2 3.9 %collective-permute-start.9 = (bf16[4,8,256]{2,1,0:T(8,128)(2,1)S(1)}, bf16[4,8,256]{2,1,0:T(8,128)(2,1)S(1)}, u32[]{:S(2)}, u32[]{:S(2)}) collective-permute-start(bf16[4,8,256]{2,1,0:T(8,128)(2,1)S(1)} %constant_dynamic-update-slice_fusion.refs_0_), channel_id=1, source_target_pairs={{0,2},{1,3},{2,0},{3,1},{4,6},{5,7},{6,4},{7,5},{8,10},{9,11},{10,... | collective-permute-start | bytes 49160 | tf_op jit(solution)/shard_map/ppermute | solution.py:854
  41.1 20.2 %copy-start.22 = (bf16[4,8,256]{2,1,0:T(8,128)(2,1)}, bf16[4,8,256]{2,1,0:T(8,128)(2,1)S(1)}, u32[]{:S(2)}) copy-start(bf16[4,8,256]{2,1,0:T(8,128)(2,1)S(1)} %collective-permute-done.10.refs_2_) | copy-start | bytes 49156
  41.1 10.0 %copy-start.23 = (bf16[4,8,256]{2,1,0:T(8,128)(2,1)}, bf16[4,8,256]{2,1,0:T(8,128)(2,1)S(1)}, u32[]{:S(2)}) copy-start(bf16[4,8,256]{2,1,0:T(8,128)(2,1)S(1)} %collective-permute-done.9.refs_1_) | copy-start | bytes 49156
  41.2 23.9 %copy-start.15 = (bf16[4,4,24,768]{3,2,1,0:T(8,128)(2,1)}, bf16[4,4,24,768]{3,2,1,0:T(8,128)(2,1)S(1)}, u32[]{:S(2)}) copy-start(bf16[4,4,24,768]{3,2,1,0:T(8,128)(2,1)S(1)} %collective-permute-done.6.refs_1_) | copy-start | bytes 1769476
  41.2 23.8 %copy-start.16 = (bf16[4,4,24,768]{3,2,1,0:T(8,128)(2,1)}, bf16[4,4,24,768]{3,2,1,0:T(8,128)(2,1)S(1)}, u32[]{:S(2)}) copy-start(bf16[4,4,24,768]{3,2,1,0:T(8,128)(2,1)S(1)} %collective-permute-done.7.refs_2_) | copy-start | bytes 1769476
  41.2 23.8 %copy-start.18 = (bf16[4,4,24,768]{3,2,1,0:T(8,128)(2,1)}, bf16[4,4,24,768]{3,2,1,0:T(8,128)(2,1)S(1)}, u32[]{:S(2)}) copy-start(bf16[4,4,24,768]{3,2,1,0:T(8,128)(2,1)S(1)} %collective-permute-done.8.refs_5_) | copy-start | bytes 1769476
  41.2 20.1 %collective-permute-start.13 = (bf16[4,4,24,768]{3,2,1,0:T(8,128)(2,1)S(1)}, bf16[4,4,24,768]{3,2,1,0:T(8,128)(2,1)S(1)}, u32[]{:S(2)}, u32[]{:S(2)}) collective-permute-start(bf16[4,4,24,768]{3,2,1,0:T(8,128)(2,1)S(1)} %collective-permute-done.6.refs_1_), channel_id=1, source_target_pairs={{0,1},{1,0},{2,3},{3,2},{4,5},{5,4},{6,7},{7,6},{8,9},{9,8},{10,11... | collective-permute-start | bytes 1769480 | tf_op jit(solution)/shard_map/ppermute | solution.py:854
  51.1 10.2 %collective-permute-start.14 = (bf16[4,4,24,768]{3,2,1,0:T(8,128)(2,1)S(1)}, bf16[4,4,24,768]{3,2,1,0:T(8,128)(2,1)S(1)}, u32[]{:S(2)}, u32[]{:S(2)}) collective-permute-start(bf16[4,4,24,768]{3,2,1,0:T(8,128)(2,1)S(1)} %collective-permute-done.7.refs_2_), channel_id=1, source_target_pairs={{0,1},{1,0},{2,3},{3,2},{4,5},{5,4},{6,7},{7,6},{8,9},{9,8},{10,11... | collective-permute-start | bytes 1769480 | tf_op jit(solution)/shard_map/ppermute | solution.py:854
  51.6 9.1 %collective-permute-start.11 = (bf16[2,4,24,768]{3,2,1,0:T(8,128)(2,1)S(1)}, bf16[2,4,24,768]{3,2,1,0:T(8,128)(2,1)}, u32[]{:S(2)}, u32[]{:S(2)}) collective-permute-start(bf16[2,4,24,768]{3,2,1,0:T(8,128)(2,1)S(1)} %slice.66), channel_id=1, source_target_pairs={{0,2},{1,3},{2,0},{3,1},{4,6},{5,7},{6,4},{7,5},{8,10},{9,11},{10,... | collective-permute-start | bytes 884744 | tf_op jit(solution)/shard_map/ppermute | solution.py:854
  52.4 8.9 %collective-permute-start.12 = (bf16[2,4,24,768]{3,2,1,0:T(8,128)(2,1)S(1)}, bf16[2,4,24,768]{3,2,1,0:T(8,128)(2,1)}, u32[]{:S(2)}, u32[]{:S(2)}) collective-permute-start(bf16[2,4,24,768]{3,2,1,0:T(8,128)(2,1)S(1)} %slice.67), channel_id=1, source_target_pairs={{0,4},{1,5},{2,6},{3,7},{4,0},{5,1},{6,2},{7,3},{8,12},{9,13},{10,... | collective-permute-start | bytes 884744 | tf_op jit(solution)/shard_map/ppermute | solution.py:854
  54.1 6.7 %collective-permute-start.15 = (bf16[4,8,256]{2,1,0:T(8,128)(2,1)S(1)}, bf16[4,8,256]{2,1,0:T(8,128)(2,1)S(1)}, u32[]{:S(2)}, u32[]{:S(2)}) collective-permute-start(bf16[4,8,256]{2,1,0:T(8,128)(2,1)S(1)} %collective-permute-done.10.refs_2_), channel_id=1, source_target_pairs={{0,2},{1,3},{2,0},{3,1},{4,6},{5,7},{6,4},{7,5},{8,10},{9,11},{10,... | collective-permute-start | bytes 49160 | tf_op jit(solution)/shard_map/ppermute | solution.py:854
  61.3 3.7 %copy-start.19 = (bf16[4,4,24,768]{3,2,1,0:T(8,128)(2,1)}, bf16[4,4,24,768]{3,2,1,0:T(8,128)(2,1)S(1)}, u32[]{:S(2)}) copy-start(bf16[4,4,24,768]{3,2,1,0:T(8,128)(2,1)S(1)} %collective-permute-done.13.refs_6_) | copy-start | bytes 1769476
  61.3 3.7 %copy-start.20 = (bf16[4,4,24,768]{3,2,1,0:T(8,128)(2,1)}, bf16[4,4,24,768]{3,2,1,0:T(8,128)(2,1)S(1)}, u32[]{:S(2)}) copy-start(bf16[4,4,24,768]{3,2,1,0:T(8,128)(2,1)S(1)} %collective-permute-done.14.refs_7_) | copy-start | bytes 1769476
  61.3 3.7 collective-permute-start.16
  62.2 2.8 collective-permute-start.17
  65.0 5.0 %copy-start.6 = (s32[2,1,6]{2,1,0:T(1,128)S(1)}, s32[2,1,6]{2,1,0:T(1,128)}, u32[]{:S(2)}) copy-start(s32[2,1,6]{2,1,0:T(1,128)} %param.16) | copy-start | bytes 148
  249.7 9.2 %collective-permute-start.18 = (bf16[16,192,384]{2,1,0:T(8,128)(2,1)}, bf16[16,192,384]{2,1,0:T(8,128)(2,1)S(1)}, u32[]{:S(2)}, u32[]{:S(2)}) collective-permute-start(bf16[16,192,384]{2,1,0:T(8,128)(2,1)} %bitcast.94), channel_id=1, source_target_pairs={{0,1},{1,0},{2,3},{3,2},{4,5},{5,4},{6,7},{7,6},{8,9},{9,8},{10,11... | collective-permute-start | bytes 7077896 | tf_op jit(solution)/shard_map/ppermute | solution.py:854
  250.0 8.9 %collective-permute-start.19 = (bf16[16,192,384]{2,1,0:T(8,128)(2,1)}, bf16[16,192,384]{2,1,0:T(8,128)(2,1)}, u32[]{:S(2)}, u32[]{:S(2)}) collective-permute-start(bf16[16,192,384]{2,1,0:T(8,128)(2,1)} %bitcast.93), channel_id=1, source_target_pairs={{0,1},{1,0},{2,3},{3,2},{4,5},{5,4},{6,7},{7,6},{8,9},{9,8},{10,11... | collective-permute-start | bytes 7077896 | tf_op jit(solution)/shard_map/ppermute | solution.py:854
  250.2 8.6 %collective-permute-start.20 = (bf16[16,48,384]{2,1,0:T(8,128)(2,1)}, bf16[16,48,384]{2,1,0:T(8,128)(2,1)S(1)}, u32[]{:S(2)}, u32[]{:S(2)}) collective-permute-start(bf16[16,48,384]{2,1,0:T(8,128)(2,1)} %get-tuple-element.193), channel_id=1, source_target_pairs={{0,1},{1,0},{2,3},{3,2},{4,5},{5,4},{6,7},{7,6},{8,9},{9,8},{10,11... | collective-permute-start | bytes 1769480 | tf_op jit(solution)/shard_map/ppermute | solution.py:854
  250.6 8.3 %copy-start.2 = (bf16[16,4,48,384]{3,2,1,0:T(8,128)(2,1)S(1)}, bf16[16,4,48,384]{3,2,1,0:T(8,128)(2,1)}, u32[]{:S(2)}) copy-start(bf16[16,4,48,384]{3,2,1,0:T(8,128)(2,1)} %get-tuple-element.188) | copy-start | bytes 7077892
  250.6 8.3 %copy-start.3 = (bf16[3072,384]{1,0:T(8,128)(2,1)S(1)}, bf16[3072,384]{1,0:T(8,128)(2,1)}, u32[]{:S(2)}) copy-start(bf16[3072,384]{1,0:T(8,128)(2,1)} %get-tuple-element.189) | copy-start | bytes 7077892
  250.6 8.3 %copy-start.5 = (bf16[16,48,384]{2,1,0:T(8,128)(2,1)S(1)}, bf16[16,48,384]{2,1,0:T(8,128)(2,1)}, u32[]{:S(2)}) copy-start(bf16[16,48,384]{2,1,0:T(8,128)(2,1)} %get-tuple-element.190.refs_2_) | copy-start | bytes 1769476
  262.0 31.1 %collective-permute-start.21 = (bf16[2,2,432,384]{3,2,1,0:T(8,128)(2,1)S(1)}, bf16[2,2,432,384]{3,2,1,0:T(8,128)(2,1)S(1)}, u32[]{:S(2)}, u32[]{:S(2)}) collective-permute-start(bf16[2,2,432,384]{3,2,1,0:T(8,128)(2,1)S(1)} %get-tuple-element.207), channel_id=1, source_target_pairs={{0,2},{1,3},{2,0},{3,1},{4,6},{5,7},{6,4},{7,5},{8,10},{9,11},{10,... | collective-permute-start | bytes 3981320 | tf_op jit(solution)/shard_map/ppermute | solution.py:854
  263.2 30.1 %collective-permute-start.22 = (bf16[2,2,432,384]{3,2,1,0:T(8,128)(2,1)S(1)}, bf16[2,2,432,384]{3,2,1,0:T(8,128)(2,1)S(1)}, u32[]{:S(2)}, u32[]{:S(2)}) collective-permute-start(bf16[2,2,432,384]{3,2,1,0:T(8,128)(2,1)S(1)} %get-tuple-element.208), channel_id=1, source_target_pairs={{0,4},{1,5},{2,6},{3,7},{4,0},{5,1},{6,2},{7,3},{8,12},{9,13},{10,... | collective-permute-start | bytes 3981320 | tf_op jit(solution)/shard_map/ppermute | solution.py:854
  292.2 16.3 %collective-permute-start.25 = (bf16[16,144,384]{2,1,0:T(8,128)(2,1)}, bf16[16,144,384]{2,1,0:T(8,128)(2,1)S(1)}, u32[]{:S(2)}, u32[]{:S(2)}) collective-permute-start(bf16[16,144,384]{2,1,0:T(8,128)(2,1)} %bitcast.95), channel_id=1, source_target_pairs={{0,1},{1,0},{2,3},{3,2},{4,5},{5,4},{6,7},{7,6},{8,9},{9,8},{10,11... | collective-permute-start | bytes 5308424 | tf_op jit(solution)/shard_map/ppermute | solution.py:854
  294.5 15.1 %collective-permute-start.23 = (bf16[2,432,384]{2,1,0:T(8,128)(2,1)S(1)}, bf16[2,432,384]{2,1,0:T(8,128)(2,1)S(1)}, u32[]{:S(2)}, u32[]{:S(2)}) collective-permute-start(bf16[2,432,384]{2,1,0:T(8,128)(2,1)S(1)} %get-tuple-element.225), channel_id=1, source_target_pairs={{0,4},{1,5},{2,6},{3,7},{4,0},{5,1},{6,2},{7,3},{8,12},{9,13},{10,... | collective-permute-start | bytes 1990664 | tf_op jit(solution)/shard_map/ppermute | solution.py:854
  295.5 15.3 %collective-permute-start.24 = (bf16[2,432,384]{2,1,0:T(8,128)(2,1)S(1)}, bf16[2,432,384]{2,1,0:T(8,128)(2,1)S(1)}, u32[]{:S(2)}, u32[]{:S(2)}) collective-permute-start(bf16[2,432,384]{2,1,0:T(8,128)(2,1)S(1)} %get-tuple-element.226), channel_id=1, source_target_pairs={{0,2},{1,3},{2,0},{3,1},{4,6},{5,7},{6,4},{7,5},{8,10},{9,11},{10,... | collective-permute-start | bytes 1990664 | tf_op jit(solution)/shard_map/ppermute | solution.py:854
  296.1 9.7 %copy-start.7 = (f32[4,1,768]{2,1,0:T(1,128)S(1)}, f32[4,1,768]{2,1,0:T(1,128)}, u32[]{:S(2)}) copy-start(f32[4,1,768]{2,1,0:T(1,128)} %get-tuple-element.236.refs_6_) | copy-start | bytes 36868
  296.1 9.7 %copy-start.8 = (f32[3,1,768]{2,1,0:T(1,128)S(1)}, f32[3,1,768]{2,1,0:T(1,128)}, u32[]{:S(2)}) copy-start(f32[3,1,768]{2,1,0:T(1,128)} %get-tuple-element.232.refs_2_) | copy-start | bytes 27652
  296.1 9.7 %copy-start.11 = (f32[1,768]{1,0:T(1,128)S(1)}, f32[1,768]{1,0:T(1,128)}, u32[]{:S(2)}) copy-start(f32[1,768]{1,0:T(1,128)} %get-tuple-element.233.refs_3_) | copy-start | bytes 9220
  296.1 9.7 %copy-start.12 = (f32[1,768]{1,0:T(1,128)S(1)}, f32[1,768]{1,0:T(1,128)}, u32[]{:S(2)}) copy-start(f32[1,768]{1,0:T(1,128)} %get-tuple-element.237.refs_7_) | copy-start | bytes 9220
  296.1 9.7 %copy-start.13 = (f32[1,768]{1,0:T(1,128)S(1)}, f32[1,768]{1,0:T(1,128)}, u32[]{:S(2)}) copy-start(f32[1,768]{1,0:T(1,128)} %get-tuple-element.234.refs_4_) | copy-start | bytes 9220
  296.1 9.7 %copy-start.14 = (f32[1,768]{1,0:T(1,128)S(1)}, f32[1,768]{1,0:T(1,128)}, u32[]{:S(2)}) copy-start(f32[1,768]{1,0:T(1,128)} %get-tuple-element.235.refs_5_) | copy-start | bytes 9220
  305.8 7.1 %copy-start.4 = (bf16[16,3,48,384]{3,2,1,0:T(8,128)(2,1)S(1)}, bf16[16,3,48,384]{3,2,1,0:T(8,128)(2,1)}, u32[]{:S(2)}) copy-start(bf16[16,3,48,384]{3,2,1,0:T(8,128)(2,1)} %get-tuple-element.213) | copy-start | bytes 5308420
  311.7 15.1 %collective-permute-start.30 = (bf16[2,432,384]{2,1,0:T(8,128)(2,1)S(1)}, bf16[2,432,384]{2,1,0:T(8,128)(2,1)S(1)}, u32[]{:S(2)}, u32[]{:S(2)}) collective-permute-start(bf16[2,432,384]{2,1,0:T(8,128)(2,1)S(1)} %get-tuple-element.250), channel_id=1, source_target_pairs={{0,8},{1,9},{2,10},{3,11},{4,12},{5,13},{6,14},{7,15},{8,0},{9,1},... | collective-permute-start | bytes 1990664 | tf_op jit(solution)/shard_map/ppermute | solution.py:854
  313.8 10.5 %collective-permute-start.26 = (bf16[2,2,160,384]{3,2,1,0:T(8,128)(2,1)S(1)}, bf16[2,2,160,384]{3,2,1,0:T(8,128)(2,1)S(1)}, u32[]{:S(2)}, u32[]{:S(2)}) collective-permute-start(bf16[2,2,160,384]{3,2,1,0:T(8,128)(2,1)S(1)} %get-tuple-element.244), channel_id=1, source_target_pairs={{0,2},{1,3},{2,0},{3,1},{4,6},{5,7},{6,4},{7,5},{8,10},{9,11},{10,... | collective-permute-start | bytes 1474568 | tf_op jit(solution)/shard_map/ppermute | solution.py:854
  314.3 10.0 %collective-permute-start.27 = (bf16[2,2,160,384]{3,2,1,0:T(8,128)(2,1)S(1)}, bf16[2,2,160,384]{3,2,1,0:T(8,128)(2,1)S(1)}, u32[]{:S(2)}, u32[]{:S(2)}) collective-permute-start(bf16[2,2,160,384]{3,2,1,0:T(8,128)(2,1)S(1)} %get-tuple-element.245), channel_id=1, source_target_pairs={{0,4},{1,5},{2,6},{3,7},{4,0},{5,1},{6,2},{7,3},{8,12},{9,13},{10,... | collective-permute-start | bytes 1474568 | tf_op jit(solution)/shard_map/ppermute | solution.py:854
  325.1 5.1 %collective-permute-start.28 = (bf16[2,160,384]{2,1,0:T(8,128)(2,1)S(1)}, bf16[2,160,384]{2,1,0:T(8,128)(2,1)S(1)}, u32[]{:S(2)}, u32[]{:S(2)}) collective-permute-start(bf16[2,160,384]{2,1,0:T(8,128)(2,1)S(1)} %get-tuple-element.248), channel_id=1, source_target_pairs={{0,4},{1,5},{2,6},{3,7},{4,0},{5,1},{6,2},{7,3},{8,12},{9,13},{10,... | collective-permute-start | bytes 737288 | tf_op jit(solution)/shard_map/ppermute | solution.py:854
  326.5 5.0 %collective-permute-start.29 = (bf16[2,160,384]{2,1,0:T(8,128)(2,1)S(1)}, bf16[2,160,384]{2,1,0:T(8,128)(2,1)S(1)}, u32[]{:S(2)}, u32[]{:S(2)}) collective-permute-start(bf16[2,160,384]{2,1,0:T(8,128)(2,1)S(1)} %get-tuple-element.249), channel_id=1, source_target_pairs={{0,2},{1,3},{2,0},{3,1},{4,6},{5,7},{6,4},{7,5},{8,10},{9,11},{10,... | collective-permute-start | bytes 737288 | tf_op jit(solution)/shard_map/ppermute | solution.py:854
  332.2 7.0 %collective-permute-start.31 = (bf16[2,160,384]{2,1,0:T(8,128)(2,1)S(1)}, bf16[2,160,384]{2,1,0:T(8,128)(2,1)S(1)}, u32[]{:S(2)}, u32[]{:S(2)}) collective-permute-start(bf16[2,160,384]{2,1,0:T(8,128)(2,1)S(1)} %get-tuple-element.254), channel_id=1, source_target_pairs={{0,8},{1,9},{2,10},{3,11},{4,12},{5,13},{6,14},{7,15},{8,0},{9,1},... | collective-permute-start | bytes 737288 | tf_op jit(solution)/shard_map/ppermute | solution.py:854
  332.6 16.8 %collective-permute-start.34 = (bf16[432,384]{1,0:T(8,128)(2,1)S(1)}, bf16[432,384]{1,0:T(8,128)(2,1)S(1)}, u32[]{:S(2)}, u32[]{:S(2)}) collective-permute-start(bf16[432,384]{1,0:T(8,128)(2,1)S(1)} %fusion), channel_id=1, source_target_pairs={{0,16},{1,17},{2,18},{3,19},{4,20},{5,21},{6,22},{7,23},{8,24},{9,... | collective-permute-start | bytes 995336 | tf_op jit(solution)/shard_map/ppermute | solution.py:854
  339.3 21.8 %copy-start.1 = (bf16[48,2304]{1,0:T(8,128)(2,1)S(1)}, bf16[48,2304]{1,0:T(8,128)(2,1)}, u32[]{:S(2)}) copy-start(bf16[48,2304]{1,0:T(8,128)(2,1)} %param.20) | copy-start | bytes 663556
  339.3 15.7 %collective-permute-start.32 = (bf16[160,384]{1,0:T(8,128)(2,1)S(1)}, bf16[160,384]{1,0:T(8,128)(2,1)S(1)}, u32[]{:S(2)}, u32[]{:S(2)}) collective-permute-start(bf16[160,384]{1,0:T(8,128)(2,1)S(1)} %fusion.1), channel_id=1, source_target_pairs={{0,16},{1,17},{2,18},{3,19},{4,20},{5,21},{6,22},{7,23},{8,24},{9,... | collective-permute-start | bytes 368648 | tf_op jit(solution)/shard_map/ppermute | solution.py:854
  349.4 10.5 %collective-permute-start.35 = (f32[432,384]{1,0:T(8,128)S(1)}, f32[432,384]{1,0:T(8,128)S(1)}, u32[]{:S(2)}, u32[]{:S(2)}) collective-permute-start(f32[432,384]{1,0:T(8,128)S(1)} %bitcast_add_fusion.half_ref), channel_id=1, source_target_pairs={{0,1},{1,0},{2,3},{3,2},{4,5},{5,4},{6,7},{7,6},{8,9},{9,8},{10,11... | collective-permute-start | bytes 1990664 | tf_op jit(solution)/shard_map/ppermute | solution.py:854
  355.0 2.3 collective-permute-start.33
  (3 other events, 2.6 us)
Sparse Core Ops, SparseCore 0:
  11.6 88.6 all-gather.2
